TPU v7x, 128 devices: a whole 4x4x4 slice. The times are simulated.
128 devices in a mesh: ap: 32 (over z, x, core), ut: 4 (over y).
Axes of the slice: x: 4, y: 4, z: 4, core: 2. Of those that a mesh axis runs over, the one named last changes fastest.
Arguments:
- channel: bfloat16 [2, 2, 128, 64, 1024], P(None, None, 'ap', None, 'ut'), may hold values from -0.001953125 to 0.001953125
- start_precoder: bfloat16 [2, 2, 128, 64, 1024], P(None, None, 'ap', None, 'ut'), may hold values from -6 to 6
- cluster: int32 [128, 4], P('ap', 'ut'), may hold values 0 or 1
- noise: float32 [2, 1024], P(None, 'ut'), may hold values from 0.2 to 2
- penalty: float32 [128], P('ap'), may hold values from 5.9604646e-09 to 1.1920929e-07
- power: float32 [128], P('ap'), may hold values from 0.5 to 2
Outputs:
- precoder: bfloat16 [2, 2, 128, 64, 1024], P(None, None, 'ap', None, 'ut')
- user_weight: float32 [2, 1024], P(None, 'ut')
All inputs are finite; a program needn't handle non-finite values. No bound on the sum of `cluster` on one device may be relied on, other than what follows from the above.
Results may differ from a plain program's by a relative error of at most 0.003.
Values may be sent and summed in bfloat16 or wider, within the bound.
No kernel may reach another device: no remote copies, remote signals or barrier semaphores. Data moves between devices by JAX's collectives and lax.ppermute only.
A program may use at most 64 MiB of HBM per device.

v0:
```python
import jax
import jax.numpy as jnp
from jax import lax
from jax.sharding import Mesh
from jax.sharding import PartitionSpec as P

AP = ("ap_0", "ap_1", "ap_2")


def copy_for_each(value, axis):
    copies = jnp.broadcast_to(value, (lax.axis_size(axis), *value.shape))
    return lax.all_to_all(copies, axis, split_axis=0, concat_axis=0, tiled=True)


def in_order(pieces, dim):
    pieces = jnp.moveaxis(pieces, 0, dim)
    dims = pieces.shape
    return pieces.reshape(*dims[:dim], dims[dim] * dims[dim + 1], *dims[dim + 2 :])


def gathered_copies(value, axis, dim):
    pieces = copy_for_each(value, axis)
    return in_order(pieces, dim)


def in_blocks(value, dim, size):
    dims = value.shape
    pieces = value.reshape(*dims[:dim], size, dims[dim] // size, *dims[dim + 1 :])
    return jnp.moveaxis(pieces, dim, 0)


def sent_and_summed(value, axis, dim):
    size = lax.axis_size(axis)
    pieces = lax.all_to_all(in_blocks(value, dim, size), axis, 0, 0, tiled=True)
    return jnp.sum(pieces.astype(jnp.float32), axis=0)


def sum_in_two_steps(value, axes, dim):
    far, near = axes
    pieces = in_blocks(value, dim, lax.axis_size(far))
    nearer = sent_and_summed(pieces, near, dim + 1)
    arrived = lax.all_to_all(
        nearer.astype(jnp.bfloat16), far, split_axis=0, concat_axis=0, tiled=True
    )
    return arrived.astype(jnp.float32).sum(axis=0)


def of_everyone(value, axis):
    return copy_for_each(value, axis).sum(axis=0)


def packed_total(arrays, axis):
    ends = [0]
    for a in arrays:
        ends.append(ends[-1] + a.size)
    total = of_everyone(jnp.concatenate([a.ravel() for a in arrays]), axis)
    return tuple((total[b:e].reshape(a.shape) for a, b, e in zip(arrays, ends, ends[1:])))


def summed_on_arrival(value, axis, dim):
    size = lax.axis_size(axis)
    pieces = lax.all_to_all(in_blocks(value, dim, size), axis, 0, 0, tiled=True)
    return jnp.sum(pieces, axis=0)


def masked_channel(channel, cluster):
    tile_users = channel.shape[-1] // cluster.shape[1]
    served = jnp.repeat(cluster, tile_users, axis=1).astype(jnp.bfloat16)
    return channel * served[None, None, :, None, :]


def stacked_rows(field):
    blocks, parts, points, antennas, users = field.shape
    return field.reshape(blocks, parts * points * antennas, users)


def partner(field):
    plain = stacked_rows(field)
    turned = stacked_rows(jnp.stack([field[:, 1], -field[:, 0]], axis=1))
    return jnp.stack([plain, turned], axis=1)


def user_terms(total, signal, noise):
    level = total + noise
    strength = signal[:, 0] * signal[:, 0] + signal[:, 1] * signal[:, 1]
    weight = level / (level - strength)
    filter_re = signal[:, 0] / level
    filter_im = signal[:, 1] / level
    coeff = weight * (filter_re * filter_re + filter_im * filter_im)
    return (weight, coeff, filter_re * weight, filter_im * weight)


def covariance(served, coeff):
    real_part = served[:, 0].astype(jnp.float32)
    imag_part = served[:, 1].astype(jnp.float32)
    first = jnp.concatenate([real_part, imag_part], axis=2)
    second = jnp.concatenate([-imag_part, real_part], axis=2)
    scaled = coeff[:, None, None, :]
    result = jnp.einsum("samk,sank->samn", first * scaled, first, precision=lax.Precision.HIGHEST)
    return result + jnp.einsum(
        "samk,sank->samn", second * scaled, second, precision=lax.Precision.HIGHEST
    )


def transmit_rhs(served, scaled_re, scaled_im):
    real_part = served[:, 0].astype(jnp.float32)
    imag_part = served[:, 1].astype(jnp.float32)
    weight_re = scaled_re[:, None, None, :]
    weight_im = scaled_im[:, None, None, :]
    out_re = real_part * weight_re - imag_part * weight_im
    out_im = real_part * weight_im + imag_part * weight_re
    return jnp.concatenate([out_re, out_im], axis=2)


def cholesky_solve(system, rhs):
    factor = jnp.linalg.cholesky(system)
    middle = lax.linalg.triangular_solve(factor, rhs, left_side=True, lower=True)
    return lax.linalg.triangular_solve(factor, middle, left_side=True, lower=True, transpose_a=True)


def split_field(raw):
    antennas = raw.shape[2] // 2
    return jnp.stack([raw[:, :, :antennas], raw[:, :, antennas:]], axis=1)


def own_signal(served, precoder):
    chan_re = served[:, 0].astype(jnp.float32)
    chan_im = served[:, 1].astype(jnp.float32)
    prec_re = precoder[:, 0].astype(jnp.float32)
    prec_im = precoder[:, 1].astype(jnp.float32)
    signal_re = jnp.sum(chan_re * prec_re + chan_im * prec_im, axis=(1, 2))
    signal_im = jnp.sum(chan_re * prec_im - chan_im * prec_re, axis=(1, 2))
    return jnp.stack([signal_re, signal_im], axis=1)


def local(channel, start_precoder, cluster, noise, penalty, power):
    served = masked_channel(channel, cluster)
    rows = stacked_rows(served)
    user_count = channel.shape[-1]
    antennas = channel.shape[3]
    all_users = user_count * lax.axis_size("ut")
    ident = jnp.eye(2 * antennas, dtype=jnp.float32)
    precoder = start_precoder
    gain = jnp.einsum(
        "srk,scrj->sckj",
        rows,
        partner(gathered_copies(precoder, "ut", 4)),
        preferred_element_type=jnp.float32,
    )
    portion = sum_in_two_steps(gain.astype(jnp.bfloat16), (("ap_0", "ap_1"), "ap_2"), 3)
    local_total = jnp.sum(portion * portion, axis=(1, 3))
    local_signal = own_signal(served, precoder)
    total, signal = packed_total((local_total, local_signal), AP)
    weight, coeff, scaled_re, scaled_im = user_terms(total, signal, noise)
    partial_cov = covariance(served, coeff)
    rhs = transmit_rhs(served, scaled_re, scaled_im)
    share = summed_on_arrival(partial_cov, "ut", 1)
    owned = share.shape[1]
    own_penalty = lax.dynamic_slice_in_dim(penalty, lax.axis_index("ut") * owned, owned, 0)
    system = share + own_penalty[None, :, None, None] * ident
    inverse = cholesky_solve(system, jnp.broadcast_to(ident, system.shape))
    inverse = gathered_copies(inverse, "ut", 1)
    raw = jnp.einsum("samn,sank->samk", inverse, rhs, precision=lax.Precision.HIGHEST)
    field = split_field(raw)
    local_power = jnp.sum(field * field, axis=(0, 1, 3, 4))
    summed_power = of_everyone(local_power, "ut")
    mean_sq = summed_power / (2.0 * field.shape[0] * antennas * all_users)
    factor = jnp.sqrt(power / (mean_sq + 1e-06))
    precoder = (field * factor[None, None, :, None, None]).astype(jnp.bfloat16)
    return (precoder, weight)


def solution(mesh):
    split = Mesh(mesh.devices.reshape(4, 4, 2, mesh.shape["ut"]), ("ap_0", "ap_1", "ap_2", "ut"))
    placed = (
        P(None, None, AP, None, "ut"),
        P(None, None, AP, None, "ut"),
        P(AP, "ut"),
        P(None, "ut"),
        P(AP),
        P(AP),
    )
    return jax.shard_map(
        local,
        mesh=split,
        in_specs=placed,
        out_specs=(P(None, None, AP, None, "ut"), P(None, "ut")),
        check_vma=False,
    )
```

profile of v0, /device:TPU:1, one launch (start us, length us, event | category | flops | bytes accessed | tf_op | source)
XLA Modules:
  0.0 184.9 jit_solution(6422263625665017685)
XLA Ops:
  0.6 2.7 %broadcast_in_dim.14 = bf16[4,2,2,4,64,256]{5,4,3,2,1,0:T(8,128)(2,1)} broadcast(bf16[2,2,4,64,256]{4,3,2,1,0:T(8,128)(2,1)} %param.7), dimensions={1,2,3,4,5} | broadcast | bytes 2621440 | tf_op jit(solution)/shard_map/broadcast_in_dim | solution.py:11
  3.3 0.0 copy-start.4
  3.3 0.0 copy-start.1
  3.3 5.1 %all-to-all-start = ((bf16[4,2,2,4,64,256]{5,4,3,2,1,0:T(8,128)(2,1)}), bf16[4,2,2,4,64,256]{5,4,3,2,1,0:T(8,128)(2,1)S(1)}, u32[]{:S(2)}, u32[]{:S(2)}) async-start(bf16[4,2,2,4,64,256]{5,4,3,2,1,0:T(8,128)(2,1)} %broadcast_in_dim.14), calls=%async_computation | async-start | bytes 4194304 | tf_op jit(solution)/shard_map/all_to_all | solution.py:12
  8.4 0.0 copy-done.4
  8.4 0.0 copy-done.1
  8.4 0.1 copy_multiply_fusion
  8.6 25.3 %all-to-all-done = bf16[4,2,2,4,64,256]{5,4,3,2,1,0:T(8,128)(2,1)S(1)} async-done(((bf16[4,2,2,4,64,256]{5,4,3,2,1,0:T(8,128)(2,1)}), bf16[4,2,2,4,64,256]{5,4,3,2,1,0:T(8,128)(2,1)S(1)}, u32[]{:S(2)}, u32[]{:S(2)}) %all-to-all-start) | async-done | bytes 2097184 | tf_op jit(solution)/shard_map/all_to_all | solution.py:12
  33.9 0.3 copy.158
  34.2 0.1 fusion.59
  34.3 1.5 pad_maximum_fusion
  35.8 4.0 %copy.123 = bf16[2,1,512,1024]{2,3,1,0:T(8,128)(2,1)} copy(bf16[2,1,512,1024]{3,2,0,1:T(8,128)(2,1)} %bitcast.130) | data formatting | bytes 4194304 | tf_op jit(solution)/shard_map/stack;reshape | solution.py:80
  39.8 4.8 %copy.146 = bf16[2,2,4,64,4,256]{3,2,1,5,4,0:T(4,128)(2,1)} copy(bf16[2,2,4,64,4,256]{5,3,2,1,0,4:T(8,128)(2,1)S(1)} %bitcast.128) | data formatting | bytes 4194304 | tf_op jit(solution)/shard_map/stack;reshape;reshape | solution.py:80
  44.6 6.6 %reshape.144 = bf16[2,1,512,1024]{2,3,1,0:T(8,128)(2,1)S(1)} reshape(bf16[2,2,4,64,4,256]{3,2,1,5,4,0:T(4,128)(2,1)} %copy.146) | data formatting | bytes 4194304 | tf_op jit(solution)/shard_map/stack;reshape;reshape | solution.py:80
  51.2 2.8 %fusion.4 = bf16[2,2,1024,256]{3,2,1,0:T(8,128)(2,1)S(1)} fusion(bf16[2,512,256,1]{2,1,3,0:T(8,128)(2,1)S(1)} %bitcast.132, bf16[2,1,512,1024]{2,3,1,0:T(8,128)(2,1)} %copy.123, bf16[2,1,512,1024]{2,3,1,0:T(8,128)(2,1)S(1)} %reshape.144), kind=kOutput, calls=%fused_computation.6 | convolution fusion | flops 1076887552 | bytes 6815744 | tf_op jit(solution)/shard_map/srk,scrj->sckj/dot_general | solution.py:144
  54.0 0.2 copy.126
  54.2 6.9 %all_to_all.37 = bf16[2,16,2,2,256,32]{4,5,1,3,2,0:T(8,128)(2,1)S(1)} all-to-all(bf16[2,16,2,2,256,32]{4,5,1,3,2,0:T(8,128)(2,1)S(1)} %copy.126), channel_id=1, replica_groups=mesh['ap_0'=4,'ap_1'=4,'ap_2'=2,'ut'=4] {'ap_2'}, dimensions={0} | all-to-all | bytes 4194304 | tf_op jit(solution)/shard_map/all_to_all | solution.py:34
  61.1 1.8 reduce_sum.86
  62.9 0.0 copy-start
  62.9 2.4 %copy.128 = bf16[16,2,2,256,32]{3,4,2,1,0:T(8,128)(2,1)} copy(bf16[16,2,2,256,32]{3,4,0,2,1:T(8,128)(2,1)} %reduce_sum.86) | data formatting | bytes 2097152 | tf_op jit(solution)/shard_map/reduce_sum | solution.py:35
  65.2 0.0 copy-start.5
  65.2 7.7 %all-to-all-start.2 = ((bf16[16,2,2,256,32]{3,4,2,1,0:T(8,128)(2,1)}), bf16[16,2,2,256,32]{3,4,2,1,0:T(8,128)(2,1)S(1)}, u32[]{:S(2)}, u32[]{:S(2)}) async-start(bf16[16,2,2,256,32]{3,4,2,1,0:T(8,128)(2,1)} %copy.128), calls=%async_computation.2 | async-start | bytes 2097152 | tf_op jit(solution)/shard_map/all_to_all | solution.py:42
  73.0 0.0 copy-done
  73.0 0.2 fusion.30
  73.2 0.0 copy-start.3
  73.3 0.0 copy-done.5
  73.3 0.7 dynamic_slice.3
  74.0 15.4 %all-to-all-done.2 = bf16[16,2,2,256,32]{3,4,2,1,0:T(8,128)(2,1)S(1)} async-done(((bf16[16,2,2,256,32]{3,4,2,1,0:T(8,128)(2,1)}), bf16[16,2,2,256,32]{3,4,2,1,0:T(8,128)(2,1)S(1)}, u32[]{:S(2)}, u32[]{:S(2)}) %all-to-all-start.2) | async-done | bytes 1048608 | tf_op jit(solution)/shard_map/all_to_all | solution.py:42
  89.3 0.2 convert_reduce_fusion
  89.6 0.8 broadcast_in_dim.15
  90.4 5.6 %all-to-all-start.3 = ((f32[32,1,1536]{2,1,0:T(1,128)}), f32[32,1,1536]{2,1,0:T(1,128)S(1)}, u32[]{:S(2)}, u32[]{:S(2)}) async-start(f32[32,1,1536]{2,1,0:T(1,128)} %broadcast_in_dim.15), calls=%async_computation.3 | async-start | bytes 393216 | tf_op jit(solution)/shard_map/all_to_all | solution.py:12
  96.0 0.1 fusion.47
  96.1 8.2 %all-to-all-done.3 = f32[32,1,1536]{2,1,0:T(1,128)S(1)} async-done(((f32[32,1,1536]{2,1,0:T(1,128)}), f32[32,1,1536]{2,1,0:T(1,128)S(1)}, u32[]{:S(2)}, u32[]{:S(2)}) %all-to-all-start.3) | async-done | bytes 196640 | tf_op jit(solution)/shard_map/all_to_all | solution.py:12
  104.3 0.1 reduce_sum.91
  104.5 0.0 copy-done.3
  104.6 0.0 copy-start.2
  104.6 0.2 fusion.27
  104.8 1.1 fusion.7
  105.9 0.0 copy-done.2
  105.9 1.1 fusion.14
  107.1 0.8 copy.133
  107.9 3.7 %all-to-all-start.4 = ((f32[4,2,1,128,128]{4,3,1,2,0:T(8,128)}), f32[4,2,1,128,128]{4,3,1,2,0:T(8,128)S(1)}, u32[]{:S(2)}, u32[]{:S(2)}) async-start(f32[4,2,1,128,128]{4,3,1,2,0:T(8,128)} %copy.133), calls=%async_computation.4 | async-start | bytes 1048576 | tf_op jit(solution)/shard_map/all_to_all | solution.py:62
  111.6 0.7 fusion.50
  112.3 0.1 copy.136
  112.4 8.3 %all-to-all-done.4 = f32[4,2,1,128,128]{4,3,1,2,0:T(8,128)S(1)} async-done(((f32[4,2,1,128,128]{4,3,1,2,0:T(8,128)}), f32[4,2,1,128,128]{4,3,1,2,0:T(8,128)S(1)}, u32[]{:S(2)}, u32[]{:S(2)}) %all-to-all-start.4) | async-done | bytes 524320 | tf_op jit(solution)/shard_map/all_to_all | solution.py:62
  120.8 0.1 copy.135
  120.9 0.1 copy.137
  121.0 23.5 %custom-call.9 = f32[2,1,128,128]{3,2,1,0:T(8,128)S(1)} custom-call(f32[2,1,128,128]{3,2,1,0:T(8,128)S(1)} %fusion.46), custom_call_target="Cholesky" | custom-call | tf_op jit(solution)/shard_map/jit(cholesky)/cholesky | solution.py:116
  144.5 0.1 compare_reduce_fusion
  144.7 0.1 fusion.45
  144.8 19.7 %custom-call.10 = f32[2,1,1,128,128]{3,4,2,1,0:T(8,128)S(1)} custom-call(f32[2,1,1,128,128]{4,3,2,1,0:T(8,128)S(1)} %fusion.45), custom_call_target="InvertDiagBlocksLowerTriangular" | custom-call | tf_op jit(solution)/shard_map/triangular_solve | solution.py:118
  164.4 0.4 fusion.40
  164.8 0.3 fusion.38
  165.1 11.0 %all_to_all.38 = f32[4,2,1,128,128]{4,3,1,2,0:T(8,128)S(1)} all-to-all(f32[4,2,1,128,128]{4,3,1,2,0:T(8,128)S(1)} %broadcast_in_dim.30), channel_id=1, replica_groups=mesh['ap_0'=4,'ap_1'=4,'ap_2'=2,'ut'=4] {'ut'}, dimensions={0} | all-to-all | bytes 1048576 | tf_op jit(solution)/shard_map/all_to_all | solution.py:12
  176.1 1.0 fusion.23
  177.1 0.0 copy-start.6
  177.1 0.1 slice_bitcast_fusion.1
  177.2 0.2 multiply_reduce_fusion
  177.4 6.5 %all_to_all.39 = f32[4,1,4]{2,1,0:T(1,128)S(1)} all-to-all(f32[4,1,4]{2,1,0:T(1,128)S(1)} %broadcast_in_dim.31), channel_id=1, replica_groups=mesh['ap_0'=4,'ap_1'=4,'ap_2'=2,'ut'=4] {'ut'}, dimensions={0} | all-to-all | bytes 128 | tf_op jit(solution)/shard_map/all_to_all | solution.py:12
  183.9 0.0 copy-done.6
  183.9 0.2 multiply_convert_fusion
  184.1 0.8 copy.143
  (27 shorter events, 0.4 us)
Async XLA Ops:
  3.3 5.1 %copy-start.4 = (s32[4,1]{0,1:T(1,128)S(1)}, s32[4,1]{0,1:T(1,128)}, u32[]{:S(2)}) copy-start(s32[4,1]{0,1:T(1,128)} %param.8) | copy-start | bytes 52
  3.3 5.1 %copy-start.1 = (bf16[2,2,4,64,256]{4,3,2,1,0:T(8,128)(2,1)S(1)}, bf16[2,2,4,64,256]{4,3,2,1,0:T(8,128)(2,1)}, u32[]{:S(2)}) copy-start(bf16[2,2,4,64,256]{4,3,2,1,0:T(8,128)(2,1)} %param.6) | copy-start | bytes 1572868
  3.3 30.6 %all-to-all-start = ((bf16[4,2,2,4,64,256]{5,4,3,2,1,0:T(8,128)(2,1)}), bf16[4,2,2,4,64,256]{5,4,3,2,1,0:T(8,128)(2,1)S(1)}, u32[]{:S(2)}, u32[]{:S(2)}) async-start(bf16[4,2,2,4,64,256]{5,4,3,2,1,0:T(8,128)(2,1)} %broadcast_in_dim.14), calls=%async_computation | async-start | bytes 4194304 | tf_op jit(solution)/shard_map/all_to_all | solution.py:12
  62.9 10.1 %copy-start = (bf16[2,2,4,64,256]{4,3,2,1,0:T(8,128)(2,1)S(1)}, bf16[2,2,4,64,256]{4,3,2,1,0:T(8,128)(2,1)}, u32[]{:S(2)}) copy-start(bf16[2,2,4,64,256]{4,3,2,1,0:T(8,128)(2,1)} %param.7) | copy-start | bytes 1572868
  65.2 8.0 %copy-start.5 = (f32[4]{0:T(128)S(1)}, f32[4]{0:T(128)}, u32[]{:S(2)}) copy-start(f32[4]{0:T(128)} %param.10) | copy-start | bytes 52
  65.2 24.1 %all-to-all-start.2 = ((bf16[16,2,2,256,32]{3,4,2,1,0:T(8,128)(2,1)}), bf16[16,2,2,256,32]{3,4,2,1,0:T(8,128)(2,1)S(1)}, u32[]{:S(2)}, u32[]{:S(2)}) async-start(bf16[16,2,2,256,32]{3,4,2,1,0:T(8,128)(2,1)} %copy.128), calls=%async_computation.2 | async-start | bytes 2097152 | tf_op jit(solution)/shard_map/all_to_all | solution.py:42
  73.2 31.3 %copy-start.3 = (f32[2,256]{1,0:T(2,128)S(1)}, f32[2,256]{1,0:T(2,128)}, u32[]{:S(2)}) copy-start(f32[2,256]{1,0:T(2,128)} %param.9) | copy-start | bytes 6148
  90.4 14.0 %all-to-all-start.3 = ((f32[32,1,1536]{2,1,0:T(1,128)}), f32[32,1,1536]{2,1,0:T(1,128)S(1)}, u32[]{:S(2)}, u32[]{:S(2)}) async-start(f32[32,1,1536]{2,1,0:T(1,128)} %broadcast_in_dim.15), calls=%async_computation.3 | async-start | bytes 393216 | tf_op jit(solution)/shard_map/all_to_all | solution.py:12
  104.6 1.4 copy-start.2
  107.9 12.9 %all-to-all-start.4 = ((f32[4,2,1,128,128]{4,3,1,2,0:T(8,128)}), f32[4,2,1,128,128]{4,3,1,2,0:T(8,128)S(1)}, u32[]{:S(2)}, u32[]{:S(2)}) async-start(f32[4,2,1,128,128]{4,3,1,2,0:T(8,128)} %copy.133), calls=%async_computation.4 | async-start | bytes 1048576 | tf_op jit(solution)/shard_map/all_to_all | solution.py:62
  177.1 6.8 %copy-start.6 = (f32[4]{0:T(128)S(1)}, f32[4]{0:T(128)}, u32[]{:S(2)}) copy-start(f32[4]{0:T(128)} %param.11) | copy-start | bytes 52
where the time goes:
time: 187 us; the launch traced here: 185 us
  waiting for transfers between devices  57.2 us (31%)
  other arithmetic  49 us (26%)
  local copies, waits for them, and re-layouts  24.4 us (13%)
  blocking collectives  24.3 us (13%)
  starting transfers between devices  22.1 us (12%)
  matrix products  6.8 us (4%)
    all_to_all x2, waiting for transfers between devices, copy_for_each(): return lax.all_to_all(copies, axis, split_axis=0, concat_axis=0, tiled=True)  33.5 us
    another operation x4, other arithmetic, cholesky_solve(): factor = jnp.linalg.cholesky(system)  23.6 us
    another operation x3, other arithmetic, cholesky_solve(): lax.linalg.triangular_solve(factor, middle, left_side=True, lower=True, t...  19.8 us
    all_to_all x2, blocking collectives, copy_for_each(): return lax.all_to_all(copies, axis, split_axis=0, concat_axis=0, tiled=True)  17.4 us
    all_to_all x1, waiting for transfers between devices, sum_in_two_steps(): lax.all_to_all(nearer.astype(jnp.bfloat16), far, split_axis=0, concat_axi...  15.4 us
    another operation x3, local copies, waits for them, and re-layouts, partner(): return jnp.stack([plain, turned], axis=1)  15.3 us
    all_to_all x2, starting transfers between devices, copy_for_each(): return lax.all_to_all(copies, axis, split_axis=0, concat_axis=0, tiled=True)  10.8 us
    all_to_all x1, waiting for transfers between devices, summed_on_arrival(): pieces = lax.all_to_all(in_blocks(value, dim, size), axis, 0, 0, tiled=True)  8.33 us
  transfers between devices with their start and end apart: 4, of which 4 were waited for; matrix products, arithmetic and copies ran while one was open for 1% of the time, Pallas kernels for 0%

commit v1 on v0

v1 whole, which is shorter than its diff:
```python
import functools

import jax
import jax.numpy as jnp
from jax import lax
from jax.experimental import pallas as pl
from jax.experimental.pallas import tpu as pltpu
from jax.sharding import Mesh
from jax.sharding import PartitionSpec as P

AP = ("z", "x", "core")
CHIPS = ("z", "x")
EVERY = ("z", "x", "core", "ut")
SLOTS = (0, 1, 3, 2)
F32 = jnp.float32
BF16 = jnp.bfloat16
HIGHEST = lax.Precision.HIGHEST


def dot(a, b, dims, precision=None):
    return lax.dot_general(a, b, (dims, ((), ())), precision=precision, preferred_element_type=F32)


def three_parts(x):
    high = x.astype(BF16)
    rest = x - high.astype(F32)
    middle = rest.astype(BF16)
    low = (rest - middle.astype(F32)).astype(BF16)
    return high, middle, low


def iota(shape, dim):
    return lax.broadcasted_iota(jnp.int32, shape, dim)


def gain_kernel(core_ref, ht_ref, ha_ref, vt_ref, vb_ref, keep_ref, send_ref):
    core = core_ref[0]
    rows, users = ht_ref.shape
    half = rows // 2
    chips = keep_ref.shape[0]
    piece = users // chips
    vt, vb = vt_ref[...], vb_ref[...]
    first = core == 0
    keep_v = jnp.where(first, vt, vb)
    send_v = jnp.where(first, vb, vt)
    on_diag = iota((users, users), 0) == iota((users, users), 1)
    for v, out_ref, own in ((keep_v, keep_ref, first), (send_v, send_ref, jnp.logical_not(first))):
        turned = jnp.concatenate([v[half:], -v[:half]], axis=0)
        for tile, h_ref in enumerate((ht_ref, ha_ref)):
            h = h_ref[...]
            for part, w in enumerate((v, turned)):
                g = dot(h, w, ((0,), (0,)))
                if tile == 0:
                    g = jnp.where(jnp.logical_and(on_diag, own), 0.0, g)
                out_ref[:, part, tile] = g.reshape(chips, piece, users).astype(out_ref.dtype)


def partial_gains(core, ht, ha, vt, vb, chips):
    users = ht.shape[-1]
    shape = (chips, 2, 2, users // chips, users)
    vm = pl.BlockSpec(memory_space=pltpu.VMEM)
    return pl.pallas_call(
        gain_kernel,
        out_shape=(jax.ShapeDtypeStruct(shape, F32), jax.ShapeDtypeStruct(shape, BF16)),
        in_specs=[pl.BlockSpec(memory_space=pltpu.SMEM)] + [vm] * 4,
        out_specs=(vm, vm),
        name="gains",
    )(core, ht, ha, vt, vb)


def total_kernel(g0_ref, g1_ref, sig_ref, noise_ref, out_ref):
    chips, _, _, piece, _ = g0_ref.shape
    columns = []
    for g_ref in (g0_ref, g1_ref):
        total = None
        for part in range(2):
            g = g_ref[0, part].astype(F32)
            for chip in range(1, chips):
                g = g + g_ref[chip, part].astype(F32)
            square = jnp.sum(g * g, axis=-1, keepdims=True)
            total = square if total is None else total + square
        columns.append(total.reshape(2 * piece, 1))
    width = 4 * piece
    lane = iota((2 * piece, out_ref.shape[1]), 1)
    row = iota((2 * piece, out_ref.shape[1]), 0)
    line = jnp.zeros((1, out_ref.shape[1]), F32)
    for block in range(2):
        line = line + jnp.sum(jnp.where(lane == row + block * width, columns[block], 0.0), axis=0, keepdims=True)
    line = line + noise_ref[...] + sig_ref[...]
    out_ref[...] = jnp.broadcast_to(line, out_ref.shape)


def totals(g0, g1, sig, noise, devices):
    vm = pl.BlockSpec(memory_space=pltpu.VMEM)
    return pl.pallas_call(
        total_kernel,
        out_shape=jax.ShapeDtypeStruct((devices, 128), F32),
        in_specs=[vm] * 4,
        out_specs=vm,
        name="totals",
    )(g0, g1, sig, noise)


def user_lines(tile, r, users, chips):
    devices = r.shape[0]
    per_chip = devices // chips
    tiles = per_chip // 2
    piece = users // chips
    rows = tiles * chips
    slot = iota((rows, devices), 0) // chips
    chip = iota((rows, devices), 0) % chips
    wanted = tile ^ jnp.where(slot == 0, SLOTS[0], jnp.where(slot == 1, SLOTS[1], jnp.where(slot == 2, SLOTS[2], SLOTS[3])))
    source = iota((rows, devices), 1)
    same_chip = source // per_chip == chip
    own = jnp.logical_and(same_chip, source % tiles == wanted).astype(F32)
    mate = jnp.logical_and(same_chip, source % tiles == (wanted ^ 1)).astype(F32)
    from_own = dot(own, r, ((1,), (0,)), HIGHEST)
    from_mate = dot(mate, r, ((1,), (0,)), HIGHEST)
    keep = iota((rows, users), 1) // piece == iota((rows, users), 0) % chips

    def spread(values, block, quantity):
        start = block * 4 * piece + quantity * piece
        pick = iota((128, users), 0) == start + iota((128, users), 1) % piece
        return dot(values, pick.astype(F32), ((1,), (0,)), HIGHEST)

    def line(values):
        values = jnp.where(keep, values, 0.0).reshape(tiles, chips, users)
        return jnp.sum(values, axis=1, keepdims=True)

    blocks = []
    for block in range(2):
        rest = line(spread(from_own, block, 0) + spread(from_mate, block, 1))
        signal_re = line(spread(from_own, block, 2))
        signal_im = line(spread(from_own, block, 3))
        strength = signal_re * signal_re + signal_im * signal_im
        level = rest + strength
        blocks.append((level / rest, strength / (rest * level), signal_re / rest, signal_im / rest))
    return blocks


def solve_kernel(tile_ref, penalty_ref, power_ref, r_ref, *refs):
    h_refs = refs[:8]
    out_ref, weight_ref, line_ref, sys_ref, low_ref, scaled_ref, y_ref = refs[8:]
    blocks = 2
    _, points, antennas, users = h_refs[0].shape
    size = 2 * antennas
    chips = 16
    systems = blocks * points

    lines = user_lines(tile_ref[0], r_ref[...], users, chips)
    for block in range(blocks):
        weight, coeff, scaled_re, scaled_im = lines[block]
        weight_ref[block] = weight[0]
        line_ref[block, 0] = coeff
        line_ref[block, 1] = scaled_re
        line_ref[block, 2] = scaled_im

    lane = iota((antennas, size), 1)
    row = iota((antennas, size), 0)
    upper = jnp.where(lane < antennas, 1.0, -1.0).astype(F32)

    def channel(block, slot, point):
        h_ref = h_refs[slot * blocks + block]
        return jnp.concatenate([h_ref[0, point], h_ref[1, point]], axis=0)

    for block in range(blocks):

        def cover(point, carry, block=block):
            acc = jnp.zeros((3 * size, size), F32)
            for slot in range(4):
                x = channel(block, slot, point)
                weighted = x.astype(F32) * line_ref[block, 0, slot]
                parts = jnp.concatenate(three_parts(weighted), axis=0)
                acc = acc + dot(parts, x, ((1,), (1,)))
            p = acc[:size] + (acc[size : 2 * size] + acc[2 * size :])
            a = p[:antennas] * upper + pltpu.roll(p[antennas:], antennas, 1)
            a = a + jnp.where(lane == row, penalty_ref[point], 0.0)
            sys_ref[:, block * points + point, :] = a
            return carry

        lax.fori_loop(0, points, cover, 0)

    lane8 = iota((systems, size), 1)
    sign = jnp.where(lane8 < antennas, -1.0, 1.0).astype(F32)
    for k in range(antennas):
        pivot_row = sys_ref[k]
        inverse = 1.0 / pivot_row[:, k : k + 1]
        here = jnp.logical_or(lane8 == k, lane8 == antennas + k)
        done = jnp.logical_or(lane8 < k, jnp.logical_and(lane8 >= antennas, lane8 < antennas + k))
        one = jnp.where(lane8 == k, 1.0, 0.0)
        unit = jnp.where(here, one, pivot_row)
        low = jnp.where(done, pivot_row, one)
        low_ref[k] = low
        scaled_ref[k] = low * inverse
        if k + 1 < antennas:
            straight = unit * inverse
            turned = pltpu.roll(unit, antennas, 1) * sign * inverse
            for i in range(k + 1, antennas):
                w = sys_ref[i]
                f_re = w[:, k : k + 1]
                f_im = w[:, antennas + k : antennas + k + 1]
                sys_ref[i] = jnp.where(here, 0.0, w) - (f_re * straight + f_im * turned)

    sums = [None] * points

    for block in range(blocks):

        def apply(point, carry, block=block):
            n = block * points + point
            q = dot(scaled_ref[:, n, :], low_ref[:, n, :], ((0,), (0,)), HIGHEST)
            top = q[:antennas] * upper + pltpu.roll(q[antennas:], antennas, 1)
            bottom = pltpu.roll(top, antennas, 1) * (-upper)
            inverse = jnp.concatenate([top, bottom], axis=0)
            parts = jnp.concatenate(three_parts(inverse), axis=0)
            total = jnp.zeros((1, users), F32)
            for slot in range(4):
                x = channel(block, slot, point)
                acc = dot(parts, x, ((1,), (0,)))
                y = acc[:size] + (acc[size : 2 * size] + acc[2 * size :])
                w_re = line_ref[block, 1, slot]
                w_im = line_ref[block, 2, slot]
                total = total + jnp.sum(y * y, axis=0, keepdims=True) * (w_re * w_re + w_im * w_im)
                if slot == 0:
                    y_ref[n] = y
            power_sum = jnp.sum(total, axis=1, keepdims=True)
            return carry + jnp.where(iota((8, 1), 0) == point, power_sum, 0.0)

        part = lax.fori_loop(0, points, apply, jnp.zeros((8, 1), F32))
        sums[block] = part

    mean = (sums[0] + sums[1]) / (2.0 * blocks * antennas * 4 * users)
    for point in range(points):
        gain = jnp.sqrt(power_ref[point] / (mean[point : point + 1] + 1e-06))
        for block in range(blocks):
            y = y_ref[block * points + point]
            y_re, y_im = y[:antennas], y[antennas:]
            w_re = line_ref[block, 1, 0] * gain
            w_im = line_ref[block, 2, 0] * gain
            out_ref[block, 0, point] = (y_re * w_re - y_im * w_im).astype(out_ref.dtype)
            out_ref[block, 1, point] = (y_re * w_im + y_im * w_re).astype(out_ref.dtype)


def solve(tile, penalty, power, r, channels, out_shape):
    blocks, _, points, antennas, users = out_shape
    size = 2 * antennas
    vm = pl.BlockSpec(memory_space=pltpu.VMEM)
    sm = pl.BlockSpec(memory_space=pltpu.SMEM)
    return pl.pallas_call(
        solve_kernel,
        out_shape=(
            jax.ShapeDtypeStruct(out_shape, BF16),
            jax.ShapeDtypeStruct((blocks, 1, users), F32),
        ),
        in_specs=[sm] * 3 + [vm] * 9,
        out_specs=(vm, vm),
        scratch_shapes=[
            pltpu.VMEM((blocks, 3, 4, 1, users), F32),
            pltpu.VMEM((antennas, blocks * points, size), F32),
            pltpu.VMEM((antennas, blocks * points, size), F32),
            pltpu.VMEM((antennas, blocks * points, size), F32),
            pltpu.VMEM((blocks * points, size, users), F32),
        ],
        name="solve",
    )(tile, penalty, power, r, *channels)


def own_signal(served, precoder):
    chan_re = served[:, 0].astype(F32)
    chan_im = served[:, 1].astype(F32)
    prec_re = precoder[:, 0].astype(F32)
    prec_im = precoder[:, 1].astype(F32)
    signal_re = jnp.sum(chan_re * prec_re + chan_im * prec_im, axis=(1, 2))
    signal_im = jnp.sum(chan_re * prec_im - chan_im * prec_re, axis=(1, 2))
    return jnp.stack([signal_re, signal_im], axis=1)


def across(value, axis, mask):
    size = lax.axis_size(axis)
    return lax.ppermute(value, axis, [(i, i ^ mask) for i in range(size)])


def local(channel, start_precoder, cluster, noise, penalty, power):
    blocks, parts, points, antennas, users = channel.shape
    chips = lax.axis_size(CHIPS)
    devices = lax.axis_size(EVERY)
    piece = users // chips
    rows = parts * points * antennas
    core = lax.axis_index("core")
    tile = lax.axis_index("ut")
    chip = lax.axis_index(CHIPS)
    mask = cluster[:, 0].astype(BF16)[None, :, None, None]
    own = [channel[b] * mask for b in range(blocks)]
    served = jnp.stack(own)

    near = [across(own[b], "ut", 1) for b in range(blocks)]
    v_far = [across(start_precoder[b], "ut", 3) for b in range(blocks)]

    signal = own_signal(served, start_precoder)
    high = signal.astype(BF16)
    low = (signal - high.astype(F32)).astype(BF16)
    pairs = jnp.stack([high, low], axis=2).reshape(8, users)
    extra = jnp.broadcast_to(pairs, (chips, 8, users))

    summed = []
    for b in range(blocks):
        flat = [x.reshape(rows, users) for x in (own[b], near[b], start_precoder[b], v_far[b])]
        keep, send = partial_gains(core.reshape(1), *flat, chips)
        came = across(send, "core", 1)
        gains = (keep + came.astype(F32)).astype(BF16)
        if b == 0:
            gains = jnp.concatenate([gains.reshape(chips, 4 * piece, users), extra], axis=1)
        summed.append(lax.all_to_all(gains, CHIPS, 0, 0, tiled=True))

    far = [across(own[b], "ut", 3) for b in range(blocks)]
    far_near = [across(near[b], "ut", 3) for b in range(blocks)]

    g0 = summed[0][:, : 4 * piece].reshape(chips, 2, 2, piece, users)
    g1 = summed[1]
    sums = jnp.sum(summed[0][:, 4 * piece :].astype(F32), axis=0)
    sums = sums.reshape(blocks, 2, 2, users).sum(axis=2)
    mine = lax.dynamic_slice_in_dim(sums, chip * piece, piece, 2)
    sig_line = jnp.concatenate([jnp.zeros((blocks, 2, piece), F32), mine], axis=1).reshape(1, 128)
    noise_mine = lax.dynamic_slice_in_dim(noise, chip * piece, piece, 1)
    noise_mine = jnp.where(core == 0, noise_mine, 0.0)[:, None, :]
    noise_line = jnp.concatenate([noise_mine, jnp.zeros((blocks, 3, piece), F32)], axis=1).reshape(1, 128)
    line = totals(g0, g1, sig_line, noise_line, devices)
    r = lax.all_to_all(line, EVERY, 0, 0, tiled=True)

    channels = [x[b] for x in (own, near, far, far_near) for b in range(blocks)]
    precoder, weight = solve(tile.reshape(1), penalty, power, r, channels, channel.shape)
    return precoder, weight[:, 0]


def solution(mesh):
    split = Mesh(mesh.devices.reshape(4, 4, 2, mesh.shape["ut"]), EVERY)
    placed = (
        P(None, None, AP, None, "ut"),
        P(None, None, AP, None, "ut"),
        P(AP, "ut"),
        P(None, "ut"),
        P(AP),
        P(AP),
    )
    return jax.shard_map(
        local,
        mesh=split,
        in_specs=placed,
        out_specs=(P(None, None, AP, None, "ut"), P(None, "ut")),
        check_vma=False,
    )
```

time: 187 us -> 104 us (0.56)
  other arithmetic: 49 us -> 5.31 us
  waiting for transfers between devices: 57.2 us -> 26.5 us
  Pallas kernels: 0 us -> 29.6 us
  blocking collectives: 24.3 us -> 0 us
  local copies, waits for them, and re-layouts: 24.4 us -> 7.5 us
  starting transfers between devices: 22.1 us -> 33.8 us
  matrix products: 6.8 us -> 0 us
    another operation x8 -> x1, other arithmetic: 44.9 us -> 0.01 us  [local(): pairs = jnp.stack([high, low], axis=2).reshape(8, users)]
    all_to_all x4 -> x3, waiting for transfers between devices: 57.2 us -> 19.7 us  [the longest x2 13.2 us: local(): summed.append(lax.all_to_all(gains, CHIPS, 0, 0, tiled=True))]
    pallas_call x0 -> x4, Pallas kernels: none -> 29.6 us  [the longest x1 21.9 us: solve(): pl.pallas_call(solve_kernel, out_shape=(jax.ShapeDtypeStruct(out_shape, B...]
    all_to_all x3 -> x0, blocking collectives: 24.3 us -> none  [the longest x2 17.4 us: copy_for_each(): return lax.all_to_all(copies, axis, split_axis=0, concat_axis=0, tiled=True)]
    another operation x4 -> x0, local copies, waits for them, and re-layouts: 15.4 us -> none  [the longest x3 15.3 us: partner(): return jnp.stack([plain, turned], axis=1)]
    ppermute x0 -> x10, starting transfers between devices: none -> 14.3 us  [across(): return lax.ppermute(value, axis, [(i, i ^ mask) for i in range(size)])]
    ppermute x0 -> x10, waiting for transfers between devices: none -> 6.83 us  [across(): return lax.ppermute(value, axis, [(i, i ^ mask) for i in range(size)])]
    dot_general x4 -> x0, matrix products: 6.15 us -> none  [the longest x1 2.84 us: local(): jnp.einsum('srk,scrj->sckj', rows, partner(gathered_copies(precoder, 'ut'...]
  transfers between devices with their start and end apart: 4 -> 13, of which waited for: 4 -> 6; matrix products, arithmetic and copies ran while one was open for 1% -> 6% of each run, Pallas kernels for 0% -> 7%
where the time goes in v1:
time: 104 us
  starting transfers between devices  33.8 us (32%)
  Pallas kernels  29.6 us (28%)
  waiting for transfers between devices  26.5 us (25%)
  local copies, waits for them, and re-layouts  7.5 us (7%)
  other arithmetic  5.31 us (5%)
    pallas_call x1, Pallas kernels, solve(): pl.pallas_call(solve_kernel, out_shape=(jax.ShapeDtypeStruct(out_shape, B...  21.9 us
    ppermute x10, starting transfers between devices, across(): return lax.ppermute(value, axis, [(i, i ^ mask) for i in range(size)])  14.3 us
    all_to_all x2, waiting for transfers between devices, local(): summed.append(lax.all_to_all(gains, CHIPS, 0, 0, tiled=True))  13.2 us
    all_to_all x2, starting transfers between devices, local(): summed.append(lax.all_to_all(gains, CHIPS, 0, 0, tiled=True))  11.2 us
    all_to_all x1, starting transfers between devices, local(): r = lax.all_to_all(line, EVERY, 0, 0, tiled=True)  8.38 us
    ppermute x10, waiting for transfers between devices, across(): return lax.ppermute(value, axis, [(i, i ^ mask) for i in range(size)])  6.83 us
    all_to_all x1, waiting for transfers between devices, local(): r = lax.all_to_all(line, EVERY, 0, 0, tiled=True)  6.55 us
    pallas_call x2, Pallas kernels, partial_gains(): pl.pallas_call(gain_kernel, out_shape=(jax.ShapeDtypeStruct(shape, F32),...  5.62 us
  transfers between devices with their start and end apart: 13, of which 6 were waited for; matrix products, arithmetic and copies ran while one was open for 6% of the time, Pallas kernels for 7%

profile of v1, /device:TPU:1, one launch (start us, length us, event | category | flops | bytes accessed | tf_op | source)
XLA Modules:
  0.0 103.7 jit_solution(8832196073028066370)
XLA Ops:
  0.6 0.0 copy-start
  0.6 0.7 convert_bitcast_fusion
  1.4 1.1 %bitcast_multiply_fusion = (bf16[2,4,64,256]{3,2,1,0:T(8,128)(2,1)S(1)}, bf16[2,4,64,256]{3,2,1,0:T(8,128)(2,1)S(1)}) fusion(bf16[4]{0:T(256)(128)(2,1)S(1)} %convert_bitcast_fusion, bf16[2,2,4,64,256]{4,3,2,1,0:T(8,128)(2,1)} %param.6), kind=kLoop, calls=%fused_computation.15 | loop fusion | flops 262144 | bytes 1048584 | tf_op jit(solution)/shard_map/mul | solution.py:292
  2.5 0.0 copy-start.6
  2.5 0.0 copy-start.5
  2.5 0.0 copy-start.2
  2.5 2.2 %collective-permute-start = (bf16[2,4,64,256]{3,2,1,0:T(8,128)(2,1)S(1)}, bf16[2,4,64,256]{3,2,1,0:T(8,128)(2,1)S(1)}, u32[]{:S(2)}, u32[]{:S(2)}) collective-permute-start(bf16[2,4,64,256]{3,2,1,0:T(8,128)(2,1)S(1)} %get-tuple-element.17.refs_0_), channel_id=1, source_target_pairs={{0,1},{1,0},{2,3},{3,2},{4,5},{5,4},{6,7},{7,6},{8,9},{9,8},{10,11... | collective-permute-start | bytes 786440 | tf_op jit(solution)/shard_map/ppermute | solution.py:279
  4.7 0.0 copy-done
  4.7 0.9 slice_bitcast_fusion
  5.6 1.9 %collective-permute-start.1 = (bf16[2,4,64,256]{3,2,1,0:T(8,128)(2,1)S(1)}, bf16[2,4,64,256]{3,2,1,0:T(8,128)(2,1)S(1)}, u32[]{:S(2)}, u32[]{:S(2)}) collective-permute-start(bf16[2,4,64,256]{3,2,1,0:T(8,128)(2,1)S(1)} %get-tuple-element.23), channel_id=1, source_target_pairs={{0,3},{1,2},{2,1},{3,0},{4,7},{5,6},{6,5},{7,4},{8,11},{9,10},{10,... | collective-permute-start | bytes 786440 | tf_op jit(solution)/shard_map/ppermute | solution.py:279
  7.5 0.4 collective-permute-start.3
  7.9 0.6 collective-permute-start.4
  8.6 0.1 broadcast_multiply_fusion.1
  8.7 0.2 fusion.3
  8.9 0.1 mul.53
  9.0 0.1 mul.54
  9.1 0.9 bitcast_multiply_fusion.1
  10.0 0.4 collective-permute-done.refs_2_
  10.4 3.4 %collective-permute-done.1 = bf16[2,4,64,256]{3,2,1,0:T(8,128)(2,1)S(1)} collective-permute-done((bf16[2,4,64,256]{3,2,1,0:T(8,128)(2,1)S(1)}, bf16[2,4,64,256]{3,2,1,0:T(8,128)(2,1)S(1)}, u32[]{:S(2)}, u32[]{:S(2)}) %collective-permute-start.1) | collective-permute-done | bytes 262176 | tf_op jit(solution)/shard_map/ppermute | solution.py:279
  13.8 0.7 copy-done.17
  14.5 2.8 %gains.2 = (f32[16,2,2,16,256]{4,3,2,1,0:T(8,128)}, bf16[16,2,2,16,256]{4,3,2,1,0:T(8,128)(2,1)}) custom-call(s32[1]{0:T(128)} %bitcast.1.core_ref, bf16[512,256]{1,0:T(8,128)(2,1)} %get-tuple-element.29.ht_ref, bf16[512,256]{1,0:T(8,128)(2,1)} %bitcast.36, bf16[512,256]{1,0:T(8,128)(2,1)} %bitcast.39, bf16[512,256]{1,0:T(8,128)(2,1)} %bitcast.43), custom_call_target="tpu_custom_call" | custom-call | tf_op jit(solution)/shard_map/gains/pallas_call | solution.py:62
  17.3 3.2 %collective-permute-start.2 = (bf16[16,2,2,16,256]{4,3,2,1,0:T(8,128)(2,1)}, bf16[16,2,2,16,256]{4,3,2,1,0:T(8,128)(2,1)S(1)}, u32[]{:S(2)}, u32[]{:S(2)}) collective-permute-start(bf16[16,2,2,16,256]{4,3,2,1,0:T(8,128)(2,1)} %get-tuple-element.9), channel_id=1, source_target_pairs={{0,4},{4,0},{1,5},{5,1},{2,6},{6,2},{3,7},{7,3},{8,12},{12,8},{9,1... | collective-permute-start | bytes 1572872 | tf_op jit(solution)/shard_map/ppermute | solution.py:279
  20.6 0.0 collective-permute-done.3.refs_3_
  20.6 0.0 collective-permute-done.4
  20.6 0.0 copy-start.16
  20.6 0.7 copy-done.9
  21.3 0.1 copy-done.16
  21.4 2.8 %gains.3 = (f32[16,2,2,16,256]{4,3,2,1,0:T(8,128)}, bf16[16,2,2,16,256]{4,3,2,1,0:T(8,128)(2,1)}) custom-call(s32[1]{0:T(128)} %bitcast.1.core_ref, bf16[512,256]{1,0:T(8,128)(2,1)} %get-tuple-element.28.ht_ref, bf16[512,256]{1,0:T(8,128)(2,1)} %bitcast.37, bf16[512,256]{1,0:T(8,128)(2,1)} %bitcast.38, bf16[512,256]{1,0:T(8,128)(2,1)} %bitcast.42), custom_call_target="tpu_custom_call" | custom-call | tf_op jit(solution)/shard_map/gains/pallas_call | solution.py:62
  24.2 0.5 collective-permute-start.5
  24.7 0.0 collective-permute-done.2
  24.7 0.0 copy-done.3
  24.7 0.2 add_convert_fusion.1
  24.9 0.9 pad_maximum_fusion
  25.8 7.6 %all-to-all-start = ((bf16[16,72,256]{2,1,0:T(8,128)(2,1)}), bf16[16,72,256]{2,1,0:T(8,128)(2,1)S(1)}, u32[]{:S(2)}, u32[]{:S(2)}) async-start(bf16[16,72,256]{2,1,0:T(8,128)(2,1)} %pad_maximum_fusion), calls=%async_computation | async-start | bytes 1179648 | tf_op jit(solution)/shard_map/all_to_all | solution.py:312
  33.4 0.0 collective-permute-done.5
  33.4 0.0 copy-done.4
  33.4 1.0 add_convert_fusion
  34.4 10.7 %all-to-all-done = bf16[16,72,256]{2,1,0:T(8,128)(2,1)S(1)} async-done(((bf16[16,72,256]{2,1,0:T(8,128)(2,1)}), bf16[16,72,256]{2,1,0:T(8,128)(2,1)S(1)}, u32[]{:S(2)}, u32[]{:S(2)}) %all-to-all-start) | async-done | bytes 589856 | tf_op jit(solution)/shard_map/all_to_all | solution.py:312
  45.1 3.6 %all-to-all-start.1 = ((bf16[16,2,2,16,256]{4,3,2,1,0:T(8,128)(2,1)}), bf16[16,2,2,16,256]{4,3,2,1,0:T(8,128)(2,1)S(1)}, u32[]{:S(2)}, u32[]{:S(2)}) async-start(bf16[16,2,2,16,256]{4,3,2,1,0:T(8,128)(2,1)} %add_convert_fusion), calls=%async_computation.1 | async-start | bytes 1048576 | tf_op jit(solution)/shard_map/all_to_all | solution.py:312
  48.7 2.0 %collective-permute-start.6 = (bf16[2,4,64,256]{3,2,1,0:T(8,128)(2,1)S(1)}, bf16[2,4,64,256]{3,2,1,0:T(8,128)(2,1)S(1)}, u32[]{:S(2)}, u32[]{:S(2)}) collective-permute-start(bf16[2,4,64,256]{3,2,1,0:T(8,128)(2,1)S(1)} %get-tuple-element.17.refs_0_), channel_id=1, source_target_pairs={{0,3},{1,2},{2,1},{3,0},{4,7},{5,6},{6,5},{7,4},{8,11},{9,10},{10,... | collective-permute-start | bytes 786440 | tf_op jit(solution)/shard_map/ppermute | solution.py:279
  50.7 0.0 copy-done.5
  50.7 0.8 collective-permute-start.7
  51.5 0.1 dynamic-slice_select_fusion
  51.6 0.6 reshape.156.noise_ref
  52.2 1.9 %collective-permute-start.8 = (bf16[2,4,64,256]{3,2,1,0:T(8,128)(2,1)S(1)}, bf16[2,4,64,256]{3,2,1,0:T(8,128)(2,1)S(1)}, u32[]{:S(2)}, u32[]{:S(2)}) collective-permute-start(bf16[2,4,64,256]{3,2,1,0:T(8,128)(2,1)S(1)} %copy-done.8), channel_id=1, source_target_pairs={{0,3},{1,2},{2,1},{3,0},{4,7},{5,6},{6,5},{7,4},{8,11},{9,10},{10,... | collective-permute-start | bytes 786440 | tf_op jit(solution)/shard_map/ppermute | solution.py:279
  54.1 0.0 copy-done.10
  54.1 0.8 collective-permute-start.9
  54.9 0.1 constant_dynamic-slice_fusion
  55.0 0.6 reshape.155.sig_ref
  55.6 0.8 slice.44
  56.5 2.5 %all-to-all-done.1.g1_ref = bf16[16,2,2,16,256]{4,3,2,1,0:T(8,128)(2,1)S(1)} async-done(((bf16[16,2,2,16,256]{4,3,2,1,0:T(8,128)(2,1)}), bf16[16,2,2,16,256]{4,3,2,1,0:T(8,128)(2,1)S(1)}, u32[]{:S(2)}, u32[]{:S(2)}) %all-to-all-start.1) | async-done | bytes 524320 | tf_op jit(solution)/shard_map/all_to_all | solution.py:312
  58.9 0.8 copy-done.1
  59.7 2.1 %totals.1 = f32[128,128]{1,0:T(8,128)} custom-call(bf16[16,2,2,16,256]{4,3,2,1,0:T(8,128)(2,1)} %bitcast.34, bf16[16,2,2,16,256]{4,3,2,1,0:T(8,128)(2,1)} %copy-done.1, f32[1,128]{1,0:T(1,128)} %reshape.155.sig_ref, f32[1,128]{1,0:T(1,128)} %reshape.156.noise_ref), custom_call_target="tpu_custom_call" | custom-call | tf_op jit(solution)/shard_map/totals/pallas_call | solution.py:95
  61.8 8.4 %all-to-all-start.2 = ((f32[128,1,128]{2,1,0:T(1,128)}), f32[128,1,128]{2,1,0:T(1,128)S(1)}, u32[]{:S(2)}, u32[]{:S(2)}) async-start(f32[128,1,128]{2,1,0:T(1,128)} %bitcast.41), calls=%async_computation.2 | async-start | bytes 131072 | tf_op jit(solution)/shard_map/all_to_all | solution.py:327
  70.2 0.0 collective-permute-done.6.refs_4_
  70.2 0.0 collective-permute-done.7.refs_5_
  70.2 0.0 copy-start.12
  70.2 0.0 collective-permute-done.8.refs_6_
  70.3 3.0 %collective-permute-done.9.refs_7_ = bf16[2,4,64,256]{3,2,1,0:T(8,128)(2,1)S(1)} collective-permute-done((bf16[2,4,64,256]{3,2,1,0:T(8,128)(2,1)S(1)}, bf16[2,4,64,256]{3,2,1,0:T(8,128)(2,1)S(1)}, u32[]{:S(2)}, u32[]{:S(2)}) %collective-permute-start.9) | collective-permute-done | bytes 262176 | tf_op jit(solution)/shard_map/ppermute | solution.py:279
  73.3 6.6 %all-to-all-done.2 = f32[128,1,128]{2,1,0:T(1,128)S(1)} async-done(((f32[128,1,128]{2,1,0:T(1,128)}), f32[128,1,128]{2,1,0:T(1,128)S(1)}, u32[]{:S(2)}, u32[]{:S(2)}) %all-to-all-start.2) | async-done | bytes 65568 | tf_op jit(solution)/shard_map/all_to_all | solution.py:327
  79.9 0.0 copy-done.12
  79.9 0.6 copy-done.15
  80.5 21.9 %solve.1 = (bf16[2,2,4,64,256]{4,3,2,1,0:T(8,128)(2,1)}, f32[2,1,256]{2,1,0:T(1,128)}) custom-call(s32[1]{0:T(128)} %bitcast.tile_ref, f32[4]{0:T(128)} %penalty_ref.1, f32[4]{0:T(128)} %power_ref.1, f32[128,128]{1,0:T(8,128)} %bitcast.40, bf16[2,4,64,256]{3,2,1,0:T(8,128)(2,1)} %copy-done.6, bf16[2,4,64,256]{3,2,1,0:T(8,128)(2,1)} %copy-done.5, ...), custom_call_target="tpu_custom_call" | custom-call | tf_op jit(solution)/shard_map/solve/pallas_call | solution.py:248
  102.4 1.3 %copy.16 = f32[2,1,256]{2,0,1:T(2,128)} copy(f32[2,1,256]{2,1,0:T(1,128)} %get-tuple-element.13) | data formatting | bytes 4096
  (32 shorter events, 0.2 us)
Async XLA Ops:
  0.6 4.1 %copy-start = (bf16[2,2,4,64,256]{4,3,2,1,0:T(8,128)(2,1)S(1)}, bf16[2,2,4,64,256]{4,3,2,1,0:T(8,128)(2,1)}, u32[]{:S(2)}) copy-start(bf16[2,2,4,64,256]{4,3,2,1,0:T(8,128)(2,1)} %param.7) | copy-start | bytes 1572868
  2.5 46.2 %copy-start.6 = (bf16[2,4,64,256]{3,2,1,0:T(8,128)(2,1)}, bf16[2,4,64,256]{3,2,1,0:T(8,128)(2,1)S(1)}, u32[]{:S(2)}) copy-start(bf16[2,4,64,256]{3,2,1,0:T(8,128)(2,1)S(1)} %get-tuple-element.17.refs_0_) | copy-start | bytes 786436
  2.5 48.2 %copy-start.5 = (bf16[2,4,64,256]{3,2,1,0:T(8,128)(2,1)}, bf16[2,4,64,256]{3,2,1,0:T(8,128)(2,1)S(1)}, u32[]{:S(2)}) copy-start(bf16[2,4,64,256]{3,2,1,0:T(8,128)(2,1)S(1)} %get-tuple-element.16.refs_1_) | copy-start | bytes 786436
  2.5 6.0 %copy-start.2 = (bf16[2,2,4,64,256]{4,3,2,1,0:T(8,128)(2,1)S(1)}, bf16[2,2,4,64,256]{4,3,2,1,0:T(8,128)(2,1)}, u32[]{:S(2)}) copy-start(bf16[2,2,4,64,256]{4,3,2,1,0:T(8,128)(2,1)} %param.6) | copy-start | bytes 1572868
  2.5 7.9 %collective-permute-start = (bf16[2,4,64,256]{3,2,1,0:T(8,128)(2,1)S(1)}, bf16[2,4,64,256]{3,2,1,0:T(8,128)(2,1)S(1)}, u32[]{:S(2)}, u32[]{:S(2)}) collective-permute-start(bf16[2,4,64,256]{3,2,1,0:T(8,128)(2,1)S(1)} %get-tuple-element.17.refs_0_), channel_id=1, source_target_pairs={{0,1},{1,0},{2,3},{3,2},{4,5},{5,4},{6,7},{7,6},{8,9},{9,8},{10,11... | collective-permute-start | bytes 786440 | tf_op jit(solution)/shard_map/ppermute | solution.py:279
  5.6 8.1 %collective-permute-start.1 = (bf16[2,4,64,256]{3,2,1,0:T(8,128)(2,1)S(1)}, bf16[2,4,64,256]{3,2,1,0:T(8,128)(2,1)S(1)}, u32[]{:S(2)}, u32[]{:S(2)}) collective-permute-start(bf16[2,4,64,256]{3,2,1,0:T(8,128)(2,1)S(1)} %get-tuple-element.23), channel_id=1, source_target_pairs={{0,3},{1,2},{2,1},{3,0},{4,7},{5,6},{6,5},{7,4},{8,11},{9,10},{10,... | collective-permute-start | bytes 786440 | tf_op jit(solution)/shard_map/ppermute | solution.py:279
  7.5 13.0 %collective-permute-start.3 = (bf16[2,4,64,256]{3,2,1,0:T(8,128)(2,1)S(1)}, bf16[2,4,64,256]{3,2,1,0:T(8,128)(2,1)S(1)}, u32[]{:S(2)}, u32[]{:S(2)}) collective-permute-start(bf16[2,4,64,256]{3,2,1,0:T(8,128)(2,1)S(1)} %get-tuple-element.16.refs_1_), channel_id=1, source_target_pairs={{0,1},{1,0},{2,3},{3,2},{4,5},{5,4},{6,7},{7,6},{8,9},{9,8},{10,11... | collective-permute-start | bytes 786440 | tf_op jit(solution)/shard_map/ppermute | solution.py:279
  7.9 12.6 %collective-permute-start.4 = (bf16[2,4,64,256]{3,2,1,0:T(8,128)(2,1)S(1)}, bf16[2,4,64,256]{3,2,1,0:T(8,128)(2,1)S(1)}, u32[]{:S(2)}, u32[]{:S(2)}) collective-permute-start(bf16[2,4,64,256]{3,2,1,0:T(8,128)(2,1)S(1)} %get-tuple-element.20), channel_id=1, source_target_pairs={{0,3},{1,2},{2,1},{3,0},{4,7},{5,6},{6,5},{7,4},{8,11},{9,10},{10,... | collective-permute-start | bytes 786440 | tf_op jit(solution)/shard_map/ppermute | solution.py:279
  10.4 3.4 %copy-start.7 = (bf16[2,4,64,256]{3,2,1,0:T(8,128)(2,1)}, bf16[2,4,64,256]{3,2,1,0:T(8,128)(2,1)S(1)}, u32[]{:S(2)}) copy-start(bf16[2,4,64,256]{3,2,1,0:T(8,128)(2,1)S(1)} %collective-permute-done.refs_2_) | copy-start | bytes 786436
  13.8 0.7 copy-start.17
  17.3 7.4 %copy-start.3 = (f32[16,2,2,16,256]{4,3,2,1,0:T(8,128)S(1)}, f32[16,2,2,16,256]{4,3,2,1,0:T(8,128)}, u32[]{:S(2)}) copy-start(f32[16,2,2,16,256]{4,3,2,1,0:T(8,128)} %get-tuple-element.8) | copy-start | bytes 3145732
  17.3 7.4 %collective-permute-start.2 = (bf16[16,2,2,16,256]{4,3,2,1,0:T(8,128)(2,1)}, bf16[16,2,2,16,256]{4,3,2,1,0:T(8,128)(2,1)S(1)}, u32[]{:S(2)}, u32[]{:S(2)}) collective-permute-start(bf16[16,2,2,16,256]{4,3,2,1,0:T(8,128)(2,1)} %get-tuple-element.9), channel_id=1, source_target_pairs={{0,4},{4,0},{1,5},{5,1},{2,6},{6,2},{3,7},{7,3},{8,12},{12,8},{9,1... | collective-permute-start | bytes 1572872 | tf_op jit(solution)/shard_map/ppermute | solution.py:279
  20.6 0.7 copy-start.9
  20.6 0.8 copy-start.16
  24.2 9.2 %collective-permute-start.5 = (bf16[16,2,2,16,256]{4,3,2,1,0:T(8,128)(2,1)}, bf16[16,2,2,16,256]{4,3,2,1,0:T(8,128)(2,1)S(1)}, u32[]{:S(2)}, u32[]{:S(2)}) collective-permute-start(bf16[16,2,2,16,256]{4,3,2,1,0:T(8,128)(2,1)} %get-tuple-element.11), channel_id=1, source_target_pairs={{0,4},{4,0},{1,5},{5,1},{2,6},{6,2},{3,7},{7,3},{8,12},{12,8},{9,1... | collective-permute-start | bytes 1572872 | tf_op jit(solution)/shard_map/ppermute | solution.py:279
  24.9 8.5 %copy-start.4 = (f32[16,2,2,16,256]{4,3,2,1,0:T(8,128)S(1)}, f32[16,2,2,16,256]{4,3,2,1,0:T(8,128)}, u32[]{:S(2)}) copy-start(f32[16,2,2,16,256]{4,3,2,1,0:T(8,128)} %get-tuple-element.10) | copy-start | bytes 3145732
  25.8 19.4 %all-to-all-start = ((bf16[16,72,256]{2,1,0:T(8,128)(2,1)}), bf16[16,72,256]{2,1,0:T(8,128)(2,1)S(1)}, u32[]{:S(2)}, u32[]{:S(2)}) async-start(bf16[16,72,256]{2,1,0:T(8,128)(2,1)} %pad_maximum_fusion), calls=%async_computation | async-start | bytes 1179648 | tf_op jit(solution)/shard_map/all_to_all | solution.py:312
  34.4 17.1 %copy-start.18 = (f32[2,256]{1,0:T(2,128)S(1)}, f32[2,256]{1,0:T(2,128)}, u32[]{:S(2)}) copy-start(f32[2,256]{1,0:T(2,128)} %param.9) | copy-start | bytes 6148
  34.4 17.8 %copy-start.8 = (bf16[2,4,64,256]{3,2,1,0:T(8,128)(2,1)S(1)}, bf16[2,4,64,256]{3,2,1,0:T(8,128)(2,1)}, u32[]{:S(2)}) copy-start(bf16[2,4,64,256]{3,2,1,0:T(8,128)(2,1)} %copy-done.7) | copy-start | bytes 786436
  34.4 19.7 %copy-start.10 = (bf16[2,4,64,256]{3,2,1,0:T(8,128)(2,1)S(1)}, bf16[2,4,64,256]{3,2,1,0:T(8,128)(2,1)}, u32[]{:S(2)}) copy-start(bf16[2,4,64,256]{3,2,1,0:T(8,128)(2,1)} %copy-done.9) | copy-start | bytes 786436
  45.1 13.8 %all-to-all-start.1 = ((bf16[16,2,2,16,256]{4,3,2,1,0:T(8,128)(2,1)}), bf16[16,2,2,16,256]{4,3,2,1,0:T(8,128)(2,1)S(1)}, u32[]{:S(2)}, u32[]{:S(2)}) async-start(bf16[16,2,2,16,256]{4,3,2,1,0:T(8,128)(2,1)} %add_convert_fusion), calls=%async_computation.1 | async-start | bytes 1048576 | tf_op jit(solution)/shard_map/all_to_all | solution.py:312
  48.7 21.5 %collective-permute-start.6 = (bf16[2,4,64,256]{3,2,1,0:T(8,128)(2,1)S(1)}, bf16[2,4,64,256]{3,2,1,0:T(8,128)(2,1)S(1)}, u32[]{:S(2)}, u32[]{:S(2)}) collective-permute-start(bf16[2,4,64,256]{3,2,1,0:T(8,128)(2,1)S(1)} %get-tuple-element.17.refs_0_), channel_id=1, source_target_pairs={{0,3},{1,2},{2,1},{3,0},{4,7},{5,6},{6,5},{7,4},{8,11},{9,10},{10,... | collective-permute-start | bytes 786440 | tf_op jit(solution)/shard_map/ppermute | solution.py:279
  50.7 19.5 %collective-permute-start.7 = (bf16[2,4,64,256]{3,2,1,0:T(8,128)(2,1)S(1)}, bf16[2,4,64,256]{3,2,1,0:T(8,128)(2,1)S(1)}, u32[]{:S(2)}, u32[]{:S(2)}) collective-permute-start(bf16[2,4,64,256]{3,2,1,0:T(8,128)(2,1)S(1)} %get-tuple-element.16.refs_1_), channel_id=1, source_target_pairs={{0,3},{1,2},{2,1},{3,0},{4,7},{5,6},{6,5},{7,4},{8,11},{9,10},{10,... | collective-permute-start | bytes 786440 | tf_op jit(solution)/shard_map/ppermute | solution.py:279
  52.2 18.0 %collective-permute-start.8 = (bf16[2,4,64,256]{3,2,1,0:T(8,128)(2,1)S(1)}, bf16[2,4,64,256]{3,2,1,0:T(8,128)(2,1)S(1)}, u32[]{:S(2)}, u32[]{:S(2)}) collective-permute-start(bf16[2,4,64,256]{3,2,1,0:T(8,128)(2,1)S(1)} %copy-done.8), channel_id=1, source_target_pairs={{0,3},{1,2},{2,1},{3,0},{4,7},{5,6},{6,5},{7,4},{8,11},{9,10},{10,... | collective-permute-start | bytes 786440 | tf_op jit(solution)/shard_map/ppermute | solution.py:279
  54.1 19.2 %collective-permute-start.9 = (bf16[2,4,64,256]{3,2,1,0:T(8,128)(2,1)S(1)}, bf16[2,4,64,256]{3,2,1,0:T(8,128)(2,1)S(1)}, u32[]{:S(2)}, u32[]{:S(2)}) collective-permute-start(bf16[2,4,64,256]{3,2,1,0:T(8,128)(2,1)S(1)} %copy-done.10), channel_id=1, source_target_pairs={{0,3},{1,2},{2,1},{3,0},{4,7},{5,6},{6,5},{7,4},{8,11},{9,10},{10,... | collective-permute-start | bytes 786440 | tf_op jit(solution)/shard_map/ppermute | solution.py:279
  58.9 0.8 copy-start.1
  61.8 18.1 %all-to-all-start.2 = ((f32[128,1,128]{2,1,0:T(1,128)}), f32[128,1,128]{2,1,0:T(1,128)S(1)}, u32[]{:S(2)}, u32[]{:S(2)}) async-start(f32[128,1,128]{2,1,0:T(1,128)} %bitcast.41), calls=%async_computation.2 | async-start | bytes 131072 | tf_op jit(solution)/shard_map/all_to_all | solution.py:327
  70.2 9.7 %copy-start.11 = (bf16[2,4,64,256]{3,2,1,0:T(8,128)(2,1)}, bf16[2,4,64,256]{3,2,1,0:T(8,128)(2,1)S(1)}, u32[]{:S(2)}) copy-start(bf16[2,4,64,256]{3,2,1,0:T(8,128)(2,1)S(1)} %collective-permute-done.6.refs_4_) | copy-start | bytes 786436
  70.2 9.6 %copy-start.12 = (bf16[2,4,64,256]{3,2,1,0:T(8,128)(2,1)}, bf16[2,4,64,256]{3,2,1,0:T(8,128)(2,1)S(1)}, u32[]{:S(2)}) copy-start(bf16[2,4,64,256]{3,2,1,0:T(8,128)(2,1)S(1)} %collective-permute-done.7.refs_5_) | copy-start | bytes 786436
  70.2 9.6 %copy-start.13 = (bf16[2,4,64,256]{3,2,1,0:T(8,128)(2,1)}, bf16[2,4,64,256]{3,2,1,0:T(8,128)(2,1)S(1)}, u32[]{:S(2)}) copy-start(bf16[2,4,64,256]{3,2,1,0:T(8,128)(2,1)S(1)} %collective-permute-done.8.refs_6_) | copy-start | bytes 786436
  73.3 6.6 %copy-start.14 = (bf16[2,4,64,256]{3,2,1,0:T(8,128)(2,1)}, bf16[2,4,64,256]{3,2,1,0:T(8,128)(2,1)S(1)}, u32[]{:S(2)}) copy-start(bf16[2,4,64,256]{3,2,1,0:T(8,128)(2,1)S(1)} %collective-permute-done.9.refs_7_) | copy-start | bytes 786436
  79.9 0.6 copy-start.15

commit v2 on v1

v2 whole, which is shorter than its diff:
```python
import functools

import jax
import jax.numpy as jnp
from jax import lax
from jax.experimental import pallas as pl
from jax.experimental.pallas import tpu as pltpu
from jax.sharding import Mesh
from jax.sharding import PartitionSpec as P

AP = ("z", "x", "core")
CHIPS = ("z", "x")
EVERY = ("z", "x", "core", "ut")
SLOTS = (0, 1, 3, 2)
F32 = jnp.float32
BF16 = jnp.bfloat16
HIGHEST = lax.Precision.HIGHEST


def dot(a, b, dims, precision=None):
    return lax.dot_general(a, b, (dims, ((), ())), precision=precision, preferred_element_type=F32)


def three_parts(x):
    high = x.astype(BF16)
    rest = x - high.astype(F32)
    middle = rest.astype(BF16)
    low = (rest - middle.astype(F32)).astype(BF16)
    return high, middle, low


def iota(shape, dim):
    return lax.broadcasted_iota(jnp.int32, shape, dim)


def gain_kernel(core_ref, ht_ref, ha_ref, vt_ref, vb_ref, keep_ref, send_ref):
    core = core_ref[0]
    rows, users = ht_ref.shape
    half = rows // 2
    chips = keep_ref.shape[0]
    piece = users // chips
    vt, vb = vt_ref[...], vb_ref[...]
    first = core == 0
    keep_v = jnp.where(first, vt, vb)
    send_v = jnp.where(first, vb, vt)
    on_diag = iota((users, users), 0) == iota((users, users), 1)
    pairs = []
    for v in (keep_v, send_v):
        pairs += [v, jnp.concatenate([v[half:], -v[:half]], axis=0)]
    for tile, h_ref in enumerate((ht_ref, ha_ref)):
        h = jnp.transpose(h_ref[...])
        for at, v in enumerate(pairs):
            side, part = at // 2, at % 2
            own = first if side == 0 else jnp.logical_not(first)
            out_ref = keep_ref if side == 0 else send_ref
            g = dot(h, v, ((1,), (0,)))
            if tile == 0:
                g = jnp.where(jnp.logical_and(on_diag, own), 0.0, g)
            out_ref[:, part, tile] = g.reshape(chips, piece, users).astype(out_ref.dtype)


def partial_gains(core, ht, ha, vt, vb, chips):
    users = ht.shape[-1]
    shape = (chips, 2, 2, users // chips, users)
    vm = pl.BlockSpec(memory_space=pltpu.VMEM)
    return pl.pallas_call(
        gain_kernel,
        out_shape=(jax.ShapeDtypeStruct(shape, F32), jax.ShapeDtypeStruct(shape, BF16)),
        in_specs=[pl.BlockSpec(memory_space=pltpu.SMEM)] + [vm] * 4,
        out_specs=(vm, vm),
        name="gains",
        cost_estimate=pl.CostEstimate(flops=8 * users * users * ht.shape[0] * 2, bytes_accessed=4 << 20, transcendentals=0),
    )(core, ht, ha, vt, vb)


def combine_kernel(keep0_ref, keep1_ref, came0_ref, came1_ref, extra_ref, out_ref):
    chips, _, _, piece, users = keep0_ref.shape
    rows = 4 * piece
    for block, (keep_ref, came_ref) in enumerate(((keep0_ref, came0_ref), (keep1_ref, came1_ref))):
        g = keep_ref[...] + came_ref[...].astype(F32)
        out_ref[:, block * rows : (block + 1) * rows] = g.reshape(chips, rows, users).astype(BF16)
    out_ref[:, 2 * rows :] = jnp.broadcast_to(extra_ref[...][None], (chips,) + extra_ref.shape)


def combined(keeps, cames, extra):
    chips, _, _, piece, users = keeps[0].shape
    vm = pl.BlockSpec(memory_space=pltpu.VMEM)
    return pl.pallas_call(
        combine_kernel,
        out_shape=jax.ShapeDtypeStruct((chips, 8 * piece + extra.shape[0], users), BF16),
        in_specs=[vm] * 5,
        out_specs=vm,
        name="combine",
    )(*keeps, *cames, extra)


def total_kernel(where_ref, g_ref, noise_ref, out_ref):
    chip, core = where_ref[0], where_ref[1]
    chips, rows, users = g_ref.shape
    piece = (rows - 16) // 8
    lanes = out_ref.shape[1]
    width = 4 * piece
    lane = iota((2 * piece, lanes), 1)
    row = iota((2 * piece, lanes), 0)

    extra = g_ref[0, 8 * piece :].astype(F32)
    for source in range(1, chips):
        extra = extra + g_ref[source, 8 * piece :].astype(F32)
    signal = extra[:8] + extra[8:]
    noise = jnp.where(core == 0, noise_ref[...], 0.0)
    signal = jnp.concatenate([signal[:4], noise, noise], axis=0)
    pick = iota((users, lanes), 0) == chip * piece + iota((users, lanes), 1) % piece
    mine = dot(signal, pick.astype(F32), ((1,), (0,)), HIGHEST)
    group = iota((1, lanes), 1) // piece
    line = jnp.zeros((1, lanes), F32)
    for block in range(2):
        for part in range(2):
            at = block * 2 + part
            line = line + jnp.where(group == block * 4 + 2 + part, mine[at : at + 1], 0.0)
        line = line + jnp.where(group == block * 4, mine[4 + block : 5 + block], 0.0)

    for block in range(2):
        total = None
        for part in range(2):
            base = (block * 2 + part) * 2 * piece
            g = g_ref[0, base : base + 2 * piece].astype(F32)
            for source in range(1, chips):
                g = g + g_ref[source, base : base + 2 * piece].astype(F32)
            square = g * g
            total = square if total is None else total + square
        total = jnp.sum(total, axis=1, keepdims=True)
        line = line + jnp.sum(jnp.where(lane == row + block * width, total, 0.0), axis=0, keepdims=True)
    out_ref[...] = jnp.broadcast_to(line, out_ref.shape)


def totals(where, g, noise, devices):
    vm = pl.BlockSpec(memory_space=pltpu.VMEM)
    return pl.pallas_call(
        total_kernel,
        out_shape=jax.ShapeDtypeStruct((devices, 128), F32),
        in_specs=[pl.BlockSpec(memory_space=pltpu.SMEM), vm, vm],
        out_specs=vm,
        name="totals",
    )(where, g, noise)


def user_lines(r_ref, line_ref, weight_ref, tile):
    chips, _, lanes = r_ref.shape
    groups = 8
    piece = lanes // groups
    halves = chips // groups
    group = iota((8, lanes), 1) // piece
    sublane = iota((8, lanes), 0)
    rolled = [r_ref[0]] + [pltpu.roll(r_ref[p], p * piece % lanes, 1) if p % groups else r_ref[p] for p in range(1, chips)]

    def gathered(g, half):
        total = None
        for p in range(half * groups, (half + 1) * groups):
            term = jnp.where(group == (p + g) % groups, rolled[p], 0.0)
            total = term if total is None else total + term
        if g:
            total = pltpu.roll(total, lanes - g * piece, 1)
        return total + pltpu.roll(total, 4, 0)

    def line(g):
        return jnp.concatenate([gathered(g, half) for half in range(halves)], axis=1)

    for block in range(2):
        base = block * 4
        from_mate = line(base + 1)
        even = iota(from_mate.shape, 0) % 2 == 0
        swapped = jnp.where(even, pltpu.roll(from_mate, 7, 0), pltpu.roll(from_mate, 1, 0))
        rest = line(base) + swapped
        signal_re = line(base + 2)
        signal_im = line(base + 3)
        strength = signal_re * signal_re + signal_im * signal_im
        level = rest + strength
        line_ref[block, 0] = strength / (rest * level)
        line_ref[block, 1] = signal_re / rest
        line_ref[block, 2] = signal_im / rest
        line_ref[block, 3] = level / rest
        weight_ref[block] = line_ref[block, 3, pl.ds(tile, 1)]


def solve_kernel(tile_ref, penalty_ref, power_ref, r_ref, *refs):
    h_refs = refs[:8]
    out_ref, weight_ref, line_ref, sys_ref, low_ref, scaled_ref, y_ref, sem = refs[8:]
    blocks = 2
    _, points, antennas, users = h_refs[0].shape
    size = 2 * antennas
    systems = blocks * points
    tile = tile_ref[0]

    user_lines(r_ref, line_ref, weight_ref, tile)

    def line(block, which, slot):
        return line_ref[block, which, pl.ds(tile ^ SLOTS[slot], 1), :]

    def channel(block, slot, point):
        h_ref = h_refs[slot * blocks + block]
        return jnp.concatenate([h_ref[0, point], h_ref[1, point]], axis=0)

    lane = iota((antennas, size), 1)
    row = iota((antennas, size), 0)
    upper = jnp.where(lane < antennas, 1.0, -1.0).astype(F32)

    for block in range(blocks):
        for point in range(points):
            acc = None
            for slot in range(4):
                x = channel(block, slot, point)
                weighted = x.astype(F32) * line(block, 0, slot)
                parts = jnp.concatenate(three_parts(weighted), axis=0)
                term = dot(parts, x, ((1,), (1,)))
                acc = term if acc is None else acc + term
            p = acc[:size] + (acc[size : 2 * size] + acc[2 * size :])
            a = p[:antennas] * upper + pltpu.roll(p[antennas:], antennas, 1)
            a = a + jnp.where(lane == row, penalty_ref[point], 0.0)
            sys_ref[:, block * points + point, :] = a

    lane8 = iota((systems, size), 1)
    sign = jnp.where(lane8 < antennas, -1.0, 1.0).astype(F32)

    def pivot(k, pivot_row):
        inverse = 1.0 / pivot_row[:, k : k + 1]
        here = jnp.logical_or(lane8 == k, lane8 == antennas + k)
        done = jnp.logical_or(lane8 < k, jnp.logical_and(lane8 >= antennas, lane8 < antennas + k))
        one = jnp.where(lane8 == k, 1.0, 0.0)
        unit = jnp.where(here, one, pivot_row)
        low = jnp.where(done, pivot_row, one)
        low_ref[k] = low
        scaled_ref[k] = low * inverse
        return unit * inverse, (pltpu.roll(unit, antennas, 1) * sign) * inverse, here

    def update(k, i, straight, turned, here):
        w = sys_ref[i]
        f_re = w[:, k : k + 1]
        f_im = w[:, antennas + k : antennas + k + 1]
        return jnp.where(here, 0.0, w) - (f_re * straight + f_im * turned)

    now = pivot(0, sys_ref[0])
    for k in range(antennas - 1):
        later = pivot(k + 1, update(k, k + 1, *now))
        for i in range(k + 2, antennas):
            sys_ref[i] = update(k, i, *now)
        now = later

    copies = []
    for point in range(points):
        total = jnp.zeros((1, users), F32)
        for block in range(blocks):
            n = block * points + point
            q = dot(scaled_ref[:, n, :], low_ref[:, n, :], ((0,), (0,)), HIGHEST)
            top = q[:antennas] * upper + pltpu.roll(q[antennas:], antennas, 1)
            bottom = pltpu.roll(top, antennas, 1) * (-upper)
            parts = three_parts(jnp.concatenate([top, bottom], axis=0))
            for slot in range(4):
                depth = 3 if slot == 0 else 2
                x = channel(block, slot, point)
                y = dot(jnp.concatenate(parts[:depth], axis=1), jnp.concatenate([x] * depth, axis=0), ((1,), (0,)))
                w_re, w_im = line(block, 1, slot), line(block, 2, slot)
                total = total + jnp.sum(y * y, axis=0, keepdims=True) * (w_re * w_re + w_im * w_im)
                if slot == 0:
                    y_ref[block] = y
        mean = jnp.sum(total, axis=1, keepdims=True) / (2.0 * blocks * antennas * 4 * users)
        gain = jnp.sqrt(power_ref[point] / (mean + 1e-06))
        for block in range(blocks):
            y_re, y_im = y_ref[block, :antennas], y_ref[block, antennas:]
            w_re = line(block, 1, 0) * gain
            w_im = line(block, 2, 0) * gain
            out_ref[block, 0, point] = (y_re * w_re - y_im * w_im).astype(out_ref.dtype)
            out_ref[block, 1, point] = (y_re * w_im + y_im * w_re).astype(out_ref.dtype)


def solve(tile, penalty, power, r, channels, out_shape):
    blocks, _, points, antennas, users = out_shape
    size = 2 * antennas
    vm = pl.BlockSpec(memory_space=pltpu.VMEM)
    sm = pl.BlockSpec(memory_space=pltpu.SMEM)
    return pl.pallas_call(
        solve_kernel,
        out_shape=(
            jax.ShapeDtypeStruct(out_shape, BF16),
            jax.ShapeDtypeStruct((blocks, 1, users), F32),
        ),
        in_specs=[sm] * 3 + [vm] * 9,
        out_specs=(vm, vm),
        scratch_shapes=[
            pltpu.VMEM((blocks, 4, 8, users), F32),
            pltpu.VMEM((antennas, blocks * points, size), F32),
            pltpu.VMEM((antennas, blocks * points, size), F32),
            pltpu.VMEM((antennas, blocks * points, size), F32),
            pltpu.VMEM((blocks, size, users), F32),
            pltpu.SemaphoreType.DMA((1,)),
        ],
        name="solve",
    )(tile, penalty, power, r, *channels)


def own_signal(served, precoder):
    chan_re, chan_im = served[0].astype(F32), served[1].astype(F32)
    prec_re, prec_im = precoder[0].astype(F32), precoder[1].astype(F32)
    signal_re = jnp.sum(chan_re * prec_re + chan_im * prec_im, axis=(0, 1))
    signal_im = jnp.sum(chan_re * prec_im - chan_im * prec_re, axis=(0, 1))
    return jnp.stack([signal_re, signal_im])


def across(value, axis, mask):
    size = lax.axis_size(axis)
    return lax.ppermute(value, axis, [(i, i ^ mask) for i in range(size)])


def local(channel, start_precoder, cluster, noise, penalty, power):
    blocks, parts, points, antennas, users = channel.shape
    chips = lax.axis_size(CHIPS)
    devices = lax.axis_size(EVERY)
    piece = users // chips
    rows = parts * points * antennas
    core = lax.axis_index("core")
    tile = lax.axis_index("ut")
    chip = lax.axis_index(CHIPS)

    v_far = [across(start_precoder[b], "ut", 3) for b in range(blocks)]
    mask = cluster[:, 0].astype(BF16)[None, :, None, None]
    own = [channel[b] * mask for b in range(blocks)]
    near = [across(own[b], "ut", 1) for b in range(blocks)]
    far = [across(own[b], "ut", 3) for b in range(blocks)]
    far_near = [across(near[b], "ut", 3) for b in range(blocks)]

    signal = jnp.concatenate([own_signal(own[b], start_precoder[b]) for b in range(blocks)])
    high = lax.reduce_precision(signal, 8, 7)
    pad = jnp.zeros_like(signal)
    extra = jnp.concatenate([high, pad, signal - high, pad]).astype(BF16)

    keeps, cames = [], []
    for b in range(blocks):
        flat = [x.reshape(rows, users) for x in (own[b], near[b], start_precoder[b], v_far[b])]
        keep, send = partial_gains(core.reshape(1), *flat, chips)
        keeps.append(keep)
        cames.append(across(send, "core", 1))
    gains = combined(keeps, cames, extra)
    summed = lax.all_to_all(gains, CHIPS, 0, 0, tiled=True)
    line = totals(jnp.stack([chip, core]), summed, noise, devices)
    r = lax.all_to_all(line, EVERY, 0, 0, tiled=True).reshape(chips, devices // chips, 128)

    channels = [x[b] for x in (own, near, far, far_near) for b in range(blocks)]
    precoder, weight = solve(tile.reshape(1), penalty, power, r, channels, channel.shape)
    return precoder, weight[:, 0]


def solution(mesh):
    split = Mesh(mesh.devices.reshape(4, 4, 2, mesh.shape["ut"]), EVERY)
    placed = (
        P(None, None, AP, None, "ut"),
        P(None, None, AP, None, "ut"),
        P(AP, "ut"),
        P(None, "ut"),
        P(AP),
        P(AP),
    )
    return jax.shard_map(
        local,
        mesh=split,
        in_specs=placed,
        out_specs=(P(None, None, AP, None, "ut"), P(None, "ut")),
        check_vma=False,
    )
```

time: 104 us -> 95.5 us (0.918)
  starting transfers between devices: 33.8 us -> 28.6 us
  local copies, waits for them, and re-layouts: 7.5 us -> 6.3 us
  other arithmetic: 5.31 us -> 4.26 us
    all_to_all x3 -> x2, starting transfers between devices: 19.6 us -> 14.4 us  [the longest x1 7.73 us: local(): summed = lax.all_to_all(gains, CHIPS, 0, 0, tiled=True)]
    pallas_call x1, Pallas kernels: 21.9 us -> 17.6 us  [solve(): pl.pallas_call(solve_kernel, out_shape=(jax.ShapeDtypeStruct(out_shape, B...]
    pallas_call x0 -> x1, Pallas kernels: none -> 3.03 us  [combined(): pl.pallas_call(combine_kernel, out_shape=jax.ShapeDtypeStruct((chips, 8 *...]
    ppermute x10, waiting for transfers between devices: 6.83 us -> 4.99 us  [across(): return lax.ppermute(value, axis, [(i, i ^ mask) for i in range(size)])]
    all_to_all x3 -> x2, waiting for transfers between devices: 19.7 us -> 21.4 us  [the longest x1 11.9 us: local(): summed = lax.all_to_all(gains, CHIPS, 0, 0, tiled=True)]
    reshape x4 -> x0, local copies, waits for them, and re-layouts: 1.22 us -> none  [the longest x1 0.6 us: local(): jnp.concatenate([jnp.zeros((blocks, 2, piece), F32), mine], axis=1)]
    convert_element_type x3 -> x0, other arithmetic: 1.18 us -> none  [the longest x2 1.17 us: local(): gains = (keep + came.astype(F32)).astype(BF16)]
    unnamed x40 -> x37, local copies, waits for them, and re-layouts: 4.24 us -> 5.19 us
  transfers between devices with their start and end apart: 13 -> 12, of which waited for: 6 -> 5; matrix products, arithmetic and copies ran while one was open for 6% -> 4% of each run, Pallas kernels for 7% -> 8%
where the time goes in v2:
time: 95.5 us; the launch traced here: 95.1 us
  starting transfers between devices  28.6 us (30%)
  Pallas kernels  28.6 us (30%)
  waiting for transfers between devices  26.4 us (28%)
  local copies, waits for them, and re-layouts  6.3 us (7%)
  other arithmetic  4.26 us (4%)
    pallas_call x1, Pallas kernels, solve(): pl.pallas_call(solve_kernel, out_shape=(jax.ShapeDtypeStruct(out_shape, B...  17.6 us
    ppermute x10, starting transfers between devices, across(): return lax.ppermute(value, axis, [(i, i ^ mask) for i in range(size)])  14.2 us
    all_to_all x1, waiting for transfers between devices, local(): summed = lax.all_to_all(gains, CHIPS, 0, 0, tiled=True)  11.9 us
    all_to_all x1, waiting for transfers between devices, local(): lax.all_to_all(line, EVERY, 0, 0, tiled=True)  9.51 us
    all_to_all x1, starting transfers between devices, local(): summed = lax.all_to_all(gains, CHIPS, 0, 0, tiled=True)  7.73 us
    all_to_all x1, starting transfers between devices, local(): lax.all_to_all(line, EVERY, 0, 0, tiled=True)  6.67 us
    pallas_call x2, Pallas kernels, partial_gains(): pl.pallas_call(gain_kernel, out_shape=(jax.ShapeDtypeStruct(shape, F32),...  5.84 us
    unnamed x37, local copies, waits for them, and re-layouts  5.19 us
  transfers between devices with their start and end apart: 12, of which 5 were waited for; matrix products, arithmetic and copies ran while one was open for 4% of the time, Pallas kernels for 8%

profile of v2, /device:TPU:1, one launch (start us, length us, event | category | flops | bytes accessed | tf_op | source)
XLA Modules:
  0.0 95.1 jit_solution(15287903429927871998)
XLA Ops:
  0.6 0.0 copy-start.3
  0.6 0.7 convert_bitcast_fusion
  1.4 1.2 %bitcast_multiply_fusion = (bf16[2,4,64,256]{3,2,1,0:T(8,128)(2,1)S(1)}, bf16[2,4,64,256]{3,2,1,0:T(8,128)(2,1)S(1)}) fusion(bf16[4]{0:T(256)(128)(2,1)S(1)} %convert_bitcast_fusion, bf16[2,2,4,64,256]{4,3,2,1,0:T(8,128)(2,1)} %param.6), kind=kLoop, calls=%fused_computation.16 | loop fusion | flops 262144 | bytes 1048584 | tf_op jit(solution)/shard_map/mul | solution.py:325
  2.6 0.0 copy-start.2
  2.6 0.0 copy-start.1
  2.6 2.2 %collective-permute-start.2 = (bf16[2,4,64,256]{3,2,1,0:T(8,128)(2,1)S(1)}, bf16[2,4,64,256]{3,2,1,0:T(8,128)(2,1)S(1)}, u32[]{:S(2)}, u32[]{:S(2)}) collective-permute-start(bf16[2,4,64,256]{3,2,1,0:T(8,128)(2,1)S(1)} %get-tuple-element.20.refs_1_), channel_id=1, source_target_pairs={{0,1},{1,0},{2,3},{3,2},{4,5},{5,4},{6,7},{7,6},{8,9},{9,8},{10,11... | collective-permute-start | bytes 786440 | tf_op jit(solution)/shard_map/ppermute | solution.py:310
  4.8 0.0 copy-done.3
  4.8 0.9 slice_bitcast_fusion.4
  5.7 1.9 %collective-permute-start.3 = (bf16[2,4,64,256]{3,2,1,0:T(8,128)(2,1)S(1)}, bf16[2,4,64,256]{3,2,1,0:T(8,128)(2,1)S(1)}, u32[]{:S(2)}, u32[]{:S(2)}) collective-permute-start(bf16[2,4,64,256]{3,2,1,0:T(8,128)(2,1)S(1)} %get-tuple-element.22), channel_id=1, source_target_pairs={{0,3},{1,2},{2,1},{3,0},{4,7},{5,6},{6,5},{7,4},{8,11},{9,10},{10,... | collective-permute-start | bytes 786440 | tf_op jit(solution)/shard_map/ppermute | solution.py:310
  7.6 0.4 collective-permute-start
  8.0 0.6 collective-permute-start.1
  8.6 0.0 copy-done.4
  8.6 0.1 mul.52
  8.7 0.1 mul.53
  8.8 0.9 bitcast_multiply_fusion.1
  9.7 0.7 collective-permute-done.2.refs_3_
  10.4 3.4 %collective-permute-done.3 = bf16[2,4,64,256]{3,2,1,0:T(8,128)(2,1)S(1)} collective-permute-done((bf16[2,4,64,256]{3,2,1,0:T(8,128)(2,1)S(1)}, bf16[2,4,64,256]{3,2,1,0:T(8,128)(2,1)S(1)}, u32[]{:S(2)}, u32[]{:S(2)}) %collective-permute-start.3) | collective-permute-done | bytes 262176 | tf_op jit(solution)/shard_map/ppermute | solution.py:310
  13.8 0.0 copy-done.7
  13.8 0.7 copy-done.17
  14.5 2.9 %gains.3 = (f32[16,2,2,16,256]{4,3,2,1,0:T(8,128)}, bf16[16,2,2,16,256]{4,3,2,1,0:T(8,128)(2,1)}) custom-call(s32[1]{0:T(128)} %bitcast.2.core_ref, bf16[512,256]{1,0:T(8,128)(2,1)} %get-tuple-element.30.ht_ref, bf16[512,256]{1,0:T(8,128)(2,1)} %bitcast.78, bf16[512,256]{1,0:T(8,128)(2,1)} %bitcast.83, bf16[512,256]{1,0:T(8,128)(2,1)} %bitcast.90), custom_call_target="tpu_custom_call" | custom-call | flops 536870912 | bytes 4194304 | tf_op jit(solution)/shard_map/gains/pallas_call | solution.py:66
  17.4 3.2 %collective-permute-start.5 = (bf16[16,2,2,16,256]{4,3,2,1,0:T(8,128)(2,1)}, bf16[16,2,2,16,256]{4,3,2,1,0:T(8,128)(2,1)S(1)}, u32[]{:S(2)}, u32[]{:S(2)}) collective-permute-start(bf16[16,2,2,16,256]{4,3,2,1,0:T(8,128)(2,1)} %get-tuple-element.11), channel_id=1, source_target_pairs={{0,4},{4,0},{1,5},{5,1},{2,6},{6,2},{3,7},{7,3},{8,12},{12,8},{9,1... | collective-permute-start | bytes 1572872 | tf_op jit(solution)/shard_map/ppermute | solution.py:310
  20.7 0.0 collective-permute-done.refs_2_
  20.7 0.0 collective-permute-done.1
  20.7 0.0 copy-start.16
  20.7 0.7 copy-done.9
  21.4 0.1 copy-done.16
  21.5 2.9 %gains.2 = (f32[16,2,2,16,256]{4,3,2,1,0:T(8,128)}, bf16[16,2,2,16,256]{4,3,2,1,0:T(8,128)(2,1)}) custom-call(s32[1]{0:T(128)} %bitcast.2.core_ref, bf16[512,256]{1,0:T(8,128)(2,1)} %get-tuple-element.31.ht_ref, bf16[512,256]{1,0:T(8,128)(2,1)} %bitcast.79, bf16[512,256]{1,0:T(8,128)(2,1)} %bitcast.82, bf16[512,256]{1,0:T(8,128)(2,1)} %bitcast.89), custom_call_target="tpu_custom_call" | custom-call | flops 536870912 | bytes 4194304 | tf_op jit(solution)/shard_map/gains/pallas_call | solution.py:66
  24.4 0.5 collective-permute-start.4
  24.9 0.2 fusion.3
  25.1 0.6 pad_maximum_fusion.extra_ref
  25.7 0.0 collective-permute-done.5.came1_ref
  25.7 0.9 collective-permute-done.4.came0_ref
  26.6 0.0 copy-done.5
  26.6 0.8 copy-done.6
  27.4 3.0 %combine.1 = bf16[16,144,256]{2,1,0:T(8,128)(2,1)} custom-call(f32[16,2,2,16,256]{4,3,2,1,0:T(8,128)} %get-tuple-element.8.keep0_ref, f32[16,2,2,16,256]{4,3,2,1,0:T(8,128)} %get-tuple-element.9.keep1_ref, bf16[16,2,2,16,256]{4,3,2,1,0:T(8,128)(2,1)} %copy-done.6, bf16[16,2,2,16,256]{4,3,2,1,0:T(8,128)(2,1)} %copy-done.5, ...), custom_call_target="tpu_custom_call" | custom-call | tf_op jit(solution)/shard_map/combine/pallas_call | solution.py:88
  30.5 7.7 %all-to-all-start = ((bf16[16,144,256]{2,1,0:T(8,128)(2,1)}), bf16[16,144,256]{2,1,0:T(8,128)(2,1)S(1)}, u32[]{:S(2)}, u32[]{:S(2)}) async-start(bf16[16,144,256]{2,1,0:T(8,128)(2,1)} %combine.1), calls=%async_computation | async-start | bytes 2359296 | tf_op jit(solution)/shard_map/all_to_all | solution.py:342
  38.2 0.0 copy-done.2
  38.2 2.0 %collective-permute-start.6 = (bf16[2,4,64,256]{3,2,1,0:T(8,128)(2,1)S(1)}, bf16[2,4,64,256]{3,2,1,0:T(8,128)(2,1)S(1)}, u32[]{:S(2)}, u32[]{:S(2)}) collective-permute-start(bf16[2,4,64,256]{3,2,1,0:T(8,128)(2,1)S(1)} %get-tuple-element.21.refs_0_), channel_id=1, source_target_pairs={{0,3},{1,2},{2,1},{3,0},{4,7},{5,6},{6,5},{7,4},{8,11},{9,10},{10,... | collective-permute-start | bytes 786440 | tf_op jit(solution)/shard_map/ppermute | solution.py:310
  40.2 0.0 copy-done.1
  40.2 0.8 collective-permute-start.7
  41.0 0.0 copy-done.10
  41.0 1.9 %collective-permute-start.8 = (bf16[2,4,64,256]{3,2,1,0:T(8,128)(2,1)S(1)}, bf16[2,4,64,256]{3,2,1,0:T(8,128)(2,1)S(1)}, u32[]{:S(2)}, u32[]{:S(2)}) collective-permute-start(bf16[2,4,64,256]{3,2,1,0:T(8,128)(2,1)S(1)} %copy-done.10), channel_id=1, source_target_pairs={{0,3},{1,2},{2,1},{3,0},{4,7},{5,6},{6,5},{7,4},{8,11},{9,10},{10,... | collective-permute-start | bytes 786440 | tf_op jit(solution)/shard_map/ppermute | solution.py:310
  42.9 0.0 copy-done.8
  42.9 0.8 collective-permute-start.9
  43.6 0.6 pad_add_fusion.where_ref
  44.2 11.9 %all-to-all-done.g_ref = bf16[16,144,256]{2,1,0:T(8,128)(2,1)S(1)} async-done(((bf16[16,144,256]{2,1,0:T(8,128)(2,1)}), bf16[16,144,256]{2,1,0:T(8,128)(2,1)S(1)}, u32[]{:S(2)}, u32[]{:S(2)}) %all-to-all-start) | async-done | bytes 1179680 | tf_op jit(solution)/shard_map/all_to_all | solution.py:342
  56.2 1.0 %copy-done = bf16[16,144,256]{2,1,0:T(8,128)(2,1)} copy-done((bf16[16,144,256]{2,1,0:T(8,128)(2,1)}, bf16[16,144,256]{2,1,0:T(8,128)(2,1)S(1)}, u32[]{:S(2)}) %copy-start) | copy-done | bytes 1179672
  57.2 2.2 %totals.1 = f32[128,128]{1,0:T(8,128)} custom-call(s32[2]{0:T(128)} %pad_add_fusion.where_ref, bf16[16,144,256]{2,1,0:T(8,128)(2,1)} %copy-done, f32[2,256]{1,0:T(2,128)} %noise_ref.1), custom_call_target="tpu_custom_call" | custom-call | tf_op jit(solution)/shard_map/totals/pallas_call | solution.py:138
  59.4 6.7 %all-to-all-start.1 = ((f32[128,1,128]{2,1,0:T(1,128)}), f32[128,1,128]{2,1,0:T(1,128)S(1)}, u32[]{:S(2)}, u32[]{:S(2)}) async-start(f32[128,1,128]{2,1,0:T(1,128)} %bitcast.81), calls=%async_computation.1 | async-start | bytes 131072 | tf_op jit(solution)/shard_map/all_to_all | solution.py:344
  66.1 0.0 collective-permute-done.6.refs_4_
  66.1 0.0 copy-start.11
  66.1 0.0 collective-permute-done.7.refs_5_
  66.1 0.0 copy-start.12
  66.1 0.0 collective-permute-done.8.refs_6_
  66.1 0.0 copy-start.13
  66.1 0.0 collective-permute-done.9.refs_7_
  66.2 0.0 copy-start.14
  66.2 9.5 %all-to-all-done.1 = f32[128,1,128]{2,1,0:T(1,128)S(1)} async-done(((f32[128,1,128]{2,1,0:T(1,128)}), f32[128,1,128]{2,1,0:T(1,128)S(1)}, u32[]{:S(2)}, u32[]{:S(2)}) %all-to-all-start.1) | async-done | bytes 65568 | tf_op jit(solution)/shard_map/all_to_all | solution.py:344
  75.7 0.0 copy-done.11
  75.7 0.0 copy-done.12
  75.7 0.0 copy-done.13
  75.7 0.6 copy-done.15
  76.3 17.6 %solve.1 = (bf16[2,2,4,64,256]{4,3,2,1,0:T(8,128)(2,1)}, f32[2,1,256]{2,1,0:T(1,128)}) custom-call(s32[1]{0:T(128)} %bitcast.tile_ref, f32[4]{0:T(128)} %penalty_ref.1, f32[4]{0:T(128)} %power_ref.1, f32[16,8,128]{2,1,0:T(8,128)} %bitcast.80, bf16[2,4,64,256]{3,2,1,0:T(8,128)(2,1)} %copy-done.2, bf16[2,4,64,256]{3,2,1,0:T(8,128)(2,1)} %copy-done.1, ...), custom_call_target="tpu_custom_call" | custom-call | tf_op jit(solution)/shard_map/solve/pallas_call | solution.py:280
  93.9 1.2 %copy.11 = f32[2,1,256]{2,0,1:T(2,128)} copy(f32[2,1,256]{2,1,0:T(1,128)} %get-tuple-element.13) | data formatting | bytes 4096
  (14 shorter events, 0.1 us)
Async XLA Ops:
  0.6 4.1 %copy-start.3 = (bf16[2,2,4,64,256]{4,3,2,1,0:T(8,128)(2,1)S(1)}, bf16[2,2,4,64,256]{4,3,2,1,0:T(8,128)(2,1)}, u32[]{:S(2)}) copy-start(bf16[2,2,4,64,256]{4,3,2,1,0:T(8,128)(2,1)} %param.7) | copy-start | bytes 1572868
  1.4 7.2 %copy-start.4 = (bf16[2,2,4,64,256]{4,3,2,1,0:T(8,128)(2,1)S(1)}, bf16[2,2,4,64,256]{4,3,2,1,0:T(8,128)(2,1)}, u32[]{:S(2)}) copy-start(bf16[2,2,4,64,256]{4,3,2,1,0:T(8,128)(2,1)} %param.6) | copy-start | bytes 1572868
  2.6 35.6 %copy-start.2 = (bf16[2,4,64,256]{3,2,1,0:T(8,128)(2,1)}, bf16[2,4,64,256]{3,2,1,0:T(8,128)(2,1)S(1)}, u32[]{:S(2)}) copy-start(bf16[2,4,64,256]{3,2,1,0:T(8,128)(2,1)S(1)} %get-tuple-element.21.refs_0_) | copy-start | bytes 786436
  2.6 37.6 %copy-start.1 = (bf16[2,4,64,256]{3,2,1,0:T(8,128)(2,1)}, bf16[2,4,64,256]{3,2,1,0:T(8,128)(2,1)S(1)}, u32[]{:S(2)}) copy-start(bf16[2,4,64,256]{3,2,1,0:T(8,128)(2,1)S(1)} %get-tuple-element.20.refs_1_) | copy-start | bytes 786436
  2.6 7.9 %collective-permute-start.2 = (bf16[2,4,64,256]{3,2,1,0:T(8,128)(2,1)S(1)}, bf16[2,4,64,256]{3,2,1,0:T(8,128)(2,1)S(1)}, u32[]{:S(2)}, u32[]{:S(2)}) collective-permute-start(bf16[2,4,64,256]{3,2,1,0:T(8,128)(2,1)S(1)} %get-tuple-element.20.refs_1_), channel_id=1, source_target_pairs={{0,1},{1,0},{2,3},{3,2},{4,5},{5,4},{6,7},{7,6},{8,9},{9,8},{10,11... | collective-permute-start | bytes 786440 | tf_op jit(solution)/shard_map/ppermute | solution.py:310
  5.7 8.1 %collective-permute-start.3 = (bf16[2,4,64,256]{3,2,1,0:T(8,128)(2,1)S(1)}, bf16[2,4,64,256]{3,2,1,0:T(8,128)(2,1)S(1)}, u32[]{:S(2)}, u32[]{:S(2)}) collective-permute-start(bf16[2,4,64,256]{3,2,1,0:T(8,128)(2,1)S(1)} %get-tuple-element.22), channel_id=1, source_target_pairs={{0,3},{1,2},{2,1},{3,0},{4,7},{5,6},{6,5},{7,4},{8,11},{9,10},{10,... | collective-permute-start | bytes 786440 | tf_op jit(solution)/shard_map/ppermute | solution.py:310
  7.6 13.1 %collective-permute-start = (bf16[2,4,64,256]{3,2,1,0:T(8,128)(2,1)S(1)}, bf16[2,4,64,256]{3,2,1,0:T(8,128)(2,1)S(1)}, u32[]{:S(2)}, u32[]{:S(2)}) collective-permute-start(bf16[2,4,64,256]{3,2,1,0:T(8,128)(2,1)S(1)} %get-tuple-element.21.refs_0_), channel_id=1, source_target_pairs={{0,1},{1,0},{2,3},{3,2},{4,5},{5,4},{6,7},{7,6},{8,9},{9,8},{10,11... | collective-permute-start | bytes 786440 | tf_op jit(solution)/shard_map/ppermute | solution.py:310
  8.0 12.7 %collective-permute-start.1 = (bf16[2,4,64,256]{3,2,1,0:T(8,128)(2,1)S(1)}, bf16[2,4,64,256]{3,2,1,0:T(8,128)(2,1)S(1)}, u32[]{:S(2)}, u32[]{:S(2)}) collective-permute-start(bf16[2,4,64,256]{3,2,1,0:T(8,128)(2,1)S(1)} %get-tuple-element.23), channel_id=1, source_target_pairs={{0,3},{1,2},{2,1},{3,0},{4,7},{5,6},{6,5},{7,4},{8,11},{9,10},{10,... | collective-permute-start | bytes 786440 | tf_op jit(solution)/shard_map/ppermute | solution.py:310
  10.4 3.4 %copy-start.7 = (bf16[2,4,64,256]{3,2,1,0:T(8,128)(2,1)}, bf16[2,4,64,256]{3,2,1,0:T(8,128)(2,1)S(1)}, u32[]{:S(2)}) copy-start(bf16[2,4,64,256]{3,2,1,0:T(8,128)(2,1)S(1)} %collective-permute-done.2.refs_3_) | copy-start | bytes 786436
  13.8 0.7 copy-start.17
  17.4 8.3 %collective-permute-start.5 = (bf16[16,2,2,16,256]{4,3,2,1,0:T(8,128)(2,1)}, bf16[16,2,2,16,256]{4,3,2,1,0:T(8,128)(2,1)S(1)}, u32[]{:S(2)}, u32[]{:S(2)}) collective-permute-start(bf16[16,2,2,16,256]{4,3,2,1,0:T(8,128)(2,1)} %get-tuple-element.11), channel_id=1, source_target_pairs={{0,4},{4,0},{1,5},{5,1},{2,6},{6,2},{3,7},{7,3},{8,12},{12,8},{9,1... | collective-permute-start | bytes 1572872 | tf_op jit(solution)/shard_map/ppermute | solution.py:310
  20.7 0.7 copy-start.9
  20.7 0.8 copy-start.16
  24.4 2.2 %collective-permute-start.4 = (bf16[16,2,2,16,256]{4,3,2,1,0:T(8,128)(2,1)}, bf16[16,2,2,16,256]{4,3,2,1,0:T(8,128)(2,1)S(1)}, u32[]{:S(2)}, u32[]{:S(2)}) collective-permute-start(bf16[16,2,2,16,256]{4,3,2,1,0:T(8,128)(2,1)} %get-tuple-element.10), channel_id=1, source_target_pairs={{0,4},{4,0},{1,5},{5,1},{2,6},{6,2},{3,7},{7,3},{8,12},{12,8},{9,1... | collective-permute-start | bytes 1572872 | tf_op jit(solution)/shard_map/ppermute | solution.py:310
  25.7 0.9 copy-start.5
  26.6 0.8 copy-start.6
  30.4 10.5 %copy-start.10 = (bf16[2,4,64,256]{3,2,1,0:T(8,128)(2,1)S(1)}, bf16[2,4,64,256]{3,2,1,0:T(8,128)(2,1)}, u32[]{:S(2)}) copy-start(bf16[2,4,64,256]{3,2,1,0:T(8,128)(2,1)} %copy-done.9) | copy-start | bytes 786436
  30.5 12.4 %copy-start.8 = (bf16[2,4,64,256]{3,2,1,0:T(8,128)(2,1)S(1)}, bf16[2,4,64,256]{3,2,1,0:T(8,128)(2,1)}, u32[]{:S(2)}) copy-start(bf16[2,4,64,256]{3,2,1,0:T(8,128)(2,1)} %copy-done.7) | copy-start | bytes 786436
  30.5 25.7 %all-to-all-start = ((bf16[16,144,256]{2,1,0:T(8,128)(2,1)}), bf16[16,144,256]{2,1,0:T(8,128)(2,1)S(1)}, u32[]{:S(2)}, u32[]{:S(2)}) async-start(bf16[16,144,256]{2,1,0:T(8,128)(2,1)} %combine.1), calls=%async_computation | async-start | bytes 2359296 | tf_op jit(solution)/shard_map/all_to_all | solution.py:342
  38.2 27.9 %collective-permute-start.6 = (bf16[2,4,64,256]{3,2,1,0:T(8,128)(2,1)S(1)}, bf16[2,4,64,256]{3,2,1,0:T(8,128)(2,1)S(1)}, u32[]{:S(2)}, u32[]{:S(2)}) collective-permute-start(bf16[2,4,64,256]{3,2,1,0:T(8,128)(2,1)S(1)} %get-tuple-element.21.refs_0_), channel_id=1, source_target_pairs={{0,3},{1,2},{2,1},{3,0},{4,7},{5,6},{6,5},{7,4},{8,11},{9,10},{10,... | collective-permute-start | bytes 786440 | tf_op jit(solution)/shard_map/ppermute | solution.py:310
  40.2 25.9 %collective-permute-start.7 = (bf16[2,4,64,256]{3,2,1,0:T(8,128)(2,1)S(1)}, bf16[2,4,64,256]{3,2,1,0:T(8,128)(2,1)S(1)}, u32[]{:S(2)}, u32[]{:S(2)}) collective-permute-start(bf16[2,4,64,256]{3,2,1,0:T(8,128)(2,1)S(1)} %get-tuple-element.20.refs_1_), channel_id=1, source_target_pairs={{0,3},{1,2},{2,1},{3,0},{4,7},{5,6},{6,5},{7,4},{8,11},{9,10},{10,... | collective-permute-start | bytes 786440 | tf_op jit(solution)/shard_map/ppermute | solution.py:310
  41.0 25.2 %collective-permute-start.8 = (bf16[2,4,64,256]{3,2,1,0:T(8,128)(2,1)S(1)}, bf16[2,4,64,256]{3,2,1,0:T(8,128)(2,1)S(1)}, u32[]{:S(2)}, u32[]{:S(2)}) collective-permute-start(bf16[2,4,64,256]{3,2,1,0:T(8,128)(2,1)S(1)} %copy-done.10), channel_id=1, source_target_pairs={{0,3},{1,2},{2,1},{3,0},{4,7},{5,6},{6,5},{7,4},{8,11},{9,10},{10,... | collective-permute-start | bytes 786440 | tf_op jit(solution)/shard_map/ppermute | solution.py:310
  42.9 23.3 %collective-permute-start.9 = (bf16[2,4,64,256]{3,2,1,0:T(8,128)(2,1)S(1)}, bf16[2,4,64,256]{3,2,1,0:T(8,128)(2,1)S(1)}, u32[]{:S(2)}, u32[]{:S(2)}) collective-permute-start(bf16[2,4,64,256]{3,2,1,0:T(8,128)(2,1)S(1)} %copy-done.8), channel_id=1, source_target_pairs={{0,3},{1,2},{2,1},{3,0},{4,7},{5,6},{6,5},{7,4},{8,11},{9,10},{10,... | collective-permute-start | bytes 786440 | tf_op jit(solution)/shard_map/ppermute | solution.py:310
  56.2 1.0 %copy-start = (bf16[16,144,256]{2,1,0:T(8,128)(2,1)}, bf16[16,144,256]{2,1,0:T(8,128)(2,1)S(1)}, u32[]{:S(2)}) copy-start(bf16[16,144,256]{2,1,0:T(8,128)(2,1)S(1)} %all-to-all-done.g_ref) | copy-start | bytes 3538948
  59.4 16.3 %all-to-all-start.1 = ((f32[128,1,128]{2,1,0:T(1,128)}), f32[128,1,128]{2,1,0:T(1,128)S(1)}, u32[]{:S(2)}, u32[]{:S(2)}) async-start(f32[128,1,128]{2,1,0:T(1,128)} %bitcast.81), calls=%async_computation.1 | async-start | bytes 131072 | tf_op jit(solution)/shard_map/all_to_all | solution.py:344
  66.1 9.6 %copy-start.11 = (bf16[2,4,64,256]{3,2,1,0:T(8,128)(2,1)}, bf16[2,4,64,256]{3,2,1,0:T(8,128)(2,1)S(1)}, u32[]{:S(2)}) copy-start(bf16[2,4,64,256]{3,2,1,0:T(8,128)(2,1)S(1)} %collective-permute-done.6.refs_4_) | copy-start | bytes 786436
  66.1 9.6 %copy-start.12 = (bf16[2,4,64,256]{3,2,1,0:T(8,128)(2,1)}, bf16[2,4,64,256]{3,2,1,0:T(8,128)(2,1)S(1)}, u32[]{:S(2)}) copy-start(bf16[2,4,64,256]{3,2,1,0:T(8,128)(2,1)S(1)} %collective-permute-done.7.refs_5_) | copy-start | bytes 786436
  66.1 9.5 %copy-start.13 = (bf16[2,4,64,256]{3,2,1,0:T(8,128)(2,1)}, bf16[2,4,64,256]{3,2,1,0:T(8,128)(2,1)S(1)}, u32[]{:S(2)}) copy-start(bf16[2,4,64,256]{3,2,1,0:T(8,128)(2,1)S(1)} %collective-permute-done.8.refs_6_) | copy-start | bytes 786436
  66.2 9.5 %copy-start.14 = (bf16[2,4,64,256]{3,2,1,0:T(8,128)(2,1)}, bf16[2,4,64,256]{3,2,1,0:T(8,128)(2,1)S(1)}, u32[]{:S(2)}) copy-start(bf16[2,4,64,256]{3,2,1,0:T(8,128)(2,1)S(1)} %collective-permute-done.9.refs_7_) | copy-start | bytes 786436
  75.7 0.6 copy-start.15

commit v3 on v2

--- a/solution.py
+++ b/solution.py
@@ -69,6 +69,7 @@
         in_specs=[pl.BlockSpec(memory_space=pltpu.SMEM)] + [vm] * 4,
         out_specs=(vm, vm),
         name="gains",
+        compiler_params=pltpu.CompilerParams(vmem_limit_bytes=8 << 20),
         cost_estimate=pl.CostEstimate(flops=8 * users * users * ht.shape[0] * 2, bytes_accessed=4 << 20, transcendentals=0),
     )(core, ht, ha, vt, vb)
 
@@ -91,6 +92,7 @@
         in_specs=[vm] * 5,
         out_specs=vm,
         name="combine",
+        compiler_params=pltpu.CompilerParams(vmem_limit_bytes=8 << 20),
     )(*keeps, *cames, extra)
 
 
@@ -141,6 +143,7 @@
         in_specs=[pl.BlockSpec(memory_space=pltpu.SMEM), vm, vm],
         out_specs=vm,
         name="totals",
+        compiler_params=pltpu.CompilerParams(vmem_limit_bytes=8 << 20),
     )(where, g, noise)
 
 
@@ -182,9 +185,94 @@
         weight_ref[block] = line_ref[block, 3, pl.ds(tile, 1)]
 
 
+def regrouped(pieces, wanted):
+    lanes = pieces[0].shape[1]
+    width = lanes // 8
+    group = iota(pieces[0].shape, 1) // width
+    rolled = [pltpu.roll(piece, s * width, 1) if s else piece for s, piece in enumerate(pieces)]
+    results = []
+    for g in range(8):
+        if not wanted[g]:
+            results.append(None)
+            continue
+        total = rolled[0]
+        for s in range(1, 8):
+            total = jnp.where(group == (s + g) % 8, rolled[s], total)
+        results.append(pltpu.roll(total, lanes - g * width, 1) if g else total)
+    return results
+
+
+def eliminate(work_ref, sys_ref, scale_ref):
+    _, rows, lanes = work_ref.shape
+    width = lanes // 8
+    lane = iota((8, lanes), 1)
+    sublane = iota((8, lanes), 0)
+    for high in range(rows // 8):
+        at = slice(high * 8, high * 8 + 8)
+        groups = regrouped([sys_ref[s, at, :] for s in range(8)], [True] * 8)
+        for g in range(8):
+            work_ref[g, at, :] = groups[g]
+
+    def spread(value, k):
+        return jnp.take_along_axis(value, lane // width * width + k % width, axis=1, mode="promise_in_bounds")
+
+    def row_of(g, k):
+        return jnp.broadcast_to(work_ref[g, k : k + 1, :], (8, lanes))
+
+    def pivot(k):
+        column = k // width
+        line = [row_of(g, k) for g in range(8)]
+        value = spread(line[column], k)
+        root = lax.rsqrt(value)
+        scale_ref[k : k + 1, :] = root[:1]
+        line[column] = line[column] + jnp.where(lane % width == k % width, 1.0, 0.0)
+        return line, 1.0 / value
+
+    def update(k, high, line, inverse):
+        column = k // width
+        at = slice(high * 8, high * 8 + 8)
+        f_re = spread(work_ref[column, at, :], k) * inverse
+        f_im = spread(work_ref[4 + column, at, :], k) * inverse
+        if high == k // 8:
+            below = sublane > k % 8
+            f_re = jnp.where(below, f_re, 0.0)
+            f_im = jnp.where(below, f_im, 0.0)
+        for c in range(4):
+            real, imag = line[c], line[4 + c]
+            work_ref[c, at, :] = work_ref[c, at, :] - (f_re * real - f_im * imag)
+            work_ref[4 + c, at, :] = work_ref[4 + c, at, :] - (f_re * imag + f_im * real)
+
+    now = pivot(0)
+    for k in range(rows - 1):
+        first = (k + 1) // 8
+        update(k, first, *now)
+        later = pivot(k + 1)
+        if first != k // 8:
+            pass
+        for high in range(first + 1, rows // 8):
+            update(k, high, *now)
+        now = later
+
+    for high in range(rows // 8):
+        at = slice(high * 8, high * 8 + 8)
+        scale = scale_ref[at, :]
+        pieces = []
+        for g in range(8):
+            start = g % 4 * width
+            here = start + lane % width
+            row = high * 8 + sublane
+            kept = jnp.where(here < row, work_ref[g, at, :], 0.0)
+            if g < 4:
+                kept = jnp.where(here == row, 1.0, kept)
+            pieces.append(kept * scale)
+        systems = regrouped(pieces, [True] * 8)
+        for s in range(8):
+            sys_ref[s, at, :] = systems[s]
+
+
 def solve_kernel(tile_ref, penalty_ref, power_ref, r_ref, *refs):
     h_refs = refs[:8]
-    out_ref, weight_ref, line_ref, sys_ref, low_ref, scaled_ref, y_ref, sem = refs[8:]
+    out_ref, weight_ref, line_ref, sys_ref, work_ref, scale_ref, y_ref = refs[8:]
     blocks = 2
     _, points, antennas, users = h_refs[0].shape
     size = 2 * antennas
@@ -216,41 +304,16 @@
             p = acc[:size] + (acc[size : 2 * size] + acc[2 * size :])
             a = p[:antennas] * upper + pltpu.roll(p[antennas:], antennas, 1)
             a = a + jnp.where(lane == row, penalty_ref[point], 0.0)
-            sys_ref[:, block * points + point, :] = a
-
-    lane8 = iota((systems, size), 1)
-    sign = jnp.where(lane8 < antennas, -1.0, 1.0).astype(F32)
-
-    def pivot(k, pivot_row):
-        inverse = 1.0 / pivot_row[:, k : k + 1]
-        here = jnp.logical_or(lane8 == k, lane8 == antennas + k)
-        done = jnp.logical_or(lane8 < k, jnp.logical_and(lane8 >= antennas, lane8 < antennas + k))
-        one = jnp.where(lane8 == k, 1.0, 0.0)
-        unit = jnp.where(here, one, pivot_row)
-        low = jnp.where(done, pivot_row, one)
-        low_ref[k] = low
-        scaled_ref[k] = low * inverse
-        return unit * inverse, (pltpu.roll(unit, antennas, 1) * sign) * inverse, here
-
-    def update(k, i, straight, turned, here):
-        w = sys_ref[i]
-        f_re = w[:, k : k + 1]
-        f_im = w[:, antennas + k : antennas + k + 1]
-        return jnp.where(here, 0.0, w) - (f_re * straight + f_im * turned)
-
-    now = pivot(0, sys_ref[0])
-    for k in range(antennas - 1):
-        later = pivot(k + 1, update(k, k + 1, *now))
-        for i in range(k + 2, antennas):
-            sys_ref[i] = update(k, i, *now)
-        now = later
-
-    copies = []
+            sys_ref[block * points + point] = a
+
+    eliminate(work_ref, sys_ref, scale_ref)
+
     for point in range(points):
         total = jnp.zeros((1, users), F32)
         for block in range(blocks):
             n = block * points + point
-            q = dot(scaled_ref[:, n, :], low_ref[:, n, :], ((0,), (0,)), HIGHEST)
+            z = sys_ref[n]
+            q = dot(z, z, ((0,), (0,)), HIGHEST)
             top = q[:antennas] * upper + pltpu.roll(q[antennas:], antennas, 1)
             bottom = pltpu.roll(top, antennas, 1) * (-upper)
             parts = three_parts(jnp.concatenate([top, bottom], axis=0))
@@ -287,13 +350,13 @@
         out_specs=(vm, vm),
         scratch_shapes=[
             pltpu.VMEM((blocks, 4, 8, users), F32),
-            pltpu.VMEM((antennas, blocks * points, size), F32),
-            pltpu.VMEM((antennas, blocks * points, size), F32),
-            pltpu.VMEM((antennas, blocks * points, size), F32),
+            pltpu.VMEM((blocks * points, antennas, size), F32),
+            pltpu.VMEM((8, antennas, size), F32),
+            pltpu.VMEM((antennas, size), F32),
             pltpu.VMEM((blocks, size, users), F32),
-            pltpu.SemaphoreType.DMA((1,)),
         ],
         name="solve",
+        compiler_params=pltpu.CompilerParams(vmem_limit_bytes=16 << 20),
     )(tile, penalty, power, r, *channels)
 
 

time: 95.5 us -> 82.9 us (0.87)
  Pallas kernels: 28.6 us -> 17.9 us
  local copies, waits for them, and re-layouts: 6.3 us -> 1.63 us
  waiting for transfers between devices: 26.4 us -> 29.9 us
  other arithmetic: 4.26 us -> 2.37 us
  starting transfers between devices: 28.6 us -> 30.1 us
    unnamed x37 -> x11, local copies, waits for them, and re-layouts: 5.19 us -> 0.6 us
    pallas_call x2, Pallas kernels: 5.84 us -> 1.47 us  [partial_gains(): pl.pallas_call(gain_kernel, out_shape=(jax.ShapeDtypeStruct(shape, F32),...]
    pallas_call x1, Pallas kernels: 17.6 us -> 13.7 us  [solve(): pl.pallas_call(solve_kernel, out_shape=(jax.ShapeDtypeStruct(out_shape, B...]
    ppermute x10, waiting for transfers between devices: 4.99 us -> 7.91 us  [across(): return lax.ppermute(value, axis, [(i, i ^ mask) for i in range(size)])]
    pallas_call x1, Pallas kernels: 3.03 us -> 1.2 us  [combined(): pl.pallas_call(combine_kernel, out_shape=jax.ShapeDtypeStruct((chips, 8 *...]
    ppermute x10, starting transfers between devices: 14.2 us -> 15.7 us  [across(): return lax.ppermute(value, axis, [(i, i ^ mask) for i in range(size)])]
  transfers between devices with their start and end apart: 12 -> 12, of which waited for: 5 -> 6; matrix products, arithmetic and copies ran while one was open for 4% -> 2% of each run, Pallas kernels for 8% -> 4%
where the time goes in v3:
time: 82.9 us; the launch traced here: 82.7 us
  starting transfers between devices  30.1 us (36%)
  waiting for transfers between devices  29.9 us (36%)
  Pallas kernels  17.9 us (22%)
  other arithmetic  2.37 us (3%)
  local copies, waits for them, and re-layouts  1.63 us (2%)
    ppermute x10, starting transfers between devices, across(): return lax.ppermute(value, axis, [(i, i ^ mask) for i in range(size)])  15.7 us
    pallas_call x1, Pallas kernels, solve(): pl.pallas_call(solve_kernel, out_shape=(jax.ShapeDtypeStruct(out_shape, B...  13.7 us
    all_to_all x1, waiting for transfers between devices, local(): summed = lax.all_to_all(gains, CHIPS, 0, 0, tiled=True)  12.4 us
    all_to_all x1, waiting for transfers between devices, local(): lax.all_to_all(line, EVERY, 0, 0, tiled=True)  9.55 us
    ppermute x10, waiting for transfers between devices, across(): return lax.ppermute(value, axis, [(i, i ^ mask) for i in range(size)])  7.91 us
    all_to_all x1, starting transfers between devices, local(): summed = lax.all_to_all(gains, CHIPS, 0, 0, tiled=True)  7.73 us
    all_to_all x1, starting transfers between devices, local(): lax.all_to_all(line, EVERY, 0, 0, tiled=True)  6.67 us
  transfers between devices with their start and end apart: 12, of which 6 were waited for; matrix products, arithmetic and copies ran while one was open for 2% of the time, Pallas kernels for 4%

profile of v3, /device:TPU:1, one launch (start us, length us, event | category | flops | bytes accessed | tf_op | source)
XLA Modules:
  0.0 82.7 jit_solution(15285680342319750218)
XLA Ops:
  0.6 0.0 copy-start.3
  0.6 0.7 convert_bitcast_fusion
  1.4 0.0 copy-start.4
  1.4 1.2 %bitcast_multiply_fusion = (bf16[2,4,64,256]{3,2,1,0:T(8,128)(2,1)S(1)}, bf16[2,4,64,256]{3,2,1,0:T(8,128)(2,1)S(1)}) fusion(bf16[4]{0:T(256)(128)(2,1)S(1)} %convert_bitcast_fusion, bf16[2,2,4,64,256]{4,3,2,1,0:T(8,128)(2,1)} %param.6), kind=kLoop, calls=%fused_computation.16 | loop fusion | flops 262144 | bytes 1048584 | tf_op jit(solution)/shard_map/mul | solution.py:388
  2.6 2.2 %collective-permute-start.2 = (bf16[2,4,64,256]{3,2,1,0:T(8,128)(2,1)S(1)}, bf16[2,4,64,256]{3,2,1,0:T(8,128)(2,1)S(1)}, u32[]{:S(2)}, u32[]{:S(2)}) collective-permute-start(bf16[2,4,64,256]{3,2,1,0:T(8,128)(2,1)S(1)} %get-tuple-element.20.refs_1_), channel_id=1, source_target_pairs={{0,1},{1,0},{2,3},{3,2},{4,5},{5,4},{6,7},{7,6},{8,9},{9,8},{10,11... | collective-permute-start | bytes 786440 | tf_op jit(solution)/shard_map/ppermute | solution.py:373
  4.7 0.0 copy-done.3
  4.8 0.8 slice_bitcast_fusion.4
  5.6 1.9 %collective-permute-start.3 = (bf16[2,4,64,256]{3,2,1,0:T(8,128)(2,1)}, bf16[2,4,64,256]{3,2,1,0:T(8,128)(2,1)S(1)}, u32[]{:S(2)}, u32[]{:S(2)}) collective-permute-start(bf16[2,4,64,256]{3,2,1,0:T(8,128)(2,1)} %get-tuple-element.22), channel_id=1, source_target_pairs={{0,3},{1,2},{2,1},{3,0},{4,7},{5,6},{6,5},{7,4},{8,11},{9,10},{10,... | collective-permute-start | bytes 786440 | tf_op jit(solution)/shard_map/ppermute | solution.py:373
  7.5 0.4 collective-permute-start
  7.9 0.6 collective-permute-start.1
  8.5 0.0 copy-done.4
  8.5 0.1 mul.52
  8.6 0.1 mul.53
  8.7 0.1 bitcast_multiply_fusion.1
  8.8 1.6 %collective-permute-done.2.refs_3_ = bf16[2,4,64,256]{3,2,1,0:T(8,128)(2,1)S(1)} collective-permute-done((bf16[2,4,64,256]{3,2,1,0:T(8,128)(2,1)S(1)}, bf16[2,4,64,256]{3,2,1,0:T(8,128)(2,1)S(1)}, u32[]{:S(2)}, u32[]{:S(2)}) %collective-permute-start.2) | collective-permute-done | bytes 262176 | tf_op jit(solution)/shard_map/ppermute | solution.py:373
  10.4 3.5 %collective-permute-done.3 = bf16[2,4,64,256]{3,2,1,0:T(8,128)(2,1)S(1)} collective-permute-done((bf16[2,4,64,256]{3,2,1,0:T(8,128)(2,1)}, bf16[2,4,64,256]{3,2,1,0:T(8,128)(2,1)S(1)}, u32[]{:S(2)}, u32[]{:S(2)}) %collective-permute-start.3) | collective-permute-done | bytes 262176 | tf_op jit(solution)/shard_map/ppermute | solution.py:373
  13.9 0.7 gains.3
  14.7 3.3 %collective-permute-start.5 = (bf16[16,2,2,16,256]{4,3,2,1,0:T(8,128)(2,1)S(1)}, bf16[16,2,2,16,256]{4,3,2,1,0:T(8,128)(2,1)S(1)}, u32[]{:S(2)}, u32[]{:S(2)}) collective-permute-start(bf16[16,2,2,16,256]{4,3,2,1,0:T(8,128)(2,1)S(1)} %get-tuple-element.11), channel_id=1, source_target_pairs={{0,4},{4,0},{1,5},{5,1},{2,6},{6,2},{3,7},{7,3},{8,12},{12,8},{9,1... | collective-permute-start | bytes 1572872 | tf_op jit(solution)/shard_map/ppermute | solution.py:373
  18.0 0.0 collective-permute-done.refs_2_
  18.0 1.6 %collective-permute-done.1 = bf16[2,4,64,256]{3,2,1,0:T(8,128)(2,1)S(1)} collective-permute-done((bf16[2,4,64,256]{3,2,1,0:T(8,128)(2,1)S(1)}, bf16[2,4,64,256]{3,2,1,0:T(8,128)(2,1)S(1)}, u32[]{:S(2)}, u32[]{:S(2)}) %collective-permute-start.1) | collective-permute-done | bytes 262176 | tf_op jit(solution)/shard_map/ppermute | solution.py:373
  19.5 0.7 gains.2
  20.3 1.9 %collective-permute-start.4 = (bf16[16,2,2,16,256]{4,3,2,1,0:T(8,128)(2,1)S(1)}, bf16[16,2,2,16,256]{4,3,2,1,0:T(8,128)(2,1)S(1)}, u32[]{:S(2)}, u32[]{:S(2)}) collective-permute-start(bf16[16,2,2,16,256]{4,3,2,1,0:T(8,128)(2,1)S(1)} %get-tuple-element.10), channel_id=1, source_target_pairs={{0,4},{4,0},{1,5},{5,1},{2,6},{6,2},{3,7},{7,3},{8,12},{12,8},{9,1... | collective-permute-start | bytes 1572872 | tf_op jit(solution)/shard_map/ppermute | solution.py:373
  22.2 0.2 fusion.3
  22.4 0.0 collective-permute-done.5.came1_ref
  22.4 1.3 %collective-permute-done.4.came0_ref = bf16[16,2,2,16,256]{4,3,2,1,0:T(8,128)(2,1)S(1)} collective-permute-done((bf16[16,2,2,16,256]{4,3,2,1,0:T(8,128)(2,1)S(1)}, bf16[16,2,2,16,256]{4,3,2,1,0:T(8,128)(2,1)S(1)}, u32[]{:S(2)}, u32[]{:S(2)}) %collective-permute-start.4) | collective-permute-done | bytes 524320 | tf_op jit(solution)/shard_map/ppermute | solution.py:373
  23.7 1.2 %combine.1 = bf16[16,144,256]{2,1,0:T(8,128)(2,1)} custom-call(f32[16,2,2,16,256]{4,3,2,1,0:T(8,128)S(1)} %get-tuple-element.8.keep0_ref, f32[16,2,2,16,256]{4,3,2,1,0:T(8,128)S(1)} %get-tuple-element.9.keep1_ref, bf16[16,2,2,16,256]{4,3,2,1,0:T(8,128)(2,1)S(1)} %collective-permute-done.4.came0_ref, ...), custom_call_target="tpu_custom_call" | custom-call | tf_op jit(solution)/shard_map/combine/pallas_call | solution.py:89
  24.9 0.0 copy-start
  24.9 7.7 %all-to-all-start = ((bf16[16,144,256]{2,1,0:T(8,128)(2,1)}), bf16[16,144,256]{2,1,0:T(8,128)(2,1)S(1)}, u32[]{:S(2)}, u32[]{:S(2)}) async-start(bf16[16,144,256]{2,1,0:T(8,128)(2,1)} %combine.1), calls=%async_computation | async-start | bytes 2359296 | tf_op jit(solution)/shard_map/all_to_all | solution.py:405
  32.6 0.0 copy-start.1
  32.7 0.0 copy-start.2
  32.7 2.0 %collective-permute-start.6 = (bf16[2,4,64,256]{3,2,1,0:T(8,128)(2,1)S(1)}, bf16[2,4,64,256]{3,2,1,0:T(8,128)(2,1)S(1)}, u32[]{:S(2)}, u32[]{:S(2)}) collective-permute-start(bf16[2,4,64,256]{3,2,1,0:T(8,128)(2,1)S(1)} %get-tuple-element.21.refs_0_), channel_id=1, source_target_pairs={{0,3},{1,2},{2,1},{3,0},{4,7},{5,6},{6,5},{7,4},{8,11},{9,10},{10,... | collective-permute-start | bytes 786440 | tf_op jit(solution)/shard_map/ppermute | solution.py:373
  34.6 0.8 collective-permute-start.7
  35.4 1.9 %collective-permute-start.8 = (bf16[2,4,64,256]{3,2,1,0:T(8,128)(2,1)S(1)}, bf16[2,4,64,256]{3,2,1,0:T(8,128)(2,1)S(1)}, u32[]{:S(2)}, u32[]{:S(2)}) collective-permute-start(bf16[2,4,64,256]{3,2,1,0:T(8,128)(2,1)S(1)} %collective-permute-done.refs_2_), channel_id=1, source_target_pairs={{0,3},{1,2},{2,1},{3,0},{4,7},{5,6},{6,5},{7,4},{8,11},{9,10},{10,... | collective-permute-start | bytes 786440 | tf_op jit(solution)/shard_map/ppermute | solution.py:373
  37.3 0.8 collective-permute-start.9
  38.1 0.1 pad_add_fusion.where_ref
  38.2 12.4 %all-to-all-done.g_ref = bf16[16,144,256]{2,1,0:T(8,128)(2,1)S(1)} async-done(((bf16[16,144,256]{2,1,0:T(8,128)(2,1)}), bf16[16,144,256]{2,1,0:T(8,128)(2,1)S(1)}, u32[]{:S(2)}, u32[]{:S(2)}) %all-to-all-start) | async-done | bytes 1179680 | tf_op jit(solution)/shard_map/all_to_all | solution.py:405
  50.6 0.0 copy-done
  50.6 1.5 %totals.1 = f32[128,128]{1,0:T(8,128)} custom-call(s32[2]{0:T(128)S(1)} %pad_add_fusion.where_ref, bf16[16,144,256]{2,1,0:T(8,128)(2,1)S(1)} %all-to-all-done.g_ref, f32[2,256]{1,0:T(2,128)S(1)} %copy-done), custom_call_target="tpu_custom_call" | custom-call | tf_op jit(solution)/shard_map/totals/pallas_call | solution.py:140
  52.1 6.7 %all-to-all-start.1 = ((f32[128,1,128]{2,1,0:T(1,128)}), f32[128,1,128]{2,1,0:T(1,128)S(1)}, u32[]{:S(2)}, u32[]{:S(2)}) async-start(f32[128,1,128]{2,1,0:T(1,128)} %bitcast.37), calls=%async_computation.1 | async-start | bytes 131072 | tf_op jit(solution)/shard_map/all_to_all | solution.py:407
  58.8 0.0 collective-permute-done.6.refs_4_
  58.8 0.0 collective-permute-done.7.refs_5_
  58.8 0.0 collective-permute-done.8.refs_6_
  58.8 0.0 collective-permute-done.9.refs_7_
  58.8 9.5 %all-to-all-done.1 = f32[128,1,128]{2,1,0:T(1,128)S(1)} async-done(((f32[128,1,128]{2,1,0:T(1,128)}), f32[128,1,128]{2,1,0:T(1,128)S(1)}, u32[]{:S(2)}, u32[]{:S(2)}) %all-to-all-start.1) | async-done | bytes 65568 | tf_op jit(solution)/shard_map/all_to_all | solution.py:407
  68.4 0.0 copy-done.1
  68.4 0.0 copy-done.2
  68.4 13.7 %solve.1 = (bf16[2,2,4,64,256]{4,3,2,1,0:T(8,128)(2,1)}, f32[2,1,256]{2,1,0:T(1,128)S(1)}) custom-call(s32[1]{0:T(128)} %bitcast.tile_ref, f32[4]{0:T(128)S(1)} %copy-done.1, f32[4]{0:T(128)S(1)} %copy-done.2, f32[16,8,128]{2,1,0:T(8,128)S(1)} %bitcast.80, bf16[2,4,64,256]{3,2,1,0:T(8,128)(2,1)S(1)} %get-tuple-element.21.refs_0_, ...), custom_call_target="tpu_custom_call" | custom-call | tf_op jit(solution)/shard_map/solve/pallas_call | solution.py:343
  82.1 0.6 copy.11
  (4 shorter events, 0.1 us)
Async XLA Ops:
  0.6 4.1 %copy-start.3 = (bf16[2,2,4,64,256]{4,3,2,1,0:T(8,128)(2,1)S(1)}, bf16[2,2,4,64,256]{4,3,2,1,0:T(8,128)(2,1)}, u32[]{:S(2)}) copy-start(bf16[2,2,4,64,256]{4,3,2,1,0:T(8,128)(2,1)} %param.7) | copy-start | bytes 1572868
  1.4 7.1 %copy-start.4 = (bf16[2,2,4,64,256]{4,3,2,1,0:T(8,128)(2,1)S(1)}, bf16[2,2,4,64,256]{4,3,2,1,0:T(8,128)(2,1)}, u32[]{:S(2)}) copy-start(bf16[2,2,4,64,256]{4,3,2,1,0:T(8,128)(2,1)} %param.6) | copy-start | bytes 1572868
  2.6 7.9 %collective-permute-start.2 = (bf16[2,4,64,256]{3,2,1,0:T(8,128)(2,1)S(1)}, bf16[2,4,64,256]{3,2,1,0:T(8,128)(2,1)S(1)}, u32[]{:S(2)}, u32[]{:S(2)}) collective-permute-start(bf16[2,4,64,256]{3,2,1,0:T(8,128)(2,1)S(1)} %get-tuple-element.20.refs_1_), channel_id=1, source_target_pairs={{0,1},{1,0},{2,3},{3,2},{4,5},{5,4},{6,7},{7,6},{8,9},{9,8},{10,11... | collective-permute-start | bytes 786440 | tf_op jit(solution)/shard_map/ppermute | solution.py:373
  5.6 8.3 %collective-permute-start.3 = (bf16[2,4,64,256]{3,2,1,0:T(8,128)(2,1)}, bf16[2,4,64,256]{3,2,1,0:T(8,128)(2,1)S(1)}, u32[]{:S(2)}, u32[]{:S(2)}) collective-permute-start(bf16[2,4,64,256]{3,2,1,0:T(8,128)(2,1)} %get-tuple-element.22), channel_id=1, source_target_pairs={{0,3},{1,2},{2,1},{3,0},{4,7},{5,6},{6,5},{7,4},{8,11},{9,10},{10,... | collective-permute-start | bytes 786440 | tf_op jit(solution)/shard_map/ppermute | solution.py:373
  7.5 10.5 %collective-permute-start = (bf16[2,4,64,256]{3,2,1,0:T(8,128)(2,1)S(1)}, bf16[2,4,64,256]{3,2,1,0:T(8,128)(2,1)S(1)}, u32[]{:S(2)}, u32[]{:S(2)}) collective-permute-start(bf16[2,4,64,256]{3,2,1,0:T(8,128)(2,1)S(1)} %get-tuple-element.21.refs_0_), channel_id=1, source_target_pairs={{0,1},{1,0},{2,3},{3,2},{4,5},{5,4},{6,7},{7,6},{8,9},{9,8},{10,11... | collective-permute-start | bytes 786440 | tf_op jit(solution)/shard_map/ppermute | solution.py:373
  7.9 11.6 %collective-permute-start.1 = (bf16[2,4,64,256]{3,2,1,0:T(8,128)(2,1)S(1)}, bf16[2,4,64,256]{3,2,1,0:T(8,128)(2,1)S(1)}, u32[]{:S(2)}, u32[]{:S(2)}) collective-permute-start(bf16[2,4,64,256]{3,2,1,0:T(8,128)(2,1)S(1)} %get-tuple-element.23), channel_id=1, source_target_pairs={{0,3},{1,2},{2,1},{3,0},{4,7},{5,6},{6,5},{7,4},{8,11},{9,10},{10,... | collective-permute-start | bytes 786440 | tf_op jit(solution)/shard_map/ppermute | solution.py:373
  14.7 7.8 %collective-permute-start.5 = (bf16[16,2,2,16,256]{4,3,2,1,0:T(8,128)(2,1)S(1)}, bf16[16,2,2,16,256]{4,3,2,1,0:T(8,128)(2,1)S(1)}, u32[]{:S(2)}, u32[]{:S(2)}) collective-permute-start(bf16[16,2,2,16,256]{4,3,2,1,0:T(8,128)(2,1)S(1)} %get-tuple-element.11), channel_id=1, source_target_pairs={{0,4},{4,0},{1,5},{5,1},{2,6},{6,2},{3,7},{7,3},{8,12},{12,8},{9,1... | collective-permute-start | bytes 1572872 | tf_op jit(solution)/shard_map/ppermute | solution.py:373
  20.3 3.4 %collective-permute-start.4 = (bf16[16,2,2,16,256]{4,3,2,1,0:T(8,128)(2,1)S(1)}, bf16[16,2,2,16,256]{4,3,2,1,0:T(8,128)(2,1)S(1)}, u32[]{:S(2)}, u32[]{:S(2)}) collective-permute-start(bf16[16,2,2,16,256]{4,3,2,1,0:T(8,128)(2,1)S(1)} %get-tuple-element.10), channel_id=1, source_target_pairs={{0,4},{4,0},{1,5},{5,1},{2,6},{6,2},{3,7},{7,3},{8,12},{12,8},{9,1... | collective-permute-start | bytes 1572872 | tf_op jit(solution)/shard_map/ppermute | solution.py:373
  24.9 25.7 %copy-start = (f32[2,256]{1,0:T(2,128)S(1)}, f32[2,256]{1,0:T(2,128)}, u32[]{:S(2)}) copy-start(f32[2,256]{1,0:T(2,128)} %noise_ref.1) | copy-start | bytes 6148
  24.9 25.7 %all-to-all-start = ((bf16[16,144,256]{2,1,0:T(8,128)(2,1)}), bf16[16,144,256]{2,1,0:T(8,128)(2,1)S(1)}, u32[]{:S(2)}, u32[]{:S(2)}) async-start(bf16[16,144,256]{2,1,0:T(8,128)(2,1)} %combine.1), calls=%async_computation | async-start | bytes 2359296 | tf_op jit(solution)/shard_map/all_to_all | solution.py:405
  32.6 35.7 %copy-start.1 = (f32[4]{0:T(128)S(1)}, f32[4]{0:T(128)}, u32[]{:S(2)}) copy-start(f32[4]{0:T(128)} %penalty_ref.1) | copy-start | bytes 52
  32.7 35.7 %copy-start.2 = (f32[4]{0:T(128)S(1)}, f32[4]{0:T(128)}, u32[]{:S(2)}) copy-start(f32[4]{0:T(128)} %power_ref.1) | copy-start | bytes 52
  32.7 26.1 %collective-permute-start.6 = (bf16[2,4,64,256]{3,2,1,0:T(8,128)(2,1)S(1)}, bf16[2,4,64,256]{3,2,1,0:T(8,128)(2,1)S(1)}, u32[]{:S(2)}, u32[]{:S(2)}) collective-permute-start(bf16[2,4,64,256]{3,2,1,0:T(8,128)(2,1)S(1)} %get-tuple-element.21.refs_0_), channel_id=1, source_target_pairs={{0,3},{1,2},{2,1},{3,0},{4,7},{5,6},{6,5},{7,4},{8,11},{9,10},{10,... | collective-permute-start | bytes 786440 | tf_op jit(solution)/shard_map/ppermute | solution.py:373
  34.6 24.1 %collective-permute-start.7 = (bf16[2,4,64,256]{3,2,1,0:T(8,128)(2,1)S(1)}, bf16[2,4,64,256]{3,2,1,0:T(8,128)(2,1)S(1)}, u32[]{:S(2)}, u32[]{:S(2)}) collective-permute-start(bf16[2,4,64,256]{3,2,1,0:T(8,128)(2,1)S(1)} %get-tuple-element.20.refs_1_), channel_id=1, source_target_pairs={{0,3},{1,2},{2,1},{3,0},{4,7},{5,6},{6,5},{7,4},{8,11},{9,10},{10,... | collective-permute-start | bytes 786440 | tf_op jit(solution)/shard_map/ppermute | solution.py:373
  35.4 23.4 %collective-permute-start.8 = (bf16[2,4,64,256]{3,2,1,0:T(8,128)(2,1)S(1)}, bf16[2,4,64,256]{3,2,1,0:T(8,128)(2,1)S(1)}, u32[]{:S(2)}, u32[]{:S(2)}) collective-permute-start(bf16[2,4,64,256]{3,2,1,0:T(8,128)(2,1)S(1)} %collective-permute-done.refs_2_), channel_id=1, source_target_pairs={{0,3},{1,2},{2,1},{3,0},{4,7},{5,6},{6,5},{7,4},{8,11},{9,10},{10,... | collective-permute-start | bytes 786440 | tf_op jit(solution)/shard_map/ppermute | solution.py:373
  37.3 21.5 %collective-permute-start.9 = (bf16[2,4,64,256]{3,2,1,0:T(8,128)(2,1)S(1)}, bf16[2,4,64,256]{3,2,1,0:T(8,128)(2,1)S(1)}, u32[]{:S(2)}, u32[]{:S(2)}) collective-permute-start(bf16[2,4,64,256]{3,2,1,0:T(8,128)(2,1)S(1)} %collective-permute-done.2.refs_3_), channel_id=1, source_target_pairs={{0,3},{1,2},{2,1},{3,0},{4,7},{5,6},{6,5},{7,4},{8,11},{9,10},{10,... | collective-permute-start | bytes 786440 | tf_op jit(solution)/shard_map/ppermute | solution.py:373
  52.1 16.3 %all-to-all-start.1 = ((f32[128,1,128]{2,1,0:T(1,128)}), f32[128,1,128]{2,1,0:T(1,128)S(1)}, u32[]{:S(2)}, u32[]{:S(2)}) async-start(f32[128,1,128]{2,1,0:T(1,128)} %bitcast.37), calls=%async_computation.1 | async-start | bytes 131072 | tf_op jit(solution)/shard_map/all_to_all | solution.py:407

commit v4 on v3

--- a/solution.py
+++ b/solution.py
@@ -21,25 +21,22 @@
     return lax.dot_general(a, b, (dims, ((), ())), precision=precision, preferred_element_type=F32)
 
 
-def three_parts(x):
+def two_parts(x):
     high = x.astype(BF16)
-    rest = x - high.astype(F32)
-    middle = rest.astype(BF16)
-    low = (rest - middle.astype(F32)).astype(BF16)
-    return high, middle, low
+    return high, (x - high.astype(F32)).astype(BF16)
 
 
 def iota(shape, dim):
     return lax.broadcasted_iota(jnp.int32, shape, dim)
 
 
-def gain_kernel(core_ref, ht_ref, ha_ref, vt_ref, vb_ref, keep_ref, send_ref):
+def gain_kernel(block, core_ref, ht_ref, ha_ref, vt_ref, vb_ref, keep_ref, send_ref):
     core = core_ref[0]
-    rows, users = ht_ref.shape
+    _, rows, users = ht_ref.shape
     half = rows // 2
     chips = keep_ref.shape[0]
     piece = users // chips
-    vt, vb = vt_ref[...], vb_ref[...]
+    vt, vb = vt_ref[block], vb_ref[block]
     first = core == 0
     keep_v = jnp.where(first, vt, vb)
     send_v = jnp.where(first, vb, vt)
@@ -48,7 +45,7 @@
     for v in (keep_v, send_v):
         pairs += [v, jnp.concatenate([v[half:], -v[:half]], axis=0)]
     for tile, h_ref in enumerate((ht_ref, ha_ref)):
-        h = jnp.transpose(h_ref[...])
+        h = jnp.transpose(h_ref[block])
         for at, v in enumerate(pairs):
             side, part = at // 2, at % 2
             own = first if side == 0 else jnp.logical_not(first)
@@ -59,18 +56,18 @@
             out_ref[:, part, tile] = g.reshape(chips, piece, users).astype(out_ref.dtype)
 
 
-def partial_gains(core, ht, ha, vt, vb, chips):
-    users = ht.shape[-1]
+def partial_gains(block, core, ht, ha, vt, vb, chips):
+    _, rows, users = ht.shape
     shape = (chips, 2, 2, users // chips, users)
     vm = pl.BlockSpec(memory_space=pltpu.VMEM)
     return pl.pallas_call(
-        gain_kernel,
-        out_shape=(jax.ShapeDtypeStruct(shape, F32), jax.ShapeDtypeStruct(shape, BF16)),
+        functools.partial(gain_kernel, block),
+        out_shape=(jax.ShapeDtypeStruct(shape, BF16), jax.ShapeDtypeStruct(shape, BF16)),
         in_specs=[pl.BlockSpec(memory_space=pltpu.SMEM)] + [vm] * 4,
         out_specs=(vm, vm),
         name="gains",
         compiler_params=pltpu.CompilerParams(vmem_limit_bytes=8 << 20),
-        cost_estimate=pl.CostEstimate(flops=8 * users * users * ht.shape[0] * 2, bytes_accessed=4 << 20, transcendentals=0),
+        cost_estimate=pl.CostEstimate(flops=8 * users * users * rows * 2, bytes_accessed=4 << 20, transcendentals=0),
     )(core, ht, ha, vt, vb)
 
 
@@ -78,7 +75,7 @@
     chips, _, _, piece, users = keep0_ref.shape
     rows = 4 * piece
     for block, (keep_ref, came_ref) in enumerate(((keep0_ref, came0_ref), (keep1_ref, came1_ref))):
-        g = keep_ref[...] + came_ref[...].astype(F32)
+        g = keep_ref[...].astype(F32) + came_ref[...].astype(F32)
         out_ref[:, block * rows : (block + 1) * rows] = g.reshape(chips, rows, users).astype(BF16)
     out_ref[:, 2 * rows :] = jnp.broadcast_to(extra_ref[...][None], (chips,) + extra_ref.shape)
 
@@ -99,7 +96,7 @@
 def total_kernel(where_ref, g_ref, noise_ref, out_ref):
     chip, core = where_ref[0], where_ref[1]
     chips, rows, users = g_ref.shape
-    piece = (rows - 16) // 8
+    piece = (rows - 8) // 8
     lanes = out_ref.shape[1]
     width = 4 * piece
     lane = iota((2 * piece, lanes), 1)
@@ -108,7 +105,7 @@
     extra = g_ref[0, 8 * piece :].astype(F32)
     for source in range(1, chips):
         extra = extra + g_ref[source, 8 * piece :].astype(F32)
-    signal = extra[:8] + extra[8:]
+    signal = extra + pltpu.roll(extra, 4, 0)
     noise = jnp.where(core == 0, noise_ref[...], 0.0)
     signal = jnp.concatenate([signal[:4], noise, noise], axis=0)
     pick = iota((users, lanes), 0) == chip * piece + iota((users, lanes), 1) % piece
@@ -182,7 +179,7 @@
         line_ref[block, 1] = signal_re / rest
         line_ref[block, 2] = signal_im / rest
         line_ref[block, 3] = level / rest
-        weight_ref[block] = line_ref[block, 3, pl.ds(tile, 1)]
+        weight_ref[block : block + 1, :] = line_ref[block, 3, pl.ds(tile, 1)]
 
 
 def regrouped(pieces, wanted):
@@ -271,10 +268,9 @@
 
 
 def solve_kernel(tile_ref, penalty_ref, power_ref, r_ref, *refs):
-    h_refs = refs[:8]
-    out_ref, weight_ref, line_ref, sys_ref, work_ref, scale_ref, y_ref = refs[8:]
-    blocks = 2
-    _, points, antennas, users = h_refs[0].shape
+    h_refs = refs[:4]
+    out_ref, weight_ref, line_ref, sys_ref, work_ref, scale_ref, y_ref, made_ref, sems = refs[4:]
+    blocks, _, points, antennas, users = h_refs[0].shape
     size = 2 * antennas
     systems = blocks * points
     tile = tile_ref[0]
@@ -285,8 +281,8 @@
         return line_ref[block, which, pl.ds(tile ^ SLOTS[slot], 1), :]
 
     def channel(block, slot, point):
-        h_ref = h_refs[slot * blocks + block]
-        return jnp.concatenate([h_ref[0, point], h_ref[1, point]], axis=0)
+        h_ref = h_refs[slot]
+        return jnp.concatenate([h_ref[block, 0, point], h_ref[block, 1, point]], axis=0)
 
     lane = iota((antennas, size), 1)
     row = iota((antennas, size), 0)
@@ -298,16 +294,17 @@
             for slot in range(4):
                 x = channel(block, slot, point)
                 weighted = x.astype(F32) * line(block, 0, slot)
-                parts = jnp.concatenate(three_parts(weighted), axis=0)
-                term = dot(parts, x, ((1,), (1,)))
+                parts = jnp.concatenate(two_parts(weighted), axis=0)
+                term = dot(x, parts, ((1,), (1,)))
                 acc = term if acc is None else acc + term
-            p = acc[:size] + (acc[size : 2 * size] + acc[2 * size :])
+            p = acc[:, :size] + acc[:, size:]
             a = p[:antennas] * upper + pltpu.roll(p[antennas:], antennas, 1)
             a = a + jnp.where(lane == row, penalty_ref[point], 0.0)
             sys_ref[block * points + point] = a
 
     eliminate(work_ref, sys_ref, scale_ref)
 
+    copies = []
     for point in range(points):
         total = jnp.zeros((1, users), F32)
         for block in range(blocks):
@@ -316,11 +313,10 @@
             q = dot(z, z, ((0,), (0,)), HIGHEST)
             top = q[:antennas] * upper + pltpu.roll(q[antennas:], antennas, 1)
             bottom = pltpu.roll(top, antennas, 1) * (-upper)
-            parts = three_parts(jnp.concatenate([top, bottom], axis=0))
+            parts = jnp.concatenate(two_parts(jnp.concatenate([top, bottom], axis=0)), axis=1)
             for slot in range(4):
-                depth = 3 if slot == 0 else 2
                 x = channel(block, slot, point)
-                y = dot(jnp.concatenate(parts[:depth], axis=1), jnp.concatenate([x] * depth, axis=0), ((1,), (0,)))
+                y = dot(parts, jnp.concatenate([x, x], axis=0), ((1,), (0,)))
                 w_re, w_im = line(block, 1, slot), line(block, 2, slot)
                 total = total + jnp.sum(y * y, axis=0, keepdims=True) * (w_re * w_re + w_im * w_im)
                 if slot == 0:
@@ -331,8 +327,13 @@
             y_re, y_im = y_ref[block, :antennas], y_ref[block, antennas:]
             w_re = line(block, 1, 0) * gain
             w_im = line(block, 2, 0) * gain
-            out_ref[block, 0, point] = (y_re * w_re - y_im * w_im).astype(out_ref.dtype)
-            out_ref[block, 1, point] = (y_re * w_im + y_im * w_re).astype(out_ref.dtype)
+            made_ref[point, block, 0] = (y_re * w_re - y_im * w_im).astype(out_ref.dtype)
+            made_ref[point, block, 1] = (y_re * w_im + y_im * w_re).astype(out_ref.dtype)
+        copy = pltpu.make_async_copy(made_ref.at[point], out_ref.at[:, :, point], sems.at[point])
+        copy.start()
+        copies.append(copy)
+    for copy in copies:
+        copy.wait()
 
 
 def solve(tile, penalty, power, r, channels, out_shape):
@@ -344,16 +345,18 @@
         solve_kernel,
         out_shape=(
             jax.ShapeDtypeStruct(out_shape, BF16),
-            jax.ShapeDtypeStruct((blocks, 1, users), F32),
+            jax.ShapeDtypeStruct((blocks, users), F32),
         ),
-        in_specs=[sm] * 3 + [vm] * 9,
-        out_specs=(vm, vm),
+        in_specs=[sm] * 3 + [vm] * 5,
+        out_specs=(pl.BlockSpec(memory_space=pl.ANY), vm),
         scratch_shapes=[
             pltpu.VMEM((blocks, 4, 8, users), F32),
             pltpu.VMEM((blocks * points, antennas, size), F32),
             pltpu.VMEM((8, antennas, size), F32),
             pltpu.VMEM((antennas, size), F32),
             pltpu.VMEM((blocks, size, users), F32),
+            pltpu.VMEM((points, blocks, 2, antennas, users), BF16),
+            pltpu.SemaphoreType.DMA((points,)),
         ],
         name="solve",
         compiler_params=pltpu.CompilerParams(vmem_limit_bytes=16 << 20),
@@ -383,22 +386,25 @@
     tile = lax.axis_index("ut")
     chip = lax.axis_index(CHIPS)
 
-    v_far = [across(start_precoder[b], "ut", 3) for b in range(blocks)]
-    mask = cluster[:, 0].astype(BF16)[None, :, None, None]
-    own = [channel[b] * mask for b in range(blocks)]
-    near = [across(own[b], "ut", 1) for b in range(blocks)]
-    far = [across(own[b], "ut", 3) for b in range(blocks)]
-    far_near = [across(near[b], "ut", 3) for b in range(blocks)]
+    def masked(field, served):
+        return field * served[:, 0].astype(BF16)[None, None, :, None, None]
+
+    near_cluster = across(cluster, "ut", 1)
+    near = across(channel, "ut", 1)
+    v_far = across(start_precoder, "ut", 3)
+    own = masked(channel, cluster)
+    near = masked(near, near_cluster)
+    far = across(own, "ut", 3)
+    far_near = across(near, "ut", 3)
 
     signal = jnp.concatenate([own_signal(own[b], start_precoder[b]) for b in range(blocks)])
     high = lax.reduce_precision(signal, 8, 7)
-    pad = jnp.zeros_like(signal)
-    extra = jnp.concatenate([high, pad, signal - high, pad]).astype(BF16)
+    extra = jnp.concatenate([high, signal - high]).astype(BF16)
 
     keeps, cames = [], []
+    flat = [x.reshape(blocks, rows, users) for x in (own, near, start_precoder, v_far)]
     for b in range(blocks):
-        flat = [x.reshape(rows, users) for x in (own[b], near[b], start_precoder[b], v_far[b])]
-        keep, send = partial_gains(core.reshape(1), *flat, chips)
+        keep, send = partial_gains(b, core.reshape(1), *flat, chips)
         keeps.append(keep)
         cames.append(across(send, "core", 1))
     gains = combined(keeps, cames, extra)
@@ -406,9 +412,8 @@
     line = totals(jnp.stack([chip, core]), summed, noise, devices)
     r = lax.all_to_all(line, EVERY, 0, 0, tiled=True).reshape(chips, devices // chips, 128)
 
-    channels = [x[b] for x in (own, near, far, far_near) for b in range(blocks)]
-    precoder, weight = solve(tile.reshape(1), penalty, power, r, channels, channel.shape)
-    return precoder, weight[:, 0]
+    precoder, weight = solve(tile.reshape(1), penalty, power, r, (own, near, far, far_near), channel.shape)
+    return precoder, weight
 
 
 def solution(mesh):

time: 82.9 us -> 79.9 us (0.964)
  waiting for transfers between devices: 29.9 us -> 34.9 us
  starting transfers between devices: 30.1 us -> 25.2 us
  local copies, waits for them, and re-layouts: 1.63 us -> 0.02 us
  Pallas kernels: 17.9 us -> 16.6 us
    ppermute x10 -> x7, starting transfers between devices: 15.7 us -> 10 us  [across(): return lax.ppermute(value, axis, [(i, i ^ mask) for i in range(size)])]
    ppermute x10 -> x7, waiting for transfers between devices: 7.91 us -> 11.2 us  [across(): return lax.ppermute(value, axis, [(i, i ^ mask) for i in range(size)])]
    all_to_all x1, waiting for transfers between devices: 12.4 us -> 14.1 us  [local(): summed = lax.all_to_all(gains, CHIPS, 0, 0, tiled=True)]
    pallas_call x1, Pallas kernels: 13.7 us -> 12.4 us  [solve(): pl.pallas_call(solve_kernel, out_shape=(jax.ShapeDtypeStruct(out_shape, B...]
  transfers between devices with their start and end apart: 12 -> 9, of which waited for: 6 -> 6; matrix products, arithmetic and copies ran while one was open for 2% -> 3% of each run, Pallas kernels for 4% -> 2%
where the time goes in v4:
time: 79.9 us; the launch traced here: 79.6 us
  waiting for transfers between devices  34.9 us (44%)
  starting transfers between devices  25.2 us (32%)
  Pallas kernels  16.6 us (21%)
  other arithmetic  2.24 us (3%)
    all_to_all x1, waiting for transfers between devices, local(): summed = lax.all_to_all(gains, CHIPS, 0, 0, tiled=True)  14.1 us
    pallas_call x1, Pallas kernels, solve(): pl.pallas_call(solve_kernel, out_shape=(jax.ShapeDtypeStruct(out_shape, B...  12.4 us
    ppermute x7, waiting for transfers between devices, across(): return lax.ppermute(value, axis, [(i, i ^ mask) for i in range(size)])  11.2 us
    ppermute x7, starting transfers between devices, across(): return lax.ppermute(value, axis, [(i, i ^ mask) for i in range(size)])  10 us
    all_to_all x1, waiting for transfers between devices, local(): lax.all_to_all(line, EVERY, 0, 0, tiled=True)  9.57 us
    all_to_all x1, starting transfers between devices, local(): summed = lax.all_to_all(gains, CHIPS, 0, 0, tiled=True)  7.73 us
    all_to_all x1, starting transfers between devices, local(): lax.all_to_all(line, EVERY, 0, 0, tiled=True)  7.39 us
  transfers between devices with their start and end apart: 9, of which 6 were waited for; matrix products, arithmetic and copies ran while one was open for 3% of the time, Pallas kernels for 2%

profile of v4, /device:TPU:1, one launch (start us, length us, event | category | flops | bytes accessed | tf_op | source)
XLA Modules:
  0.0 79.6 jit_solution(810410389063740469)
XLA Ops:
  0.6 0.0 copy-start
  0.6 2.2 %collective-permute-start = (bf16[2,2,4,64,256]{4,3,2,1,0:T(8,128)(2,1)}, bf16[2,2,4,64,256]{4,3,2,1,0:T(8,128)(2,1)S(1)}, u32[]{:S(2)}, u32[]{:S(2)}) collective-permute-start(bf16[2,2,4,64,256]{4,3,2,1,0:T(8,128)(2,1)} %param.6), channel_id=1, source_target_pairs={{0,1},{1,0},{2,3},{3,2},{4,5},{5,4},{6,7},{7,6},{8,9},{9,8},{10,11... | collective-permute-start | bytes 1572872 | tf_op jit(solution)/shard_map/ppermute | solution.py:376
  2.8 0.1 collective-permute-start.1
  2.9 2.8 %collective-permute-start.2 = (bf16[2,2,4,64,256]{4,3,2,1,0:T(8,128)(2,1)}, bf16[2,2,4,64,256]{4,3,2,1,0:T(8,128)(2,1)S(1)}, u32[]{:S(2)}, u32[]{:S(2)}) collective-permute-start(bf16[2,2,4,64,256]{4,3,2,1,0:T(8,128)(2,1)} %param.7), channel_id=1, source_target_pairs={{0,3},{1,2},{2,1},{3,0},{4,7},{5,6},{6,5},{7,4},{8,11},{9,10},{10,... | collective-permute-start | bytes 1572872 | tf_op jit(solution)/shard_map/ppermute | solution.py:376
  5.7 0.7 convert_bitcast_fusion.1
  6.4 1.1 %broadcast_multiply_fusion.1.refs_0_ = bf16[2,2,4,64,256]{4,3,2,1,0:T(8,128)(2,1)S(1)} fusion(bf16[2,2,4,64,256]{4,3,2,1,0:T(8,128)(2,1)} %param.6, bf16[4]{0:T(256)(128)(2,1)S(1)} %convert_bitcast_fusion.1), kind=kLoop, calls=%fused_computation.17 | loop fusion | flops 262144 | bytes 1048584 | tf_op jit(solution)/shard_map/mul | solution.py:390
  7.6 6.8 %collective-permute-done.1 = s32[4,1]{0,1:T(1,128)S(1)} collective-permute-done((s32[4,1]{0,1:T(1,128)}, s32[4,1]{0,1:T(1,128)S(1)}, u32[]{:S(2)}, u32[]{:S(2)}) %collective-permute-start.1) | collective-permute-done | bytes 48 | tf_op jit(solution)/shard_map/ppermute | solution.py:376
  14.4 0.0 collective-permute-done
  14.4 0.1 broadcast_multiply_fusion.refs_1_
  14.5 2.4 %collective-permute-done.2 = bf16[2,2,4,64,256]{4,3,2,1,0:T(8,128)(2,1)S(1)} collective-permute-done((bf16[2,2,4,64,256]{4,3,2,1,0:T(8,128)(2,1)}, bf16[2,2,4,64,256]{4,3,2,1,0:T(8,128)(2,1)S(1)}, u32[]{:S(2)}, u32[]{:S(2)}) %collective-permute-start.2) | collective-permute-done | bytes 524320 | tf_op jit(solution)/shard_map/ppermute | solution.py:376
  16.9 0.0 copy-done
  16.9 0.7 gains.2
  17.6 0.7 gains.3
  18.4 2.0 %collective-permute-start.3 = (bf16[16,2,2,16,256]{4,3,2,1,0:T(8,128)(2,1)S(1)}, bf16[16,2,2,16,256]{4,3,2,1,0:T(8,128)(2,1)S(1)}, u32[]{:S(2)}, u32[]{:S(2)}) collective-permute-start(bf16[16,2,2,16,256]{4,3,2,1,0:T(8,128)(2,1)S(1)} %get-tuple-element.8), channel_id=1, source_target_pairs={{0,4},{4,0},{1,5},{5,1},{2,6},{6,2},{3,7},{7,3},{8,12},{12,8},{9,1... | collective-permute-start | bytes 1572872 | tf_op jit(solution)/shard_map/ppermute | solution.py:376
  20.4 0.1 collective-permute-start.4
  20.5 0.2 fusion.1
  20.7 1.2 %collective-permute-done.3.came0_ref = bf16[16,2,2,16,256]{4,3,2,1,0:T(8,128)(2,1)S(1)} collective-permute-done((bf16[16,2,2,16,256]{4,3,2,1,0:T(8,128)(2,1)S(1)}, bf16[16,2,2,16,256]{4,3,2,1,0:T(8,128)(2,1)S(1)}, u32[]{:S(2)}, u32[]{:S(2)}) %collective-permute-start.3) | collective-permute-done | bytes 524320 | tf_op jit(solution)/shard_map/ppermute | solution.py:376
  21.9 0.7 collective-permute-done.4.came1_ref
  22.7 1.2 %combine.1 = bf16[16,136,256]{2,1,0:T(8,128)(2,1)} custom-call(bf16[16,2,2,16,256]{4,3,2,1,0:T(8,128)(2,1)S(1)} %get-tuple-element.6.keep0_ref, bf16[16,2,2,16,256]{4,3,2,1,0:T(8,128)(2,1)S(1)} %get-tuple-element.7.keep1_ref, bf16[16,2,2,16,256]{4,3,2,1,0:T(8,128)(2,1)S(1)} %collective-permute-done.3.came0_ref, ...), custom_call_target="tpu_custom_call" | custom-call | tf_op jit(solution)/shard_map/combine/pallas_call | solution.py:86
  23.9 0.0 copy-start.1
  23.9 7.7 %all-to-all-start = ((bf16[16,136,256]{2,1,0:T(8,128)(2,1)}), bf16[16,136,256]{2,1,0:T(8,128)(2,1)S(1)}, u32[]{:S(2)}, u32[]{:S(2)}) async-start(bf16[16,136,256]{2,1,0:T(8,128)(2,1)} %combine.1), calls=%async_computation | async-start | bytes 2228224 | tf_op jit(solution)/shard_map/all_to_all | solution.py:411
  31.6 0.0 copy-start.2
  31.6 0.0 copy-start.3
  31.7 2.8 %collective-permute-start.5 = (bf16[2,2,4,64,256]{4,3,2,1,0:T(8,128)(2,1)S(1)}, bf16[2,2,4,64,256]{4,3,2,1,0:T(8,128)(2,1)S(1)}, u32[]{:S(2)}, u32[]{:S(2)}) collective-permute-start(bf16[2,2,4,64,256]{4,3,2,1,0:T(8,128)(2,1)S(1)} %broadcast_multiply_fusion.1.refs_0_), channel_id=1, source_target_pairs={{0,3},{1,2},{2,1},{3,0},{4,7},{5,6},{6,5},{7,4},{8,11},{9,10},{10,... | collective-permute-start | bytes 1572872 | tf_op jit(solution)/shard_map/ppermute | solution.py:376
  34.4 0.1 collective-permute-start.6
  34.5 0.1 pad_add_fusion.where_ref
  34.6 14.1 %all-to-all-done.g_ref = bf16[16,136,256]{2,1,0:T(8,128)(2,1)S(1)} async-done(((bf16[16,136,256]{2,1,0:T(8,128)(2,1)}), bf16[16,136,256]{2,1,0:T(8,128)(2,1)S(1)}, u32[]{:S(2)}, u32[]{:S(2)}) %all-to-all-start) | async-done | bytes 1114144 | tf_op jit(solution)/shard_map/all_to_all | solution.py:411
  48.7 0.0 copy-done.1
  48.7 1.5 %totals.1 = f32[128,128]{1,0:T(8,128)} custom-call(s32[2]{0:T(128)S(1)} %pad_add_fusion.where_ref, bf16[16,136,256]{2,1,0:T(8,128)(2,1)S(1)} %all-to-all-done.g_ref, f32[2,256]{1,0:T(2,128)S(1)} %copy-done.1), custom_call_target="tpu_custom_call" | custom-call | tf_op jit(solution)/shard_map/totals/pallas_call | solution.py:137
  50.2 7.4 %all-to-all-start.1 = ((f32[128,1,128]{2,1,0:T(1,128)}), f32[128,1,128]{2,1,0:T(1,128)S(1)}, u32[]{:S(2)}, u32[]{:S(2)}) async-start(f32[128,1,128]{2,1,0:T(1,128)} %bitcast.14), calls=%async_computation.1 | async-start | bytes 131072 | tf_op jit(solution)/shard_map/all_to_all | solution.py:413
  57.6 0.0 collective-permute-done.5.refs_2_
  57.6 0.0 collective-permute-done.6.refs_3_
  57.6 9.6 %all-to-all-done.1 = f32[128,1,128]{2,1,0:T(1,128)S(1)} async-done(((f32[128,1,128]{2,1,0:T(1,128)}), f32[128,1,128]{2,1,0:T(1,128)S(1)}, u32[]{:S(2)}, u32[]{:S(2)}) %all-to-all-start.1) | async-done | bytes 65568 | tf_op jit(solution)/shard_map/all_to_all | solution.py:413
  67.2 0.0 copy-done.2
  67.2 0.0 copy-done.3
  67.2 12.4 %solve.1 = (bf16[2,2,4,64,256]{4,3,2,1,0:T(8,128)(2,1)}, f32[2,256]{1,0:T(2,128)}) custom-call(s32[1]{0:T(128)} %bitcast.tile_ref, f32[4]{0:T(128)S(1)} %copy-done.2, f32[4]{0:T(128)S(1)} %copy-done.3, f32[16,8,128]{2,1,0:T(8,128)S(1)} %bitcast.27, bf16[2,2,4,64,256]{4,3,2,1,0:T(8,128)(2,1)S(1)} %broadcast_multiply_fusion.1.refs_0_, ...), custom_call_target="tpu_custom_call" | custom-call | tf_op jit(solution)/shard_map/solve/pallas_call | solution.py:344
  (3 shorter events, 0.0 us)
Async XLA Ops:
  0.6 16.3 %copy-start = (bf16[2,2,4,64,256]{4,3,2,1,0:T(8,128)(2,1)S(1)}, bf16[2,2,4,64,256]{4,3,2,1,0:T(8,128)(2,1)}, u32[]{:S(2)}) copy-start(bf16[2,2,4,64,256]{4,3,2,1,0:T(8,128)(2,1)} %param.7) | copy-start | bytes 1572868
  0.6 13.7 %collective-permute-start = (bf16[2,2,4,64,256]{4,3,2,1,0:T(8,128)(2,1)}, bf16[2,2,4,64,256]{4,3,2,1,0:T(8,128)(2,1)S(1)}, u32[]{:S(2)}, u32[]{:S(2)}) collective-permute-start(bf16[2,2,4,64,256]{4,3,2,1,0:T(8,128)(2,1)} %param.6), channel_id=1, source_target_pairs={{0,1},{1,0},{2,3},{3,2},{4,5},{5,4},{6,7},{7,6},{8,9},{9,8},{10,11... | collective-permute-start | bytes 1572872 | tf_op jit(solution)/shard_map/ppermute | solution.py:376
  2.8 11.5 %collective-permute-start.1 = (s32[4,1]{0,1:T(1,128)}, s32[4,1]{0,1:T(1,128)S(1)}, u32[]{:S(2)}, u32[]{:S(2)}) collective-permute-start(s32[4,1]{0,1:T(1,128)} %param.8), channel_id=1, source_target_pairs={{0,1},{1,0},{2,3},{3,2},{4,5},{5,4},{6,7},{7,6},{8,9},{9,8},{10,11... | collective-permute-start | bytes 56 | tf_op jit(solution)/shard_map/ppermute | solution.py:376
  2.9 14.0 %collective-permute-start.2 = (bf16[2,2,4,64,256]{4,3,2,1,0:T(8,128)(2,1)}, bf16[2,2,4,64,256]{4,3,2,1,0:T(8,128)(2,1)S(1)}, u32[]{:S(2)}, u32[]{:S(2)}) collective-permute-start(bf16[2,2,4,64,256]{4,3,2,1,0:T(8,128)(2,1)} %param.7), channel_id=1, source_target_pairs={{0,3},{1,2},{2,1},{3,0},{4,7},{5,6},{6,5},{7,4},{8,11},{9,10},{10,... | collective-permute-start | bytes 1572872 | tf_op jit(solution)/shard_map/ppermute | solution.py:376
  18.4 3.5 %collective-permute-start.3 = (bf16[16,2,2,16,256]{4,3,2,1,0:T(8,128)(2,1)S(1)}, bf16[16,2,2,16,256]{4,3,2,1,0:T(8,128)(2,1)S(1)}, u32[]{:S(2)}, u32[]{:S(2)}) collective-permute-start(bf16[16,2,2,16,256]{4,3,2,1,0:T(8,128)(2,1)S(1)} %get-tuple-element.8), channel_id=1, source_target_pairs={{0,4},{4,0},{1,5},{5,1},{2,6},{6,2},{3,7},{7,3},{8,12},{12,8},{9,1... | collective-permute-start | bytes 1572872 | tf_op jit(solution)/shard_map/ppermute | solution.py:376
  20.4 2.3 %collective-permute-start.4 = (bf16[16,2,2,16,256]{4,3,2,1,0:T(8,128)(2,1)S(1)}, bf16[16,2,2,16,256]{4,3,2,1,0:T(8,128)(2,1)S(1)}, u32[]{:S(2)}, u32[]{:S(2)}) collective-permute-start(bf16[16,2,2,16,256]{4,3,2,1,0:T(8,128)(2,1)S(1)} %get-tuple-element.9), channel_id=1, source_target_pairs={{0,4},{4,0},{1,5},{5,1},{2,6},{6,2},{3,7},{7,3},{8,12},{12,8},{9,1... | collective-permute-start | bytes 1572872 | tf_op jit(solution)/shard_map/ppermute | solution.py:376
  23.9 24.8 %copy-start.1 = (f32[2,256]{1,0:T(2,128)S(1)}, f32[2,256]{1,0:T(2,128)}, u32[]{:S(2)}) copy-start(f32[2,256]{1,0:T(2,128)} %noise_ref.1) | copy-start | bytes 6148
  23.9 24.8 %all-to-all-start = ((bf16[16,136,256]{2,1,0:T(8,128)(2,1)}), bf16[16,136,256]{2,1,0:T(8,128)(2,1)S(1)}, u32[]{:S(2)}, u32[]{:S(2)}) async-start(bf16[16,136,256]{2,1,0:T(8,128)(2,1)} %combine.1), calls=%async_computation | async-start | bytes 2228224 | tf_op jit(solution)/shard_map/all_to_all | solution.py:411
  31.6 35.5 %copy-start.2 = (f32[4]{0:T(128)S(1)}, f32[4]{0:T(128)}, u32[]{:S(2)}) copy-start(f32[4]{0:T(128)} %penalty_ref.1) | copy-start | bytes 52
  31.6 35.5 %copy-start.3 = (f32[4]{0:T(128)S(1)}, f32[4]{0:T(128)}, u32[]{:S(2)}) copy-start(f32[4]{0:T(128)} %power_ref.1) | copy-start | bytes 52
  31.7 25.9 %collective-permute-start.5 = (bf16[2,2,4,64,256]{4,3,2,1,0:T(8,128)(2,1)S(1)}, bf16[2,2,4,64,256]{4,3,2,1,0:T(8,128)(2,1)S(1)}, u32[]{:S(2)}, u32[]{:S(2)}) collective-permute-start(bf16[2,2,4,64,256]{4,3,2,1,0:T(8,128)(2,1)S(1)} %broadcast_multiply_fusion.1.refs_0_), channel_id=1, source_target_pairs={{0,3},{1,2},{2,1},{3,0},{4,7},{5,6},{6,5},{7,4},{8,11},{9,10},{10,... | collective-permute-start | bytes 1572872 | tf_op jit(solution)/shard_map/ppermute | solution.py:376
  34.4 23.2 %collective-permute-start.6 = (bf16[2,2,4,64,256]{4,3,2,1,0:T(8,128)(2,1)S(1)}, bf16[2,2,4,64,256]{4,3,2,1,0:T(8,128)(2,1)S(1)}, u32[]{:S(2)}, u32[]{:S(2)}) collective-permute-start(bf16[2,2,4,64,256]{4,3,2,1,0:T(8,128)(2,1)S(1)} %broadcast_multiply_fusion.refs_1_), channel_id=1, source_target_pairs={{0,3},{1,2},{2,1},{3,0},{4,7},{5,6},{6,5},{7,4},{8,11},{9,10},{10,... | collective-permute-start | bytes 1572872 | tf_op jit(solution)/shard_map/ppermute | solution.py:376
  50.2 17.0 %all-to-all-start.1 = ((f32[128,1,128]{2,1,0:T(1,128)}), f32[128,1,128]{2,1,0:T(1,128)S(1)}, u32[]{:S(2)}, u32[]{:S(2)}) async-start(f32[128,1,128]{2,1,0:T(1,128)} %bitcast.14), calls=%async_computation.1 | async-start | bytes 131072 | tf_op jit(solution)/shard_map/all_to_all | solution.py:413

commit v5 on v4

--- a/solution.py
+++ b/solution.py
@@ -30,35 +30,68 @@
     return lax.broadcasted_iota(jnp.int32, shape, dim)
 
 
+def turned(v):
+    half = v.shape[0] // 2
+    return jnp.concatenate([v[half:], -v[:half]], axis=0)
+
+
+def own_kernel(h_ref, v_ref, out_ref):
+    blocks, _, users = h_ref.shape
+    chips = out_ref.shape[0]
+    piece = users // chips
+    on_diag = iota((users, users), 0) == iota((users, users), 1)
+    high, low = [], []
+    for block in range(blocks):
+        h = jnp.transpose(h_ref[block])
+        v = v_ref[block]
+        for part, w in enumerate((v, turned(v))):
+            g = dot(h, w, ((1,), (0,)))
+            own = jnp.sum(jnp.where(on_diag, g, 0.0), axis=0, keepdims=True)
+            first, second = two_parts(own)
+            high.append(first.astype(F32))
+            low.append(second.astype(F32))
+            g = jnp.where(on_diag, 0.0, g)
+            at = (block * 2 + part) * piece
+            out_ref[:, at : at + piece] = g.reshape(chips, piece, users).astype(BF16)
+    extra = jnp.concatenate(high + low, axis=0).astype(BF16)
+    out_ref[:, 4 * piece :] = jnp.broadcast_to(extra[None], (chips,) + extra.shape)
+
+
+def own_gains(h, v, chips):
+    blocks, _, users = h.shape
+    vm = pl.BlockSpec(memory_space=pltpu.VMEM)
+    return pl.pallas_call(
+        own_kernel,
+        out_shape=jax.ShapeDtypeStruct((chips, 4 * (users // chips) + 8, users), BF16),
+        in_specs=[vm] * 2,
+        out_specs=vm,
+        name="own_gains",
+        compiler_params=pltpu.CompilerParams(vmem_limit_bytes=8 << 20),
+    )(h, v)
+
+
 def gain_kernel(block, core_ref, ht_ref, ha_ref, vt_ref, vb_ref, keep_ref, send_ref):
-    core = core_ref[0]
-    _, rows, users = ht_ref.shape
-    half = rows // 2
+    _, _, users = ht_ref.shape
+    half = users // 2
     chips = keep_ref.shape[0]
     piece = users // chips
+    first = core_ref[0] == 0
     vt, vb = vt_ref[block], vb_ref[block]
-    first = core == 0
-    keep_v = jnp.where(first, vt, vb)
-    send_v = jnp.where(first, vb, vt)
-    on_diag = iota((users, users), 0) == iota((users, users), 1)
-    pairs = []
-    for v in (keep_v, send_v):
-        pairs += [v, jnp.concatenate([v[half:], -v[:half]], axis=0)]
-    for tile, h_ref in enumerate((ht_ref, ha_ref)):
-        h = jnp.transpose(h_ref[block])
-        for at, v in enumerate(pairs):
-            side, part = at // 2, at % 2
-            own = first if side == 0 else jnp.logical_not(first)
-            out_ref = keep_ref if side == 0 else send_ref
-            g = dot(h, v, ((1,), (0,)))
-            if tile == 0:
-                g = jnp.where(jnp.logical_and(on_diag, own), 0.0, g)
-            out_ref[:, part, tile] = g.reshape(chips, piece, users).astype(out_ref.dtype)
+    ht, ha = jnp.transpose(ht_ref[block]), jnp.transpose(ha_ref[block])
+    for out_ref, low in ((keep_ref, first), (send_ref, jnp.logical_not(first))):
+        own = jnp.where(low, vt[:, :half], vt[:, half:])
+        far = jnp.where(low, vb[:, :half], vb[:, half:])
+        both = jnp.concatenate([own, far], axis=1)
+        g = dot(ht, jnp.concatenate([far, turned(far)], axis=1), ((1,), (0,)))
+        for part in range(2):
+            out_ref[:, part, :, :half] = g[:, part * half : (part + 1) * half].reshape(chips, piece, half).astype(BF16)
+        for part, w in enumerate((both, turned(both))):
+            out_ref[:, part, :, half:] = dot(ha, w, ((1,), (0,))).reshape(chips, piece, users).astype(BF16)
 
 
 def partial_gains(block, core, ht, ha, vt, vb, chips):
     _, rows, users = ht.shape
-    shape = (chips, 2, 2, users // chips, users)
+    shape = (chips, 2, users // chips, users + users // 2)
     vm = pl.BlockSpec(memory_space=pltpu.VMEM)
     return pl.pallas_call(
         functools.partial(gain_kernel, block),
@@ -67,44 +100,45 @@
         out_specs=(vm, vm),
         name="gains",
         compiler_params=pltpu.CompilerParams(vmem_limit_bytes=8 << 20),
-        cost_estimate=pl.CostEstimate(flops=8 * users * users * rows * 2, bytes_accessed=4 << 20, transcendentals=0),
+        cost_estimate=pl.CostEstimate(flops=12 * users * users * rows, bytes_accessed=4 << 20, transcendentals=0),
     )(core, ht, ha, vt, vb)
 
 
-def combine_kernel(keep0_ref, keep1_ref, came0_ref, came1_ref, extra_ref, out_ref):
-    chips, _, _, piece, users = keep0_ref.shape
-    rows = 4 * piece
+def combine_kernel(keep0_ref, keep1_ref, came0_ref, came1_ref, out_ref):
+    chips, _, piece, width = keep0_ref.shape
+    rows = 2 * piece
     for block, (keep_ref, came_ref) in enumerate(((keep0_ref, came0_ref), (keep1_ref, came1_ref))):
-        g = keep_ref[...].astype(F32) + came_ref[...].astype(F32)
-        out_ref[:, block * rows : (block + 1) * rows] = g.reshape(chips, rows, users).astype(BF16)
-    out_ref[:, 2 * rows :] = jnp.broadcast_to(extra_ref[...][None], (chips,) + extra_ref.shape)
-
-
-def combined(keeps, cames, extra):
-    chips, _, _, piece, users = keeps[0].shape
+        g = keep_ref[...] + came_ref[...]
+        out_ref[:, block * rows : (block + 1) * rows] = g.reshape(chips, rows, width)
+
+
+def combined(keeps, cames):
+    chips, _, piece, width = keeps[0].shape
     vm = pl.BlockSpec(memory_space=pltpu.VMEM)
     return pl.pallas_call(
         combine_kernel,
-        out_shape=jax.ShapeDtypeStruct((chips, 8 * piece + extra.shape[0], users), BF16),
-        in_specs=[vm] * 5,
+        out_shape=jax.ShapeDtypeStruct((chips, 4 * piece, width), BF16),
+        in_specs=[vm] * 4,
         out_specs=vm,
         name="combine",
         compiler_params=pltpu.CompilerParams(vmem_limit_bytes=8 << 20),
-    )(*keeps, *cames, extra)
-
-
-def total_kernel(where_ref, g_ref, noise_ref, out_ref):
+    )(*keeps, *cames)
+
+
+def own_sum_kernel(where_ref, g_ref, noise_ref, sum_ref, line_ref):
     chip, core = where_ref[0], where_ref[1]
     chips, rows, users = g_ref.shape
-    piece = (rows - 8) // 8
-    lanes = out_ref.shape[1]
-    width = 4 * piece
-    lane = iota((2 * piece, lanes), 1)
-    row = iota((2 * piece, lanes), 0)
-
-    extra = g_ref[0, 8 * piece :].astype(F32)
-    for source in range(1, chips):
-        extra = extra + g_ref[source, 8 * piece :].astype(F32)
+    piece = (rows - 8) // 4
+    lanes = line_ref.shape[1]
+
+    def summed(at):
+        total = g_ref[0, at].astype(F32)
+        for source in range(1, chips):
+            total = total + g_ref[source, at].astype(F32)
+        return total
+
+    sum_ref[...] = summed(slice(0, 4 * piece))
+    extra = summed(slice(4 * piece, 4 * piece + 8))
     signal = extra + pltpu.roll(extra, 4, 0)
     noise = jnp.where(core == 0, noise_ref[...], 0.0)
     signal = jnp.concatenate([signal[:4], noise, noise], axis=0)
@@ -117,31 +151,63 @@
             at = block * 2 + part
             line = line + jnp.where(group == block * 4 + 2 + part, mine[at : at + 1], 0.0)
         line = line + jnp.where(group == block * 4, mine[4 + block : 5 + block], 0.0)
-
+    line_ref[...] = line
+
+
+def own_sum(where, g, noise):
+    chips, rows, users = g.shape
+    vm = pl.BlockSpec(memory_space=pltpu.VMEM)
+    return pl.pallas_call(
+        own_sum_kernel,
+        out_shape=(jax.ShapeDtypeStruct((rows - 8, users), F32), jax.ShapeDtypeStruct((1, 128), F32)),
+        in_specs=[pl.BlockSpec(memory_space=pltpu.SMEM), vm, vm],
+        out_specs=(vm, vm),
+        name="own_sum",
+        compiler_params=pltpu.CompilerParams(vmem_limit_bytes=8 << 20),
+    )(where, g, noise)
+
+
+def total_kernel(where_ref, g_ref, mine_ref, came_ref, line_ref, out_ref):
+    core = where_ref[1]
+    chips, rows, width = g_ref.shape
+    piece = rows // 4
+    users = mine_ref.shape[1]
+    half = width - users
+    lanes = out_ref.shape[1]
+    lane = iota((piece, lanes), 1)
+    row = iota((piece, lanes), 0)
+    line = line_ref[...]
     for block in range(2):
-        total = None
+        own, near = None, None
         for part in range(2):
-            base = (block * 2 + part) * 2 * piece
-            g = g_ref[0, base : base + 2 * piece].astype(F32)
+            at = slice((block * 2 + part) * piece, (block * 2 + part + 1) * piece)
+            g = g_ref[0, at].astype(F32)
             for source in range(1, chips):
-                g = g + g_ref[source, base : base + 2 * piece].astype(F32)
+                g = g + g_ref[source, at].astype(F32)
             square = g * g
-            total = square if total is None else total + square
-        total = jnp.sum(total, axis=1, keepdims=True)
-        line = line + jnp.sum(jnp.where(lane == row + block * width, total, 0.0), axis=0, keepdims=True)
+            g = mine_ref[at] + came_ref[at]
+            g = jnp.where(core == 0, g, 0.0)
+            here = square[:, :half] + g[:, :half] * g[:, :half] + g[:, half:] * g[:, half:]
+            there = square[:, half : 2 * half] + square[:, 2 * half :]
+            own = here if own is None else own + here
+            near = there if near is None else near + there
+        for quantity, total in enumerate((own, near)):
+            total = jnp.sum(total, axis=1, keepdims=True)
+            at = (block * 4 + quantity) * piece
+            line = line + jnp.sum(jnp.where(lane == row + at, total, 0.0), axis=0, keepdims=True)
     out_ref[...] = jnp.broadcast_to(line, out_ref.shape)
 
 
-def totals(where, g, noise, devices):
+def totals(where, g, mine, came, line, devices):
     vm = pl.BlockSpec(memory_space=pltpu.VMEM)
     return pl.pallas_call(
         total_kernel,
         out_shape=jax.ShapeDtypeStruct((devices, 128), F32),
-        in_specs=[pl.BlockSpec(memory_space=pltpu.SMEM), vm, vm],
+        in_specs=[pl.BlockSpec(memory_space=pltpu.SMEM)] + [vm] * 4,
         out_specs=vm,
         name="totals",
         compiler_params=pltpu.CompilerParams(vmem_limit_bytes=8 << 20),
-    )(where, g, noise)
+    )(where, g, mine, came, line)
 
 
 def user_lines(r_ref, line_ref, weight_ref, tile):
@@ -182,21 +248,13 @@
         weight_ref[block : block + 1, :] = line_ref[block, 3, pl.ds(tile, 1)]
 
 
-def regrouped(pieces, wanted):
+def picked(pieces, g):
     lanes = pieces[0].shape[1]
-    width = lanes // 8
-    group = iota(pieces[0].shape, 1) // width
-    rolled = [pltpu.roll(piece, s * width, 1) if s else piece for s, piece in enumerate(pieces)]
-    results = []
-    for g in range(8):
-        if not wanted[g]:
-            results.append(None)
-            continue
-        total = rolled[0]
-        for s in range(1, 8):
-            total = jnp.where(group == (s + g) % 8, rolled[s], total)
-        results.append(pltpu.roll(total, lanes - g * width, 1) if g else total)
-    return results
+    group = iota(pieces[0].shape, 1) // (lanes // 8)
+    total = pieces[0]
+    for s in range(1, 8):
+        total = jnp.where(group == (s + g) % 8, pieces[s], total)
+    return total
 
 
 def eliminate(work_ref, sys_ref, scale_ref):
@@ -206,9 +264,10 @@
     sublane = iota((8, lanes), 0)
     for high in range(rows // 8):
         at = slice(high * 8, high * 8 + 8)
-        groups = regrouped([sys_ref[s, at, :] for s in range(8)], [True] * 8)
+        pieces = [sys_ref[s, at, :] for s in range(8)]
         for g in range(8):
-            work_ref[g, at, :] = groups[g]
+            group = picked(pieces, g)
+            work_ref[g, at, :] = pltpu.roll(group, lanes - g * width, 1) if g else group
 
     def spread(value, k):
         return jnp.take_along_axis(value, lane // width * width + k % width, axis=1, mode="promise_in_bounds")
@@ -244,8 +303,6 @@
         first = (k + 1) // 8
         update(k, first, *now)
         later = pivot(k + 1)
-        if first != k // 8:
-            pass
         for high in range(first + 1, rows // 8):
             update(k, high, *now)
         now = later
@@ -261,10 +318,10 @@
             kept = jnp.where(here < row, work_ref[g, at, :], 0.0)
             if g < 4:
                 kept = jnp.where(here == row, 1.0, kept)
-            pieces.append(kept * scale)
-        systems = regrouped(pieces, [True] * 8)
+            kept = kept * scale
+            pieces.append(pltpu.roll(kept, g * width, 1) if g else kept)
         for s in range(8):
-            sys_ref[s, at, :] = systems[s]
+            sys_ref[s, at, :] = picked(pieces, s)
 
 
 def solve_kernel(tile_ref, penalty_ref, power_ref, r_ref, *refs):
@@ -284,23 +341,33 @@
         h_ref = h_refs[slot]
         return jnp.concatenate([h_ref[block, 0, point], h_ref[block, 1, point]], axis=0)
 
+    width = size // systems
     lane = iota((antennas, size), 1)
     row = iota((antennas, size), 0)
-    upper = jnp.where(lane < antennas, 1.0, -1.0).astype(F32)
+
+    def turn(x, n):
+        cut = size - n * width
+        return jnp.concatenate([x[cut:], x[:cut]], axis=0) if n else x
+
+    def column(n):
+        return (lane + (size - n * width)) % size
 
     for block in range(blocks):
         for point in range(points):
-            acc = None
+            n = block * points + point
+            xs, highs, lows = [], [], []
             for slot in range(4):
                 x = channel(block, slot, point)
-                weighted = x.astype(F32) * line(block, 0, slot)
-                parts = jnp.concatenate(two_parts(weighted), axis=0)
-                term = dot(x, parts, ((1,), (1,)))
-                acc = term if acc is None else acc + term
+                high, low = two_parts(turn(x, n).astype(F32) * line(block, 0, slot))
+                xs.append(x)
+                highs.append(high)
+                lows.append(low)
+            parts = jnp.concatenate([jnp.concatenate(highs, axis=1), jnp.concatenate(lows, axis=1)], axis=0)
+            acc = dot(jnp.concatenate(xs, axis=1), parts, ((1,), (1,)))
             p = acc[:, :size] + acc[:, size:]
-            a = p[:antennas] * upper + pltpu.roll(p[antennas:], antennas, 1)
-            a = a + jnp.where(lane == row, penalty_ref[point], 0.0)
-            sys_ref[block * points + point] = a
+            a = jnp.where(column(n) < antennas, p[:antennas], -p[:antennas]) + pltpu.roll(p[antennas:], antennas, 1)
+            a = a + jnp.where(column(n) == row, penalty_ref[point], 0.0)
+            sys_ref[n] = a
 
     eliminate(work_ref, sys_ref, scale_ref)
 
@@ -309,13 +376,16 @@
         total = jnp.zeros((1, users), F32)
         for block in range(blocks):
             n = block * points + point
-            z = sys_ref[n]
-            q = dot(z, z, ((0,), (0,)), HIGHEST)
-            top = q[:antennas] * upper + pltpu.roll(q[antennas:], antennas, 1)
-            bottom = pltpu.roll(top, antennas, 1) * (-upper)
+            high, low = two_parts(sys_ref[n])
+            left = jnp.concatenate([high, high, low, low], axis=0)
+            right = jnp.concatenate([high, low, high, low], axis=0)
+            q = turn(dot(left, right, ((0,), (0,))), (systems - n) % systems)
+            top = jnp.where(column(n) < antennas, q[:antennas], -q[:antennas]) + pltpu.roll(q[antennas:], antennas, 1)
+            bottom = pltpu.roll(top, antennas, 1)
+            bottom = jnp.where(column(n) < antennas, -bottom, bottom)
             parts = jnp.concatenate(two_parts(jnp.concatenate([top, bottom], axis=0)), axis=1)
             for slot in range(4):
-                x = channel(block, slot, point)
+                x = turn(channel(block, slot, point), n)
                 y = dot(parts, jnp.concatenate([x, x], axis=0), ((1,), (0,)))
                 w_re, w_im = line(block, 1, slot), line(block, 2, slot)
                 total = total + jnp.sum(y * y, axis=0, keepdims=True) * (w_re * w_re + w_im * w_im)
@@ -363,14 +433,6 @@
     )(tile, penalty, power, r, *channels)
 
 
-def own_signal(served, precoder):
-    chan_re, chan_im = served[0].astype(F32), served[1].astype(F32)
-    prec_re, prec_im = precoder[0].astype(F32), precoder[1].astype(F32)
-    signal_re = jnp.sum(chan_re * prec_re + chan_im * prec_im, axis=(0, 1))
-    signal_im = jnp.sum(chan_re * prec_im - chan_im * prec_re, axis=(0, 1))
-    return jnp.stack([signal_re, signal_im])
-
-
 def across(value, axis, mask):
     size = lax.axis_size(axis)
     return lax.ppermute(value, axis, [(i, i ^ mask) for i in range(size)])
@@ -397,19 +459,20 @@
     far = across(own, "ut", 3)
     far_near = across(near, "ut", 3)
 
-    signal = jnp.concatenate([own_signal(own[b], start_precoder[b]) for b in range(blocks)])
-    high = lax.reduce_precision(signal, 8, 7)
-    extra = jnp.concatenate([high, signal - high]).astype(BF16)
+    where = jnp.stack([chip, core])
+    flat = [x.reshape(blocks, rows, users) for x in (own, near, start_precoder, v_far)]
+    early = lax.all_to_all(own_gains(flat[0], flat[2], chips), CHIPS, 0, 0, tiled=True)
 
     keeps, cames = [], []
-    flat = [x.reshape(blocks, rows, users) for x in (own, near, start_precoder, v_far)]
     for b in range(blocks):
         keep, send = partial_gains(b, core.reshape(1), *flat, chips)
         keeps.append(keep)
         cames.append(across(send, "core", 1))
-    gains = combined(keeps, cames, extra)
-    summed = lax.all_to_all(gains, CHIPS, 0, 0, tiled=True)
-    line = totals(jnp.stack([chip, core]), summed, noise, devices)
+    late = lax.all_to_all(combined(keeps, cames), CHIPS, 0, 0, tiled=True)
+
+    mine, line = own_sum(where, early, noise)
+    came = across(mine, "core", 1)
+    line = totals(where, late, mine, came, line, devices)
     r = lax.all_to_all(line, EVERY, 0, 0, tiled=True).reshape(chips, devices // chips, 128)
 
     precoder, weight = solve(tile.reshape(1), penalty, power, r, (own, near, far, far_near), channel.shape)

time: 79.9 us -> 75.7 us (0.947)
  waiting for transfers between devices: 34.9 us -> 20.2 us
  starting transfers between devices: 25.2 us -> 32.6 us
  Pallas kernels: 16.6 us -> 18.5 us
  local copies, waits for them, and re-layouts: 0.02 us -> 1.28 us
    all_to_all x1 -> x2, waiting for transfers between devices: 14.1 us -> 7.76 us  [the longest x1 4.18 us: local(): lax.all_to_all(own_gains(flat[0], flat[2], chips), CHIPS, 0, 0, tiled=True)]
    ppermute x7 -> x8, waiting for transfers between devices: 11.2 us -> 6.2 us  [across(): return lax.ppermute(value, axis, [(i, i ^ mask) for i in range(size)])]
    all_to_all x1 -> x2, starting transfers between devices: 7.73 us -> 11.2 us  [the longest x1 7.59 us: local(): lax.all_to_all(own_gains(flat[0], flat[2], chips), CHIPS, 0, 0, tiled=True)]
    all_to_all x1, waiting for transfers between devices: 9.57 us -> 6.22 us  [local(): lax.all_to_all(line, EVERY, 0, 0, tiled=True)]
    ppermute x7 -> x8, starting transfers between devices: 10 us -> 13.2 us  [across(): return lax.ppermute(value, axis, [(i, i ^ mask) for i in range(size)])]
    pallas_call x1 -> x3, Pallas kernels: 1.23 us -> 3.12 us  [the longest x1 1.32 us: own_gains(): pl.pallas_call(own_kernel, out_shape=jax.ShapeDtypeStruct((chips, 4 * (us...]
    unnamed x8, local copies, waits for them, and re-layouts: 0.02 us -> 1.28 us
    all_to_all x1, starting transfers between devices: 7.39 us -> 8.23 us  [local(): lax.all_to_all(line, EVERY, 0, 0, tiled=True)]
  transfers between devices with their start and end apart: 9 -> 11, of which waited for: 6 -> 8; matrix products, arithmetic and copies ran while one was open for 3% -> 3% of each run, Pallas kernels for 2% -> 8%
where the time goes in v5:
time: 75.7 us; the launch traced here: 75.3 us
  starting transfers between devices  32.6 us (43%)
  waiting for transfers between devices  20.2 us (27%)
  Pallas kernels  18.5 us (24%)
  other arithmetic  2.05 us (3%)
  local copies, waits for them, and re-layouts  1.28 us (2%)
    ppermute x8, starting transfers between devices, across(): return lax.ppermute(value, axis, [(i, i ^ mask) for i in range(size)])  13.2 us
    pallas_call x1, Pallas kernels, solve(): pl.pallas_call(solve_kernel, out_shape=(jax.ShapeDtypeStruct(out_shape, B...  12.7 us
    all_to_all x1, starting transfers between devices, local(): lax.all_to_all(line, EVERY, 0, 0, tiled=True)  8.23 us
    all_to_all x1, starting transfers between devices, local(): lax.all_to_all(own_gains(flat[0], flat[2], chips), CHIPS, 0, 0, tiled=True)  7.59 us
    all_to_all x1, waiting for transfers between devices, local(): lax.all_to_all(line, EVERY, 0, 0, tiled=True)  6.22 us
    ppermute x8, waiting for transfers between devices, across(): return lax.ppermute(value, axis, [(i, i ^ mask) for i in range(size)])  6.2 us
    all_to_all x1, waiting for transfers between devices, local(): lax.all_to_all(own_gains(flat[0], flat[2], chips), CHIPS, 0, 0, tiled=True)  4.18 us
    all_to_all x1, starting transfers between devices, local(): late = lax.all_to_all(combined(keeps, cames), CHIPS, 0, 0, tiled=True)  3.61 us
  transfers between devices with their start and end apart: 11, of which 8 were waited for; matrix products, arithmetic and copies ran while one was open for 3% of the time, Pallas kernels for 8%

profile of v5, /device:TPU:1, one launch (start us, length us, event | category | flops | bytes accessed | tf_op | source)
XLA Modules:
  0.0 75.3 jit_solution(2666896508516153507)
XLA Ops:
  0.6 2.2 %collective-permute-start = (bf16[2,2,4,64,256]{4,3,2,1,0:T(8,128)(2,1)}, bf16[2,2,4,64,256]{4,3,2,1,0:T(8,128)(2,1)S(1)}, u32[]{:S(2)}, u32[]{:S(2)}) collective-permute-start(bf16[2,2,4,64,256]{4,3,2,1,0:T(8,128)(2,1)} %param.6), channel_id=1, source_target_pairs={{0,1},{1,0},{2,3},{3,2},{4,5},{5,4},{6,7},{7,6},{8,9},{9,8},{10,11... | collective-permute-start | bytes 1572872 | tf_op jit(solution)/shard_map/ppermute | solution.py:438
  2.8 0.1 collective-permute-start.1
  2.9 2.8 %collective-permute-start.2 = (bf16[2,2,4,64,256]{4,3,2,1,0:T(8,128)(2,1)}, bf16[2,2,4,64,256]{4,3,2,1,0:T(8,128)(2,1)S(1)}, u32[]{:S(2)}, u32[]{:S(2)}) collective-permute-start(bf16[2,2,4,64,256]{4,3,2,1,0:T(8,128)(2,1)} %param.7), channel_id=1, source_target_pairs={{0,3},{1,2},{2,1},{3,0},{4,7},{5,6},{6,5},{7,4},{8,11},{9,10},{10,... | collective-permute-start | bytes 1572872 | tf_op jit(solution)/shard_map/ppermute | solution.py:438
  5.7 0.7 convert_bitcast_fusion.1
  6.4 0.0 copy-start
  6.4 1.2 %broadcast_multiply_fusion.1.refs_0_ = bf16[2,2,4,64,256]{4,3,2,1,0:T(8,128)(2,1)S(1)} fusion(bf16[2,2,4,64,256]{4,3,2,1,0:T(8,128)(2,1)} %param.6, bf16[4]{0:T(256)(128)(2,1)S(1)} %convert_bitcast_fusion.1), kind=kLoop, calls=%fused_computation.1 | loop fusion | flops 262144 | bytes 1048584 | tf_op jit(solution)/shard_map/mul | solution.py:452
  7.6 0.0 copy-done
  7.6 1.3 %own_gains.1 = bf16[16,72,256]{2,1,0:T(8,128)(2,1)} custom-call(bf16[2,512,256]{2,1,0:T(8,128)(2,1)S(1)} %bitcast.15, bf16[2,512,256]{2,1,0:T(8,128)(2,1)S(1)} %bitcast.20), custom_call_target="tpu_custom_call" | custom-call | tf_op jit(solution)/shard_map/own_gains/pallas_call | solution.py:63
  8.9 7.6 %all-to-all-start.1 = ((bf16[16,72,256]{2,1,0:T(8,128)(2,1)}), bf16[16,72,256]{2,1,0:T(8,128)(2,1)S(1)}, u32[]{:S(2)}, u32[]{:S(2)}) async-start(bf16[16,72,256]{2,1,0:T(8,128)(2,1)} %own_gains.1), calls=%async_computation.1 | async-start | bytes 1179648 | tf_op jit(solution)/shard_map/all_to_all | solution.py:464
  16.5 0.0 collective-permute-done.1
  16.6 0.0 collective-permute-done
  16.6 0.1 broadcast_multiply_fusion.refs_1_
  16.7 0.2 collective-permute-done.2
  16.9 0.6 gains.2
  17.5 2.0 %collective-permute-start.3 = (bf16[16,2,16,384]{3,2,1,0:T(8,128)(2,1)S(1)}, bf16[16,2,16,384]{3,2,1,0:T(8,128)(2,1)S(1)}, u32[]{:S(2)}, u32[]{:S(2)}) collective-permute-start(bf16[16,2,16,384]{3,2,1,0:T(8,128)(2,1)S(1)} %get-tuple-element.10), channel_id=1, source_target_pairs={{0,4},{4,0},{1,5},{5,1},{2,6},{6,2},{3,7},{7,3},{8,12},{12,8},{9,1... | collective-permute-start | bytes 1179656 | tf_op jit(solution)/shard_map/ppermute | solution.py:438
  19.5 0.6 gains.3
  20.2 0.1 collective-permute-start.4
  20.3 0.6 collective-permute-done.3.came0_ref
  20.9 1.1 %collective-permute-done.4.came1_ref = bf16[16,2,16,384]{3,2,1,0:T(8,128)(2,1)S(1)} collective-permute-done((bf16[16,2,16,384]{3,2,1,0:T(8,128)(2,1)S(1)}, bf16[16,2,16,384]{3,2,1,0:T(8,128)(2,1)S(1)}, u32[]{:S(2)}, u32[]{:S(2)}) %collective-permute-start.4) | collective-permute-done | bytes 393248 | tf_op jit(solution)/shard_map/ppermute | solution.py:438
  22.0 1.0 %combine.1 = bf16[16,64,384]{2,1,0:T(8,128)(2,1)} custom-call(bf16[16,2,16,384]{3,2,1,0:T(8,128)(2,1)S(1)} %get-tuple-element.8.keep0_ref, bf16[16,2,16,384]{3,2,1,0:T(8,128)(2,1)S(1)} %get-tuple-element.9.keep1_ref, bf16[16,2,16,384]{3,2,1,0:T(8,128)(2,1)S(1)} %collective-permute-done.3.came0_ref, bf16[16,2,16,384]{3,2,1,0:T(8,128)(2,1)S(1)} %collective-permute-done.4.came1_ref), custom_call_target="tpu_custom_call" | custom-call | tf_op jit(solution)/shard_map/combine/pallas_call | solution.py:118
  23.0 4.2 %all-to-all-done.1.g_ref = bf16[16,72,256]{2,1,0:T(8,128)(2,1)S(1)} async-done(((bf16[16,72,256]{2,1,0:T(8,128)(2,1)}), bf16[16,72,256]{2,1,0:T(8,128)(2,1)S(1)}, u32[]{:S(2)}, u32[]{:S(2)}) %all-to-all-start.1) | async-done | bytes 589856 | tf_op jit(solution)/shard_map/all_to_all | solution.py:464
  27.1 3.6 %all-to-all-start = ((bf16[16,64,384]{2,1,0:T(8,128)(2,1)}), bf16[16,64,384]{2,1,0:T(8,128)(2,1)S(1)}, u32[]{:S(2)}, u32[]{:S(2)}) async-start(bf16[16,64,384]{2,1,0:T(8,128)(2,1)} %combine.1), calls=%async_computation | async-start | bytes 1572864 | tf_op jit(solution)/shard_map/all_to_all | solution.py:471
  30.8 2.6 %collective-permute-start.6 = (bf16[2,2,4,64,256]{4,3,2,1,0:T(8,128)(2,1)S(1)}, bf16[2,2,4,64,256]{4,3,2,1,0:T(8,128)(2,1)S(1)}, u32[]{:S(2)}, u32[]{:S(2)}) collective-permute-start(bf16[2,2,4,64,256]{4,3,2,1,0:T(8,128)(2,1)S(1)} %broadcast_multiply_fusion.1.refs_0_), channel_id=1, source_target_pairs={{0,3},{1,2},{2,1},{3,0},{4,7},{5,6},{6,5},{7,4},{8,11},{9,10},{10,... | collective-permute-start | bytes 1572872 | tf_op jit(solution)/shard_map/ppermute | solution.py:438
  33.3 0.2 collective-permute-start.7
  33.5 0.0 copy-start.1
  33.5 0.1 pad_add_fusion.where_ref
  33.6 0.6 copy-done.1
  34.2 0.8 %own_sum.1 = (f32[64,256]{1,0:T(8,128)S(1)}, f32[1,128]{1,0:T(1,128)S(1)}) custom-call(s32[2]{0:T(128)S(1)} %pad_add_fusion.where_ref, bf16[16,72,256]{2,1,0:T(8,128)(2,1)S(1)} %all-to-all-done.1.g_ref, f32[2,256]{1,0:T(2,128)S(1)} %copy-done.1), custom_call_target="tpu_custom_call" | custom-call | tf_op jit(solution)/shard_map/own_sum/pallas_call | solution.py:160
  35.0 3.2 %collective-permute-start.5 = (f32[64,256]{1,0:T(8,128)S(1)}, f32[64,256]{1,0:T(8,128)S(1)}, u32[]{:S(2)}, u32[]{:S(2)}) collective-permute-start(f32[64,256]{1,0:T(8,128)S(1)} %get-tuple-element.12.mine_ref), channel_id=1, source_target_pairs={{0,4},{4,0},{1,5},{5,1},{2,6},{6,2},{3,7},{7,3},{8,12},{12,8},{9,1... | collective-permute-start | bytes 196616 | tf_op jit(solution)/shard_map/ppermute | solution.py:438
  38.2 0.9 %collective-permute-done.5.came_ref = f32[64,256]{1,0:T(8,128)S(1)} collective-permute-done((f32[64,256]{1,0:T(8,128)S(1)}, f32[64,256]{1,0:T(8,128)S(1)}, u32[]{:S(2)}, u32[]{:S(2)}) %collective-permute-start.5) | collective-permute-done | bytes 65568 | tf_op jit(solution)/shard_map/ppermute | solution.py:438
  39.1 3.6 %all-to-all-done.g_ref = bf16[16,64,384]{2,1,0:T(8,128)(2,1)S(1)} async-done(((bf16[16,64,384]{2,1,0:T(8,128)(2,1)}), bf16[16,64,384]{2,1,0:T(8,128)(2,1)S(1)}, u32[]{:S(2)}, u32[]{:S(2)}) %all-to-all-start) | async-done | bytes 786464 | tf_op jit(solution)/shard_map/all_to_all | solution.py:471
  42.7 1.4 %totals.1 = f32[128,128]{1,0:T(8,128)} custom-call(s32[2]{0:T(128)S(1)} %pad_add_fusion.where_ref, bf16[16,64,384]{2,1,0:T(8,128)(2,1)S(1)} %all-to-all-done.g_ref, f32[64,256]{1,0:T(8,128)S(1)} %get-tuple-element.12.mine_ref, f32[64,256]{1,0:T(8,128)S(1)} %collective-permute-done.5.came_ref, f32[1,128]{1,0:T(1,128)S(1)} %get-tuple-element.13.line_ref), custom_call_target="tpu_custom_call" | custom-call | tf_op jit(solution)/shard_map/totals/pallas_call | solution.py:203
  44.1 8.2 %all-to-all-start.2 = ((f32[128,1,128]{2,1,0:T(1,128)}), f32[128,1,128]{2,1,0:T(1,128)S(1)}, u32[]{:S(2)}, u32[]{:S(2)}) async-start(f32[128,1,128]{2,1,0:T(1,128)} %bitcast.10), calls=%async_computation.2 | async-start | bytes 131072 | tf_op jit(solution)/shard_map/all_to_all | solution.py:476
  52.3 0.0 collective-permute-done.6.refs_2_
  52.4 3.4 %collective-permute-done.7.refs_3_ = bf16[2,2,4,64,256]{4,3,2,1,0:T(8,128)(2,1)S(1)} collective-permute-done((bf16[2,2,4,64,256]{4,3,2,1,0:T(8,128)(2,1)S(1)}, bf16[2,2,4,64,256]{4,3,2,1,0:T(8,128)(2,1)S(1)}, u32[]{:S(2)}, u32[]{:S(2)}) %collective-permute-start.7) | collective-permute-done | bytes 524320 | tf_op jit(solution)/shard_map/ppermute | solution.py:438
  55.7 6.2 %all-to-all-done.2 = f32[128,1,128]{2,1,0:T(1,128)S(1)} async-done(((f32[128,1,128]{2,1,0:T(1,128)}), f32[128,1,128]{2,1,0:T(1,128)S(1)}, u32[]{:S(2)}, u32[]{:S(2)}) %all-to-all-start.2) | async-done | bytes 65568 | tf_op jit(solution)/shard_map/all_to_all | solution.py:476
  61.9 0.0 copy-start.2
  61.9 0.0 copy-start.3
  61.9 0.7 copy-done.2
  62.6 0.0 copy-done.3
  62.6 12.7 %solve.1 = (bf16[2,2,4,64,256]{4,3,2,1,0:T(8,128)(2,1)}, f32[2,256]{1,0:T(2,128)}) custom-call(s32[1]{0:T(128)} %bitcast.tile_ref, f32[4]{0:T(128)S(1)} %copy-done.2, f32[4]{0:T(128)S(1)} %copy-done.3, f32[16,8,128]{2,1,0:T(8,128)S(1)} %bitcast.25, bf16[2,2,4,64,256]{4,3,2,1,0:T(8,128)(2,1)S(1)} %broadcast_multiply_fusion.1.refs_0_, ...), custom_call_target="tpu_custom_call" | custom-call | tf_op jit(solution)/shard_map/solve/pallas_call | solution.py:414
  (1 shorter events, 0.0 us)
Async XLA Ops:
  0.6 15.9 %collective-permute-start = (bf16[2,2,4,64,256]{4,3,2,1,0:T(8,128)(2,1)}, bf16[2,2,4,64,256]{4,3,2,1,0:T(8,128)(2,1)S(1)}, u32[]{:S(2)}, u32[]{:S(2)}) collective-permute-start(bf16[2,2,4,64,256]{4,3,2,1,0:T(8,128)(2,1)} %param.6), channel_id=1, source_target_pairs={{0,1},{1,0},{2,3},{3,2},{4,5},{5,4},{6,7},{7,6},{8,9},{9,8},{10,11... | collective-permute-start | bytes 1572872 | tf_op jit(solution)/shard_map/ppermute | solution.py:438
  2.8 13.7 %collective-permute-start.1 = (s32[4,1]{0,1:T(1,128)}, s32[4,1]{0,1:T(1,128)S(1)}, u32[]{:S(2)}, u32[]{:S(2)}) collective-permute-start(s32[4,1]{0,1:T(1,128)} %param.8), channel_id=1, source_target_pairs={{0,1},{1,0},{2,3},{3,2},{4,5},{5,4},{6,7},{7,6},{8,9},{9,8},{10,11... | collective-permute-start | bytes 56 | tf_op jit(solution)/shard_map/ppermute | solution.py:438
  2.9 14.0 %collective-permute-start.2 = (bf16[2,2,4,64,256]{4,3,2,1,0:T(8,128)(2,1)}, bf16[2,2,4,64,256]{4,3,2,1,0:T(8,128)(2,1)S(1)}, u32[]{:S(2)}, u32[]{:S(2)}) collective-permute-start(bf16[2,2,4,64,256]{4,3,2,1,0:T(8,128)(2,1)} %param.7), channel_id=1, source_target_pairs={{0,3},{1,2},{2,1},{3,0},{4,7},{5,6},{6,5},{7,4},{8,11},{9,10},{10,... | collective-permute-start | bytes 1572872 | tf_op jit(solution)/shard_map/ppermute | solution.py:438
  6.4 1.2 %copy-start = (bf16[2,2,4,64,256]{4,3,2,1,0:T(8,128)(2,1)S(1)}, bf16[2,2,4,64,256]{4,3,2,1,0:T(8,128)(2,1)}, u32[]{:S(2)}) copy-start(bf16[2,2,4,64,256]{4,3,2,1,0:T(8,128)(2,1)} %param.7) | copy-start | bytes 1572868
  8.9 18.2 %all-to-all-start.1 = ((bf16[16,72,256]{2,1,0:T(8,128)(2,1)}), bf16[16,72,256]{2,1,0:T(8,128)(2,1)S(1)}, u32[]{:S(2)}, u32[]{:S(2)}) async-start(bf16[16,72,256]{2,1,0:T(8,128)(2,1)} %own_gains.1), calls=%async_computation.1 | async-start | bytes 1179648 | tf_op jit(solution)/shard_map/all_to_all | solution.py:464
  17.5 3.3 %collective-permute-start.3 = (bf16[16,2,16,384]{3,2,1,0:T(8,128)(2,1)S(1)}, bf16[16,2,16,384]{3,2,1,0:T(8,128)(2,1)S(1)}, u32[]{:S(2)}, u32[]{:S(2)}) collective-permute-start(bf16[16,2,16,384]{3,2,1,0:T(8,128)(2,1)S(1)} %get-tuple-element.10), channel_id=1, source_target_pairs={{0,4},{4,0},{1,5},{5,1},{2,6},{6,2},{3,7},{7,3},{8,12},{12,8},{9,1... | collective-permute-start | bytes 1179656 | tf_op jit(solution)/shard_map/ppermute | solution.py:438
  20.2 1.8 %collective-permute-start.4 = (bf16[16,2,16,384]{3,2,1,0:T(8,128)(2,1)S(1)}, bf16[16,2,16,384]{3,2,1,0:T(8,128)(2,1)S(1)}, u32[]{:S(2)}, u32[]{:S(2)}) collective-permute-start(bf16[16,2,16,384]{3,2,1,0:T(8,128)(2,1)S(1)} %get-tuple-element.11), channel_id=1, source_target_pairs={{0,4},{4,0},{1,5},{5,1},{2,6},{6,2},{3,7},{7,3},{8,12},{12,8},{9,1... | collective-permute-start | bytes 1179656 | tf_op jit(solution)/shard_map/ppermute | solution.py:438
  27.1 15.6 %all-to-all-start = ((bf16[16,64,384]{2,1,0:T(8,128)(2,1)}), bf16[16,64,384]{2,1,0:T(8,128)(2,1)S(1)}, u32[]{:S(2)}, u32[]{:S(2)}) async-start(bf16[16,64,384]{2,1,0:T(8,128)(2,1)} %combine.1), calls=%async_computation | async-start | bytes 1572864 | tf_op jit(solution)/shard_map/all_to_all | solution.py:471
  30.8 21.6 %collective-permute-start.6 = (bf16[2,2,4,64,256]{4,3,2,1,0:T(8,128)(2,1)S(1)}, bf16[2,2,4,64,256]{4,3,2,1,0:T(8,128)(2,1)S(1)}, u32[]{:S(2)}, u32[]{:S(2)}) collective-permute-start(bf16[2,2,4,64,256]{4,3,2,1,0:T(8,128)(2,1)S(1)} %broadcast_multiply_fusion.1.refs_0_), channel_id=1, source_target_pairs={{0,3},{1,2},{2,1},{3,0},{4,7},{5,6},{6,5},{7,4},{8,11},{9,10},{10,... | collective-permute-start | bytes 1572872 | tf_op jit(solution)/shard_map/ppermute | solution.py:438
  33.3 22.4 %collective-permute-start.7 = (bf16[2,2,4,64,256]{4,3,2,1,0:T(8,128)(2,1)S(1)}, bf16[2,2,4,64,256]{4,3,2,1,0:T(8,128)(2,1)S(1)}, u32[]{:S(2)}, u32[]{:S(2)}) collective-permute-start(bf16[2,2,4,64,256]{4,3,2,1,0:T(8,128)(2,1)S(1)} %broadcast_multiply_fusion.refs_1_), channel_id=1, source_target_pairs={{0,3},{1,2},{2,1},{3,0},{4,7},{5,6},{6,5},{7,4},{8,11},{9,10},{10,... | collective-permute-start | bytes 1572872 | tf_op jit(solution)/shard_map/ppermute | solution.py:438
  33.5 0.7 copy-start.1
  35.0 4.1 %collective-permute-start.5 = (f32[64,256]{1,0:T(8,128)S(1)}, f32[64,256]{1,0:T(8,128)S(1)}, u32[]{:S(2)}, u32[]{:S(2)}) collective-permute-start(f32[64,256]{1,0:T(8,128)S(1)} %get-tuple-element.12.mine_ref), channel_id=1, source_target_pairs={{0,4},{4,0},{1,5},{5,1},{2,6},{6,2},{3,7},{7,3},{8,12},{12,8},{9,1... | collective-permute-start | bytes 196616 | tf_op jit(solution)/shard_map/ppermute | solution.py:438
  44.1 17.8 %all-to-all-start.2 = ((f32[128,1,128]{2,1,0:T(1,128)}), f32[128,1,128]{2,1,0:T(1,128)S(1)}, u32[]{:S(2)}, u32[]{:S(2)}) async-start(f32[128,1,128]{2,1,0:T(1,128)} %bitcast.10), calls=%async_computation.2 | async-start | bytes 131072 | tf_op jit(solution)/shard_map/all_to_all | solution.py:476
  61.9 0.7 copy-start.2
  61.9 0.7 copy-start.3

commit v6 on v5

--- a/solution.py
+++ b/solution.py
@@ -8,6 +8,7 @@
 from jax.sharding import Mesh
 from jax.sharding import PartitionSpec as P
 
+
 AP = ("z", "x", "core")
 CHIPS = ("z", "x")
 EVERY = ("z", "x", "core", "ut")
@@ -35,63 +36,77 @@
     return jnp.concatenate([v[half:], -v[:half]], axis=0)
 
 
-def own_kernel(h_ref, v_ref, out_ref):
-    blocks, _, users = h_ref.shape
-    chips = out_ref.shape[0]
+def signal_kernel(core_ref, cluster_ref, noise_ref, penalty_ref, power_ref, h_ref, v_ref, out_ref, noise_out, penalty_out, power_out):
+    blocks, _, points, _, users = h_ref.shape
+    chips, lanes = out_ref.shape
     piece = users // chips
-    on_diag = iota((users, users), 0) == iota((users, users), 1)
-    high, low = [], []
+    at_chip = iota((chips, users), 1) // piece == iota((chips, users), 0)
+    placed = []
     for block in range(blocks):
-        h = jnp.transpose(h_ref[block])
-        v = v_ref[block]
-        for part, w in enumerate((v, turned(v))):
-            g = dot(h, w, ((1,), (0,)))
-            own = jnp.sum(jnp.where(on_diag, g, 0.0), axis=0, keepdims=True)
-            first, second = two_parts(own)
-            high.append(first.astype(F32))
-            low.append(second.astype(F32))
-            g = jnp.where(on_diag, 0.0, g)
-            at = (block * 2 + part) * piece
-            out_ref[:, at : at + piece] = g.reshape(chips, piece, users).astype(BF16)
-    extra = jnp.concatenate(high + low, axis=0).astype(BF16)
-    out_ref[:, 4 * piece :] = jnp.broadcast_to(extra[None], (chips,) + extra.shape)
-
-
-def own_gains(h, v, chips):
-    blocks, _, users = h.shape
+        real = jnp.zeros((1, users), F32)
+        imag = jnp.zeros((1, users), F32)
+        for point in range(points):
+            h_re, h_im = h_ref[block, 0, point].astype(F32), h_ref[block, 1, point].astype(F32)
+            v_re, v_im = v_ref[block, 0, point].astype(F32), v_ref[block, 1, point].astype(F32)
+            served = cluster_ref[point, 0].astype(F32)
+            real = real + jnp.sum(h_re * v_re + h_im * v_im, axis=0, keepdims=True) * served
+            imag = imag + jnp.sum(h_re * v_im - h_im * v_re, axis=0, keepdims=True) * served
+        noise = jnp.where(core_ref[0] == 0, noise_ref[block : block + 1], 0.0)
+        placed += [jnp.where(at_chip, x, 0.0) for x in (real, imag)]
+        noise_out[block : block + 1] = noise
+    pick = (iota((users, lanes), 0) % piece == iota((users, lanes), 1) % piece).astype(F32)
+    mine = dot(jnp.concatenate(placed, axis=0), pick, ((1,), (0,)), HIGHEST)
+    group = iota((chips, lanes), 1) // piece
+    line = jnp.zeros((chips, lanes), F32)
+    for block in range(blocks):
+        for part in range(2):
+            at = block * 2 + part
+            line = line + jnp.where(group == block * 4 + 2 + part, mine[at * chips : (at + 1) * chips], 0.0)
+    out_ref[...] = line
+    penalty_out[...] = penalty_ref[...]
+    power_out[...] = power_ref[...]
+
+
+def signals(core, cluster, noise, penalty, power, h, v, chips):
     vm = pl.BlockSpec(memory_space=pltpu.VMEM)
+    sm = pl.BlockSpec(memory_space=pltpu.SMEM)
+    points = penalty.shape[0]
     return pl.pallas_call(
-        own_kernel,
-        out_shape=jax.ShapeDtypeStruct((chips, 4 * (users // chips) + 8, users), BF16),
-        in_specs=[vm] * 2,
-        out_specs=vm,
-        name="own_gains",
+        signal_kernel,
+        out_shape=(
+            jax.ShapeDtypeStruct((chips, 128), F32),
+            jax.ShapeDtypeStruct(noise.shape, F32),
+            jax.ShapeDtypeStruct((1, points), F32),
+            jax.ShapeDtypeStruct((1, points), F32),
+        ),
+        in_specs=[sm] * 2 + [vm] * 5,
+        out_specs=(vm,) * 4,
+        name="signals",
         compiler_params=pltpu.CompilerParams(vmem_limit_bytes=8 << 20),
-    )(h, v)
+    )(core, cluster, noise, penalty.reshape(1, points), power.reshape(1, points), h, v)
 
 
 def gain_kernel(block, core_ref, ht_ref, ha_ref, vt_ref, vb_ref, keep_ref, send_ref):
     _, _, users = ht_ref.shape
-    half = users // 2
     chips = keep_ref.shape[0]
     piece = users // chips
+    vt, vb = vt_ref[block], vb_ref[block]
     first = core_ref[0] == 0
-    vt, vb = vt_ref[block], vb_ref[block]
-    ht, ha = jnp.transpose(ht_ref[block]), jnp.transpose(ha_ref[block])
-    for out_ref, low in ((keep_ref, first), (send_ref, jnp.logical_not(first))):
-        own = jnp.where(low, vt[:, :half], vt[:, half:])
-        far = jnp.where(low, vb[:, :half], vb[:, half:])
-        both = jnp.concatenate([own, far], axis=1)
-        g = dot(ht, jnp.concatenate([far, turned(far)], axis=1), ((1,), (0,)))
-        for part in range(2):
-            out_ref[:, part, :, :half] = g[:, part * half : (part + 1) * half].reshape(chips, piece, half).astype(BF16)
-        for part, w in enumerate((both, turned(both))):
-            out_ref[:, part, :, half:] = dot(ha, w, ((1,), (0,))).reshape(chips, piece, users).astype(BF16)
+    on_diag = iota((users, users), 0) == iota((users, users), 1)
+    hs = [jnp.transpose(h_ref[block]) for h_ref in (ht_ref, ha_ref)]
+    for out_ref, own in ((keep_ref, first), (send_ref, jnp.logical_not(first))):
+        v = jnp.where(own, vt, vb)
+        for part, w in enumerate((v, turned(v))):
+            for tile, h in enumerate(hs):
+                g = dot(h, w, ((1,), (0,)))
+                if tile == 0:
+                    g = jnp.where(jnp.logical_and(on_diag, own), 0.0, g)
+                out_ref[:, part, tile] = g.reshape(chips, piece, users).astype(BF16)
 
 
 def partial_gains(block, core, ht, ha, vt, vb, chips):
     _, rows, users = ht.shape
-    shape = (chips, 2, users // chips, users + users // 2)
+    shape = (chips, 2, 2, users // chips, users)
     vm = pl.BlockSpec(memory_space=pltpu.VMEM)
     return pl.pallas_call(
         functools.partial(gain_kernel, block),
@@ -100,24 +115,24 @@
         out_specs=(vm, vm),
         name="gains",
         compiler_params=pltpu.CompilerParams(vmem_limit_bytes=8 << 20),
-        cost_estimate=pl.CostEstimate(flops=12 * users * users * rows, bytes_accessed=4 << 20, transcendentals=0),
+        cost_estimate=pl.CostEstimate(flops=16 * users * users * rows, bytes_accessed=4 << 20, transcendentals=0),
     )(core, ht, ha, vt, vb)
 
 
 def combine_kernel(keep0_ref, keep1_ref, came0_ref, came1_ref, out_ref):
-    chips, _, piece, width = keep0_ref.shape
-    rows = 2 * piece
+    chips, _, _, piece, users = keep0_ref.shape
+    rows = 4 * piece
     for block, (keep_ref, came_ref) in enumerate(((keep0_ref, came0_ref), (keep1_ref, came1_ref))):
         g = keep_ref[...] + came_ref[...]
-        out_ref[:, block * rows : (block + 1) * rows] = g.reshape(chips, rows, width)
+        out_ref[:, block * rows : (block + 1) * rows] = g.reshape(chips, rows, users)
 
 
 def combined(keeps, cames):
-    chips, _, piece, width = keeps[0].shape
+    chips, _, _, piece, users = keeps[0].shape
     vm = pl.BlockSpec(memory_space=pltpu.VMEM)
     return pl.pallas_call(
         combine_kernel,
-        out_shape=jax.ShapeDtypeStruct((chips, 4 * piece, width), BF16),
+        out_shape=jax.ShapeDtypeStruct((chips, 8 * piece, users), BF16),
         in_specs=[vm] * 4,
         out_specs=vm,
         name="combine",
@@ -125,89 +140,42 @@
     )(*keeps, *cames)
 
 
-def own_sum_kernel(where_ref, g_ref, noise_ref, sum_ref, line_ref):
-    chip, core = where_ref[0], where_ref[1]
+def total_kernel(chip_ref, g_ref, signal_ref, noise_ref, out_ref):
+    chip = chip_ref[0]
     chips, rows, users = g_ref.shape
-    piece = (rows - 8) // 4
-    lanes = line_ref.shape[1]
-
-    def summed(at):
-        total = g_ref[0, at].astype(F32)
-        for source in range(1, chips):
-            total = total + g_ref[source, at].astype(F32)
-        return total
-
-    sum_ref[...] = summed(slice(0, 4 * piece))
-    extra = summed(slice(4 * piece, 4 * piece + 8))
-    signal = extra + pltpu.roll(extra, 4, 0)
-    noise = jnp.where(core == 0, noise_ref[...], 0.0)
-    signal = jnp.concatenate([signal[:4], noise, noise], axis=0)
+    piece = rows // 8
+    lanes = out_ref.shape[1]
+    lane = iota((2 * piece, lanes), 1)
+    row = iota((2 * piece, lanes), 0)
+    line = jnp.sum(signal_ref[...], axis=0)
+    noise = noise_ref[...]
     pick = iota((users, lanes), 0) == chip * piece + iota((users, lanes), 1) % piece
-    mine = dot(signal, pick.astype(F32), ((1,), (0,)), HIGHEST)
+    noise = dot(jnp.concatenate([noise] * 4, axis=0), pick.astype(F32), ((1,), (0,)), HIGHEST)
     group = iota((1, lanes), 1) // piece
-    line = jnp.zeros((1, lanes), F32)
     for block in range(2):
+        line = line + jnp.where(group == block * 4, noise[block : block + 1], 0.0)
+        total = None
         for part in range(2):
-            at = block * 2 + part
-            line = line + jnp.where(group == block * 4 + 2 + part, mine[at : at + 1], 0.0)
-        line = line + jnp.where(group == block * 4, mine[4 + block : 5 + block], 0.0)
-    line_ref[...] = line
-
-
-def own_sum(where, g, noise):
-    chips, rows, users = g.shape
-    vm = pl.BlockSpec(memory_space=pltpu.VMEM)
-    return pl.pallas_call(
-        own_sum_kernel,
-        out_shape=(jax.ShapeDtypeStruct((rows - 8, users), F32), jax.ShapeDtypeStruct((1, 128), F32)),
-        in_specs=[pl.BlockSpec(memory_space=pltpu.SMEM), vm, vm],
-        out_specs=(vm, vm),
-        name="own_sum",
-        compiler_params=pltpu.CompilerParams(vmem_limit_bytes=8 << 20),
-    )(where, g, noise)
-
-
-def total_kernel(where_ref, g_ref, mine_ref, came_ref, line_ref, out_ref):
-    core = where_ref[1]
-    chips, rows, width = g_ref.shape
-    piece = rows // 4
-    users = mine_ref.shape[1]
-    half = width - users
-    lanes = out_ref.shape[1]
-    lane = iota((piece, lanes), 1)
-    row = iota((piece, lanes), 0)
-    line = line_ref[...]
-    for block in range(2):
-        own, near = None, None
-        for part in range(2):
-            at = slice((block * 2 + part) * piece, (block * 2 + part + 1) * piece)
+            at = slice((block * 2 + part) * 2 * piece, (block * 2 + part + 1) * 2 * piece)
             g = g_ref[0, at].astype(F32)
             for source in range(1, chips):
                 g = g + g_ref[source, at].astype(F32)
-            square = g * g
-            g = mine_ref[at] + came_ref[at]
-            g = jnp.where(core == 0, g, 0.0)
-            here = square[:, :half] + g[:, :half] * g[:, :half] + g[:, half:] * g[:, half:]
-            there = square[:, half : 2 * half] + square[:, 2 * half :]
-            own = here if own is None else own + here
-            near = there if near is None else near + there
-        for quantity, total in enumerate((own, near)):
-            total = jnp.sum(total, axis=1, keepdims=True)
-            at = (block * 4 + quantity) * piece
-            line = line + jnp.sum(jnp.where(lane == row + at, total, 0.0), axis=0, keepdims=True)
+            total = g * g if total is None else total + g * g
+        total = jnp.sum(total, axis=1, keepdims=True)
+        line = line + jnp.sum(jnp.where(lane == row + block * 4 * piece, total, 0.0), axis=0, keepdims=True)
     out_ref[...] = jnp.broadcast_to(line, out_ref.shape)
 
 
-def totals(where, g, mine, came, line, devices):
+def totals(chip, g, signal, noise, devices):
     vm = pl.BlockSpec(memory_space=pltpu.VMEM)
     return pl.pallas_call(
         total_kernel,
         out_shape=jax.ShapeDtypeStruct((devices, 128), F32),
-        in_specs=[pl.BlockSpec(memory_space=pltpu.SMEM)] + [vm] * 4,
+        in_specs=[pl.BlockSpec(memory_space=pltpu.SMEM)] + [vm] * 3,
         out_specs=vm,
         name="totals",
         compiler_params=pltpu.CompilerParams(vmem_limit_bytes=8 << 20),
-    )(where, g, mine, came, line)
+    )(chip, g, signal, noise)
 
 
 def user_lines(r_ref, line_ref, weight_ref, tile):
@@ -366,7 +334,7 @@
             acc = dot(jnp.concatenate(xs, axis=1), parts, ((1,), (1,)))
             p = acc[:, :size] + acc[:, size:]
             a = jnp.where(column(n) < antennas, p[:antennas], -p[:antennas]) + pltpu.roll(p[antennas:], antennas, 1)
-            a = a + jnp.where(column(n) == row, penalty_ref[point], 0.0)
+            a = a + jnp.where(column(n) == row, penalty_ref[0, point], 0.0)
             sys_ref[n] = a
 
     eliminate(work_ref, sys_ref, scale_ref)
@@ -392,7 +360,7 @@
                 if slot == 0:
                     y_ref[block] = y
         mean = jnp.sum(total, axis=1, keepdims=True) / (2.0 * blocks * antennas * 4 * users)
-        gain = jnp.sqrt(power_ref[point] / (mean + 1e-06))
+        gain = jnp.sqrt(power_ref[0, point] / (mean + 1e-06))
         for block in range(blocks):
             y_re, y_im = y_ref[block, :antennas], y_ref[block, antennas:]
             w_re = line(block, 1, 0) * gain
@@ -442,7 +410,6 @@
     blocks, parts, points, antennas, users = channel.shape
     chips = lax.axis_size(CHIPS)
     devices = lax.axis_size(EVERY)
-    piece = users // chips
     rows = parts * points * antennas
     core = lax.axis_index("core")
     tile = lax.axis_index("ut")
@@ -459,20 +426,18 @@
     far = across(own, "ut", 3)
     far_near = across(near, "ut", 3)
 
-    where = jnp.stack([chip, core])
+    core, chip = core.reshape(1), chip.reshape(1)
+    signal, noise, penalty, power = signals(core, cluster, noise, penalty, power, channel, start_precoder, chips)
+    signal = lax.all_to_all(signal.reshape(chips, 1, 128), CHIPS, 0, 0, tiled=True)
+
     flat = [x.reshape(blocks, rows, users) for x in (own, near, start_precoder, v_far)]
-    early = lax.all_to_all(own_gains(flat[0], flat[2], chips), CHIPS, 0, 0, tiled=True)
-
     keeps, cames = [], []
     for b in range(blocks):
-        keep, send = partial_gains(b, core.reshape(1), *flat, chips)
+        keep, send = partial_gains(b, core, *flat, chips)
         keeps.append(keep)
         cames.append(across(send, "core", 1))
     late = lax.all_to_all(combined(keeps, cames), CHIPS, 0, 0, tiled=True)
-
-    mine, line = own_sum(where, early, noise)
-    came = across(mine, "core", 1)
-    line = totals(where, late, mine, came, line, devices)
+    line = totals(chip, late, signal, noise, devices)
     r = lax.all_to_all(line, EVERY, 0, 0, tiled=True).reshape(chips, devices // chips, 128)
 
     precoder, weight = solve(tile.reshape(1), penalty, power, r, (own, near, far, far_near), channel.shape)
@@ -489,6 +454,7 @@
         P(AP),
         P(AP),
     )
+
     return jax.shard_map(
         local,
         mesh=split,

time: 75.7 us -> 89.8 us (1.19)
  waiting for transfers between devices: 20.2 us -> 35.2 us
  starting transfers between devices: 32.6 us -> 29.2 us
  Pallas kernels: 18.5 us -> 20.8 us
    all_to_all x1, waiting for transfers between devices: 3.59 us -> 12.3 us  [local(): late = lax.all_to_all(combined(keeps, cames), CHIPS, 0, 0, tiled=True)]
    all_to_all x1, waiting for transfers between devices: 6.22 us -> 9.57 us  [local(): lax.all_to_all(line, EVERY, 0, 0, tiled=True)]
    ppermute x8 -> x7, starting transfers between devices: 13.2 us -> 9.86 us  [across(): return lax.ppermute(value, axis, [(i, i ^ mask) for i in range(size)])]
    ppermute x8 -> x7, waiting for transfers between devices: 6.2 us -> 9.24 us  [across(): return lax.ppermute(value, axis, [(i, i ^ mask) for i in range(size)])]
    pallas_call x2, Pallas kernels: 1.27 us -> 3.09 us  [partial_gains(): pl.pallas_call(functools.partial(gain_kernel, block), out_shape=(jax.Shap...]
    pallas_call x3 -> x2, Pallas kernels: 3.12 us -> 4.02 us  [the longest x1 2.3 us: combined(): pl.pallas_call(combine_kernel, out_shape=jax.ShapeDtypeStruct((chips, 8 *...]
  transfers between devices with their start and end apart: 11 -> 10, of which waited for: 8 -> 5; matrix products, arithmetic and copies ran while one was open for 3% -> 2% of each run, Pallas kernels for 8% -> 6%
where the time goes in v6:
time: 89.8 us; the launch traced here: 89.4 us
  waiting for transfers between devices  35.2 us (39%)
  starting transfers between devices  29.2 us (33%)
  Pallas kernels  20.8 us (23%)
  other arithmetic  1.92 us (2%)
  local copies, waits for them, and re-layouts  1.58 us (2%)
    pallas_call x1, Pallas kernels, solve(): pl.pallas_call(solve_kernel, out_shape=(jax.ShapeDtypeStruct(out_shape, B...  12.7 us
    all_to_all x1, waiting for transfers between devices, local(): late = lax.all_to_all(combined(keeps, cames), CHIPS, 0, 0, tiled=True)  12.3 us
    ppermute x7, starting transfers between devices, across(): return lax.ppermute(value, axis, [(i, i ^ mask) for i in range(size)])  9.86 us
    all_to_all x1, waiting for transfers between devices, local(): lax.all_to_all(line, EVERY, 0, 0, tiled=True)  9.57 us
    ppermute x7, waiting for transfers between devices, across(): return lax.ppermute(value, axis, [(i, i ^ mask) for i in range(size)])  9.24 us
    all_to_all x1, starting transfers between devices, local(): lax.all_to_all(line, EVERY, 0, 0, tiled=True)  8.1 us
    all_to_all x1, starting transfers between devices, local(): lax.all_to_all(signal.reshape(chips, 1, 128), CHIPS, 0, 0, tiled=True)  7.6 us
    all_to_all x1, waiting for transfers between devices, local(): lax.all_to_all(signal.reshape(chips, 1, 128), CHIPS, 0, 0, tiled=True)  4.1 us
  transfers between devices with their start and end apart: 10, of which 5 were waited for; matrix products, arithmetic and copies ran while one was open for 2% of the time, Pallas kernels for 6%

profile of v6, /device:TPU:1, one launch (start us, length us, event | category | flops | bytes accessed | tf_op | source)
XLA Modules:
  0.0 89.4 jit_solution(10380715605655787987)
XLA Ops:
  0.6 2.2 %collective-permute-start = (bf16[2,2,4,64,256]{4,3,2,1,0:T(8,128)(2,1)}, bf16[2,2,4,64,256]{4,3,2,1,0:T(8,128)(2,1)S(1)}, u32[]{:S(2)}, u32[]{:S(2)}) collective-permute-start(bf16[2,2,4,64,256]{4,3,2,1,0:T(8,128)(2,1)} %h_ref.1), channel_id=1, source_target_pairs={{0,1},{1,0},{2,3},{3,2},{4,5},{5,4},{6,7},{7,6},{8,9},{9,8},{10,11... | collective-permute-start | bytes 1572872 | tf_op jit(solution)/shard_map/ppermute | solution.py:406
  2.8 0.1 collective-permute-start.1
  2.9 2.8 %collective-permute-start.2 = (bf16[2,2,4,64,256]{4,3,2,1,0:T(8,128)(2,1)}, bf16[2,2,4,64,256]{4,3,2,1,0:T(8,128)(2,1)S(1)}, u32[]{:S(2)}, u32[]{:S(2)}) collective-permute-start(bf16[2,2,4,64,256]{4,3,2,1,0:T(8,128)(2,1)} %v_ref.1), channel_id=1, source_target_pairs={{0,3},{1,2},{2,1},{3,0},{4,7},{5,6},{6,5},{7,4},{8,11},{9,10},{10,... | collective-permute-start | bytes 1572872 | tf_op jit(solution)/shard_map/ppermute | solution.py:406
  5.7 0.7 convert_bitcast_fusion.1
  6.4 1.1 %broadcast_multiply_fusion.1.refs_0_ = bf16[2,2,4,64,256]{4,3,2,1,0:T(8,128)(2,1)S(1)} fusion(bf16[2,2,4,64,256]{4,3,2,1,0:T(8,128)(2,1)} %h_ref.1, bf16[4]{0:T(256)(128)(2,1)S(1)} %convert_bitcast_fusion.1), kind=kLoop, calls=%fused_computation.1 | loop fusion | flops 262144 | bytes 1048584 | tf_op jit(solution)/shard_map/mul | solution.py:419
  7.5 6.8 %collective-permute-done.1 = s32[4,1]{0,1:T(1,128)S(1)} collective-permute-done((s32[4,1]{0,1:T(1,128)}, s32[4,1]{0,1:T(1,128)S(1)}, u32[]{:S(2)}, u32[]{:S(2)}) %collective-permute-start.1) | collective-permute-done | bytes 48 | tf_op jit(solution)/shard_map/ppermute | solution.py:406
  14.3 0.0 copy-start
  14.3 0.0 collective-permute-done
  14.4 0.1 broadcast_multiply_fusion.refs_1_
  14.5 2.4 %collective-permute-done.2 = bf16[2,2,4,64,256]{4,3,2,1,0:T(8,128)(2,1)S(1)} collective-permute-done((bf16[2,2,4,64,256]{4,3,2,1,0:T(8,128)(2,1)}, bf16[2,2,4,64,256]{4,3,2,1,0:T(8,128)(2,1)S(1)}, u32[]{:S(2)}, u32[]{:S(2)}) %collective-permute-start.2) | collective-permute-done | bytes 524320 | tf_op jit(solution)/shard_map/ppermute | solution.py:406
  16.9 0.0 copy-done
  16.9 1.5 %gains.2 = (bf16[16,2,2,16,256]{4,3,2,1,0:T(8,128)(2,1)S(1)}, bf16[16,2,2,16,256]{4,3,2,1,0:T(8,128)(2,1)}) custom-call(s32[1]{0:T(128)} %bitcast.1.core_ref, bf16[2,512,256]{2,1,0:T(8,128)(2,1)S(1)} %bitcast.18, bf16[2,512,256]{2,1,0:T(8,128)(2,1)S(1)} %bitcast.20, bf16[2,512,256]{2,1,0:T(8,128)(2,1)S(1)} %bitcast.22, bf16[2,512,256]{2,1,0:T(8,128)(2,1)S(1)} %bitcast.24), custom_call_target="tpu_custom_call" | custom-call | flops 536870912 | bytes 4194304 | tf_op jit(solution)/shard_map/gains/pallas_call | solution.py:111
  18.4 0.0 copy-start.1
  18.4 1.5 %gains.3 = (bf16[16,2,2,16,256]{4,3,2,1,0:T(8,128)(2,1)S(1)}, bf16[16,2,2,16,256]{4,3,2,1,0:T(8,128)(2,1)}) custom-call(s32[1]{0:T(128)} %bitcast.1.core_ref, bf16[2,512,256]{2,1,0:T(8,128)(2,1)S(1)} %bitcast.19, bf16[2,512,256]{2,1,0:T(8,128)(2,1)S(1)} %bitcast.21, bf16[2,512,256]{2,1,0:T(8,128)(2,1)S(1)} %bitcast.23, bf16[2,512,256]{2,1,0:T(8,128)(2,1)S(1)} %bitcast.25), custom_call_target="tpu_custom_call" | custom-call | flops 536870912 | bytes 4194304 | tf_op jit(solution)/shard_map/gains/pallas_call | solution.py:111
  20.0 0.0 copy-start.2
  20.0 0.8 copy-done.2
  20.8 0.0 copy-start.7
  20.8 1.9 %collective-permute-start.3 = (bf16[16,2,2,16,256]{4,3,2,1,0:T(8,128)(2,1)}, bf16[16,2,2,16,256]{4,3,2,1,0:T(8,128)(2,1)}, u32[]{:S(2)}, u32[]{:S(2)}) collective-permute-start(bf16[16,2,2,16,256]{4,3,2,1,0:T(8,128)(2,1)} %get-tuple-element.14), channel_id=1, source_target_pairs={{0,4},{4,0},{1,5},{5,1},{2,6},{6,2},{3,7},{7,3},{8,12},{12,8},{9,1... | collective-permute-start | bytes 1572872 | tf_op jit(solution)/shard_map/ppermute | solution.py:406
  22.7 0.0 collective-permute-start.4
  22.7 0.0 copy-done.7
  22.7 0.1 copy.9.cluster_ref
  22.8 0.0 copy-start.4
  22.8 0.0 copy-start.5
  22.8 0.0 copy-start.6
  22.8 0.0 copy-done.1
  22.8 0.7 copy-done.4
  23.5 0.0 copy-done.5
  23.5 0.0 copy-done.6
  23.5 0.0 copy-start.3
  23.5 1.7 %signals.1 = (f32[16,128]{1,0:T(8,128)}, f32[2,256]{1,0:T(2,128)S(1)}, f32[1,4]{1,0:T(1,128)S(1)}, f32[1,4]{1,0:T(1,128)S(1)}) custom-call(s32[1]{0:T(128)} %bitcast.1.core_ref, s32[4,1]{1,0:T(4,128)S(1)} %copy.9.cluster_ref, f32[2,256]{1,0:T(2,128)S(1)} %copy-done.4, f32[1,4]{1,0:T(1,128)S(1)} %bitcast.27, f32[1,4]{1,0:T(1,128)S(1)} %bitcast.28, ...), custom_call_target="tpu_custom_call" | custom-call | tf_op jit(solution)/shard_map/signals/pallas_call | solution.py:74
  25.2 7.6 %all-to-all-start.1 = ((f32[16,1,128]{2,1,0:T(1,128)}), f32[16,1,128]{2,1,0:T(1,128)S(1)}, u32[]{:S(2)}, u32[]{:S(2)}) async-start(f32[16,1,128]{2,1,0:T(1,128)} %bitcast.11), calls=%async_computation.1 | async-start | bytes 16384 | tf_op jit(solution)/shard_map/all_to_all | solution.py:431
  32.8 0.0 collective-permute-done.3.came0_ref
  32.8 0.0 collective-permute-done.4.came1_ref
  32.8 0.0 copy-done.3
  32.9 2.3 %combine.1 = bf16[16,128,256]{2,1,0:T(8,128)(2,1)} custom-call(bf16[16,2,2,16,256]{4,3,2,1,0:T(8,128)(2,1)S(1)} %get-tuple-element.12.keep0_ref, bf16[16,2,2,16,256]{4,3,2,1,0:T(8,128)(2,1)S(1)} %copy-done.3, bf16[16,2,2,16,256]{4,3,2,1,0:T(8,128)(2,1)} %collective-permute-done.3.came0_ref, bf16[16,2,2,16,256]{4,3,2,1,0:T(8,128)(2,1)} %collective-permute-done.4.came1_ref), custom_call_target="tpu_custom_call" | custom-call | tf_op jit(solution)/shard_map/combine/pallas_call | solution.py:133
  35.2 4.1 %all-to-all-done.1.signal_ref = f32[16,1,128]{2,1,0:T(1,128)S(1)} async-done(((f32[16,1,128]{2,1,0:T(1,128)}), f32[16,1,128]{2,1,0:T(1,128)S(1)}, u32[]{:S(2)}, u32[]{:S(2)}) %all-to-all-start.1) | async-done | bytes 8224 | tf_op jit(solution)/shard_map/all_to_all | solution.py:431
  39.3 3.7 %all-to-all-start = ((bf16[16,128,256]{2,1,0:T(8,128)(2,1)}), bf16[16,128,256]{2,1,0:T(8,128)(2,1)S(1)}, u32[]{:S(2)}, u32[]{:S(2)}) async-start(bf16[16,128,256]{2,1,0:T(8,128)(2,1)} %combine.1), calls=%async_computation | async-start | bytes 2097152 | tf_op jit(solution)/shard_map/all_to_all | solution.py:439
  42.9 2.7 %collective-permute-start.5 = (bf16[2,2,4,64,256]{4,3,2,1,0:T(8,128)(2,1)S(1)}, bf16[2,2,4,64,256]{4,3,2,1,0:T(8,128)(2,1)S(1)}, u32[]{:S(2)}, u32[]{:S(2)}) collective-permute-start(bf16[2,2,4,64,256]{4,3,2,1,0:T(8,128)(2,1)S(1)} %broadcast_multiply_fusion.1.refs_0_), channel_id=1, source_target_pairs={{0,3},{1,2},{2,1},{3,0},{4,7},{5,6},{6,5},{7,4},{8,11},{9,10},{10,... | collective-permute-start | bytes 1572872 | tf_op jit(solution)/shard_map/ppermute | solution.py:406
  45.7 0.1 collective-permute-start.6
  45.8 12.3 %all-to-all-done.g_ref = bf16[16,128,256]{2,1,0:T(8,128)(2,1)S(1)} async-done(((bf16[16,128,256]{2,1,0:T(8,128)(2,1)}), bf16[16,128,256]{2,1,0:T(8,128)(2,1)S(1)}, u32[]{:S(2)}, u32[]{:S(2)}) %all-to-all-start) | async-done | bytes 1048608 | tf_op jit(solution)/shard_map/all_to_all | solution.py:439
  58.1 0.9 %totals.1 = f32[128,128]{1,0:T(8,128)} custom-call(s32[1]{0:T(128)} %bitcast.4.chip_ref, bf16[16,128,256]{2,1,0:T(8,128)(2,1)S(1)} %all-to-all-done.g_ref, f32[16,1,128]{2,1,0:T(1,128)S(1)} %all-to-all-done.1.signal_ref, f32[2,256]{1,0:T(2,128)S(1)} %get-tuple-element.17.noise_ref), custom_call_target="tpu_custom_call" | custom-call | tf_op jit(solution)/shard_map/totals/pallas_call | solution.py:171
  59.0 8.1 %all-to-all-start.2 = ((f32[128,1,128]{2,1,0:T(1,128)}), f32[128,1,128]{2,1,0:T(1,128)S(1)}, u32[]{:S(2)}, u32[]{:S(2)}) async-start(f32[128,1,128]{2,1,0:T(1,128)} %bitcast.13), calls=%async_computation.2 | async-start | bytes 131072 | tf_op jit(solution)/shard_map/all_to_all | solution.py:441
  67.1 0.0 collective-permute-done.5.refs_2_
  67.1 0.0 collective-permute-done.6.refs_3_
  67.1 9.6 %all-to-all-done.2 = f32[128,1,128]{2,1,0:T(1,128)S(1)} async-done(((f32[128,1,128]{2,1,0:T(1,128)}), f32[128,1,128]{2,1,0:T(1,128)S(1)}, u32[]{:S(2)}, u32[]{:S(2)}) %all-to-all-start.2) | async-done | bytes 65568 | tf_op jit(solution)/shard_map/all_to_all | solution.py:441
  76.7 12.7 %solve.1 = (bf16[2,2,4,64,256]{4,3,2,1,0:T(8,128)(2,1)}, f32[2,256]{1,0:T(2,128)}) custom-call(s32[1]{0:T(128)} %bitcast.tile_ref, f32[1,4]{1,0:T(1,128)S(1)} %get-tuple-element.10.penalty_ref, f32[1,4]{1,0:T(1,128)S(1)} %get-tuple-element.11.power_ref, f32[16,8,128]{2,1,0:T(8,128)S(1)} %bitcast.26, ...), custom_call_target="tpu_custom_call" | custom-call | tf_op jit(solution)/shard_map/solve/pallas_call | solution.py:382
  (1 shorter events, 0.0 us)
Async XLA Ops:
  0.6 13.7 %collective-permute-start = (bf16[2,2,4,64,256]{4,3,2,1,0:T(8,128)(2,1)}, bf16[2,2,4,64,256]{4,3,2,1,0:T(8,128)(2,1)S(1)}, u32[]{:S(2)}, u32[]{:S(2)}) collective-permute-start(bf16[2,2,4,64,256]{4,3,2,1,0:T(8,128)(2,1)} %h_ref.1), channel_id=1, source_target_pairs={{0,1},{1,0},{2,3},{3,2},{4,5},{5,4},{6,7},{7,6},{8,9},{9,8},{10,11... | collective-permute-start | bytes 1572872 | tf_op jit(solution)/shard_map/ppermute | solution.py:406
  2.8 11.5 %collective-permute-start.1 = (s32[4,1]{0,1:T(1,128)}, s32[4,1]{0,1:T(1,128)S(1)}, u32[]{:S(2)}, u32[]{:S(2)}) collective-permute-start(s32[4,1]{0,1:T(1,128)} %param.8), channel_id=1, source_target_pairs={{0,1},{1,0},{2,3},{3,2},{4,5},{5,4},{6,7},{7,6},{8,9},{9,8},{10,11... | collective-permute-start | bytes 56 | tf_op jit(solution)/shard_map/ppermute | solution.py:406
  2.9 14.0 %collective-permute-start.2 = (bf16[2,2,4,64,256]{4,3,2,1,0:T(8,128)(2,1)}, bf16[2,2,4,64,256]{4,3,2,1,0:T(8,128)(2,1)S(1)}, u32[]{:S(2)}, u32[]{:S(2)}) collective-permute-start(bf16[2,2,4,64,256]{4,3,2,1,0:T(8,128)(2,1)} %v_ref.1), channel_id=1, source_target_pairs={{0,3},{1,2},{2,1},{3,0},{4,7},{5,6},{6,5},{7,4},{8,11},{9,10},{10,... | collective-permute-start | bytes 1572872 | tf_op jit(solution)/shard_map/ppermute | solution.py:406
  14.3 2.6 %copy-start = (bf16[2,2,4,64,256]{4,3,2,1,0:T(8,128)(2,1)S(1)}, bf16[2,2,4,64,256]{4,3,2,1,0:T(8,128)(2,1)}, u32[]{:S(2)}) copy-start(bf16[2,2,4,64,256]{4,3,2,1,0:T(8,128)(2,1)} %v_ref.1) | copy-start | bytes 1572868
  18.4 4.4 %copy-start.1 = (bf16[2,2,4,64,256]{4,3,2,1,0:T(8,128)(2,1)S(1)}, bf16[2,2,4,64,256]{4,3,2,1,0:T(8,128)(2,1)}, u32[]{:S(2)}) copy-start(bf16[2,2,4,64,256]{4,3,2,1,0:T(8,128)(2,1)} %h_ref.1) | copy-start | bytes 1572868
  20.0 0.8 copy-start.2
  20.8 1.9 %copy-start.7 = (s32[4,1]{0,1:T(1,128)S(1)}, s32[4,1]{0,1:T(1,128)}, u32[]{:S(2)}) copy-start(s32[4,1]{0,1:T(1,128)} %param.8) | copy-start | bytes 52
  20.8 12.0 %collective-permute-start.3 = (bf16[16,2,2,16,256]{4,3,2,1,0:T(8,128)(2,1)}, bf16[16,2,2,16,256]{4,3,2,1,0:T(8,128)(2,1)}, u32[]{:S(2)}, u32[]{:S(2)}) collective-permute-start(bf16[16,2,2,16,256]{4,3,2,1,0:T(8,128)(2,1)} %get-tuple-element.14), channel_id=1, source_target_pairs={{0,4},{4,0},{1,5},{5,1},{2,6},{6,2},{3,7},{7,3},{8,12},{12,8},{9,1... | collective-permute-start | bytes 1572872 | tf_op jit(solution)/shard_map/ppermute | solution.py:406
  22.7 10.1 %collective-permute-start.4 = (bf16[16,2,2,16,256]{4,3,2,1,0:T(8,128)(2,1)}, bf16[16,2,2,16,256]{4,3,2,1,0:T(8,128)(2,1)}, u32[]{:S(2)}, u32[]{:S(2)}) collective-permute-start(bf16[16,2,2,16,256]{4,3,2,1,0:T(8,128)(2,1)} %get-tuple-element.15), channel_id=1, source_target_pairs={{0,4},{4,0},{1,5},{5,1},{2,6},{6,2},{3,7},{7,3},{8,12},{12,8},{9,1... | collective-permute-start | bytes 1572872 | tf_op jit(solution)/shard_map/ppermute | solution.py:406
  22.8 0.7 copy-start.4
  22.8 0.7 copy-start.5
  22.8 0.7 copy-start.6
  23.5 9.4 %copy-start.3 = (bf16[16,2,2,16,256]{4,3,2,1,0:T(8,128)(2,1)S(1)}, bf16[16,2,2,16,256]{4,3,2,1,0:T(8,128)(2,1)}, u32[]{:S(2)}) copy-start(bf16[16,2,2,16,256]{4,3,2,1,0:T(8,128)(2,1)} %copy-done.2) | copy-start | bytes 1572868
  25.2 14.0 %all-to-all-start.1 = ((f32[16,1,128]{2,1,0:T(1,128)}), f32[16,1,128]{2,1,0:T(1,128)S(1)}, u32[]{:S(2)}, u32[]{:S(2)}) async-start(f32[16,1,128]{2,1,0:T(1,128)} %bitcast.11), calls=%async_computation.1 | async-start | bytes 16384 | tf_op jit(solution)/shard_map/all_to_all | solution.py:431
  39.3 18.8 %all-to-all-start = ((bf16[16,128,256]{2,1,0:T(8,128)(2,1)}), bf16[16,128,256]{2,1,0:T(8,128)(2,1)S(1)}, u32[]{:S(2)}, u32[]{:S(2)}) async-start(bf16[16,128,256]{2,1,0:T(8,128)(2,1)} %combine.1), calls=%async_computation | async-start | bytes 2097152 | tf_op jit(solution)/shard_map/all_to_all | solution.py:439
  42.9 24.2 %collective-permute-start.5 = (bf16[2,2,4,64,256]{4,3,2,1,0:T(8,128)(2,1)S(1)}, bf16[2,2,4,64,256]{4,3,2,1,0:T(8,128)(2,1)S(1)}, u32[]{:S(2)}, u32[]{:S(2)}) collective-permute-start(bf16[2,2,4,64,256]{4,3,2,1,0:T(8,128)(2,1)S(1)} %broadcast_multiply_fusion.1.refs_0_), channel_id=1, source_target_pairs={{0,3},{1,2},{2,1},{3,0},{4,7},{5,6},{6,5},{7,4},{8,11},{9,10},{10,... | collective-permute-start | bytes 1572872 | tf_op jit(solution)/shard_map/ppermute | solution.py:406
  45.7 21.5 %collective-permute-start.6 = (bf16[2,2,4,64,256]{4,3,2,1,0:T(8,128)(2,1)S(1)}, bf16[2,2,4,64,256]{4,3,2,1,0:T(8,128)(2,1)S(1)}, u32[]{:S(2)}, u32[]{:S(2)}) collective-permute-start(bf16[2,2,4,64,256]{4,3,2,1,0:T(8,128)(2,1)S(1)} %broadcast_multiply_fusion.refs_1_), channel_id=1, source_target_pairs={{0,3},{1,2},{2,1},{3,0},{4,7},{5,6},{6,5},{7,4},{8,11},{9,10},{10,... | collective-permute-start | bytes 1572872 | tf_op jit(solution)/shard_map/ppermute | solution.py:406
  59.0 17.7 %all-to-all-start.2 = ((f32[128,1,128]{2,1,0:T(1,128)}), f32[128,1,128]{2,1,0:T(1,128)S(1)}, u32[]{:S(2)}, u32[]{:S(2)}) async-start(f32[128,1,128]{2,1,0:T(1,128)} %bitcast.13), calls=%async_computation.2 | async-start | bytes 131072 | tf_op jit(solution)/shard_map/all_to_all | solution.py:441

commit v7 on v5

--- a/solution.py
+++ b/solution.py
@@ -8,6 +8,7 @@
 from jax.sharding import Mesh
 from jax.sharding import PartitionSpec as P
 
+
 AP = ("z", "x", "core")
 CHIPS = ("z", "x")
 EVERY = ("z", "x", "core", "ut")
@@ -35,15 +36,27 @@
     return jnp.concatenate([v[half:], -v[:half]], axis=0)
 
 
-def own_kernel(h_ref, v_ref, out_ref):
-    blocks, _, users = h_ref.shape
+def own_kernel(cluster_ref, h_any, v_any, out_ref, own_ref, v_ref, h_ref, sems):
+    blocks, parts, points, antennas, users = h_ref.shape
     chips = out_ref.shape[0]
     piece = users // chips
+    copies = []
+    for block in range(blocks):
+        for source, target in ((h_any, h_ref), (v_any, v_ref)):
+            copy = pltpu.make_async_copy(source.at[block], target.at[block], sems.at[len(copies)])
+            copy.start()
+            copies.append(copy)
     on_diag = iota((users, users), 0) == iota((users, users), 1)
     high, low = [], []
     for block in range(blocks):
-        h = jnp.transpose(h_ref[block])
-        v = v_ref[block]
+        copies[2 * block].wait()
+        for point in range(points):
+            served = cluster_ref[point, 0].astype(F32)
+            for part in range(parts):
+                own_ref[block, part, point] = (h_ref[block, part, point].astype(F32) * served).astype(BF16)
+        copies[2 * block + 1].wait()
+        h = jnp.transpose(own_ref[block].reshape(parts * points * antennas, users))
+        v = v_ref[block].reshape(parts * points * antennas, users)
         for part, w in enumerate((v, turned(v))):
             g = dot(h, w, ((1,), (0,)))
             own = jnp.sum(jnp.where(on_diag, g, 0.0), axis=0, keepdims=True)
@@ -57,17 +70,23 @@
     out_ref[:, 4 * piece :] = jnp.broadcast_to(extra[None], (chips,) + extra.shape)
 
 
-def own_gains(h, v, chips):
-    blocks, _, users = h.shape
-    vm = pl.BlockSpec(memory_space=pltpu.VMEM)
+def own_gains(cluster, h, v, chips):
+    users = h.shape[-1]
+    vm = pl.BlockSpec(memory_space=pltpu.VMEM)
+    raw = pl.BlockSpec(memory_space=pltpu.HBM)
     return pl.pallas_call(
         own_kernel,
-        out_shape=jax.ShapeDtypeStruct((chips, 4 * (users // chips) + 8, users), BF16),
-        in_specs=[vm] * 2,
-        out_specs=vm,
+        out_shape=(
+            jax.ShapeDtypeStruct((chips, 4 * (users // chips) + 8, users), BF16),
+            jax.ShapeDtypeStruct(h.shape, BF16),
+            jax.ShapeDtypeStruct(v.shape, BF16),
+        ),
+        in_specs=[pl.BlockSpec(memory_space=pltpu.SMEM), raw, raw],
+        out_specs=(vm,) * 3,
+        scratch_shapes=[pltpu.VMEM(h.shape, BF16), pltpu.SemaphoreType.DMA((2 * h.shape[0],))],
         name="own_gains",
         compiler_params=pltpu.CompilerParams(vmem_limit_bytes=8 << 20),
-    )(h, v)
+    )(cluster, h, v)
 
 
 def gain_kernel(block, core_ref, ht_ref, ha_ref, vt_ref, vb_ref, keep_ref, send_ref):
@@ -125,7 +144,7 @@
     )(*keeps, *cames)
 
 
-def own_sum_kernel(where_ref, g_ref, noise_ref, sum_ref, line_ref):
+def own_sum_kernel(where_ref, g_ref, noise_ref, penalty_ref, power_ref, sum_ref, line_ref, penalty_out, power_out):
     chip, core = where_ref[0], where_ref[1]
     chips, rows, users = g_ref.shape
     piece = (rows - 8) // 4
@@ -152,62 +171,87 @@
             line = line + jnp.where(group == block * 4 + 2 + part, mine[at : at + 1], 0.0)
         line = line + jnp.where(group == block * 4, mine[4 + block : 5 + block], 0.0)
     line_ref[...] = line
-
-
-def own_sum(where, g, noise):
-    chips, rows, users = g.shape
+    penalty_out[...] = penalty_ref[...]
+    power_out[...] = power_ref[...]
+
+
+def own_sum(where, g, noise, penalty, power):
+    _, rows, users = g.shape
+    points = penalty.shape[0]
     vm = pl.BlockSpec(memory_space=pltpu.VMEM)
     return pl.pallas_call(
         own_sum_kernel,
-        out_shape=(jax.ShapeDtypeStruct((rows - 8, users), F32), jax.ShapeDtypeStruct((1, 128), F32)),
-        in_specs=[pl.BlockSpec(memory_space=pltpu.SMEM), vm, vm],
-        out_specs=(vm, vm),
+        out_shape=(
+            jax.ShapeDtypeStruct((rows - 8, users), F32),
+            jax.ShapeDtypeStruct((1, 128), F32),
+            jax.ShapeDtypeStruct((1, points), F32),
+            jax.ShapeDtypeStruct((1, points), F32),
+        ),
+        in_specs=[pl.BlockSpec(memory_space=pltpu.SMEM)] + [vm] * 4,
+        out_specs=(vm,) * 4,
         name="own_sum",
         compiler_params=pltpu.CompilerParams(vmem_limit_bytes=8 << 20),
-    )(where, g, noise)
-
-
-def total_kernel(where_ref, g_ref, mine_ref, came_ref, line_ref, out_ref):
-    core = where_ref[1]
+    )(where, g, noise, penalty.reshape(1, points), power.reshape(1, points))
+
+
+def placed(line, total, start):
+    lane = iota((total.shape[0], line.shape[1]), 1)
+    row = iota((total.shape[0], line.shape[1]), 0)
+    return line + jnp.sum(jnp.where(lane == row + start, total, 0.0), axis=0, keepdims=True)
+
+
+def own_total_kernel(where_ref, mine_ref, came_ref, line_ref, out_ref):
+    piece = mine_ref.shape[0] // 4
+    line = line_ref[...]
+    g = jnp.where(where_ref[1] == 0, mine_ref[...] + came_ref[...], 0.0)
+    square = jnp.sum(g * g, axis=1, keepdims=True)
+    for block in range(2):
+        at = 2 * block * piece
+        line = placed(line, square[at : at + piece] + square[at + piece : at + 2 * piece], 4 * block * piece)
+    out_ref[...] = line
+
+
+def own_total(where, mine, came, line):
+    vm = pl.BlockSpec(memory_space=pltpu.VMEM)
+    return pl.pallas_call(
+        own_total_kernel,
+        out_shape=jax.ShapeDtypeStruct(line.shape, F32),
+        in_specs=[pl.BlockSpec(memory_space=pltpu.SMEM)] + [vm] * 3,
+        out_specs=vm,
+        name="own_total",
+        compiler_params=pltpu.CompilerParams(vmem_limit_bytes=4 << 20),
+    )(where, mine, came, line)
+
+
+def total_kernel(g_ref, line_ref, out_ref):
     chips, rows, width = g_ref.shape
     piece = rows // 4
-    users = mine_ref.shape[1]
-    half = width - users
-    lanes = out_ref.shape[1]
-    lane = iota((piece, lanes), 1)
-    row = iota((piece, lanes), 0)
+    half = width // 3
     line = line_ref[...]
     for block in range(2):
-        own, near = None, None
+        square = None
         for part in range(2):
             at = slice((block * 2 + part) * piece, (block * 2 + part + 1) * piece)
             g = g_ref[0, at].astype(F32)
             for source in range(1, chips):
                 g = g + g_ref[source, at].astype(F32)
-            square = g * g
-            g = mine_ref[at] + came_ref[at]
-            g = jnp.where(core == 0, g, 0.0)
-            here = square[:, :half] + g[:, :half] * g[:, :half] + g[:, half:] * g[:, half:]
-            there = square[:, half : 2 * half] + square[:, 2 * half :]
-            own = here if own is None else own + here
-            near = there if near is None else near + there
-        for quantity, total in enumerate((own, near)):
-            total = jnp.sum(total, axis=1, keepdims=True)
-            at = (block * 4 + quantity) * piece
-            line = line + jnp.sum(jnp.where(lane == row + at, total, 0.0), axis=0, keepdims=True)
+            square = g * g if square is None else square + g * g
+        own = jnp.sum(square[:, :half], axis=1, keepdims=True)
+        near = jnp.sum(square[:, half : 2 * half] + square[:, 2 * half :], axis=1, keepdims=True)
+        line = placed(placed(line, own, block * 4 * piece), near, (block * 4 + 1) * piece)
     out_ref[...] = jnp.broadcast_to(line, out_ref.shape)
 
 
-def totals(where, g, mine, came, line, devices):
+def totals(g, line, devices):
     vm = pl.BlockSpec(memory_space=pltpu.VMEM)
     return pl.pallas_call(
         total_kernel,
         out_shape=jax.ShapeDtypeStruct((devices, 128), F32),
-        in_specs=[pl.BlockSpec(memory_space=pltpu.SMEM)] + [vm] * 4,
+        in_specs=[vm] * 2,
         out_specs=vm,
         name="totals",
         compiler_params=pltpu.CompilerParams(vmem_limit_bytes=8 << 20),
-    )(where, g, mine, came, line)
+    )(g, line)
 
 
 def user_lines(r_ref, line_ref, weight_ref, tile):
@@ -366,7 +410,7 @@
             acc = dot(jnp.concatenate(xs, axis=1), parts, ((1,), (1,)))
             p = acc[:, :size] + acc[:, size:]
             a = jnp.where(column(n) < antennas, p[:antennas], -p[:antennas]) + pltpu.roll(p[antennas:], antennas, 1)
-            a = a + jnp.where(column(n) == row, penalty_ref[point], 0.0)
+            a = a + jnp.where(column(n) == row, penalty_ref[0, point], 0.0)
             sys_ref[n] = a
 
     eliminate(work_ref, sys_ref, scale_ref)
@@ -392,7 +436,7 @@
                 if slot == 0:
                     y_ref[block] = y
         mean = jnp.sum(total, axis=1, keepdims=True) / (2.0 * blocks * antennas * 4 * users)
-        gain = jnp.sqrt(power_ref[point] / (mean + 1e-06))
+        gain = jnp.sqrt(power_ref[0, point] / (mean + 1e-06))
         for block in range(blocks):
             y_re, y_im = y_ref[block, :antennas], y_ref[block, antennas:]
             w_re = line(block, 1, 0) * gain
@@ -442,37 +486,35 @@
     blocks, parts, points, antennas, users = channel.shape
     chips = lax.axis_size(CHIPS)
     devices = lax.axis_size(EVERY)
-    piece = users // chips
     rows = parts * points * antennas
     core = lax.axis_index("core")
     tile = lax.axis_index("ut")
     chip = lax.axis_index(CHIPS)
 
-    def masked(field, served):
-        return field * served[:, 0].astype(BF16)[None, None, :, None, None]
-
     near_cluster = across(cluster, "ut", 1)
     near = across(channel, "ut", 1)
     v_far = across(start_precoder, "ut", 3)
-    own = masked(channel, cluster)
-    near = masked(near, near_cluster)
+
+    early, own, v_own = own_gains(cluster, channel, start_precoder, chips)
+    early = lax.all_to_all(early, CHIPS, 0, 0, tiled=True)
+    near = near * near_cluster[:, 0].astype(BF16)[None, None, :, None, None]
+
     far = across(own, "ut", 3)
     far_near = across(near, "ut", 3)
 
     where = jnp.stack([chip, core])
-    flat = [x.reshape(blocks, rows, users) for x in (own, near, start_precoder, v_far)]
-    early = lax.all_to_all(own_gains(flat[0], flat[2], chips), CHIPS, 0, 0, tiled=True)
-
+    flat = [x.reshape(blocks, rows, users) for x in (own, near, v_own, v_far)]
     keeps, cames = [], []
     for b in range(blocks):
         keep, send = partial_gains(b, core.reshape(1), *flat, chips)
         keeps.append(keep)
         cames.append(across(send, "core", 1))
-    late = lax.all_to_all(combined(keeps, cames), CHIPS, 0, 0, tiled=True)
-
-    mine, line = own_sum(where, early, noise)
-    came = across(mine, "core", 1)
-    line = totals(where, late, mine, came, line, devices)
+    late = combined(keeps, cames)
+    late = lax.all_to_all(late, CHIPS, 0, 0, tiled=True)
+
+    mine, line, penalty, power = own_sum(where, early, noise, penalty, power)
+    line = own_total(where, mine, across(mine, "core", 1), line)
+    line = totals(late, line, devices)
     r = lax.all_to_all(line, EVERY, 0, 0, tiled=True).reshape(chips, devices // chips, 128)
 
     precoder, weight = solve(tile.reshape(1), penalty, power, r, (own, near, far, far_near), channel.shape)
@@ -489,6 +531,7 @@
         P(AP),
         P(AP),
     )
+
     return jax.shard_map(
         local,
         mesh=split,

time: 75.7 us -> 75.2 us (level)
  local copies, waits for them, and re-layouts: 1.28 us -> 3.54 us
  other arithmetic: 2.05 us -> 0.19 us
  starting transfers between devices: 32.6 us -> 31.1 us
  Pallas kernels: 18.5 us -> 19.6 us
    unnamed x8 -> x11, local copies, waits for them, and re-layouts: 1.28 us -> 3.54 us
    pallas_call x1 -> x2, Pallas kernels: 1.32 us -> 2.96 us  [the longest x1 2.32 us: own_gains(): pl.pallas_call(own_kernel, out_shape=(jax.ShapeDtypeStruct((chips, 4 * (u...]
    mul x2 -> x1, other arithmetic: 1.31 us -> 0.11 us  [local(): near = near * near_cluster[:, 0].astype(BF16)[None, None, :, None, None]]
    all_to_all x1, starting transfers between devices: 8.23 us -> 7.44 us  [local(): lax.all_to_all(line, EVERY, 0, 0, tiled=True)]
  transfers between devices with their start and end apart: 11 -> 11, of which waited for: 8 -> 7; matrix products, arithmetic and copies ran while one was open for 3% -> 1% of each run, Pallas kernels for 8% -> 9%
where the time goes in v7:
time: 75.2 us; the launch traced here: 74.8 us
  starting transfers between devices  31.1 us (41%)
  Pallas kernels  19.6 us (26%)
  waiting for transfers between devices  19.5 us (26%)
  local copies, waits for them, and re-layouts  3.54 us (5%)
    pallas_call x1, Pallas kernels, solve(): pl.pallas_call(solve_kernel, out_shape=(jax.ShapeDtypeStruct(out_shape, B...  12.7 us
    ppermute x8, starting transfers between devices, across(): return lax.ppermute(value, axis, [(i, i ^ mask) for i in range(size)])  12.4 us
    all_to_all x1, starting transfers between devices, local(): early = lax.all_to_all(early, CHIPS, 0, 0, tiled=True)  7.62 us
    all_to_all x1, starting transfers between devices, local(): lax.all_to_all(line, EVERY, 0, 0, tiled=True)  7.44 us
    all_to_all x1, waiting for transfers between devices, local(): lax.all_to_all(line, EVERY, 0, 0, tiled=True)  6.39 us
    ppermute x8, waiting for transfers between devices, across(): return lax.ppermute(value, axis, [(i, i ^ mask) for i in range(size)])  5.8 us
    all_to_all x1, waiting for transfers between devices, local(): early = lax.all_to_all(early, CHIPS, 0, 0, tiled=True)  4.47 us
    all_to_all x1, starting transfers between devices, local(): late = lax.all_to_all(late, CHIPS, 0, 0, tiled=True)  3.61 us
  transfers between devices with their start and end apart: 11, of which 7 were waited for; matrix products, arithmetic and copies ran while one was open for 1% of the time, Pallas kernels for 9%

profile of v7, /device:TPU:1, one launch (start us, length us, event | category | flops | bytes accessed | tf_op | source)
XLA Modules:
  0.0 74.8 jit_solution(11653352246831657159)
XLA Ops:
  0.6 2.2 %collective-permute-start = (bf16[2,2,4,64,256]{4,3,2,1,0:T(8,128)(2,1)}, bf16[2,2,4,64,256]{4,3,2,1,0:T(8,128)(2,1)S(1)}, u32[]{:S(2)}, u32[]{:S(2)}) collective-permute-start(bf16[2,2,4,64,256]{4,3,2,1,0:T(8,128)(2,1)} %h_any.1), channel_id=1, source_target_pairs={{0,1},{1,0},{2,3},{3,2},{4,5},{5,4},{6,7},{7,6},{8,9},{9,8},{10,11... | collective-permute-start | bytes 1572872 | tf_op jit(solution)/shard_map/ppermute | solution.py:482
  2.8 1.9 %collective-permute-start.2 = (bf16[2,2,4,64,256]{4,3,2,1,0:T(8,128)(2,1)}, bf16[2,2,4,64,256]{4,3,2,1,0:T(8,128)(2,1)S(1)}, u32[]{:S(2)}, u32[]{:S(2)}) collective-permute-start(bf16[2,2,4,64,256]{4,3,2,1,0:T(8,128)(2,1)} %v_any.1), channel_id=1, source_target_pairs={{0,3},{1,2},{2,1},{3,0},{4,7},{5,6},{6,5},{7,4},{8,11},{9,10},{10,... | collective-permute-start | bytes 1572872 | tf_op jit(solution)/shard_map/ppermute | solution.py:482
  4.7 0.4 collective-permute-start.1
  5.1 0.8 %copy.9.cluster_ref = s32[4,1]{1,0:T(4,128)S(1)} copy(s32[4,1]{0,1:T(1,128)} %param.8) | data formatting | bytes 32 | tf_op args[2]
  5.9 0.0 copy-start
  5.9 1.0 %copy-done = bf16[2,2,4,64,256]{4,3,2,1,0:T(8,128)(2,1)S(1)} copy-done((bf16[2,2,4,64,256]{4,3,2,1,0:T(8,128)(2,1)S(1)}, bf16[2,2,4,64,256]{4,3,2,1,0:T(8,128)(2,1)}, u32[]{:S(2)}) %copy-start) | copy-done | bytes 524312
  6.9 0.0 copy-start.1
  6.9 1.0 %copy-done.1 = bf16[2,2,4,64,256]{4,3,2,1,0:T(8,128)(2,1)S(1)} copy-done((bf16[2,2,4,64,256]{4,3,2,1,0:T(8,128)(2,1)S(1)}, bf16[2,2,4,64,256]{4,3,2,1,0:T(8,128)(2,1)}, u32[]{:S(2)}) %copy-start.1) | copy-done | bytes 524312
  8.0 2.3 %own_gains.1 = (bf16[16,72,256]{2,1,0:T(8,128)(2,1)}, bf16[2,2,4,64,256]{4,3,2,1,0:T(8,128)(2,1)S(1)}, bf16[2,2,4,64,256]{4,3,2,1,0:T(8,128)(2,1)S(1)}) custom-call(s32[4,1]{1,0:T(4,128)S(1)} %copy.9.cluster_ref, bf16[2,2,4,64,256]{4,3,2,1,0:T(8,128)(2,1)S(1)} %copy-done, bf16[2,2,4,64,256]{4,3,2,1,0:T(8,128)(2,1)S(1)} %copy-done.1), custom_call_target="tpu_custom_call" | custom-call | tf_op jit(solution)/shard_map/own_gains/pallas_call | solution.py:77
  10.3 7.6 %all-to-all-start = ((bf16[16,72,256]{2,1,0:T(8,128)(2,1)}), bf16[16,72,256]{2,1,0:T(8,128)(2,1)S(1)}, u32[]{:S(2)}, u32[]{:S(2)}) async-start(bf16[16,72,256]{2,1,0:T(8,128)(2,1)} %get-tuple-element.13), calls=%async_computation | async-start | bytes 1179648 | tf_op jit(solution)/shard_map/all_to_all | solution.py:499
  17.9 0.0 collective-permute-done.1
  18.0 0.0 collective-permute-done
  18.0 0.1 broadcast_multiply_fusion.refs_1_
  18.1 0.0 collective-permute-done.2
  18.1 0.6 gains.2
  18.7 1.9 %collective-permute-start.3 = (bf16[16,2,16,384]{3,2,1,0:T(8,128)(2,1)S(1)}, bf16[16,2,16,384]{3,2,1,0:T(8,128)(2,1)S(1)}, u32[]{:S(2)}, u32[]{:S(2)}) collective-permute-start(bf16[16,2,16,384]{3,2,1,0:T(8,128)(2,1)S(1)} %get-tuple-element.20), channel_id=1, source_target_pairs={{0,4},{4,0},{1,5},{5,1},{2,6},{6,2},{3,7},{7,3},{8,12},{12,8},{9,1... | collective-permute-start | bytes 1179656 | tf_op jit(solution)/shard_map/ppermute | solution.py:482
  20.6 0.6 gains.3
  21.3 0.1 collective-permute-start.4
  21.4 0.6 collective-permute-done.3.came0_ref
  22.0 1.1 %collective-permute-done.4.came1_ref = bf16[16,2,16,384]{3,2,1,0:T(8,128)(2,1)S(1)} collective-permute-done((bf16[16,2,16,384]{3,2,1,0:T(8,128)(2,1)S(1)}, bf16[16,2,16,384]{3,2,1,0:T(8,128)(2,1)S(1)}, u32[]{:S(2)}, u32[]{:S(2)}) %collective-permute-start.4) | collective-permute-done | bytes 393248 | tf_op jit(solution)/shard_map/ppermute | solution.py:482
  23.1 1.0 %combine.1 = bf16[16,64,384]{2,1,0:T(8,128)(2,1)} custom-call(bf16[16,2,16,384]{3,2,1,0:T(8,128)(2,1)S(1)} %get-tuple-element.18.keep0_ref, bf16[16,2,16,384]{3,2,1,0:T(8,128)(2,1)S(1)} %get-tuple-element.19.keep1_ref, bf16[16,2,16,384]{3,2,1,0:T(8,128)(2,1)S(1)} %collective-permute-done.3.came0_ref, ...), custom_call_target="tpu_custom_call" | custom-call | tf_op jit(solution)/shard_map/combine/pallas_call | solution.py:137
  24.1 4.5 %all-to-all-done.g_ref = bf16[16,72,256]{2,1,0:T(8,128)(2,1)S(1)} async-done(((bf16[16,72,256]{2,1,0:T(8,128)(2,1)}), bf16[16,72,256]{2,1,0:T(8,128)(2,1)S(1)}, u32[]{:S(2)}, u32[]{:S(2)}) %all-to-all-start) | async-done | bytes 589856 | tf_op jit(solution)/shard_map/all_to_all | solution.py:499
  28.6 3.6 %all-to-all-start.1 = ((bf16[16,64,384]{2,1,0:T(8,128)(2,1)}), bf16[16,64,384]{2,1,0:T(8,128)(2,1)S(1)}, u32[]{:S(2)}, u32[]{:S(2)}) async-start(bf16[16,64,384]{2,1,0:T(8,128)(2,1)} %combine.1), calls=%async_computation.1 | async-start | bytes 1572864 | tf_op jit(solution)/shard_map/all_to_all | solution.py:513
  32.2 0.9 %collective-permute-start.6 = (bf16[2,2,4,64,256]{4,3,2,1,0:T(8,128)(2,1)S(1)}, bf16[2,2,4,64,256]{4,3,2,1,0:T(8,128)(2,1)S(1)}, u32[]{:S(2)}, u32[]{:S(2)}) collective-permute-start(bf16[2,2,4,64,256]{4,3,2,1,0:T(8,128)(2,1)S(1)} %get-tuple-element.16.refs_0_), channel_id=1, source_target_pairs={{0,3},{1,2},{2,1},{3,0},{4,7},{5,6},{6,5},{7,4},{8,11},{9,10},{10,... | collective-permute-start | bytes 1572872 | tf_op jit(solution)/shard_map/ppermute | solution.py:482
  33.1 1.8 %collective-permute-start.7 = (bf16[2,2,4,64,256]{4,3,2,1,0:T(8,128)(2,1)S(1)}, bf16[2,2,4,64,256]{4,3,2,1,0:T(8,128)(2,1)S(1)}, u32[]{:S(2)}, u32[]{:S(2)}) collective-permute-start(bf16[2,2,4,64,256]{4,3,2,1,0:T(8,128)(2,1)S(1)} %broadcast_multiply_fusion.refs_1_), channel_id=1, source_target_pairs={{0,3},{1,2},{2,1},{3,0},{4,7},{5,6},{6,5},{7,4},{8,11},{9,10},{10,... | collective-permute-start | bytes 1572872 | tf_op jit(solution)/shard_map/ppermute | solution.py:482
  34.9 0.1 pad_add_fusion.where_ref
  35.0 0.0 copy-start.2
  35.0 0.0 copy-start.3
  35.0 0.0 copy-start.4
  35.0 0.7 copy-done.2
  35.7 0.0 copy-done.3
  35.7 0.0 copy-done.4
  35.7 0.8 %own_sum.1 = (f32[64,256]{1,0:T(8,128)S(1)}, f32[1,128]{1,0:T(1,128)S(1)}, f32[1,4]{1,0:T(1,128)S(1)}, f32[1,4]{1,0:T(1,128)S(1)}) custom-call(s32[2]{0:T(128)S(1)} %pad_add_fusion.where_ref, bf16[16,72,256]{2,1,0:T(8,128)(2,1)S(1)} %all-to-all-done.g_ref, f32[2,256]{1,0:T(2,128)S(1)} %copy-done.2, f32[1,4]{1,0:T(1,128)S(1)} %bitcast.24, f32[1,4]{1,0:T(1,128)S(1)} %bitcast.25), custom_call_target="tpu_custom_call" | custom-call | tf_op jit(solution)/shard_map/own_sum/pallas_call | solution.py:182
  36.5 3.2 %collective-permute-start.5 = (f32[64,256]{1,0:T(8,128)S(1)}, f32[64,256]{1,0:T(8,128)S(1)}, u32[]{:S(2)}, u32[]{:S(2)}) collective-permute-start(f32[64,256]{1,0:T(8,128)S(1)} %get-tuple-element.22.mine_ref), channel_id=1, source_target_pairs={{0,4},{4,0},{1,5},{5,1},{2,6},{6,2},{3,7},{7,3},{8,12},{12,8},{9,1... | collective-permute-start | bytes 196616 | tf_op jit(solution)/shard_map/ppermute | solution.py:482
  39.7 0.9 %collective-permute-done.5.came_ref = f32[64,256]{1,0:T(8,128)S(1)} collective-permute-done((f32[64,256]{1,0:T(8,128)S(1)}, f32[64,256]{1,0:T(8,128)S(1)}, u32[]{:S(2)}, u32[]{:S(2)}) %collective-permute-start.5) | collective-permute-done | bytes 65568 | tf_op jit(solution)/shard_map/ppermute | solution.py:482
  40.6 0.6 own_total.1.line_ref
  41.3 2.9 %all-to-all-done.1.g_ref = bf16[16,64,384]{2,1,0:T(8,128)(2,1)S(1)} async-done(((bf16[16,64,384]{2,1,0:T(8,128)(2,1)}), bf16[16,64,384]{2,1,0:T(8,128)(2,1)S(1)}, u32[]{:S(2)}, u32[]{:S(2)}) %all-to-all-start.1) | async-done | bytes 786464 | tf_op jit(solution)/shard_map/all_to_all | solution.py:513
  44.1 0.8 %totals.1 = f32[128,128]{1,0:T(8,128)} custom-call(bf16[16,64,384]{2,1,0:T(8,128)(2,1)S(1)} %all-to-all-done.1.g_ref, f32[1,128]{1,0:T(1,128)S(1)} %own_total.1.line_ref), custom_call_target="tpu_custom_call" | custom-call | tf_op jit(solution)/shard_map/totals/pallas_call | solution.py:247
  45.0 7.4 %all-to-all-start.2 = ((f32[128,1,128]{2,1,0:T(1,128)}), f32[128,1,128]{2,1,0:T(1,128)S(1)}, u32[]{:S(2)}, u32[]{:S(2)}) async-start(f32[128,1,128]{2,1,0:T(1,128)} %bitcast.11), calls=%async_computation.2 | async-start | bytes 131072 | tf_op jit(solution)/shard_map/all_to_all | solution.py:518
  52.4 0.0 collective-permute-done.6.refs_2_
  52.4 3.2 %collective-permute-done.7.refs_3_ = bf16[2,2,4,64,256]{4,3,2,1,0:T(8,128)(2,1)S(1)} collective-permute-done((bf16[2,2,4,64,256]{4,3,2,1,0:T(8,128)(2,1)S(1)}, bf16[2,2,4,64,256]{4,3,2,1,0:T(8,128)(2,1)S(1)}, u32[]{:S(2)}, u32[]{:S(2)}) %collective-permute-start.7) | collective-permute-done | bytes 524320 | tf_op jit(solution)/shard_map/ppermute | solution.py:482
  55.6 6.4 %all-to-all-done.2 = f32[128,1,128]{2,1,0:T(1,128)S(1)} async-done(((f32[128,1,128]{2,1,0:T(1,128)}), f32[128,1,128]{2,1,0:T(1,128)S(1)}, u32[]{:S(2)}, u32[]{:S(2)}) %all-to-all-start.2) | async-done | bytes 65568 | tf_op jit(solution)/shard_map/all_to_all | solution.py:518
  62.0 12.7 %solve.1 = (bf16[2,2,4,64,256]{4,3,2,1,0:T(8,128)(2,1)}, f32[2,256]{1,0:T(2,128)}) custom-call(s32[1]{0:T(128)} %bitcast.tile_ref, f32[1,4]{1,0:T(1,128)S(1)} %get-tuple-element.14.penalty_ref, f32[1,4]{1,0:T(1,128)S(1)} %get-tuple-element.15.power_ref, f32[16,8,128]{2,1,0:T(8,128)S(1)} %bitcast.23, ...), custom_call_target="tpu_custom_call" | custom-call | tf_op jit(solution)/shard_map/solve/pallas_call | solution.py:458
  (1 shorter events, 0.0 us)
Async XLA Ops:
  0.6 17.3 %collective-permute-start = (bf16[2,2,4,64,256]{4,3,2,1,0:T(8,128)(2,1)}, bf16[2,2,4,64,256]{4,3,2,1,0:T(8,128)(2,1)S(1)}, u32[]{:S(2)}, u32[]{:S(2)}) collective-permute-start(bf16[2,2,4,64,256]{4,3,2,1,0:T(8,128)(2,1)} %h_any.1), channel_id=1, source_target_pairs={{0,1},{1,0},{2,3},{3,2},{4,5},{5,4},{6,7},{7,6},{8,9},{9,8},{10,11... | collective-permute-start | bytes 1572872 | tf_op jit(solution)/shard_map/ppermute | solution.py:482
  2.8 15.3 %collective-permute-start.2 = (bf16[2,2,4,64,256]{4,3,2,1,0:T(8,128)(2,1)}, bf16[2,2,4,64,256]{4,3,2,1,0:T(8,128)(2,1)S(1)}, u32[]{:S(2)}, u32[]{:S(2)}) collective-permute-start(bf16[2,2,4,64,256]{4,3,2,1,0:T(8,128)(2,1)} %v_any.1), channel_id=1, source_target_pairs={{0,3},{1,2},{2,1},{3,0},{4,7},{5,6},{6,5},{7,4},{8,11},{9,10},{10,... | collective-permute-start | bytes 1572872 | tf_op jit(solution)/shard_map/ppermute | solution.py:482
  4.7 13.2 %collective-permute-start.1 = (s32[4,1]{0,1:T(1,128)}, s32[4,1]{0,1:T(1,128)S(1)}, u32[]{:S(2)}, u32[]{:S(2)}) collective-permute-start(s32[4,1]{0,1:T(1,128)} %param.8), channel_id=1, source_target_pairs={{0,1},{1,0},{2,3},{3,2},{4,5},{5,4},{6,7},{7,6},{8,9},{9,8},{10,11... | collective-permute-start | bytes 56 | tf_op jit(solution)/shard_map/ppermute | solution.py:482
  5.9 1.0 %copy-start = (bf16[2,2,4,64,256]{4,3,2,1,0:T(8,128)(2,1)S(1)}, bf16[2,2,4,64,256]{4,3,2,1,0:T(8,128)(2,1)}, u32[]{:S(2)}) copy-start(bf16[2,2,4,64,256]{4,3,2,1,0:T(8,128)(2,1)} %h_any.1) | copy-start | bytes 1572868
  6.9 1.0 %copy-start.1 = (bf16[2,2,4,64,256]{4,3,2,1,0:T(8,128)(2,1)S(1)}, bf16[2,2,4,64,256]{4,3,2,1,0:T(8,128)(2,1)}, u32[]{:S(2)}) copy-start(bf16[2,2,4,64,256]{4,3,2,1,0:T(8,128)(2,1)} %v_any.1) | copy-start | bytes 1572868
  10.3 18.2 %all-to-all-start = ((bf16[16,72,256]{2,1,0:T(8,128)(2,1)}), bf16[16,72,256]{2,1,0:T(8,128)(2,1)S(1)}, u32[]{:S(2)}, u32[]{:S(2)}) async-start(bf16[16,72,256]{2,1,0:T(8,128)(2,1)} %get-tuple-element.13), calls=%async_computation | async-start | bytes 1179648 | tf_op jit(solution)/shard_map/all_to_all | solution.py:499
  18.7 3.2 %collective-permute-start.3 = (bf16[16,2,16,384]{3,2,1,0:T(8,128)(2,1)S(1)}, bf16[16,2,16,384]{3,2,1,0:T(8,128)(2,1)S(1)}, u32[]{:S(2)}, u32[]{:S(2)}) collective-permute-start(bf16[16,2,16,384]{3,2,1,0:T(8,128)(2,1)S(1)} %get-tuple-element.20), channel_id=1, source_target_pairs={{0,4},{4,0},{1,5},{5,1},{2,6},{6,2},{3,7},{7,3},{8,12},{12,8},{9,1... | collective-permute-start | bytes 1179656 | tf_op jit(solution)/shard_map/ppermute | solution.py:482
  21.3 1.8 %collective-permute-start.4 = (bf16[16,2,16,384]{3,2,1,0:T(8,128)(2,1)S(1)}, bf16[16,2,16,384]{3,2,1,0:T(8,128)(2,1)S(1)}, u32[]{:S(2)}, u32[]{:S(2)}) collective-permute-start(bf16[16,2,16,384]{3,2,1,0:T(8,128)(2,1)S(1)} %get-tuple-element.21), channel_id=1, source_target_pairs={{0,4},{4,0},{1,5},{5,1},{2,6},{6,2},{3,7},{7,3},{8,12},{12,8},{9,1... | collective-permute-start | bytes 1179656 | tf_op jit(solution)/shard_map/ppermute | solution.py:482
  28.6 15.6 %all-to-all-start.1 = ((bf16[16,64,384]{2,1,0:T(8,128)(2,1)}), bf16[16,64,384]{2,1,0:T(8,128)(2,1)S(1)}, u32[]{:S(2)}, u32[]{:S(2)}) async-start(bf16[16,64,384]{2,1,0:T(8,128)(2,1)} %combine.1), calls=%async_computation.1 | async-start | bytes 1572864 | tf_op jit(solution)/shard_map/all_to_all | solution.py:513
  32.2 20.2 %collective-permute-start.6 = (bf16[2,2,4,64,256]{4,3,2,1,0:T(8,128)(2,1)S(1)}, bf16[2,2,4,64,256]{4,3,2,1,0:T(8,128)(2,1)S(1)}, u32[]{:S(2)}, u32[]{:S(2)}) collective-permute-start(bf16[2,2,4,64,256]{4,3,2,1,0:T(8,128)(2,1)S(1)} %get-tuple-element.16.refs_0_), channel_id=1, source_target_pairs={{0,3},{1,2},{2,1},{3,0},{4,7},{5,6},{6,5},{7,4},{8,11},{9,10},{10,... | collective-permute-start | bytes 1572872 | tf_op jit(solution)/shard_map/ppermute | solution.py:482
  33.1 22.5 %collective-permute-start.7 = (bf16[2,2,4,64,256]{4,3,2,1,0:T(8,128)(2,1)S(1)}, bf16[2,2,4,64,256]{4,3,2,1,0:T(8,128)(2,1)S(1)}, u32[]{:S(2)}, u32[]{:S(2)}) collective-permute-start(bf16[2,2,4,64,256]{4,3,2,1,0:T(8,128)(2,1)S(1)} %broadcast_multiply_fusion.refs_1_), channel_id=1, source_target_pairs={{0,3},{1,2},{2,1},{3,0},{4,7},{5,6},{6,5},{7,4},{8,11},{9,10},{10,... | collective-permute-start | bytes 1572872 | tf_op jit(solution)/shard_map/ppermute | solution.py:482
  35.0 0.7 copy-start.2
  35.0 0.7 copy-start.3
  35.0 0.7 copy-start.4
  36.5 4.1 %collective-permute-start.5 = (f32[64,256]{1,0:T(8,128)S(1)}, f32[64,256]{1,0:T(8,128)S(1)}, u32[]{:S(2)}, u32[]{:S(2)}) collective-permute-start(f32[64,256]{1,0:T(8,128)S(1)} %get-tuple-element.22.mine_ref), channel_id=1, source_target_pairs={{0,4},{4,0},{1,5},{5,1},{2,6},{6,2},{3,7},{7,3},{8,12},{12,8},{9,1... | collective-permute-start | bytes 196616 | tf_op jit(solution)/shard_map/ppermute | solution.py:482
  45.0 17.0 %all-to-all-start.2 = ((f32[128,1,128]{2,1,0:T(1,128)}), f32[128,1,128]{2,1,0:T(1,128)S(1)}, u32[]{:S(2)}, u32[]{:S(2)}) async-start(f32[128,1,128]{2,1,0:T(1,128)} %bitcast.11), calls=%async_computation.2 | async-start | bytes 131072 | tf_op jit(solution)/shard_map/all_to_all | solution.py:518

commit v8 on v7

--- a/solution.py
+++ b/solution.py
@@ -36,27 +36,15 @@
     return jnp.concatenate([v[half:], -v[:half]], axis=0)
 
 
-def own_kernel(cluster_ref, h_any, v_any, out_ref, own_ref, v_ref, h_ref, sems):
-    blocks, parts, points, antennas, users = h_ref.shape
+def own_kernel(h_ref, v_ref, out_ref):
+    blocks, _, users = h_ref.shape
     chips = out_ref.shape[0]
     piece = users // chips
-    copies = []
-    for block in range(blocks):
-        for source, target in ((h_any, h_ref), (v_any, v_ref)):
-            copy = pltpu.make_async_copy(source.at[block], target.at[block], sems.at[len(copies)])
-            copy.start()
-            copies.append(copy)
     on_diag = iota((users, users), 0) == iota((users, users), 1)
     high, low = [], []
     for block in range(blocks):
-        copies[2 * block].wait()
-        for point in range(points):
-            served = cluster_ref[point, 0].astype(F32)
-            for part in range(parts):
-                own_ref[block, part, point] = (h_ref[block, part, point].astype(F32) * served).astype(BF16)
-        copies[2 * block + 1].wait()
-        h = jnp.transpose(own_ref[block].reshape(parts * points * antennas, users))
-        v = v_ref[block].reshape(parts * points * antennas, users)
+        h = jnp.transpose(h_ref[block])
+        v = v_ref[block]
         for part, w in enumerate((v, turned(v))):
             g = dot(h, w, ((1,), (0,)))
             own = jnp.sum(jnp.where(on_diag, g, 0.0), axis=0, keepdims=True)
@@ -70,23 +58,17 @@
     out_ref[:, 4 * piece :] = jnp.broadcast_to(extra[None], (chips,) + extra.shape)
 
 
-def own_gains(cluster, h, v, chips):
-    users = h.shape[-1]
-    vm = pl.BlockSpec(memory_space=pltpu.VMEM)
-    raw = pl.BlockSpec(memory_space=pltpu.HBM)
+def own_gains(h, v, chips):
+    _, _, users = h.shape
+    vm = pl.BlockSpec(memory_space=pltpu.VMEM)
     return pl.pallas_call(
         own_kernel,
-        out_shape=(
-            jax.ShapeDtypeStruct((chips, 4 * (users // chips) + 8, users), BF16),
-            jax.ShapeDtypeStruct(h.shape, BF16),
-            jax.ShapeDtypeStruct(v.shape, BF16),
-        ),
-        in_specs=[pl.BlockSpec(memory_space=pltpu.SMEM), raw, raw],
-        out_specs=(vm,) * 3,
-        scratch_shapes=[pltpu.VMEM(h.shape, BF16), pltpu.SemaphoreType.DMA((2 * h.shape[0],))],
+        out_shape=jax.ShapeDtypeStruct((chips, 4 * (users // chips) + 8, users), BF16),
+        in_specs=[vm] * 2,
+        out_specs=vm,
         name="own_gains",
         compiler_params=pltpu.CompilerParams(vmem_limit_bytes=8 << 20),
-    )(cluster, h, v)
+    )(h, v)
 
 
 def gain_kernel(block, core_ref, ht_ref, ha_ref, vt_ref, vb_ref, keep_ref, send_ref):
@@ -370,7 +352,7 @@
 
 def solve_kernel(tile_ref, penalty_ref, power_ref, r_ref, *refs):
     h_refs = refs[:4]
-    out_ref, weight_ref, line_ref, sys_ref, work_ref, scale_ref, y_ref, made_ref, sems = refs[4:]
+    out_ref, weight_ref, line_ref, sys_ref, work_ref, scale_ref, y_ref, made_ref, inverse_ref, sems = refs[4:]
     blocks, _, points, antennas, users = h_refs[0].shape
     size = 2 * antennas
     systems = blocks * points
@@ -415,19 +397,25 @@
 
     eliminate(work_ref, sys_ref, scale_ref)
 
+    for n in range(systems):
+        high, low = two_parts(sys_ref[n])
+        left = jnp.concatenate([high, high, low, low], axis=0)
+        right = jnp.concatenate([high, low, high, low], axis=0)
+        q = turn(dot(left, right, ((0,), (0,))), (systems - n) % systems)
+        top = jnp.where(column(n) < antennas, q[:antennas], -q[:antennas]) + pltpu.roll(q[antennas:], antennas, 1)
+        bottom = pltpu.roll(top, antennas, 1)
+        bottom = jnp.where(column(n) < antennas, -bottom, bottom)
+        for at, half in enumerate((top, bottom)):
+            high, low = two_parts(half)
+            inverse_ref[n, at * antennas : (at + 1) * antennas, :size] = high
+            inverse_ref[n, at * antennas : (at + 1) * antennas, size:] = low
+
     copies = []
     for point in range(points):
         total = jnp.zeros((1, users), F32)
         for block in range(blocks):
             n = block * points + point
-            high, low = two_parts(sys_ref[n])
-            left = jnp.concatenate([high, high, low, low], axis=0)
-            right = jnp.concatenate([high, low, high, low], axis=0)
-            q = turn(dot(left, right, ((0,), (0,))), (systems - n) % systems)
-            top = jnp.where(column(n) < antennas, q[:antennas], -q[:antennas]) + pltpu.roll(q[antennas:], antennas, 1)
-            bottom = pltpu.roll(top, antennas, 1)
-            bottom = jnp.where(column(n) < antennas, -bottom, bottom)
-            parts = jnp.concatenate(two_parts(jnp.concatenate([top, bottom], axis=0)), axis=1)
+            parts = inverse_ref[n]
             for slot in range(4):
                 x = turn(channel(block, slot, point), n)
                 y = dot(parts, jnp.concatenate([x, x], axis=0), ((1,), (0,)))
@@ -470,6 +458,7 @@
             pltpu.VMEM((antennas, size), F32),
             pltpu.VMEM((blocks, size, users), F32),
             pltpu.VMEM((points, blocks, 2, antennas, users), BF16),
+            pltpu.VMEM((blocks * points, size, 2 * size), BF16),
             pltpu.SemaphoreType.DMA((points,)),
         ],
         name="solve",
@@ -495,7 +484,8 @@
     near = across(channel, "ut", 1)
     v_far = across(start_precoder, "ut", 3)
 
-    early, own, v_own = own_gains(cluster, channel, start_precoder, chips)
+    own = channel * cluster[:, 0].astype(BF16)[None, None, :, None, None]
+    early = own_gains(own.reshape(blocks, rows, users), start_precoder.reshape(blocks, rows, users), chips)
     early = lax.all_to_all(early, CHIPS, 0, 0, tiled=True)
     near = near * near_cluster[:, 0].astype(BF16)[None, None, :, None, None]
 
@@ -503,7 +493,7 @@
     far_near = across(near, "ut", 3)
 
     where = jnp.stack([chip, core])
-    flat = [x.reshape(blocks, rows, users) for x in (own, near, v_own, v_far)]
+    flat = [x.reshape(blocks, rows, users) for x in (own, near, start_precoder, v_far)]
     keeps, cames = [], []
     for b in range(blocks):
         keep, send = partial_gains(b, core.reshape(1), *flat, chips)

time: 75.2 us -> 72.9 us (0.969)
  local copies, waits for them, and re-layouts: 3.54 us -> 0.69 us
  Pallas kernels: 19.6 us -> 17 us
  other arithmetic: 0.19 us -> 2.05 us
  starting transfers between devices: 31.1 us -> 32.6 us
    unnamed x11 -> x8, local copies, waits for them, and re-layouts: 3.54 us -> 0.69 us
    pallas_call x1, Pallas kernels: 12.7 us -> 11.1 us  [solve(): pl.pallas_call(solve_kernel, out_shape=(jax.ShapeDtypeStruct(out_shape, B...]
    mul x0 -> x1, other arithmetic: none -> 1.2 us  [local(): own = channel * cluster[:, 0].astype(BF16)[None, None, :, None, None]]
    ppermute x8, waiting for transfers between devices: 5.8 us -> 6.84 us  [across(): return lax.ppermute(value, axis, [(i, i ^ mask) for i in range(size)])]
    pallas_call x1, Pallas kernels: 2.32 us -> 1.32 us  [own_gains(): pl.pallas_call(own_kernel, out_shape=jax.ShapeDtypeStruct((chips, 4 * (us...]
    all_to_all x1, waiting for transfers between devices: 6.39 us -> 5.57 us  [local(): lax.all_to_all(line, EVERY, 0, 0, tiled=True)]
    all_to_all x1, starting transfers between devices: 7.44 us -> 8.25 us  [local(): lax.all_to_all(line, EVERY, 0, 0, tiled=True)]
  transfers between devices with their start and end apart: 11 -> 11, of which waited for: 7 -> 8; matrix products, arithmetic and copies ran while one was open for 1% -> 3% of each run, Pallas kernels for 9% -> 8%
where the time goes in v8:
time: 72.9 us; the launch traced here: 72.5 us
  starting transfers between devices  32.6 us (45%)
  waiting for transfers between devices  19.4 us (27%)
  Pallas kernels  17 us (23%)
  other arithmetic  2.05 us (3%)
  between operations  0.74 us (1%)
    ppermute x8, starting transfers between devices, across(): return lax.ppermute(value, axis, [(i, i ^ mask) for i in range(size)])  13.2 us
    pallas_call x1, Pallas kernels, solve(): pl.pallas_call(solve_kernel, out_shape=(jax.ShapeDtypeStruct(out_shape, B...  11.1 us
    all_to_all x1, starting transfers between devices, local(): lax.all_to_all(line, EVERY, 0, 0, tiled=True)  8.25 us
    all_to_all x1, starting transfers between devices, local(): early = lax.all_to_all(early, CHIPS, 0, 0, tiled=True)  7.59 us
    ppermute x8, waiting for transfers between devices, across(): return lax.ppermute(value, axis, [(i, i ^ mask) for i in range(size)])  6.84 us
    all_to_all x1, waiting for transfers between devices, local(): lax.all_to_all(line, EVERY, 0, 0, tiled=True)  5.57 us
    all_to_all x1, waiting for transfers between devices, local(): early = lax.all_to_all(early, CHIPS, 0, 0, tiled=True)  4.15 us
    all_to_all x1, starting transfers between devices, local(): late = lax.all_to_all(late, CHIPS, 0, 0, tiled=True)  3.61 us
  transfers between devices with their start and end apart: 11, of which 8 were waited for; matrix products, arithmetic and copies ran while one was open for 3% of the time, Pallas kernels for 8%

profile of v8, /device:TPU:1, one launch (start us, length us, event | category | flops | bytes accessed | tf_op | source)
XLA Modules:
  0.0 72.5 jit_solution(1738219002720059191)
XLA Ops:
  0.6 2.2 %collective-permute-start = (bf16[2,2,4,64,256]{4,3,2,1,0:T(8,128)(2,1)}, bf16[2,2,4,64,256]{4,3,2,1,0:T(8,128)(2,1)S(1)}, u32[]{:S(2)}, u32[]{:S(2)}) collective-permute-start(bf16[2,2,4,64,256]{4,3,2,1,0:T(8,128)(2,1)} %param.6), channel_id=1, source_target_pairs={{0,1},{1,0},{2,3},{3,2},{4,5},{5,4},{6,7},{7,6},{8,9},{9,8},{10,11... | collective-permute-start | bytes 1572872 | tf_op jit(solution)/shard_map/ppermute | solution.py:471
  2.8 0.1 collective-permute-start.1
  2.9 2.8 %collective-permute-start.2 = (bf16[2,2,4,64,256]{4,3,2,1,0:T(8,128)(2,1)}, bf16[2,2,4,64,256]{4,3,2,1,0:T(8,128)(2,1)S(1)}, u32[]{:S(2)}, u32[]{:S(2)}) collective-permute-start(bf16[2,2,4,64,256]{4,3,2,1,0:T(8,128)(2,1)} %param.7), channel_id=1, source_target_pairs={{0,3},{1,2},{2,1},{3,0},{4,7},{5,6},{6,5},{7,4},{8,11},{9,10},{10,... | collective-permute-start | bytes 1572872 | tf_op jit(solution)/shard_map/ppermute | solution.py:471
  5.7 0.7 convert_bitcast_fusion.1
  6.4 0.0 copy-start
  6.4 1.2 %broadcast_multiply_fusion.1.refs_0_ = bf16[2,2,4,64,256]{4,3,2,1,0:T(8,128)(2,1)S(1)} fusion(bf16[2,2,4,64,256]{4,3,2,1,0:T(8,128)(2,1)} %param.6, bf16[4]{0:T(256)(128)(2,1)S(1)} %convert_bitcast_fusion.1), kind=kLoop, calls=%fused_computation.1 | loop fusion | flops 262144 | bytes 1048584 | tf_op jit(solution)/shard_map/mul | solution.py:487
  7.6 0.0 copy-done
  7.6 1.3 %own_gains.1 = bf16[16,72,256]{2,1,0:T(8,128)(2,1)} custom-call(bf16[2,512,256]{2,1,0:T(8,128)(2,1)S(1)} %bitcast.17, bf16[2,512,256]{2,1,0:T(8,128)(2,1)S(1)} %bitcast.22), custom_call_target="tpu_custom_call" | custom-call | tf_op jit(solution)/shard_map/own_gains/pallas_call | solution.py:64
  8.9 7.6 %all-to-all-start = ((bf16[16,72,256]{2,1,0:T(8,128)(2,1)}), bf16[16,72,256]{2,1,0:T(8,128)(2,1)S(1)}, u32[]{:S(2)}, u32[]{:S(2)}) async-start(bf16[16,72,256]{2,1,0:T(8,128)(2,1)} %own_gains.1), calls=%async_computation | async-start | bytes 1179648 | tf_op jit(solution)/shard_map/all_to_all | solution.py:489
  16.5 0.0 collective-permute-done.1
  16.6 0.0 collective-permute-done
  16.6 0.1 broadcast_multiply_fusion.refs_1_
  16.7 0.2 collective-permute-done.2
  16.9 0.6 gains.2
  17.5 2.0 %collective-permute-start.3 = (bf16[16,2,16,384]{3,2,1,0:T(8,128)(2,1)S(1)}, bf16[16,2,16,384]{3,2,1,0:T(8,128)(2,1)S(1)}, u32[]{:S(2)}, u32[]{:S(2)}) collective-permute-start(bf16[16,2,16,384]{3,2,1,0:T(8,128)(2,1)S(1)} %get-tuple-element.14), channel_id=1, source_target_pairs={{0,4},{4,0},{1,5},{5,1},{2,6},{6,2},{3,7},{7,3},{8,12},{12,8},{9,1... | collective-permute-start | bytes 1179656 | tf_op jit(solution)/shard_map/ppermute | solution.py:471
  19.5 0.6 gains.3
  20.2 0.1 collective-permute-start.4
  20.3 0.6 collective-permute-done.3.came0_ref
  20.9 1.1 %collective-permute-done.4.came1_ref = bf16[16,2,16,384]{3,2,1,0:T(8,128)(2,1)S(1)} collective-permute-done((bf16[16,2,16,384]{3,2,1,0:T(8,128)(2,1)S(1)}, bf16[16,2,16,384]{3,2,1,0:T(8,128)(2,1)S(1)}, u32[]{:S(2)}, u32[]{:S(2)}) %collective-permute-start.4) | collective-permute-done | bytes 393248 | tf_op jit(solution)/shard_map/ppermute | solution.py:471
  22.0 1.0 %combine.1 = bf16[16,64,384]{2,1,0:T(8,128)(2,1)} custom-call(bf16[16,2,16,384]{3,2,1,0:T(8,128)(2,1)S(1)} %get-tuple-element.12.keep0_ref, bf16[16,2,16,384]{3,2,1,0:T(8,128)(2,1)S(1)} %get-tuple-element.13.keep1_ref, bf16[16,2,16,384]{3,2,1,0:T(8,128)(2,1)S(1)} %collective-permute-done.3.came0_ref, ...), custom_call_target="tpu_custom_call" | custom-call | tf_op jit(solution)/shard_map/combine/pallas_call | solution.py:119
  23.0 4.2 %all-to-all-done.g_ref = bf16[16,72,256]{2,1,0:T(8,128)(2,1)S(1)} async-done(((bf16[16,72,256]{2,1,0:T(8,128)(2,1)}), bf16[16,72,256]{2,1,0:T(8,128)(2,1)S(1)}, u32[]{:S(2)}, u32[]{:S(2)}) %all-to-all-start) | async-done | bytes 589856 | tf_op jit(solution)/shard_map/all_to_all | solution.py:489
  27.1 3.6 %all-to-all-start.1 = ((bf16[16,64,384]{2,1,0:T(8,128)(2,1)}), bf16[16,64,384]{2,1,0:T(8,128)(2,1)S(1)}, u32[]{:S(2)}, u32[]{:S(2)}) async-start(bf16[16,64,384]{2,1,0:T(8,128)(2,1)} %combine.1), calls=%async_computation.1 | async-start | bytes 1572864 | tf_op jit(solution)/shard_map/all_to_all | solution.py:503
  30.8 2.6 %collective-permute-start.6 = (bf16[2,2,4,64,256]{4,3,2,1,0:T(8,128)(2,1)S(1)}, bf16[2,2,4,64,256]{4,3,2,1,0:T(8,128)(2,1)S(1)}, u32[]{:S(2)}, u32[]{:S(2)}) collective-permute-start(bf16[2,2,4,64,256]{4,3,2,1,0:T(8,128)(2,1)S(1)} %broadcast_multiply_fusion.1.refs_0_), channel_id=1, source_target_pairs={{0,3},{1,2},{2,1},{3,0},{4,7},{5,6},{6,5},{7,4},{8,11},{9,10},{10,... | collective-permute-start | bytes 1572872 | tf_op jit(solution)/shard_map/ppermute | solution.py:471
  33.4 0.2 collective-permute-start.7
  33.5 0.1 pad_add_fusion.where_ref
  33.6 0.0 copy-start.1
  33.6 0.0 copy-start.2
  33.6 0.0 copy-start.3
  33.6 0.7 copy-done.1
  34.3 0.0 copy-done.2
  34.3 0.0 copy-done.3
  34.3 0.8 %own_sum.1 = (f32[64,256]{1,0:T(8,128)S(1)}, f32[1,128]{1,0:T(1,128)S(1)}, f32[1,4]{1,0:T(1,128)S(1)}, f32[1,4]{1,0:T(1,128)S(1)}) custom-call(s32[2]{0:T(128)S(1)} %pad_add_fusion.where_ref, bf16[16,72,256]{2,1,0:T(8,128)(2,1)S(1)} %all-to-all-done.g_ref, f32[2,256]{1,0:T(2,128)S(1)} %copy-done.1, f32[1,4]{1,0:T(1,128)S(1)} %bitcast.28, f32[1,4]{1,0:T(1,128)S(1)} %bitcast.29), custom_call_target="tpu_custom_call" | custom-call | tf_op jit(solution)/shard_map/own_sum/pallas_call | solution.py:164
  35.1 3.2 %collective-permute-start.5 = (f32[64,256]{1,0:T(8,128)S(1)}, f32[64,256]{1,0:T(8,128)S(1)}, u32[]{:S(2)}, u32[]{:S(2)}) collective-permute-start(f32[64,256]{1,0:T(8,128)S(1)} %get-tuple-element.16.mine_ref), channel_id=1, source_target_pairs={{0,4},{4,0},{1,5},{5,1},{2,6},{6,2},{3,7},{7,3},{8,12},{12,8},{9,1... | collective-permute-start | bytes 196616 | tf_op jit(solution)/shard_map/ppermute | solution.py:471
  38.3 0.9 %collective-permute-done.5.came_ref = f32[64,256]{1,0:T(8,128)S(1)} collective-permute-done((f32[64,256]{1,0:T(8,128)S(1)}, f32[64,256]{1,0:T(8,128)S(1)}, u32[]{:S(2)}, u32[]{:S(2)}) %collective-permute-start.5) | collective-permute-done | bytes 65568 | tf_op jit(solution)/shard_map/ppermute | solution.py:471
  39.2 0.6 own_total.1.line_ref
  39.9 2.9 %all-to-all-done.1.g_ref = bf16[16,64,384]{2,1,0:T(8,128)(2,1)S(1)} async-done(((bf16[16,64,384]{2,1,0:T(8,128)(2,1)}), bf16[16,64,384]{2,1,0:T(8,128)(2,1)S(1)}, u32[]{:S(2)}, u32[]{:S(2)}) %all-to-all-start.1) | async-done | bytes 786464 | tf_op jit(solution)/shard_map/all_to_all | solution.py:503
  42.7 0.8 %totals.1 = f32[128,128]{1,0:T(8,128)} custom-call(bf16[16,64,384]{2,1,0:T(8,128)(2,1)S(1)} %all-to-all-done.1.g_ref, f32[1,128]{1,0:T(1,128)S(1)} %own_total.1.line_ref), custom_call_target="tpu_custom_call" | custom-call | tf_op jit(solution)/shard_map/totals/pallas_call | solution.py:229
  43.6 8.3 %all-to-all-start.2 = ((f32[128,1,128]{2,1,0:T(1,128)}), f32[128,1,128]{2,1,0:T(1,128)S(1)}, u32[]{:S(2)}, u32[]{:S(2)}) async-start(f32[128,1,128]{2,1,0:T(1,128)} %bitcast.12), calls=%async_computation.2 | async-start | bytes 131072 | tf_op jit(solution)/shard_map/all_to_all | solution.py:508
  51.8 0.0 collective-permute-done.6.refs_2_
  51.8 4.0 %collective-permute-done.7.refs_3_ = bf16[2,2,4,64,256]{4,3,2,1,0:T(8,128)(2,1)S(1)} collective-permute-done((bf16[2,2,4,64,256]{4,3,2,1,0:T(8,128)(2,1)S(1)}, bf16[2,2,4,64,256]{4,3,2,1,0:T(8,128)(2,1)S(1)}, u32[]{:S(2)}, u32[]{:S(2)}) %collective-permute-start.7) | collective-permute-done | bytes 524320 | tf_op jit(solution)/shard_map/ppermute | solution.py:471
  55.8 5.6 %all-to-all-done.2 = f32[128,1,128]{2,1,0:T(1,128)S(1)} async-done(((f32[128,1,128]{2,1,0:T(1,128)}), f32[128,1,128]{2,1,0:T(1,128)S(1)}, u32[]{:S(2)}, u32[]{:S(2)}) %all-to-all-start.2) | async-done | bytes 65568 | tf_op jit(solution)/shard_map/all_to_all | solution.py:508
  61.4 11.1 %solve.1 = (bf16[2,2,4,64,256]{4,3,2,1,0:T(8,128)(2,1)}, f32[2,256]{1,0:T(2,128)}) custom-call(s32[1]{0:T(128)} %bitcast.tile_ref, f32[1,4]{1,0:T(1,128)S(1)} %get-tuple-element.10.penalty_ref, f32[1,4]{1,0:T(1,128)S(1)} %get-tuple-element.11.power_ref, f32[16,8,128]{2,1,0:T(8,128)S(1)} %bitcast.27, ...), custom_call_target="tpu_custom_call" | custom-call | tf_op jit(solution)/shard_map/solve/pallas_call | solution.py:446
  (1 shorter events, 0.0 us)
Async XLA Ops:
  0.6 15.9 %collective-permute-start = (bf16[2,2,4,64,256]{4,3,2,1,0:T(8,128)(2,1)}, bf16[2,2,4,64,256]{4,3,2,1,0:T(8,128)(2,1)S(1)}, u32[]{:S(2)}, u32[]{:S(2)}) collective-permute-start(bf16[2,2,4,64,256]{4,3,2,1,0:T(8,128)(2,1)} %param.6), channel_id=1, source_target_pairs={{0,1},{1,0},{2,3},{3,2},{4,5},{5,4},{6,7},{7,6},{8,9},{9,8},{10,11... | collective-permute-start | bytes 1572872 | tf_op jit(solution)/shard_map/ppermute | solution.py:471
  2.8 13.7 %collective-permute-start.1 = (s32[4,1]{0,1:T(1,128)}, s32[4,1]{0,1:T(1,128)S(1)}, u32[]{:S(2)}, u32[]{:S(2)}) collective-permute-start(s32[4,1]{0,1:T(1,128)} %param.8), channel_id=1, source_target_pairs={{0,1},{1,0},{2,3},{3,2},{4,5},{5,4},{6,7},{7,6},{8,9},{9,8},{10,11... | collective-permute-start | bytes 56 | tf_op jit(solution)/shard_map/ppermute | solution.py:471
  2.9 14.0 %collective-permute-start.2 = (bf16[2,2,4,64,256]{4,3,2,1,0:T(8,128)(2,1)}, bf16[2,2,4,64,256]{4,3,2,1,0:T(8,128)(2,1)S(1)}, u32[]{:S(2)}, u32[]{:S(2)}) collective-permute-start(bf16[2,2,4,64,256]{4,3,2,1,0:T(8,128)(2,1)} %param.7), channel_id=1, source_target_pairs={{0,3},{1,2},{2,1},{3,0},{4,7},{5,6},{6,5},{7,4},{8,11},{9,10},{10,... | collective-permute-start | bytes 1572872 | tf_op jit(solution)/shard_map/ppermute | solution.py:471
  6.4 1.2 %copy-start = (bf16[2,2,4,64,256]{4,3,2,1,0:T(8,128)(2,1)S(1)}, bf16[2,2,4,64,256]{4,3,2,1,0:T(8,128)(2,1)}, u32[]{:S(2)}) copy-start(bf16[2,2,4,64,256]{4,3,2,1,0:T(8,128)(2,1)} %param.7) | copy-start | bytes 1572868
  8.9 18.2 %all-to-all-start = ((bf16[16,72,256]{2,1,0:T(8,128)(2,1)}), bf16[16,72,256]{2,1,0:T(8,128)(2,1)S(1)}, u32[]{:S(2)}, u32[]{:S(2)}) async-start(bf16[16,72,256]{2,1,0:T(8,128)(2,1)} %own_gains.1), calls=%async_computation | async-start | bytes 1179648 | tf_op jit(solution)/shard_map/all_to_all | solution.py:489
  17.5 3.3 %collective-permute-start.3 = (bf16[16,2,16,384]{3,2,1,0:T(8,128)(2,1)S(1)}, bf16[16,2,16,384]{3,2,1,0:T(8,128)(2,1)S(1)}, u32[]{:S(2)}, u32[]{:S(2)}) collective-permute-start(bf16[16,2,16,384]{3,2,1,0:T(8,128)(2,1)S(1)} %get-tuple-element.14), channel_id=1, source_target_pairs={{0,4},{4,0},{1,5},{5,1},{2,6},{6,2},{3,7},{7,3},{8,12},{12,8},{9,1... | collective-permute-start | bytes 1179656 | tf_op jit(solution)/shard_map/ppermute | solution.py:471
  20.2 1.8 %collective-permute-start.4 = (bf16[16,2,16,384]{3,2,1,0:T(8,128)(2,1)S(1)}, bf16[16,2,16,384]{3,2,1,0:T(8,128)(2,1)S(1)}, u32[]{:S(2)}, u32[]{:S(2)}) collective-permute-start(bf16[16,2,16,384]{3,2,1,0:T(8,128)(2,1)S(1)} %get-tuple-element.15), channel_id=1, source_target_pairs={{0,4},{4,0},{1,5},{5,1},{2,6},{6,2},{3,7},{7,3},{8,12},{12,8},{9,1... | collective-permute-start | bytes 1179656 | tf_op jit(solution)/shard_map/ppermute | solution.py:471
  27.1 15.6 %all-to-all-start.1 = ((bf16[16,64,384]{2,1,0:T(8,128)(2,1)}), bf16[16,64,384]{2,1,0:T(8,128)(2,1)S(1)}, u32[]{:S(2)}, u32[]{:S(2)}) async-start(bf16[16,64,384]{2,1,0:T(8,128)(2,1)} %combine.1), calls=%async_computation.1 | async-start | bytes 1572864 | tf_op jit(solution)/shard_map/all_to_all | solution.py:503
  30.8 21.1 %collective-permute-start.6 = (bf16[2,2,4,64,256]{4,3,2,1,0:T(8,128)(2,1)S(1)}, bf16[2,2,4,64,256]{4,3,2,1,0:T(8,128)(2,1)S(1)}, u32[]{:S(2)}, u32[]{:S(2)}) collective-permute-start(bf16[2,2,4,64,256]{4,3,2,1,0:T(8,128)(2,1)S(1)} %broadcast_multiply_fusion.1.refs_0_), channel_id=1, source_target_pairs={{0,3},{1,2},{2,1},{3,0},{4,7},{5,6},{6,5},{7,4},{8,11},{9,10},{10,... | collective-permute-start | bytes 1572872 | tf_op jit(solution)/shard_map/ppermute | solution.py:471
  33.4 22.5 %collective-permute-start.7 = (bf16[2,2,4,64,256]{4,3,2,1,0:T(8,128)(2,1)S(1)}, bf16[2,2,4,64,256]{4,3,2,1,0:T(8,128)(2,1)S(1)}, u32[]{:S(2)}, u32[]{:S(2)}) collective-permute-start(bf16[2,2,4,64,256]{4,3,2,1,0:T(8,128)(2,1)S(1)} %broadcast_multiply_fusion.refs_1_), channel_id=1, source_target_pairs={{0,3},{1,2},{2,1},{3,0},{4,7},{5,6},{6,5},{7,4},{8,11},{9,10},{10,... | collective-permute-start | bytes 1572872 | tf_op jit(solution)/shard_map/ppermute | solution.py:471
  33.6 0.7 copy-start.1
  33.6 0.7 copy-start.2
  33.6 0.7 copy-start.3
  35.1 4.1 %collective-permute-start.5 = (f32[64,256]{1,0:T(8,128)S(1)}, f32[64,256]{1,0:T(8,128)S(1)}, u32[]{:S(2)}, u32[]{:S(2)}) collective-permute-start(f32[64,256]{1,0:T(8,128)S(1)} %get-tuple-element.16.mine_ref), channel_id=1, source_target_pairs={{0,4},{4,0},{1,5},{5,1},{2,6},{6,2},{3,7},{7,3},{8,12},{12,8},{9,1... | collective-permute-start | bytes 196616 | tf_op jit(solution)/shard_map/ppermute | solution.py:471
  43.6 17.9 %all-to-all-start.2 = ((f32[128,1,128]{2,1,0:T(1,128)}), f32[128,1,128]{2,1,0:T(1,128)S(1)}, u32[]{:S(2)}, u32[]{:S(2)}) async-start(f32[128,1,128]{2,1,0:T(1,128)} %bitcast.12), calls=%async_computation.2 | async-start | bytes 131072 | tf_op jit(solution)/shard_map/all_to_all | solution.py:508

commit v9 on v8

--- a/solution.py
+++ b/solution.py
@@ -71,14 +71,20 @@
     )(h, v)
 
 
-def gain_kernel(block, core_ref, ht_ref, ha_ref, vt_ref, vb_ref, keep_ref, send_ref):
+def gain_kernel(block, core_ref, cluster_ref, ht_ref, ha_ref, vt_ref, vb_ref, keep_ref, send_ref):
     _, _, users = ht_ref.shape
     half = users // 2
     chips = keep_ref.shape[0]
     piece = users // chips
     first = core_ref[0] == 0
     vt, vb = vt_ref[block], vb_ref[block]
-    ht, ha = jnp.transpose(ht_ref[block]), jnp.transpose(ha_ref[block])
+    _, parts, points, _, _ = ha_ref.shape
+    ha = []
+    for part in range(parts):
+        for point in range(points):
+            near = ha_ref[block, part, point]
+            ha.append(jnp.where(cluster_ref[point] != 0, near, jnp.zeros_like(near)))
+    ht, ha = jnp.transpose(ht_ref[block]), jnp.transpose(jnp.concatenate(ha, axis=0))
     for out_ref, low in ((keep_ref, first), (send_ref, jnp.logical_not(first))):
         own = jnp.where(low, vt[:, :half], vt[:, half:])
         far = jnp.where(low, vb[:, :half], vb[:, half:])
@@ -90,19 +96,19 @@
             out_ref[:, part, :, half:] = dot(ha, w, ((1,), (0,))).reshape(chips, piece, users).astype(BF16)
 
 
-def partial_gains(block, core, ht, ha, vt, vb, chips):
+def partial_gains(block, core, near_cluster, ht, ha, vt, vb, chips):
     _, rows, users = ht.shape
     shape = (chips, 2, users // chips, users + users // 2)
     vm = pl.BlockSpec(memory_space=pltpu.VMEM)
     return pl.pallas_call(
         functools.partial(gain_kernel, block),
         out_shape=(jax.ShapeDtypeStruct(shape, BF16), jax.ShapeDtypeStruct(shape, BF16)),
-        in_specs=[pl.BlockSpec(memory_space=pltpu.SMEM)] + [vm] * 4,
+        in_specs=[pl.BlockSpec(memory_space=pltpu.SMEM)] * 2 + [vm] * 4,
         out_specs=(vm, vm),
         name="gains",
         compiler_params=pltpu.CompilerParams(vmem_limit_bytes=8 << 20),
         cost_estimate=pl.CostEstimate(flops=12 * users * users * rows, bytes_accessed=4 << 20, transcendentals=0),
-    )(core, ht, ha, vt, vb)
+    )(core, near_cluster, ht, ha, vt, vb)
 
 
 def combine_kernel(keep0_ref, keep1_ref, came0_ref, came1_ref, out_ref):
@@ -480,25 +486,25 @@
     tile = lax.axis_index("ut")
     chip = lax.axis_index(CHIPS)
 
-    near_cluster = across(cluster, "ut", 1)
+    near_cluster = across(cluster[:, 0], "ut", 1)
     near = across(channel, "ut", 1)
     v_far = across(start_precoder, "ut", 3)
 
     own = channel * cluster[:, 0].astype(BF16)[None, None, :, None, None]
     early = own_gains(own.reshape(blocks, rows, users), start_precoder.reshape(blocks, rows, users), chips)
     early = lax.all_to_all(early, CHIPS, 0, 0, tiled=True)
-    near = near * near_cluster[:, 0].astype(BF16)[None, None, :, None, None]
 
     far = across(own, "ut", 3)
-    far_near = across(near, "ut", 3)
 
     where = jnp.stack([chip, core])
-    flat = [x.reshape(blocks, rows, users) for x in (own, near, start_precoder, v_far)]
+    ht, vt, vb = (x.reshape(blocks, rows, users) for x in (own, start_precoder, v_far))
     keeps, cames = [], []
     for b in range(blocks):
-        keep, send = partial_gains(b, core.reshape(1), *flat, chips)
+        keep, send = partial_gains(b, core.reshape(1), near_cluster, ht, near, vt, vb, chips)
         keeps.append(keep)
         cames.append(across(send, "core", 1))
+    near = near * near_cluster.astype(BF16)[None, None, :, None, None]
+    far_near = across(near, "ut", 3)
     late = combined(keeps, cames)
     late = lax.all_to_all(late, CHIPS, 0, 0, tiled=True)
 

time: 72.9 us -> 74.4 us (1.021)
  starting transfers between devices: 32.6 us -> 30.7 us
  waiting for transfers between devices: 19.4 us -> 21.1 us
  Pallas kernels: 17 us -> 18.1 us
    ppermute x8, waiting for transfers between devices: 6.84 us -> 11.2 us  [across(): return lax.ppermute(value, axis, [(i, i ^ mask) for i in range(size)])]
    all_to_all x1, waiting for transfers between devices: 4.15 us -> 0.01 us  [local(): early = lax.all_to_all(early, CHIPS, 0, 0, tiled=True)]
    all_to_all x1, waiting for transfers between devices: 2.87 us -> 6.6 us  [local(): late = lax.all_to_all(late, CHIPS, 0, 0, tiled=True)]
    all_to_all x1, starting transfers between devices: 3.61 us -> 6.94 us  [local(): late = lax.all_to_all(late, CHIPS, 0, 0, tiled=True)]
    all_to_all x1, starting transfers between devices: 8.25 us -> 4.95 us  [local(): lax.all_to_all(line, EVERY, 0, 0, tiled=True)]
    all_to_all x1, waiting for transfers between devices: 5.57 us -> 3.28 us  [local(): lax.all_to_all(line, EVERY, 0, 0, tiled=True)]
    ppermute x8, starting transfers between devices: 13.2 us -> 11.2 us  [across(): return lax.ppermute(value, axis, [(i, i ^ mask) for i in range(size)])]
    pallas_call x2, Pallas kernels: 1.27 us -> 2.37 us  [partial_gains(): pl.pallas_call(functools.partial(gain_kernel, block), out_shape=(jax.Shap...]
  transfers between devices with their start and end apart: 11 -> 11, of which waited for: 8 -> 7; matrix products, arithmetic and copies ran while one was open for 3% -> 3% of each run, Pallas kernels for 8% -> 9%
where the time goes in v9:
time: 74.4 us; the launch traced here: 74 us
  starting transfers between devices  30.7 us (41%)
  waiting for transfers between devices  21.1 us (28%)
  Pallas kernels  18.1 us (24%)
  other arithmetic  2.05 us (3%)
  local copies, waits for them, and re-layouts  1.34 us (2%)
    ppermute x8, waiting for transfers between devices, across(): return lax.ppermute(value, axis, [(i, i ^ mask) for i in range(size)])  11.2 us
    ppermute x8, starting transfers between devices, across(): return lax.ppermute(value, axis, [(i, i ^ mask) for i in range(size)])  11.2 us
    pallas_call x1, Pallas kernels, solve(): pl.pallas_call(solve_kernel, out_shape=(jax.ShapeDtypeStruct(out_shape, B...  11.1 us
    all_to_all x1, starting transfers between devices, local(): early = lax.all_to_all(early, CHIPS, 0, 0, tiled=True)  7.61 us
    all_to_all x1, starting transfers between devices, local(): late = lax.all_to_all(late, CHIPS, 0, 0, tiled=True)  6.94 us
    all_to_all x1, waiting for transfers between devices, local(): late = lax.all_to_all(late, CHIPS, 0, 0, tiled=True)  6.6 us
    all_to_all x1, starting transfers between devices, local(): lax.all_to_all(line, EVERY, 0, 0, tiled=True)  4.95 us
    all_to_all x1, waiting for transfers between devices, local(): lax.all_to_all(line, EVERY, 0, 0, tiled=True)  3.28 us
  transfers between devices with their start and end apart: 11, of which 7 were waited for; matrix products, arithmetic and copies ran while one was open for 3% of the time, Pallas kernels for 9%

profile of v9, /device:TPU:1, one launch (start us, length us, event | category | flops | bytes accessed | tf_op | source)
XLA Modules:
  0.0 74.0 jit_solution(2291538404513076937)
XLA Ops:
  0.6 2.2 %collective-permute-start.1 = (bf16[2,2,4,64,256]{4,3,2,1,0:T(8,128)(2,1)}, bf16[2,2,4,64,256]{4,3,2,1,0:T(8,128)(2,1)S(1)}, u32[]{:S(2)}, u32[]{:S(2)}) collective-permute-start(bf16[2,2,4,64,256]{4,3,2,1,0:T(8,128)(2,1)} %param.6), channel_id=1, source_target_pairs={{0,1},{1,0},{2,3},{3,2},{4,5},{5,4},{6,7},{7,6},{8,9},{9,8},{10,11... | collective-permute-start | bytes 1572872 | tf_op jit(solution)/shard_map/ppermute | solution.py:477
  2.8 1.9 %collective-permute-start.2 = (bf16[2,2,4,64,256]{4,3,2,1,0:T(8,128)(2,1)}, bf16[2,2,4,64,256]{4,3,2,1,0:T(8,128)(2,1)S(1)}, u32[]{:S(2)}, u32[]{:S(2)}) collective-permute-start(bf16[2,2,4,64,256]{4,3,2,1,0:T(8,128)(2,1)} %param.7), channel_id=1, source_target_pairs={{0,3},{1,2},{2,1},{3,0},{4,7},{5,6},{6,5},{7,4},{8,11},{9,10},{10,... | collective-permute-start | bytes 1572872 | tf_op jit(solution)/shard_map/ppermute | solution.py:477
  4.7 0.7 bitcast_convert_fusion
  5.4 0.0 copy-start
  5.4 1.2 %broadcast_multiply_fusion.1.refs_0_ = bf16[2,2,4,64,256]{4,3,2,1,0:T(8,128)(2,1)S(1)} fusion(bf16[2,2,4,64,256]{4,3,2,1,0:T(8,128)(2,1)} %param.6, bf16[4]{0:T(256)(128)(2,1)S(1)} %bitcast_convert_fusion), kind=kLoop, calls=%fused_computation.1 | loop fusion | flops 262144 | bytes 1048584 | tf_op jit(solution)/shard_map/mul | solution.py:493
  6.6 0.0 copy-done
  6.6 1.3 %own_gains.1 = bf16[16,72,256]{2,1,0:T(8,128)(2,1)} custom-call(bf16[2,512,256]{2,1,0:T(8,128)(2,1)S(1)} %bitcast.14, bf16[2,512,256]{2,1,0:T(8,128)(2,1)S(1)} %bitcast.17), custom_call_target="tpu_custom_call" | custom-call | tf_op jit(solution)/shard_map/own_gains/pallas_call | solution.py:64
  7.9 7.6 %all-to-all-start = ((bf16[16,72,256]{2,1,0:T(8,128)(2,1)}), bf16[16,72,256]{2,1,0:T(8,128)(2,1)S(1)}, u32[]{:S(2)}, u32[]{:S(2)}) async-start(bf16[16,72,256]{2,1,0:T(8,128)(2,1)} %own_gains.1), calls=%async_computation | async-start | bytes 1179648 | tf_op jit(solution)/shard_map/all_to_all | solution.py:495
  15.5 0.0 copy-start.4
  15.6 0.6 copy-done.4
  16.2 0.4 collective-permute-start
  16.6 2.0 %collective-permute-done.cluster_ref = s32[4]{0:T(128)S(1)} collective-permute-done((s32[4]{0:T(128)S(1)}, s32[4]{0:T(128)S(1)}, u32[]{:S(2)}, u32[]{:S(2)}) %collective-permute-start) | collective-permute-done | bytes 48 | tf_op jit(solution)/shard_map/ppermute | solution.py:477
  18.6 0.0 collective-permute-done.1.ha_ref
  18.6 0.0 collective-permute-done.2
  18.6 1.2 %gains.2 = (bf16[16,2,16,384]{3,2,1,0:T(8,128)(2,1)S(1)}, bf16[16,2,16,384]{3,2,1,0:T(8,128)(2,1)S(1)}) custom-call(s32[1]{0:T(128)} %bitcast.2.core_ref, s32[4]{0:T(128)S(1)} %collective-permute-done.cluster_ref, bf16[2,512,256]{2,1,0:T(8,128)(2,1)S(1)} %bitcast.15, bf16[2,2,4,64,256]{4,3,2,1,0:T(8,128)(2,1)S(1)} %collective-permute-done.1.ha_ref, ...), custom_call_target="tpu_custom_call" | custom-call | flops 402653184 | bytes 4194304 | tf_op jit(solution)/shard_map/gains/pallas_call | solution.py:103
  19.8 2.7 %collective-permute-start.3 = (bf16[16,2,16,384]{3,2,1,0:T(8,128)(2,1)S(1)}, bf16[16,2,16,384]{3,2,1,0:T(8,128)(2,1)S(1)}, u32[]{:S(2)}, u32[]{:S(2)}) collective-permute-start(bf16[16,2,16,384]{3,2,1,0:T(8,128)(2,1)S(1)} %get-tuple-element.14), channel_id=1, source_target_pairs={{0,4},{4,0},{1,5},{5,1},{2,6},{6,2},{3,7},{7,3},{8,12},{12,8},{9,1... | collective-permute-start | bytes 1179656 | tf_op jit(solution)/shard_map/ppermute | solution.py:477
  22.6 1.2 %gains.3 = (bf16[16,2,16,384]{3,2,1,0:T(8,128)(2,1)S(1)}, bf16[16,2,16,384]{3,2,1,0:T(8,128)(2,1)S(1)}) custom-call(s32[1]{0:T(128)} %bitcast.2.core_ref, s32[4]{0:T(128)S(1)} %collective-permute-done.cluster_ref, bf16[2,512,256]{2,1,0:T(8,128)(2,1)S(1)} %bitcast.16, bf16[2,2,4,64,256]{4,3,2,1,0:T(8,128)(2,1)S(1)} %collective-permute-done.1.ha_ref, ...), custom_call_target="tpu_custom_call" | custom-call | flops 402653184 | bytes 4194304 | tf_op jit(solution)/shard_map/gains/pallas_call | solution.py:103
  23.7 0.1 collective-permute-start.4
  23.8 0.1 collective-permute-done.3.came0_ref
  23.9 1.6 %collective-permute-done.4.came1_ref = bf16[16,2,16,384]{3,2,1,0:T(8,128)(2,1)S(1)} collective-permute-done((bf16[16,2,16,384]{3,2,1,0:T(8,128)(2,1)S(1)}, bf16[16,2,16,384]{3,2,1,0:T(8,128)(2,1)S(1)}, u32[]{:S(2)}, u32[]{:S(2)}) %collective-permute-start.4) | collective-permute-done | bytes 393248 | tf_op jit(solution)/shard_map/ppermute | solution.py:477
  25.5 1.0 %combine.1 = bf16[16,64,384]{2,1,0:T(8,128)(2,1)} custom-call(bf16[16,2,16,384]{3,2,1,0:T(8,128)(2,1)S(1)} %get-tuple-element.12.keep0_ref, bf16[16,2,16,384]{3,2,1,0:T(8,128)(2,1)S(1)} %get-tuple-element.13.keep1_ref, bf16[16,2,16,384]{3,2,1,0:T(8,128)(2,1)S(1)} %collective-permute-done.3.came0_ref, ...), custom_call_target="tpu_custom_call" | custom-call | tf_op jit(solution)/shard_map/combine/pallas_call | solution.py:125
  26.5 0.0 all-to-all-done.g_ref
  26.5 6.9 %all-to-all-start.1 = ((bf16[16,64,384]{2,1,0:T(8,128)(2,1)}), bf16[16,64,384]{2,1,0:T(8,128)(2,1)S(1)}, u32[]{:S(2)}, u32[]{:S(2)}) async-start(bf16[16,64,384]{2,1,0:T(8,128)(2,1)} %combine.1), calls=%async_computation.1 | async-start | bytes 1572864 | tf_op jit(solution)/shard_map/all_to_all | solution.py:509
  33.5 0.9 %collective-permute-start.6 = (bf16[2,2,4,64,256]{4,3,2,1,0:T(8,128)(2,1)S(1)}, bf16[2,2,4,64,256]{4,3,2,1,0:T(8,128)(2,1)S(1)}, u32[]{:S(2)}, u32[]{:S(2)}) collective-permute-start(bf16[2,2,4,64,256]{4,3,2,1,0:T(8,128)(2,1)S(1)} %broadcast_multiply_fusion.1.refs_0_), channel_id=1, source_target_pairs={{0,3},{1,2},{2,1},{3,0},{4,7},{5,6},{6,5},{7,4},{8,11},{9,10},{10,... | collective-permute-start | bytes 1572872 | tf_op jit(solution)/shard_map/ppermute | solution.py:477
  34.4 0.1 broadcast_multiply_fusion.refs_1_
  34.5 2.0 %collective-permute-start.7 = (bf16[2,2,4,64,256]{4,3,2,1,0:T(8,128)(2,1)S(1)}, bf16[2,2,4,64,256]{4,3,2,1,0:T(8,128)(2,1)S(1)}, u32[]{:S(2)}, u32[]{:S(2)}) collective-permute-start(bf16[2,2,4,64,256]{4,3,2,1,0:T(8,128)(2,1)S(1)} %broadcast_multiply_fusion.refs_1_), channel_id=1, source_target_pairs={{0,3},{1,2},{2,1},{3,0},{4,7},{5,6},{6,5},{7,4},{8,11},{9,10},{10,... | collective-permute-start | bytes 1572872 | tf_op jit(solution)/shard_map/ppermute | solution.py:477
  36.4 0.1 pad_add_fusion.where_ref
  36.5 0.0 copy-start.1
  36.5 0.0 copy-start.2
  36.5 0.0 copy-start.3
  36.5 0.7 copy-done.1
  37.2 0.0 copy-done.2
  37.2 0.0 copy-done.3
  37.2 0.8 %own_sum.1 = (f32[64,256]{1,0:T(8,128)S(1)}, f32[1,128]{1,0:T(1,128)S(1)}, f32[1,4]{1,0:T(1,128)S(1)}, f32[1,4]{1,0:T(1,128)S(1)}) custom-call(s32[2]{0:T(128)S(1)} %pad_add_fusion.where_ref, bf16[16,72,256]{2,1,0:T(8,128)(2,1)S(1)} %all-to-all-done.g_ref, f32[2,256]{1,0:T(2,128)S(1)} %copy-done.1, f32[1,4]{1,0:T(1,128)S(1)} %bitcast.23, f32[1,4]{1,0:T(1,128)S(1)} %bitcast.24), custom_call_target="tpu_custom_call" | custom-call | tf_op jit(solution)/shard_map/own_sum/pallas_call | solution.py:170
  38.0 1.1 %collective-permute-start.5 = (f32[64,256]{1,0:T(8,128)S(1)}, f32[64,256]{1,0:T(8,128)S(1)}, u32[]{:S(2)}, u32[]{:S(2)}) collective-permute-start(f32[64,256]{1,0:T(8,128)S(1)} %get-tuple-element.16.mine_ref), channel_id=1, source_target_pairs={{0,4},{4,0},{1,5},{5,1},{2,6},{6,2},{3,7},{7,3},{8,12},{12,8},{9,1... | collective-permute-start | bytes 196616 | tf_op jit(solution)/shard_map/ppermute | solution.py:477
  39.1 0.9 %collective-permute-done.5.came_ref = f32[64,256]{1,0:T(8,128)S(1)} collective-permute-done((f32[64,256]{1,0:T(8,128)S(1)}, f32[64,256]{1,0:T(8,128)S(1)}, u32[]{:S(2)}, u32[]{:S(2)}) %collective-permute-start.5) | collective-permute-done | bytes 65568 | tf_op jit(solution)/shard_map/ppermute | solution.py:477
  40.0 0.6 own_total.1.line_ref
  40.6 6.6 %all-to-all-done.1.g_ref = bf16[16,64,384]{2,1,0:T(8,128)(2,1)S(1)} async-done(((bf16[16,64,384]{2,1,0:T(8,128)(2,1)}), bf16[16,64,384]{2,1,0:T(8,128)(2,1)S(1)}, u32[]{:S(2)}, u32[]{:S(2)}) %all-to-all-start.1) | async-done | bytes 786464 | tf_op jit(solution)/shard_map/all_to_all | solution.py:509
  47.2 0.8 %totals.1 = f32[128,128]{1,0:T(8,128)} custom-call(bf16[16,64,384]{2,1,0:T(8,128)(2,1)S(1)} %all-to-all-done.1.g_ref, f32[1,128]{1,0:T(1,128)S(1)} %own_total.1.line_ref), custom_call_target="tpu_custom_call" | custom-call | tf_op jit(solution)/shard_map/totals/pallas_call | solution.py:235
  48.1 4.9 %all-to-all-start.2 = ((f32[128,1,128]{2,1,0:T(1,128)}), f32[128,1,128]{2,1,0:T(1,128)S(1)}, u32[]{:S(2)}, u32[]{:S(2)}) async-start(f32[128,1,128]{2,1,0:T(1,128)} %bitcast.10), calls=%async_computation.2 | async-start | bytes 131072 | tf_op jit(solution)/shard_map/all_to_all | solution.py:514
  53.0 0.0 collective-permute-done.6.refs_2_
  53.0 6.6 %collective-permute-done.7.refs_3_ = bf16[2,2,4,64,256]{4,3,2,1,0:T(8,128)(2,1)S(1)} collective-permute-done((bf16[2,2,4,64,256]{4,3,2,1,0:T(8,128)(2,1)S(1)}, bf16[2,2,4,64,256]{4,3,2,1,0:T(8,128)(2,1)S(1)}, u32[]{:S(2)}, u32[]{:S(2)}) %collective-permute-start.7) | collective-permute-done | bytes 524320 | tf_op jit(solution)/shard_map/ppermute | solution.py:477
  59.6 3.3 %all-to-all-done.2 = f32[128,1,128]{2,1,0:T(1,128)S(1)} async-done(((f32[128,1,128]{2,1,0:T(1,128)}), f32[128,1,128]{2,1,0:T(1,128)S(1)}, u32[]{:S(2)}, u32[]{:S(2)}) %all-to-all-start.2) | async-done | bytes 65568 | tf_op jit(solution)/shard_map/all_to_all | solution.py:514
  62.9 11.1 %solve.1 = (bf16[2,2,4,64,256]{4,3,2,1,0:T(8,128)(2,1)}, f32[2,256]{1,0:T(2,128)}) custom-call(s32[1]{0:T(128)} %bitcast.tile_ref, f32[1,4]{1,0:T(1,128)S(1)} %get-tuple-element.10.penalty_ref, f32[1,4]{1,0:T(1,128)S(1)} %get-tuple-element.11.power_ref, f32[16,8,128]{2,1,0:T(8,128)S(1)} %bitcast.22, ...), custom_call_target="tpu_custom_call" | custom-call | tf_op jit(solution)/shard_map/solve/pallas_call | solution.py:452
  (1 shorter events, 0.0 us)
Async XLA Ops:
  0.6 18.0 %collective-permute-start.1 = (bf16[2,2,4,64,256]{4,3,2,1,0:T(8,128)(2,1)}, bf16[2,2,4,64,256]{4,3,2,1,0:T(8,128)(2,1)S(1)}, u32[]{:S(2)}, u32[]{:S(2)}) collective-permute-start(bf16[2,2,4,64,256]{4,3,2,1,0:T(8,128)(2,1)} %param.6), channel_id=1, source_target_pairs={{0,1},{1,0},{2,3},{3,2},{4,5},{5,4},{6,7},{7,6},{8,9},{9,8},{10,11... | collective-permute-start | bytes 1572872 | tf_op jit(solution)/shard_map/ppermute | solution.py:477
  2.8 15.8 %collective-permute-start.2 = (bf16[2,2,4,64,256]{4,3,2,1,0:T(8,128)(2,1)}, bf16[2,2,4,64,256]{4,3,2,1,0:T(8,128)(2,1)S(1)}, u32[]{:S(2)}, u32[]{:S(2)}) collective-permute-start(bf16[2,2,4,64,256]{4,3,2,1,0:T(8,128)(2,1)} %param.7), channel_id=1, source_target_pairs={{0,3},{1,2},{2,1},{3,0},{4,7},{5,6},{6,5},{7,4},{8,11},{9,10},{10,... | collective-permute-start | bytes 1572872 | tf_op jit(solution)/shard_map/ppermute | solution.py:477
  5.4 1.2 %copy-start = (bf16[2,2,4,64,256]{4,3,2,1,0:T(8,128)(2,1)S(1)}, bf16[2,2,4,64,256]{4,3,2,1,0:T(8,128)(2,1)}, u32[]{:S(2)}) copy-start(bf16[2,2,4,64,256]{4,3,2,1,0:T(8,128)(2,1)} %param.7) | copy-start | bytes 1572868
  7.9 18.6 %all-to-all-start = ((bf16[16,72,256]{2,1,0:T(8,128)(2,1)}), bf16[16,72,256]{2,1,0:T(8,128)(2,1)S(1)}, u32[]{:S(2)}, u32[]{:S(2)}) async-start(bf16[16,72,256]{2,1,0:T(8,128)(2,1)} %own_gains.1), calls=%async_computation | async-start | bytes 1179648 | tf_op jit(solution)/shard_map/all_to_all | solution.py:495
  15.5 0.7 copy-start.4
  16.2 2.4 %collective-permute-start = (s32[4]{0:T(128)S(1)}, s32[4]{0:T(128)S(1)}, u32[]{:S(2)}, u32[]{:S(2)}) collective-permute-start(s32[4]{0:T(128)S(1)} %bitcast.25), channel_id=1, source_target_pairs={{0,1},{1,0},{2,3},{3,2},{4,5},{5,4},{6,7},{7,6},{8,9},{9,8},{10,11... | collective-permute-start | bytes 56 | tf_op jit(solution)/shard_map/ppermute | solution.py:477
  19.8 4.1 %collective-permute-start.3 = (bf16[16,2,16,384]{3,2,1,0:T(8,128)(2,1)S(1)}, bf16[16,2,16,384]{3,2,1,0:T(8,128)(2,1)S(1)}, u32[]{:S(2)}, u32[]{:S(2)}) collective-permute-start(bf16[16,2,16,384]{3,2,1,0:T(8,128)(2,1)S(1)} %get-tuple-element.14), channel_id=1, source_target_pairs={{0,4},{4,0},{1,5},{5,1},{2,6},{6,2},{3,7},{7,3},{8,12},{12,8},{9,1... | collective-permute-start | bytes 1179656 | tf_op jit(solution)/shard_map/ppermute | solution.py:477
  23.7 1.8 %collective-permute-start.4 = (bf16[16,2,16,384]{3,2,1,0:T(8,128)(2,1)S(1)}, bf16[16,2,16,384]{3,2,1,0:T(8,128)(2,1)S(1)}, u32[]{:S(2)}, u32[]{:S(2)}) collective-permute-start(bf16[16,2,16,384]{3,2,1,0:T(8,128)(2,1)S(1)} %get-tuple-element.15), channel_id=1, source_target_pairs={{0,4},{4,0},{1,5},{5,1},{2,6},{6,2},{3,7},{7,3},{8,12},{12,8},{9,1... | collective-permute-start | bytes 1179656 | tf_op jit(solution)/shard_map/ppermute | solution.py:477
  26.5 20.7 %all-to-all-start.1 = ((bf16[16,64,384]{2,1,0:T(8,128)(2,1)}), bf16[16,64,384]{2,1,0:T(8,128)(2,1)S(1)}, u32[]{:S(2)}, u32[]{:S(2)}) async-start(bf16[16,64,384]{2,1,0:T(8,128)(2,1)} %combine.1), calls=%async_computation.1 | async-start | bytes 1572864 | tf_op jit(solution)/shard_map/all_to_all | solution.py:509
  33.5 19.5 %collective-permute-start.6 = (bf16[2,2,4,64,256]{4,3,2,1,0:T(8,128)(2,1)S(1)}, bf16[2,2,4,64,256]{4,3,2,1,0:T(8,128)(2,1)S(1)}, u32[]{:S(2)}, u32[]{:S(2)}) collective-permute-start(bf16[2,2,4,64,256]{4,3,2,1,0:T(8,128)(2,1)S(1)} %broadcast_multiply_fusion.1.refs_0_), channel_id=1, source_target_pairs={{0,3},{1,2},{2,1},{3,0},{4,7},{5,6},{6,5},{7,4},{8,11},{9,10},{10,... | collective-permute-start | bytes 1572872 | tf_op jit(solution)/shard_map/ppermute | solution.py:477
  34.5 25.1 %collective-permute-start.7 = (bf16[2,2,4,64,256]{4,3,2,1,0:T(8,128)(2,1)S(1)}, bf16[2,2,4,64,256]{4,3,2,1,0:T(8,128)(2,1)S(1)}, u32[]{:S(2)}, u32[]{:S(2)}) collective-permute-start(bf16[2,2,4,64,256]{4,3,2,1,0:T(8,128)(2,1)S(1)} %broadcast_multiply_fusion.refs_1_), channel_id=1, source_target_pairs={{0,3},{1,2},{2,1},{3,0},{4,7},{5,6},{6,5},{7,4},{8,11},{9,10},{10,... | collective-permute-start | bytes 1572872 | tf_op jit(solution)/shard_map/ppermute | solution.py:477
  36.5 0.7 copy-start.1
  36.5 0.7 copy-start.2
  36.5 0.7 copy-start.3
  38.0 2.0 %collective-permute-start.5 = (f32[64,256]{1,0:T(8,128)S(1)}, f32[64,256]{1,0:T(8,128)S(1)}, u32[]{:S(2)}, u32[]{:S(2)}) collective-permute-start(f32[64,256]{1,0:T(8,128)S(1)} %get-tuple-element.16.mine_ref), channel_id=1, source_target_pairs={{0,4},{4,0},{1,5},{5,1},{2,6},{6,2},{3,7},{7,3},{8,12},{12,8},{9,1... | collective-permute-start | bytes 196616 | tf_op jit(solution)/shard_map/ppermute | solution.py:477
  48.1 14.8 %all-to-all-start.2 = ((f32[128,1,128]{2,1,0:T(1,128)}), f32[128,1,128]{2,1,0:T(1,128)S(1)}, u32[]{:S(2)}, u32[]{:S(2)}) async-start(f32[128,1,128]{2,1,0:T(1,128)} %bitcast.10), calls=%async_computation.2 | async-start | bytes 131072 | tf_op jit(solution)/shard_map/all_to_all | solution.py:514

commit v10 on v9

--- a/solution.py
+++ b/solution.py
@@ -36,12 +36,18 @@
     return jnp.concatenate([v[half:], -v[:half]], axis=0)
 
 
-def own_kernel(h_ref, v_ref, out_ref):
+def sent(source, target, sems, at, rows):
+    copy = pltpu.make_async_copy(source.at[:, rows], target.at[:, rows], sems.at[at])
+    copy.start()
+    return copy
+
+
+def own_kernel(h_ref, v_ref, result_ref, out_ref, sems):
     blocks, _, users = h_ref.shape
     chips = out_ref.shape[0]
     piece = users // chips
     on_diag = iota((users, users), 0) == iota((users, users), 1)
-    high, low = [], []
+    high, low, copies = [], [], []
     for block in range(blocks):
         h = jnp.transpose(h_ref[block])
         v = v_ref[block]
@@ -54,18 +60,24 @@
             g = jnp.where(on_diag, 0.0, g)
             at = (block * 2 + part) * piece
             out_ref[:, at : at + piece] = g.reshape(chips, piece, users).astype(BF16)
+            copies.append(sent(out_ref, result_ref, sems, len(copies), slice(at, at + piece)))
     extra = jnp.concatenate(high + low, axis=0).astype(BF16)
     out_ref[:, 4 * piece :] = jnp.broadcast_to(extra[None], (chips,) + extra.shape)
+    copies.append(sent(out_ref, result_ref, sems, len(copies), slice(4 * piece, 4 * piece + 8)))
+    for copy in copies:
+        copy.wait()
 
 
 def own_gains(h, v, chips):
     _, _, users = h.shape
+    shape = (chips, 4 * (users // chips) + 8, users)
     vm = pl.BlockSpec(memory_space=pltpu.VMEM)
     return pl.pallas_call(
         own_kernel,
-        out_shape=jax.ShapeDtypeStruct((chips, 4 * (users // chips) + 8, users), BF16),
+        out_shape=jax.ShapeDtypeStruct(shape, BF16),
         in_specs=[vm] * 2,
-        out_specs=vm,
+        out_specs=pl.BlockSpec(memory_space=pl.ANY),
+        scratch_shapes=[pltpu.VMEM(shape, BF16), pltpu.SemaphoreType.DMA((5,))],
         name="own_gains",
         compiler_params=pltpu.CompilerParams(vmem_limit_bytes=8 << 20),
     )(h, v)
@@ -78,13 +90,14 @@
     piece = users // chips
     first = core_ref[0] == 0
     vt, vb = vt_ref[block], vb_ref[block]
-    _, parts, points, _, _ = ha_ref.shape
-    ha = []
-    for part in range(parts):
-        for point in range(points):
-            near = ha_ref[block, part, point]
-            ha.append(jnp.where(cluster_ref[point] != 0, near, jnp.zeros_like(near)))
-    ht, ha = jnp.transpose(ht_ref[block]), jnp.transpose(jnp.concatenate(ha, axis=0))
+    points = cluster_ref.shape[0]
+    lane = iota((1, ht_ref.shape[1]), 1)
+    point = lane // (ht_ref.shape[1] // (2 * points)) % points
+    served = jnp.zeros(lane.shape, F32)
+    for p in range(points):
+        served = jnp.where(point == p, cluster_ref[p].astype(F32), served)
+    ht, ha = jnp.transpose(ht_ref[block]), jnp.transpose(ha_ref[block])
+    ha = ha * served.astype(BF16)
     for out_ref, low in ((keep_ref, first), (send_ref, jnp.logical_not(first))):
         own = jnp.where(low, vt[:, :half], vt[:, half:])
         far = jnp.where(low, vb[:, :half], vb[:, half:])
@@ -111,22 +124,29 @@
     )(core, near_cluster, ht, ha, vt, vb)
 
 
-def combine_kernel(keep0_ref, keep1_ref, came0_ref, came1_ref, out_ref):
+def combine_kernel(keep0_ref, keep1_ref, came0_ref, came1_ref, result_ref, out_ref, sems):
     chips, _, piece, width = keep0_ref.shape
     rows = 2 * piece
+    copies = []
     for block, (keep_ref, came_ref) in enumerate(((keep0_ref, came0_ref), (keep1_ref, came1_ref))):
         g = keep_ref[...] + came_ref[...]
-        out_ref[:, block * rows : (block + 1) * rows] = g.reshape(chips, rows, width)
+        at = slice(block * rows, (block + 1) * rows)
+        out_ref[:, at] = g.reshape(chips, rows, width)
+        copies.append(sent(out_ref, result_ref, sems, block, at))
+    for copy in copies:
+        copy.wait()
 
 
 def combined(keeps, cames):
     chips, _, piece, width = keeps[0].shape
+    shape = (chips, 4 * piece, width)
     vm = pl.BlockSpec(memory_space=pltpu.VMEM)
     return pl.pallas_call(
         combine_kernel,
-        out_shape=jax.ShapeDtypeStruct((chips, 4 * piece, width), BF16),
+        out_shape=jax.ShapeDtypeStruct(shape, BF16),
         in_specs=[vm] * 4,
-        out_specs=vm,
+        out_specs=pl.BlockSpec(memory_space=pl.ANY),
+        scratch_shapes=[pltpu.VMEM(shape, BF16), pltpu.SemaphoreType.DMA((2,))],
         name="combine",
         compiler_params=pltpu.CompilerParams(vmem_limit_bytes=8 << 20),
     )(*keeps, *cames)
@@ -497,10 +517,10 @@
     far = across(own, "ut", 3)
 
     where = jnp.stack([chip, core])
-    ht, vt, vb = (x.reshape(blocks, rows, users) for x in (own, start_precoder, v_far))
+    ht, ha, vt, vb = (x.reshape(blocks, rows, users) for x in (own, near, start_precoder, v_far))
     keeps, cames = [], []
     for b in range(blocks):
-        keep, send = partial_gains(b, core.reshape(1), near_cluster, ht, near, vt, vb, chips)
+        keep, send = partial_gains(b, core.reshape(1), near_cluster, ht, ha, vt, vb, chips)
         keeps.append(keep)
         cames.append(across(send, "core", 1))
     near = near * near_cluster.astype(BF16)[None, None, :, None, None]

time: 74.4 us -> 74.3 us (level)
  no operation moved by 1% of the time
where the time goes in v10:
time: 74.3 us; the launch traced here: 73.9 us
  starting transfers between devices  30.7 us (41%)
  waiting for transfers between devices  21.1 us (28%)
  Pallas kernels  17.9 us (24%)
  other arithmetic  2.05 us (3%)
  local copies, waits for them, and re-layouts  1.34 us (2%)
    ppermute x8, waiting for transfers between devices, across(): return lax.ppermute(value, axis, [(i, i ^ mask) for i in range(size)])  11.2 us
    ppermute x8, starting transfers between devices, across(): return lax.ppermute(value, axis, [(i, i ^ mask) for i in range(size)])  11.2 us
    pallas_call x1, Pallas kernels, solve(): pl.pallas_call(solve_kernel, out_shape=(jax.ShapeDtypeStruct(out_shape, B...  11.1 us
    all_to_all x1, starting transfers between devices, local(): early = lax.all_to_all(early, CHIPS, 0, 0, tiled=True)  7.62 us
    all_to_all x1, starting transfers between devices, local(): late = lax.all_to_all(late, CHIPS, 0, 0, tiled=True)  6.95 us
    all_to_all x1, waiting for transfers between devices, local(): late = lax.all_to_all(late, CHIPS, 0, 0, tiled=True)  6.6 us
    all_to_all x1, starting transfers between devices, local(): lax.all_to_all(line, EVERY, 0, 0, tiled=True)  4.95 us
    all_to_all x1, waiting for transfers between devices, local(): lax.all_to_all(line, EVERY, 0, 0, tiled=True)  3.28 us
  transfers between devices with their start and end apart: 11, of which 7 were waited for; matrix products, arithmetic and copies ran while one was open for 3% of the time, Pallas kernels for 9%

profile of v10, /device:TPU:1, one launch (start us, length us, event | category | flops | bytes accessed | tf_op | source)
XLA Modules:
  0.0 73.9 jit_solution(8907520596178326312)
XLA Ops:
  0.6 2.2 %collective-permute-start.1 = (bf16[2,2,4,64,256]{4,3,2,1,0:T(8,128)(2,1)}, bf16[2,2,4,64,256]{4,3,2,1,0:T(8,128)(2,1)S(1)}, u32[]{:S(2)}, u32[]{:S(2)}) collective-permute-start(bf16[2,2,4,64,256]{4,3,2,1,0:T(8,128)(2,1)} %param.6), channel_id=1, source_target_pairs={{0,1},{1,0},{2,3},{3,2},{4,5},{5,4},{6,7},{7,6},{8,9},{9,8},{10,11... | collective-permute-start | bytes 1572872 | tf_op jit(solution)/shard_map/ppermute | solution.py:497
  2.8 1.9 %collective-permute-start.2 = (bf16[2,2,4,64,256]{4,3,2,1,0:T(8,128)(2,1)}, bf16[2,2,4,64,256]{4,3,2,1,0:T(8,128)(2,1)S(1)}, u32[]{:S(2)}, u32[]{:S(2)}) collective-permute-start(bf16[2,2,4,64,256]{4,3,2,1,0:T(8,128)(2,1)} %param.7), channel_id=1, source_target_pairs={{0,3},{1,2},{2,1},{3,0},{4,7},{5,6},{6,5},{7,4},{8,11},{9,10},{10,... | collective-permute-start | bytes 1572872 | tf_op jit(solution)/shard_map/ppermute | solution.py:497
  4.7 0.7 bitcast_convert_fusion
  5.4 0.0 copy-start
  5.4 1.2 %broadcast_multiply_fusion.1.refs_0_ = bf16[2,2,4,64,256]{4,3,2,1,0:T(8,128)(2,1)S(1)} fusion(bf16[2,2,4,64,256]{4,3,2,1,0:T(8,128)(2,1)} %param.6, bf16[4]{0:T(256)(128)(2,1)S(1)} %bitcast_convert_fusion), kind=kLoop, calls=%fused_computation.1 | loop fusion | flops 262144 | bytes 1048584 | tf_op jit(solution)/shard_map/mul | solution.py:513
  6.6 0.0 copy-done
  6.6 1.3 %own_gains.1 = bf16[16,72,256]{2,1,0:T(8,128)(2,1)} custom-call(bf16[2,512,256]{2,1,0:T(8,128)(2,1)S(1)} %bitcast.15, bf16[2,512,256]{2,1,0:T(8,128)(2,1)S(1)} %bitcast.18), custom_call_target="tpu_custom_call" | custom-call | tf_op jit(solution)/shard_map/own_gains/pallas_call | solution.py:75
  7.9 7.6 %all-to-all-start = ((bf16[16,72,256]{2,1,0:T(8,128)(2,1)}), bf16[16,72,256]{2,1,0:T(8,128)(2,1)S(1)}, u32[]{:S(2)}, u32[]{:S(2)}) async-start(bf16[16,72,256]{2,1,0:T(8,128)(2,1)} %own_gains.1), calls=%async_computation | async-start | bytes 1179648 | tf_op jit(solution)/shard_map/all_to_all | solution.py:515
  15.5 0.0 copy-start.4
  15.5 0.6 copy-done.4
  16.2 0.4 collective-permute-start
  16.6 2.0 %collective-permute-done.cluster_ref = s32[4]{0:T(128)S(1)} collective-permute-done((s32[4]{0:T(128)S(1)}, s32[4]{0:T(128)S(1)}, u32[]{:S(2)}, u32[]{:S(2)}) %collective-permute-start) | collective-permute-done | bytes 48 | tf_op jit(solution)/shard_map/ppermute | solution.py:497
  18.6 0.0 collective-permute-done.1
  18.6 0.0 collective-permute-done.2
  18.6 1.2 %gains.2 = (bf16[16,2,16,384]{3,2,1,0:T(8,128)(2,1)S(1)}, bf16[16,2,16,384]{3,2,1,0:T(8,128)(2,1)S(1)}) custom-call(s32[1]{0:T(128)} %bitcast.2.core_ref, s32[4]{0:T(128)S(1)} %collective-permute-done.cluster_ref, bf16[2,512,256]{2,1,0:T(8,128)(2,1)S(1)} %bitcast.16, bf16[2,512,256]{2,1,0:T(8,128)(2,1)S(1)} %bitcast.21, bf16[2,512,256]{2,1,0:T(8,128)(2,1)S(1)} %bitcast.19, ...), custom_call_target="tpu_custom_call" | custom-call | flops 402653184 | bytes 4194304 | tf_op jit(solution)/shard_map/gains/pallas_call | solution.py:116
  19.8 2.7 %collective-permute-start.3 = (bf16[16,2,16,384]{3,2,1,0:T(8,128)(2,1)S(1)}, bf16[16,2,16,384]{3,2,1,0:T(8,128)(2,1)S(1)}, u32[]{:S(2)}, u32[]{:S(2)}) collective-permute-start(bf16[16,2,16,384]{3,2,1,0:T(8,128)(2,1)S(1)} %get-tuple-element.14), channel_id=1, source_target_pairs={{0,4},{4,0},{1,5},{5,1},{2,6},{6,2},{3,7},{7,3},{8,12},{12,8},{9,1... | collective-permute-start | bytes 1179656 | tf_op jit(solution)/shard_map/ppermute | solution.py:497
  22.5 1.2 %gains.3 = (bf16[16,2,16,384]{3,2,1,0:T(8,128)(2,1)S(1)}, bf16[16,2,16,384]{3,2,1,0:T(8,128)(2,1)S(1)}) custom-call(s32[1]{0:T(128)} %bitcast.2.core_ref, s32[4]{0:T(128)S(1)} %collective-permute-done.cluster_ref, bf16[2,512,256]{2,1,0:T(8,128)(2,1)S(1)} %bitcast.17, bf16[2,512,256]{2,1,0:T(8,128)(2,1)S(1)} %bitcast.22, bf16[2,512,256]{2,1,0:T(8,128)(2,1)S(1)} %bitcast.20, ...), custom_call_target="tpu_custom_call" | custom-call | flops 402653184 | bytes 4194304 | tf_op jit(solution)/shard_map/gains/pallas_call | solution.py:116
  23.7 0.1 collective-permute-start.4
  23.8 0.1 collective-permute-done.3.came0_ref
  23.9 1.6 %collective-permute-done.4.came1_ref = bf16[16,2,16,384]{3,2,1,0:T(8,128)(2,1)S(1)} collective-permute-done((bf16[16,2,16,384]{3,2,1,0:T(8,128)(2,1)S(1)}, bf16[16,2,16,384]{3,2,1,0:T(8,128)(2,1)S(1)}, u32[]{:S(2)}, u32[]{:S(2)}) %collective-permute-start.4) | collective-permute-done | bytes 393248 | tf_op jit(solution)/shard_map/ppermute | solution.py:497
  25.5 1.0 %combine.1 = bf16[16,64,384]{2,1,0:T(8,128)(2,1)} custom-call(bf16[16,2,16,384]{3,2,1,0:T(8,128)(2,1)S(1)} %get-tuple-element.12.keep0_ref, bf16[16,2,16,384]{3,2,1,0:T(8,128)(2,1)S(1)} %get-tuple-element.13.keep1_ref, bf16[16,2,16,384]{3,2,1,0:T(8,128)(2,1)S(1)} %collective-permute-done.3.came0_ref, ...), custom_call_target="tpu_custom_call" | custom-call | tf_op jit(solution)/shard_map/combine/pallas_call | solution.py:144
  26.4 0.0 all-to-all-done.g_ref
  26.5 6.9 %all-to-all-start.1 = ((bf16[16,64,384]{2,1,0:T(8,128)(2,1)}), bf16[16,64,384]{2,1,0:T(8,128)(2,1)S(1)}, u32[]{:S(2)}, u32[]{:S(2)}) async-start(bf16[16,64,384]{2,1,0:T(8,128)(2,1)} %combine.1), calls=%async_computation.1 | async-start | bytes 1572864 | tf_op jit(solution)/shard_map/all_to_all | solution.py:529
  33.4 0.9 %collective-permute-start.6 = (bf16[2,2,4,64,256]{4,3,2,1,0:T(8,128)(2,1)S(1)}, bf16[2,2,4,64,256]{4,3,2,1,0:T(8,128)(2,1)S(1)}, u32[]{:S(2)}, u32[]{:S(2)}) collective-permute-start(bf16[2,2,4,64,256]{4,3,2,1,0:T(8,128)(2,1)S(1)} %broadcast_multiply_fusion.1.refs_0_), channel_id=1, source_target_pairs={{0,3},{1,2},{2,1},{3,0},{4,7},{5,6},{6,5},{7,4},{8,11},{9,10},{10,... | collective-permute-start | bytes 1572872 | tf_op jit(solution)/shard_map/ppermute | solution.py:497
  34.3 0.1 broadcast_multiply_fusion.refs_1_
  34.4 2.0 %collective-permute-start.7 = (bf16[2,2,4,64,256]{4,3,2,1,0:T(8,128)(2,1)S(1)}, bf16[2,2,4,64,256]{4,3,2,1,0:T(8,128)(2,1)S(1)}, u32[]{:S(2)}, u32[]{:S(2)}) collective-permute-start(bf16[2,2,4,64,256]{4,3,2,1,0:T(8,128)(2,1)S(1)} %broadcast_multiply_fusion.refs_1_), channel_id=1, source_target_pairs={{0,3},{1,2},{2,1},{3,0},{4,7},{5,6},{6,5},{7,4},{8,11},{9,10},{10,... | collective-permute-start | bytes 1572872 | tf_op jit(solution)/shard_map/ppermute | solution.py:497
  36.4 0.1 pad_add_fusion.where_ref
  36.4 0.0 copy-start.1
  36.4 0.0 copy-start.2
  36.4 0.0 copy-start.3
  36.4 0.7 copy-done.1
  37.1 0.0 copy-done.2
  37.1 0.0 copy-done.3
  37.1 0.8 %own_sum.1 = (f32[64,256]{1,0:T(8,128)S(1)}, f32[1,128]{1,0:T(1,128)S(1)}, f32[1,4]{1,0:T(1,128)S(1)}, f32[1,4]{1,0:T(1,128)S(1)}) custom-call(s32[2]{0:T(128)S(1)} %pad_add_fusion.where_ref, bf16[16,72,256]{2,1,0:T(8,128)(2,1)S(1)} %all-to-all-done.g_ref, f32[2,256]{1,0:T(2,128)S(1)} %copy-done.1, f32[1,4]{1,0:T(1,128)S(1)} %bitcast.26, f32[1,4]{1,0:T(1,128)S(1)} %bitcast.27), custom_call_target="tpu_custom_call" | custom-call | tf_op jit(solution)/shard_map/own_sum/pallas_call | solution.py:190
  37.9 1.1 %collective-permute-start.5 = (f32[64,256]{1,0:T(8,128)S(1)}, f32[64,256]{1,0:T(8,128)S(1)}, u32[]{:S(2)}, u32[]{:S(2)}) collective-permute-start(f32[64,256]{1,0:T(8,128)S(1)} %get-tuple-element.16.mine_ref), channel_id=1, source_target_pairs={{0,4},{4,0},{1,5},{5,1},{2,6},{6,2},{3,7},{7,3},{8,12},{12,8},{9,1... | collective-permute-start | bytes 196616 | tf_op jit(solution)/shard_map/ppermute | solution.py:497
  39.0 0.9 %collective-permute-done.5.came_ref = f32[64,256]{1,0:T(8,128)S(1)} collective-permute-done((f32[64,256]{1,0:T(8,128)S(1)}, f32[64,256]{1,0:T(8,128)S(1)}, u32[]{:S(2)}, u32[]{:S(2)}) %collective-permute-start.5) | collective-permute-done | bytes 65568 | tf_op jit(solution)/shard_map/ppermute | solution.py:497
  39.9 0.6 own_total.1.line_ref
  40.5 6.6 %all-to-all-done.1.g_ref = bf16[16,64,384]{2,1,0:T(8,128)(2,1)S(1)} async-done(((bf16[16,64,384]{2,1,0:T(8,128)(2,1)}), bf16[16,64,384]{2,1,0:T(8,128)(2,1)S(1)}, u32[]{:S(2)}, u32[]{:S(2)}) %all-to-all-start.1) | async-done | bytes 786464 | tf_op jit(solution)/shard_map/all_to_all | solution.py:529
  47.1 0.8 %totals.1 = f32[128,128]{1,0:T(8,128)} custom-call(bf16[16,64,384]{2,1,0:T(8,128)(2,1)S(1)} %all-to-all-done.1.g_ref, f32[1,128]{1,0:T(1,128)S(1)} %own_total.1.line_ref), custom_call_target="tpu_custom_call" | custom-call | tf_op jit(solution)/shard_map/totals/pallas_call | solution.py:255
  48.0 4.9 %all-to-all-start.2 = ((f32[128,1,128]{2,1,0:T(1,128)}), f32[128,1,128]{2,1,0:T(1,128)S(1)}, u32[]{:S(2)}, u32[]{:S(2)}) async-start(f32[128,1,128]{2,1,0:T(1,128)} %bitcast.11), calls=%async_computation.2 | async-start | bytes 131072 | tf_op jit(solution)/shard_map/all_to_all | solution.py:534
  52.9 0.0 collective-permute-done.6.refs_2_
  53.0 6.6 %collective-permute-done.7.refs_3_ = bf16[2,2,4,64,256]{4,3,2,1,0:T(8,128)(2,1)S(1)} collective-permute-done((bf16[2,2,4,64,256]{4,3,2,1,0:T(8,128)(2,1)S(1)}, bf16[2,2,4,64,256]{4,3,2,1,0:T(8,128)(2,1)S(1)}, u32[]{:S(2)}, u32[]{:S(2)}) %collective-permute-start.7) | collective-permute-done | bytes 524320 | tf_op jit(solution)/shard_map/ppermute | solution.py:497
  59.5 3.3 %all-to-all-done.2 = f32[128,1,128]{2,1,0:T(1,128)S(1)} async-done(((f32[128,1,128]{2,1,0:T(1,128)}), f32[128,1,128]{2,1,0:T(1,128)S(1)}, u32[]{:S(2)}, u32[]{:S(2)}) %all-to-all-start.2) | async-done | bytes 65568 | tf_op jit(solution)/shard_map/all_to_all | solution.py:534
  62.8 11.1 %solve.1 = (bf16[2,2,4,64,256]{4,3,2,1,0:T(8,128)(2,1)}, f32[2,256]{1,0:T(2,128)}) custom-call(s32[1]{0:T(128)} %bitcast.tile_ref, f32[1,4]{1,0:T(1,128)S(1)} %get-tuple-element.10.penalty_ref, f32[1,4]{1,0:T(1,128)S(1)} %get-tuple-element.11.power_ref, f32[16,8,128]{2,1,0:T(8,128)S(1)} %bitcast.25, ...), custom_call_target="tpu_custom_call" | custom-call | tf_op jit(solution)/shard_map/solve/pallas_call | solution.py:472
  (1 shorter events, 0.0 us)
Async XLA Ops:
  0.6 18.0 %collective-permute-start.1 = (bf16[2,2,4,64,256]{4,3,2,1,0:T(8,128)(2,1)}, bf16[2,2,4,64,256]{4,3,2,1,0:T(8,128)(2,1)S(1)}, u32[]{:S(2)}, u32[]{:S(2)}) collective-permute-start(bf16[2,2,4,64,256]{4,3,2,1,0:T(8,128)(2,1)} %param.6), channel_id=1, source_target_pairs={{0,1},{1,0},{2,3},{3,2},{4,5},{5,4},{6,7},{7,6},{8,9},{9,8},{10,11... | collective-permute-start | bytes 1572872 | tf_op jit(solution)/shard_map/ppermute | solution.py:497
  2.8 15.8 %collective-permute-start.2 = (bf16[2,2,4,64,256]{4,3,2,1,0:T(8,128)(2,1)}, bf16[2,2,4,64,256]{4,3,2,1,0:T(8,128)(2,1)S(1)}, u32[]{:S(2)}, u32[]{:S(2)}) collective-permute-start(bf16[2,2,4,64,256]{4,3,2,1,0:T(8,128)(2,1)} %param.7), channel_id=1, source_target_pairs={{0,3},{1,2},{2,1},{3,0},{4,7},{5,6},{6,5},{7,4},{8,11},{9,10},{10,... | collective-permute-start | bytes 1572872 | tf_op jit(solution)/shard_map/ppermute | solution.py:497
  5.4 1.2 %copy-start = (bf16[2,2,4,64,256]{4,3,2,1,0:T(8,128)(2,1)S(1)}, bf16[2,2,4,64,256]{4,3,2,1,0:T(8,128)(2,1)}, u32[]{:S(2)}) copy-start(bf16[2,2,4,64,256]{4,3,2,1,0:T(8,128)(2,1)} %param.7) | copy-start | bytes 1572868
  7.9 18.6 %all-to-all-start = ((bf16[16,72,256]{2,1,0:T(8,128)(2,1)}), bf16[16,72,256]{2,1,0:T(8,128)(2,1)S(1)}, u32[]{:S(2)}, u32[]{:S(2)}) async-start(bf16[16,72,256]{2,1,0:T(8,128)(2,1)} %own_gains.1), calls=%async_computation | async-start | bytes 1179648 | tf_op jit(solution)/shard_map/all_to_all | solution.py:515
  15.5 0.7 copy-start.4
  16.2 2.4 %collective-permute-start = (s32[4]{0:T(128)S(1)}, s32[4]{0:T(128)S(1)}, u32[]{:S(2)}, u32[]{:S(2)}) collective-permute-start(s32[4]{0:T(128)S(1)} %bitcast.28), channel_id=1, source_target_pairs={{0,1},{1,0},{2,3},{3,2},{4,5},{5,4},{6,7},{7,6},{8,9},{9,8},{10,11... | collective-permute-start | bytes 56 | tf_op jit(solution)/shard_map/ppermute | solution.py:497
  19.8 4.1 %collective-permute-start.3 = (bf16[16,2,16,384]{3,2,1,0:T(8,128)(2,1)S(1)}, bf16[16,2,16,384]{3,2,1,0:T(8,128)(2,1)S(1)}, u32[]{:S(2)}, u32[]{:S(2)}) collective-permute-start(bf16[16,2,16,384]{3,2,1,0:T(8,128)(2,1)S(1)} %get-tuple-element.14), channel_id=1, source_target_pairs={{0,4},{4,0},{1,5},{5,1},{2,6},{6,2},{3,7},{7,3},{8,12},{12,8},{9,1... | collective-permute-start | bytes 1179656 | tf_op jit(solution)/shard_map/ppermute | solution.py:497
  23.7 1.8 %collective-permute-start.4 = (bf16[16,2,16,384]{3,2,1,0:T(8,128)(2,1)S(1)}, bf16[16,2,16,384]{3,2,1,0:T(8,128)(2,1)S(1)}, u32[]{:S(2)}, u32[]{:S(2)}) collective-permute-start(bf16[16,2,16,384]{3,2,1,0:T(8,128)(2,1)S(1)} %get-tuple-element.15), channel_id=1, source_target_pairs={{0,4},{4,0},{1,5},{5,1},{2,6},{6,2},{3,7},{7,3},{8,12},{12,8},{9,1... | collective-permute-start | bytes 1179656 | tf_op jit(solution)/shard_map/ppermute | solution.py:497
  26.5 20.7 %all-to-all-start.1 = ((bf16[16,64,384]{2,1,0:T(8,128)(2,1)}), bf16[16,64,384]{2,1,0:T(8,128)(2,1)S(1)}, u32[]{:S(2)}, u32[]{:S(2)}) async-start(bf16[16,64,384]{2,1,0:T(8,128)(2,1)} %combine.1), calls=%async_computation.1 | async-start | bytes 1572864 | tf_op jit(solution)/shard_map/all_to_all | solution.py:529
  33.4 19.5 %collective-permute-start.6 = (bf16[2,2,4,64,256]{4,3,2,1,0:T(8,128)(2,1)S(1)}, bf16[2,2,4,64,256]{4,3,2,1,0:T(8,128)(2,1)S(1)}, u32[]{:S(2)}, u32[]{:S(2)}) collective-permute-start(bf16[2,2,4,64,256]{4,3,2,1,0:T(8,128)(2,1)S(1)} %broadcast_multiply_fusion.1.refs_0_), channel_id=1, source_target_pairs={{0,3},{1,2},{2,1},{3,0},{4,7},{5,6},{6,5},{7,4},{8,11},{9,10},{10,... | collective-permute-start | bytes 1572872 | tf_op jit(solution)/shard_map/ppermute | solution.py:497
  34.4 25.1 %collective-permute-start.7 = (bf16[2,2,4,64,256]{4,3,2,1,0:T(8,128)(2,1)S(1)}, bf16[2,2,4,64,256]{4,3,2,1,0:T(8,128)(2,1)S(1)}, u32[]{:S(2)}, u32[]{:S(2)}) collective-permute-start(bf16[2,2,4,64,256]{4,3,2,1,0:T(8,128)(2,1)S(1)} %broadcast_multiply_fusion.refs_1_), channel_id=1, source_target_pairs={{0,3},{1,2},{2,1},{3,0},{4,7},{5,6},{6,5},{7,4},{8,11},{9,10},{10,... | collective-permute-start | bytes 1572872 | tf_op jit(solution)/shard_map/ppermute | solution.py:497
  36.4 0.7 copy-start.1
  36.4 0.7 copy-start.2
  36.4 0.7 copy-start.3
  37.9 2.0 %collective-permute-start.5 = (f32[64,256]{1,0:T(8,128)S(1)}, f32[64,256]{1,0:T(8,128)S(1)}, u32[]{:S(2)}, u32[]{:S(2)}) collective-permute-start(f32[64,256]{1,0:T(8,128)S(1)} %get-tuple-element.16.mine_ref), channel_id=1, source_target_pairs={{0,4},{4,0},{1,5},{5,1},{2,6},{6,2},{3,7},{7,3},{8,12},{12,8},{9,1... | collective-permute-start | bytes 196616 | tf_op jit(solution)/shard_map/ppermute | solution.py:497
  48.0 14.8 %all-to-all-start.2 = ((f32[128,1,128]{2,1,0:T(1,128)}), f32[128,1,128]{2,1,0:T(1,128)S(1)}, u32[]{:S(2)}, u32[]{:S(2)}) async-start(f32[128,1,128]{2,1,0:T(1,128)} %bitcast.11), calls=%async_computation.2 | async-start | bytes 131072 | tf_op jit(solution)/shard_map/all_to_all | solution.py:534

commit v11 on v10

--- a/solution.py
+++ b/solution.py
@@ -90,12 +90,12 @@
     piece = users // chips
     first = core_ref[0] == 0
     vt, vb = vt_ref[block], vb_ref[block]
-    points = cluster_ref.shape[0]
+    points = cluster_ref.shape[1]
     lane = iota((1, ht_ref.shape[1]), 1)
     point = lane // (ht_ref.shape[1] // (2 * points)) % points
     served = jnp.zeros(lane.shape, F32)
     for p in range(points):
-        served = jnp.where(point == p, cluster_ref[p].astype(F32), served)
+        served = jnp.where(point == p, cluster_ref[:, p : p + 1].astype(F32), served)
     ht, ha = jnp.transpose(ht_ref[block]), jnp.transpose(ha_ref[block])
     ha = ha * served.astype(BF16)
     for out_ref, low in ((keep_ref, first), (send_ref, jnp.logical_not(first))):
@@ -116,12 +116,12 @@
     return pl.pallas_call(
         functools.partial(gain_kernel, block),
         out_shape=(jax.ShapeDtypeStruct(shape, BF16), jax.ShapeDtypeStruct(shape, BF16)),
-        in_specs=[pl.BlockSpec(memory_space=pltpu.SMEM)] * 2 + [vm] * 4,
+        in_specs=[pl.BlockSpec(memory_space=pltpu.SMEM)] + [vm] * 5,
         out_specs=(vm, vm),
         name="gains",
         compiler_params=pltpu.CompilerParams(vmem_limit_bytes=8 << 20),
         cost_estimate=pl.CostEstimate(flops=12 * users * users * rows, bytes_accessed=4 << 20, transcendentals=0),
-    )(core, near_cluster, ht, ha, vt, vb)
+    )(core, near_cluster.reshape(1, -1), ht, ha, vt, vb)
 
 
 def combine_kernel(keep0_ref, keep1_ref, came0_ref, came1_ref, result_ref, out_ref, sems):

time: 74.3 us -> 73.3 us (0.987)
  Pallas kernels: 17.9 us -> 16.9 us
  starting transfers between devices: 30.7 us -> 29.7 us
  waiting for transfers between devices: 21.1 us -> 22.1 us
    pallas_call x2, Pallas kernels: 2.31 us -> 1.26 us  [partial_gains(): pl.pallas_call(functools.partial(gain_kernel, block), out_shape=(jax.Shap...]
    all_to_all x1, waiting for transfers between devices: 0.01 us -> 0.99 us  [local(): early = lax.all_to_all(early, CHIPS, 0, 0, tiled=True)]
    all_to_all x1, starting transfers between devices: 6.95 us -> 5.97 us  [local(): late = lax.all_to_all(late, CHIPS, 0, 0, tiled=True)]
  transfers between devices with their start and end apart: 11 -> 11, of which waited for: 7 -> 8; matrix products, arithmetic and copies ran while one was open for 3% -> 3% of each run, Pallas kernels for 9% -> 8%
where the time goes in v11:
time: 73.3 us; the launch traced here: 72.9 us
  starting transfers between devices  29.7 us (41%)
  waiting for transfers between devices  22.1 us (30%)
  Pallas kernels  16.9 us (23%)
  other arithmetic  2.05 us (3%)
  local copies, waits for them, and re-layouts  1.34 us (2%)
    ppermute x8, starting transfers between devices, across(): return lax.ppermute(value, axis, [(i, i ^ mask) for i in range(size)])  11.2 us
    ppermute x8, waiting for transfers between devices, across(): return lax.ppermute(value, axis, [(i, i ^ mask) for i in range(size)])  11.2 us
    pallas_call x1, Pallas kernels, solve(): pl.pallas_call(solve_kernel, out_shape=(jax.ShapeDtypeStruct(out_shape, B...  11.1 us
    all_to_all x1, starting transfers between devices, local(): early = lax.all_to_all(early, CHIPS, 0, 0, tiled=True)  7.62 us
    all_to_all x1, waiting for transfers between devices, local(): late = lax.all_to_all(late, CHIPS, 0, 0, tiled=True)  6.6 us
    all_to_all x1, starting transfers between devices, local(): late = lax.all_to_all(late, CHIPS, 0, 0, tiled=True)  5.97 us
    all_to_all x1, starting transfers between devices, local(): lax.all_to_all(line, EVERY, 0, 0, tiled=True)  4.95 us
    all_to_all x1, waiting for transfers between devices, local(): lax.all_to_all(line, EVERY, 0, 0, tiled=True)  3.28 us
  transfers between devices with their start and end apart: 11, of which 8 were waited for; matrix products, arithmetic and copies ran while one was open for 3% of the time, Pallas kernels for 8%

profile of v11, /device:TPU:1, one launch (start us, length us, event | category | flops | bytes accessed | tf_op | source)
XLA Modules:
  0.0 72.9 jit_solution(17085536696607703224)
XLA Ops:
  0.6 2.2 %collective-permute-start.1 = (bf16[2,2,4,64,256]{4,3,2,1,0:T(8,128)(2,1)}, bf16[2,2,4,64,256]{4,3,2,1,0:T(8,128)(2,1)S(1)}, u32[]{:S(2)}, u32[]{:S(2)}) collective-permute-start(bf16[2,2,4,64,256]{4,3,2,1,0:T(8,128)(2,1)} %param.6), channel_id=1, source_target_pairs={{0,1},{1,0},{2,3},{3,2},{4,5},{5,4},{6,7},{7,6},{8,9},{9,8},{10,11... | collective-permute-start | bytes 1572872 | tf_op jit(solution)/shard_map/ppermute | solution.py:497
  2.8 1.9 %collective-permute-start.2 = (bf16[2,2,4,64,256]{4,3,2,1,0:T(8,128)(2,1)}, bf16[2,2,4,64,256]{4,3,2,1,0:T(8,128)(2,1)S(1)}, u32[]{:S(2)}, u32[]{:S(2)}) collective-permute-start(bf16[2,2,4,64,256]{4,3,2,1,0:T(8,128)(2,1)} %param.7), channel_id=1, source_target_pairs={{0,3},{1,2},{2,1},{3,0},{4,7},{5,6},{6,5},{7,4},{8,11},{9,10},{10,... | collective-permute-start | bytes 1572872 | tf_op jit(solution)/shard_map/ppermute | solution.py:497
  4.7 0.7 bitcast_convert_fusion
  5.4 0.0 copy-start
  5.4 1.2 %broadcast_multiply_fusion.1.refs_0_ = bf16[2,2,4,64,256]{4,3,2,1,0:T(8,128)(2,1)S(1)} fusion(bf16[2,2,4,64,256]{4,3,2,1,0:T(8,128)(2,1)} %param.6, bf16[4]{0:T(256)(128)(2,1)S(1)} %bitcast_convert_fusion), kind=kLoop, calls=%fused_computation.1 | loop fusion | flops 262144 | bytes 1048584 | tf_op jit(solution)/shard_map/mul | solution.py:513
  6.6 0.0 copy-done
  6.6 1.3 %own_gains.1 = bf16[16,72,256]{2,1,0:T(8,128)(2,1)} custom-call(bf16[2,512,256]{2,1,0:T(8,128)(2,1)S(1)} %bitcast.16, bf16[2,512,256]{2,1,0:T(8,128)(2,1)S(1)} %bitcast.19), custom_call_target="tpu_custom_call" | custom-call | tf_op jit(solution)/shard_map/own_gains/pallas_call | solution.py:75
  7.9 7.6 %all-to-all-start = ((bf16[16,72,256]{2,1,0:T(8,128)(2,1)}), bf16[16,72,256]{2,1,0:T(8,128)(2,1)S(1)}, u32[]{:S(2)}, u32[]{:S(2)}) async-start(bf16[16,72,256]{2,1,0:T(8,128)(2,1)} %own_gains.1), calls=%async_computation | async-start | bytes 1179648 | tf_op jit(solution)/shard_map/all_to_all | solution.py:515
  15.5 0.0 copy-start.4
  15.5 0.6 copy-done.4
  16.2 0.4 collective-permute-start
  16.6 2.0 %collective-permute-done = s32[4]{0:T(128)S(1)} collective-permute-done((s32[4]{0:T(128)S(1)}, s32[4]{0:T(128)S(1)}, u32[]{:S(2)}, u32[]{:S(2)}) %collective-permute-start) | collective-permute-done | bytes 48 | tf_op jit(solution)/shard_map/ppermute | solution.py:497
  18.6 0.0 collective-permute-done.1
  18.6 0.0 collective-permute-done.2
  18.6 0.6 gains.2
  19.2 2.7 %collective-permute-start.3 = (bf16[16,2,16,384]{3,2,1,0:T(8,128)(2,1)S(1)}, bf16[16,2,16,384]{3,2,1,0:T(8,128)(2,1)S(1)}, u32[]{:S(2)}, u32[]{:S(2)}) collective-permute-start(bf16[16,2,16,384]{3,2,1,0:T(8,128)(2,1)S(1)} %get-tuple-element.14), channel_id=1, source_target_pairs={{0,4},{4,0},{1,5},{5,1},{2,6},{6,2},{3,7},{7,3},{8,12},{12,8},{9,1... | collective-permute-start | bytes 1179656 | tf_op jit(solution)/shard_map/ppermute | solution.py:497
  22.0 0.6 gains.3
  22.6 0.1 collective-permute-start.4
  22.7 0.6 collective-permute-done.3.came0_ref
  23.3 1.1 %collective-permute-done.4.came1_ref = bf16[16,2,16,384]{3,2,1,0:T(8,128)(2,1)S(1)} collective-permute-done((bf16[16,2,16,384]{3,2,1,0:T(8,128)(2,1)S(1)}, bf16[16,2,16,384]{3,2,1,0:T(8,128)(2,1)S(1)}, u32[]{:S(2)}, u32[]{:S(2)}) %collective-permute-start.4) | collective-permute-done | bytes 393248 | tf_op jit(solution)/shard_map/ppermute | solution.py:497
  24.4 1.0 %combine.1 = bf16[16,64,384]{2,1,0:T(8,128)(2,1)} custom-call(bf16[16,2,16,384]{3,2,1,0:T(8,128)(2,1)S(1)} %get-tuple-element.12.keep0_ref, bf16[16,2,16,384]{3,2,1,0:T(8,128)(2,1)S(1)} %get-tuple-element.13.keep1_ref, bf16[16,2,16,384]{3,2,1,0:T(8,128)(2,1)S(1)} %collective-permute-done.3.came0_ref, ...), custom_call_target="tpu_custom_call" | custom-call | tf_op jit(solution)/shard_map/combine/pallas_call | solution.py:144
  25.4 1.0 %all-to-all-done.g_ref = bf16[16,72,256]{2,1,0:T(8,128)(2,1)S(1)} async-done(((bf16[16,72,256]{2,1,0:T(8,128)(2,1)}), bf16[16,72,256]{2,1,0:T(8,128)(2,1)S(1)}, u32[]{:S(2)}, u32[]{:S(2)}) %all-to-all-start) | async-done | bytes 589856 | tf_op jit(solution)/shard_map/all_to_all | solution.py:515
  26.4 6.0 %all-to-all-start.1 = ((bf16[16,64,384]{2,1,0:T(8,128)(2,1)}), bf16[16,64,384]{2,1,0:T(8,128)(2,1)S(1)}, u32[]{:S(2)}, u32[]{:S(2)}) async-start(bf16[16,64,384]{2,1,0:T(8,128)(2,1)} %combine.1), calls=%async_computation.1 | async-start | bytes 1572864 | tf_op jit(solution)/shard_map/all_to_all | solution.py:529
  32.4 0.9 %collective-permute-start.6 = (bf16[2,2,4,64,256]{4,3,2,1,0:T(8,128)(2,1)S(1)}, bf16[2,2,4,64,256]{4,3,2,1,0:T(8,128)(2,1)S(1)}, u32[]{:S(2)}, u32[]{:S(2)}) collective-permute-start(bf16[2,2,4,64,256]{4,3,2,1,0:T(8,128)(2,1)S(1)} %broadcast_multiply_fusion.1.refs_0_), channel_id=1, source_target_pairs={{0,3},{1,2},{2,1},{3,0},{4,7},{5,6},{6,5},{7,4},{8,11},{9,10},{10,... | collective-permute-start | bytes 1572872 | tf_op jit(solution)/shard_map/ppermute | solution.py:497
  33.2 0.1 broadcast_multiply_fusion.refs_1_
  33.3 2.0 %collective-permute-start.7 = (bf16[2,2,4,64,256]{4,3,2,1,0:T(8,128)(2,1)S(1)}, bf16[2,2,4,64,256]{4,3,2,1,0:T(8,128)(2,1)S(1)}, u32[]{:S(2)}, u32[]{:S(2)}) collective-permute-start(bf16[2,2,4,64,256]{4,3,2,1,0:T(8,128)(2,1)S(1)} %broadcast_multiply_fusion.refs_1_), channel_id=1, source_target_pairs={{0,3},{1,2},{2,1},{3,0},{4,7},{5,6},{6,5},{7,4},{8,11},{9,10},{10,... | collective-permute-start | bytes 1572872 | tf_op jit(solution)/shard_map/ppermute | solution.py:497
  35.3 0.1 pad_add_fusion.where_ref
  35.4 0.0 copy-start.1
  35.4 0.0 copy-start.2
  35.4 0.0 copy-start.3
  35.4 0.7 copy-done.1
  36.1 0.0 copy-done.2
  36.1 0.0 copy-done.3
  36.1 0.8 %own_sum.1 = (f32[64,256]{1,0:T(8,128)S(1)}, f32[1,128]{1,0:T(1,128)S(1)}, f32[1,4]{1,0:T(1,128)S(1)}, f32[1,4]{1,0:T(1,128)S(1)}) custom-call(s32[2]{0:T(128)S(1)} %pad_add_fusion.where_ref, bf16[16,72,256]{2,1,0:T(8,128)(2,1)S(1)} %all-to-all-done.g_ref, f32[2,256]{1,0:T(2,128)S(1)} %copy-done.1, f32[1,4]{1,0:T(1,128)S(1)} %bitcast.29, f32[1,4]{1,0:T(1,128)S(1)} %bitcast.30), custom_call_target="tpu_custom_call" | custom-call | tf_op jit(solution)/shard_map/own_sum/pallas_call | solution.py:190
  36.9 1.1 %collective-permute-start.5 = (f32[64,256]{1,0:T(8,128)S(1)}, f32[64,256]{1,0:T(8,128)S(1)}, u32[]{:S(2)}, u32[]{:S(2)}) collective-permute-start(f32[64,256]{1,0:T(8,128)S(1)} %get-tuple-element.16.mine_ref), channel_id=1, source_target_pairs={{0,4},{4,0},{1,5},{5,1},{2,6},{6,2},{3,7},{7,3},{8,12},{12,8},{9,1... | collective-permute-start | bytes 196616 | tf_op jit(solution)/shard_map/ppermute | solution.py:497
  38.0 0.9 %collective-permute-done.5.came_ref = f32[64,256]{1,0:T(8,128)S(1)} collective-permute-done((f32[64,256]{1,0:T(8,128)S(1)}, f32[64,256]{1,0:T(8,128)S(1)}, u32[]{:S(2)}, u32[]{:S(2)}) %collective-permute-start.5) | collective-permute-done | bytes 65568 | tf_op jit(solution)/shard_map/ppermute | solution.py:497
  38.9 0.6 own_total.1.line_ref
  39.5 6.6 %all-to-all-done.1.g_ref = bf16[16,64,384]{2,1,0:T(8,128)(2,1)S(1)} async-done(((bf16[16,64,384]{2,1,0:T(8,128)(2,1)}), bf16[16,64,384]{2,1,0:T(8,128)(2,1)S(1)}, u32[]{:S(2)}, u32[]{:S(2)}) %all-to-all-start.1) | async-done | bytes 786464 | tf_op jit(solution)/shard_map/all_to_all | solution.py:529
  46.1 0.8 %totals.1 = f32[128,128]{1,0:T(8,128)} custom-call(bf16[16,64,384]{2,1,0:T(8,128)(2,1)S(1)} %all-to-all-done.1.g_ref, f32[1,128]{1,0:T(1,128)S(1)} %own_total.1.line_ref), custom_call_target="tpu_custom_call" | custom-call | tf_op jit(solution)/shard_map/totals/pallas_call | solution.py:255
  46.9 4.9 %all-to-all-start.2 = ((f32[128,1,128]{2,1,0:T(1,128)}), f32[128,1,128]{2,1,0:T(1,128)S(1)}, u32[]{:S(2)}, u32[]{:S(2)}) async-start(f32[128,1,128]{2,1,0:T(1,128)} %bitcast.12), calls=%async_computation.2 | async-start | bytes 131072 | tf_op jit(solution)/shard_map/all_to_all | solution.py:534
  51.9 0.0 collective-permute-done.6.refs_2_
  51.9 6.6 %collective-permute-done.7.refs_3_ = bf16[2,2,4,64,256]{4,3,2,1,0:T(8,128)(2,1)S(1)} collective-permute-done((bf16[2,2,4,64,256]{4,3,2,1,0:T(8,128)(2,1)S(1)}, bf16[2,2,4,64,256]{4,3,2,1,0:T(8,128)(2,1)S(1)}, u32[]{:S(2)}, u32[]{:S(2)}) %collective-permute-start.7) | collective-permute-done | bytes 524320 | tf_op jit(solution)/shard_map/ppermute | solution.py:497
  58.5 3.3 %all-to-all-done.2 = f32[128,1,128]{2,1,0:T(1,128)S(1)} async-done(((f32[128,1,128]{2,1,0:T(1,128)}), f32[128,1,128]{2,1,0:T(1,128)S(1)}, u32[]{:S(2)}, u32[]{:S(2)}) %all-to-all-start.2) | async-done | bytes 65568 | tf_op jit(solution)/shard_map/all_to_all | solution.py:534
  61.7 11.1 %solve.1 = (bf16[2,2,4,64,256]{4,3,2,1,0:T(8,128)(2,1)}, f32[2,256]{1,0:T(2,128)}) custom-call(s32[1]{0:T(128)} %bitcast.tile_ref, f32[1,4]{1,0:T(1,128)S(1)} %get-tuple-element.10.penalty_ref, f32[1,4]{1,0:T(1,128)S(1)} %get-tuple-element.11.power_ref, f32[16,8,128]{2,1,0:T(8,128)S(1)} %bitcast.26, ...), custom_call_target="tpu_custom_call" | custom-call | tf_op jit(solution)/shard_map/solve/pallas_call | solution.py:472
  (1 shorter events, 0.0 us)
Async XLA Ops:
  0.6 18.0 %collective-permute-start.1 = (bf16[2,2,4,64,256]{4,3,2,1,0:T(8,128)(2,1)}, bf16[2,2,4,64,256]{4,3,2,1,0:T(8,128)(2,1)S(1)}, u32[]{:S(2)}, u32[]{:S(2)}) collective-permute-start(bf16[2,2,4,64,256]{4,3,2,1,0:T(8,128)(2,1)} %param.6), channel_id=1, source_target_pairs={{0,1},{1,0},{2,3},{3,2},{4,5},{5,4},{6,7},{7,6},{8,9},{9,8},{10,11... | collective-permute-start | bytes 1572872 | tf_op jit(solution)/shard_map/ppermute | solution.py:497
  2.8 15.8 %collective-permute-start.2 = (bf16[2,2,4,64,256]{4,3,2,1,0:T(8,128)(2,1)}, bf16[2,2,4,64,256]{4,3,2,1,0:T(8,128)(2,1)S(1)}, u32[]{:S(2)}, u32[]{:S(2)}) collective-permute-start(bf16[2,2,4,64,256]{4,3,2,1,0:T(8,128)(2,1)} %param.7), channel_id=1, source_target_pairs={{0,3},{1,2},{2,1},{3,0},{4,7},{5,6},{6,5},{7,4},{8,11},{9,10},{10,... | collective-permute-start | bytes 1572872 | tf_op jit(solution)/shard_map/ppermute | solution.py:497
  5.4 1.2 %copy-start = (bf16[2,2,4,64,256]{4,3,2,1,0:T(8,128)(2,1)S(1)}, bf16[2,2,4,64,256]{4,3,2,1,0:T(8,128)(2,1)}, u32[]{:S(2)}) copy-start(bf16[2,2,4,64,256]{4,3,2,1,0:T(8,128)(2,1)} %param.7) | copy-start | bytes 1572868
  7.9 18.5 %all-to-all-start = ((bf16[16,72,256]{2,1,0:T(8,128)(2,1)}), bf16[16,72,256]{2,1,0:T(8,128)(2,1)S(1)}, u32[]{:S(2)}, u32[]{:S(2)}) async-start(bf16[16,72,256]{2,1,0:T(8,128)(2,1)} %own_gains.1), calls=%async_computation | async-start | bytes 1179648 | tf_op jit(solution)/shard_map/all_to_all | solution.py:515
  15.5 0.7 copy-start.4
  16.2 2.4 %collective-permute-start = (s32[4]{0:T(128)S(1)}, s32[4]{0:T(128)S(1)}, u32[]{:S(2)}, u32[]{:S(2)}) collective-permute-start(s32[4]{0:T(128)S(1)} %bitcast.31), channel_id=1, source_target_pairs={{0,1},{1,0},{2,3},{3,2},{4,5},{5,4},{6,7},{7,6},{8,9},{9,8},{10,11... | collective-permute-start | bytes 56 | tf_op jit(solution)/shard_map/ppermute | solution.py:497
  19.2 4.1 %collective-permute-start.3 = (bf16[16,2,16,384]{3,2,1,0:T(8,128)(2,1)S(1)}, bf16[16,2,16,384]{3,2,1,0:T(8,128)(2,1)S(1)}, u32[]{:S(2)}, u32[]{:S(2)}) collective-permute-start(bf16[16,2,16,384]{3,2,1,0:T(8,128)(2,1)S(1)} %get-tuple-element.14), channel_id=1, source_target_pairs={{0,4},{4,0},{1,5},{5,1},{2,6},{6,2},{3,7},{7,3},{8,12},{12,8},{9,1... | collective-permute-start | bytes 1179656 | tf_op jit(solution)/shard_map/ppermute | solution.py:497
  22.6 1.8 %collective-permute-start.4 = (bf16[16,2,16,384]{3,2,1,0:T(8,128)(2,1)S(1)}, bf16[16,2,16,384]{3,2,1,0:T(8,128)(2,1)S(1)}, u32[]{:S(2)}, u32[]{:S(2)}) collective-permute-start(bf16[16,2,16,384]{3,2,1,0:T(8,128)(2,1)S(1)} %get-tuple-element.15), channel_id=1, source_target_pairs={{0,4},{4,0},{1,5},{5,1},{2,6},{6,2},{3,7},{7,3},{8,12},{12,8},{9,1... | collective-permute-start | bytes 1179656 | tf_op jit(solution)/shard_map/ppermute | solution.py:497
  26.4 19.7 %all-to-all-start.1 = ((bf16[16,64,384]{2,1,0:T(8,128)(2,1)}), bf16[16,64,384]{2,1,0:T(8,128)(2,1)S(1)}, u32[]{:S(2)}, u32[]{:S(2)}) async-start(bf16[16,64,384]{2,1,0:T(8,128)(2,1)} %combine.1), calls=%async_computation.1 | async-start | bytes 1572864 | tf_op jit(solution)/shard_map/all_to_all | solution.py:529
  32.4 19.5 %collective-permute-start.6 = (bf16[2,2,4,64,256]{4,3,2,1,0:T(8,128)(2,1)S(1)}, bf16[2,2,4,64,256]{4,3,2,1,0:T(8,128)(2,1)S(1)}, u32[]{:S(2)}, u32[]{:S(2)}) collective-permute-start(bf16[2,2,4,64,256]{4,3,2,1,0:T(8,128)(2,1)S(1)} %broadcast_multiply_fusion.1.refs_0_), channel_id=1, source_target_pairs={{0,3},{1,2},{2,1},{3,0},{4,7},{5,6},{6,5},{7,4},{8,11},{9,10},{10,... | collective-permute-start | bytes 1572872 | tf_op jit(solution)/shard_map/ppermute | solution.py:497
  33.3 25.1 %collective-permute-start.7 = (bf16[2,2,4,64,256]{4,3,2,1,0:T(8,128)(2,1)S(1)}, bf16[2,2,4,64,256]{4,3,2,1,0:T(8,128)(2,1)S(1)}, u32[]{:S(2)}, u32[]{:S(2)}) collective-permute-start(bf16[2,2,4,64,256]{4,3,2,1,0:T(8,128)(2,1)S(1)} %broadcast_multiply_fusion.refs_1_), channel_id=1, source_target_pairs={{0,3},{1,2},{2,1},{3,0},{4,7},{5,6},{6,5},{7,4},{8,11},{9,10},{10,... | collective-permute-start | bytes 1572872 | tf_op jit(solution)/shard_map/ppermute | solution.py:497
  35.4 0.7 copy-start.1
  35.4 0.7 copy-start.2
  35.4 0.7 copy-start.3
  36.9 2.0 %collective-permute-start.5 = (f32[64,256]{1,0:T(8,128)S(1)}, f32[64,256]{1,0:T(8,128)S(1)}, u32[]{:S(2)}, u32[]{:S(2)}) collective-permute-start(f32[64,256]{1,0:T(8,128)S(1)} %get-tuple-element.16.mine_ref), channel_id=1, source_target_pairs={{0,4},{4,0},{1,5},{5,1},{2,6},{6,2},{3,7},{7,3},{8,12},{12,8},{9,1... | collective-permute-start | bytes 196616 | tf_op jit(solution)/shard_map/ppermute | solution.py:497
  46.9 14.8 %all-to-all-start.2 = ((f32[128,1,128]{2,1,0:T(1,128)}), f32[128,1,128]{2,1,0:T(1,128)S(1)}, u32[]{:S(2)}, u32[]{:S(2)}) async-start(f32[128,1,128]{2,1,0:T(1,128)} %bitcast.12), calls=%async_computation.2 | async-start | bytes 131072 | tf_op jit(solution)/shard_map/all_to_all | solution.py:534
